TPU v7x, 32 devices: a whole 2x2x4 slice. The times are simulated.
32 devices in a mesh: wide: 8 (over z, y), narrow: 4 (over x, core).
Axes of the slice: x: 2, y: 2, z: 4, core: 2. Of those that a mesh axis runs over, the one named last changes fastest.
Arguments:
- frames: float32 [32768, 440], P(('wide', 'narrow')), may hold values from -8 to 8
- targets: float32 [32768, 2048], P(('wide', 'narrow')), may hold values from -7 to 7
- projection: float32 [32, 440, 512], P(('wide', 'narrow')), may hold values from -0.25 to 0.25
- phases: float32 [32, 512], P(('wide', 'narrow')), may hold values from 0 to 6.283185
- block_order: int32 [32], replicated, may hold values from 0 to 31, each once
Outputs:
- residual: float32 [32768, 2048], P(('wide', 'narrow'))
- weights: float32 [2, 512, 2048], replicated
Inputs may be any that keep to these rules, and one draw needn't show every extreme that they name: `block_order`: a permutation; steps use its first 2 entries.
All inputs are finite; a program needn't handle non-finite values.
Results may differ from a plain program's by a relative error of at most 0.0003.
Values sent between devices are 32-bit elements; how exact they have to be, the bound alone decides.
No kernel may reach another device: no remote copies, remote signals or barrier semaphores. Data moves between devices by JAX's collectives and lax.ppermute only.
A program may use at most 128 MiB of HBM per device.

v0:
```python
import functools
import math

import jax
import jax.numpy as jnp
from jax import lax
from jax.experimental import pallas as pl
from jax.experimental.pallas import tpu as pltpu
from jax.sharding import PartitionSpec as P

ALL = ("wide", "narrow")
F32 = jnp.float32
BF16 = jnp.bfloat16
HIGHEST = lax.Precision.HIGHEST


BASE_OWN, BASE_OTH, CORE, FAR, PLACE, ORDER_OWN, ORDER_OTH, QUARTER_OWN, QUARTER_OTH, DEVICE = range(10)


def params(mib=24):
    return pltpu.CompilerParams(vmem_limit_bytes=mib * 1024 * 1024)


def cost(flops, nbytes):
    return pl.CostEstimate(flops=int(flops), bytes_accessed=int(nbytes), transcendentals=0)


def split(value):
    high = value.astype(BF16)
    return high, (value - high.astype(F32)).astype(BF16)


def dot_bf16(left, right):
    return jnp.dot(left, right, preferred_element_type=F32)


def dot3(left, right):
    (lh, ll), (rh, rl) = left, right
    return dot_bf16(lh, rh) + (dot_bf16(lh, rl) + dot_bf16(ll, rh))


def dot_full(left, right):
    return jnp.dot(left, right, precision=HIGHEST, preferred_element_type=F32)


TWO_PI = 2.0 * math.pi
PART_A = 6.28125
PART_B = 2.0 ** -24 * round((TWO_PI - PART_A) * 2.0 ** 24 / 2 ** 5) * 2 ** 5
PART_C = TWO_PI - PART_A - PART_B
SIN_POLY = [(-1.0) ** k / math.factorial(2 * k + 1) for k in range(7)]


def cosine(value):
    turns = jnp.floor(value * (1.0 / TWO_PI) + 0.5)
    rest = value - turns * PART_A
    rest = rest - turns * PART_B
    rest = rest - turns * PART_C
    half = rest * 0.5
    square = half * half
    poly = SIN_POLY[-1]
    for coefficient in SIN_POLY[-2::-1]:
        poly = poly * square + coefficient
    sine = half * poly
    return 1.0 - 2.0 * sine * sine


def pack_kernel(s_ref, order_ref, own_ref, oth_ref, pown_ref, poth_ref, out_ref):
    depth = own_ref.shape[1]
    wanted = order_ref[s_ref[CORE]]
    take_own = wanted == s_ref[DEVICE]
    take_oth = wanted == (s_ref[DEVICE] ^ 1)
    value = jnp.where(take_own, own_ref[0], jnp.where(take_oth, oth_ref[0], 0.0))
    phase = jnp.where(take_own, pown_ref[0], jnp.where(take_oth, poth_ref[0], 0.0))
    out_ref[0, :depth, :] = value
    tail = out_ref.shape[1] - depth
    rows = lax.broadcasted_iota(jnp.int32, (tail, out_ref.shape[2]), 0)
    out_ref[0, depth:, :] = jnp.where(rows == 0, jnp.broadcast_to(phase, rows.shape), 0.0)


def pack(scalars, block_order, own, oth, phase_own, phase_oth, padded):
    _, depth, feats = own.shape
    width = feats // 4
    block = pl.BlockSpec((1, depth, width), lambda q, s, o: (0, 0, q ^ s[QUARTER_OWN]))
    phase = pl.BlockSpec((1, 1, width), lambda q, s, o: (0, 0, q ^ s[QUARTER_OWN]))
    return pl.pallas_call(
        pack_kernel,
        out_shape=jax.ShapeDtypeStruct((4, padded, width), F32),
        grid_spec=pltpu.PrefetchScalarGridSpec(
            num_scalar_prefetch=2,
            grid=(4,),
            in_specs=[block, block, phase, phase],
            out_specs=pl.BlockSpec((1, padded, width), lambda q, s, o: (q, 0, 0)),
        ),
        compiler_params=params(),
        name="pack",
    )(scalars, block_order, own, oth, phase_own[:, None, :], phase_oth[:, None, :])


def features_kernel(quarter, s_ref, x_ref, p_ref, fh_ref, fl_ref, th_ref, tl_ref):
    depth = x_ref.shape[0]
    order = s_ref[quarter]
    turned = jnp.concatenate([p_ref[i ^ order] for i in range(4)], axis=1).T
    inner = dot_full(turned[:, :depth], x_ref[...]) + turned[:, depth : depth + 1]
    feats = math.sqrt(2.0 / turned.shape[0]) * cosine(inner)
    th_ref[...], tl_ref[...] = split(feats)
    fh_ref[...], fl_ref[...] = split(feats.T)


def features(quarter, scalars, frames_turned, blocks):
    depth, rows = frames_turned.shape
    feats = blocks.shape[0] * blocks.shape[2]
    tile = 256
    flat = pl.BlockSpec((tile, feats), lambda i, s: (i, 0))
    turned = pl.BlockSpec((feats, tile), lambda i, s: (0, i))
    return pl.pallas_call(
        functools.partial(features_kernel, quarter),
        out_shape=[jax.ShapeDtypeStruct((rows, feats), BF16)] * 2 + [jax.ShapeDtypeStruct((feats, rows), BF16)] * 2,
        grid_spec=pltpu.PrefetchScalarGridSpec(
            num_scalar_prefetch=1,
            grid=(rows // tile,),
            in_specs=[
                pl.BlockSpec((depth, tile), lambda i, s: (0, i)),
                pl.BlockSpec(blocks.shape, lambda i, s: (0, 0, 0)),
            ],
            out_specs=[flat, flat, turned, turned],
        ),
        compiler_params=params(),
        cost_estimate=cost(12 * rows * depth * feats, 4 * rows * depth + 8 * rows * feats),
        name="features",
    )(scalars, frames_turned, blocks)


def gram_kernel(kept, s_ref, mh, ml, mth, mtl, oh, ol, oth, otl, out_ref):
    order = s_ref[ORDER_OWN if kept else ORDER_OTH]
    half_row = s_ref[CORE] if kept else 1 - s_ref[CORE]
    m_is_second = half_row
    feats, _ = mth.shape
    half = feats // 2
    pieces, _, height, _ = out_ref.shape

    def put(tile, value):
        for g in range(pieces):
            out_ref[g ^ order, tile] = value[g * height : (g + 1) * height]

    top = (mth[:half], mtl[:half])
    low = (mth[half:], mtl[half:])
    left = (mh[:, :half], ml[:, :half])
    right = (mh[:, half:], ml[:, half:])
    put(0, dot3(top, left))
    put(1, dot3(low, left))
    put(2, dot3(low, right))

    def cross(th, tl, h, l):
        start = pl.multiple_of(half_row * half, half)
        side = (th[pl.ds(start, half)], tl[pl.ds(start, half)])
        put(3, dot3(side, (h[:, :half], l[:, :half])))
        put(4, dot3(side, (h[:, half:], l[:, half:])))

    @pl.when(m_is_second == 1)
    def _():
        cross(mth, mtl, oh, ol)

    @pl.when(m_is_second == 0)
    def _():
        cross(oth, otl, mh, ml)


def gram(kept, scalars, mine, other):
    rows, feats = mine[0].shape
    return pl.pallas_call(
        functools.partial(gram_kernel, kept),
        out_shape=jax.ShapeDtypeStruct((16, 5, feats // 32, feats // 2), F32),
        in_specs=[pl.BlockSpec(memory_space=pltpu.SMEM)] + [pl.BlockSpec(memory_space=pltpu.VMEM)] * 8,
        out_specs=pl.BlockSpec(memory_space=pltpu.VMEM),
        compiler_params=params(),
        cost_estimate=cost(6 * rows * feats * feats * 1.25, 16 * rows * feats),
        name="gram",
    )(scalars, *mine, *other)


def cross_kernel(base, s_ref, t_ref, ath, atl, bth, btl, *rest):
    out_ref = rest[-1]
    place, swap = s_ref[PLACE], s_ref[base] & 1
    feats = ath.shape[0]
    half = feats // 2
    width = out_ref.shape[2]
    right = split(t_ref[...])

    def rows_of(th, tl, start):
        def body(i, carry):
            at = pl.multiple_of(i * half, half)
            value = dot3((th[pl.ds(at, half), :], tl[pl.ds(at, half), :]), right)
            to = pl.ds(pl.multiple_of(start + at, half), half)
            for k in range(2):
                part = value[:, k * width : (k + 1) * width]
                if len(rest) == 2:
                    part = part + rest[0][k ^ swap, to, :]
                out_ref[k ^ swap, to, :] = part
            return carry

        lax.fori_loop(0, 2, body, 0)

    rows_of(ath, atl, place * feats)
    rows_of(bth, btl, (1 - place) * feats)


def cross(base, group, scalars, targets, mine, other, before=()):
    rows, columns = targets.shape
    feats = mine[2].shape[0]
    width = columns // 16
    whole = pl.BlockSpec((feats, rows), lambda k, s: (0, 0))
    pair = pl.BlockSpec((2, 2 * feats, width), lambda k, s: (k, 0, 0))
    return pl.pallas_call(
        functools.partial(cross_kernel, base),
        out_shape=jax.ShapeDtypeStruct((4, 2 * feats, width), F32),
        grid_spec=pltpu.PrefetchScalarGridSpec(
            num_scalar_prefetch=1,
            grid=(2,),
            in_specs=[pl.BlockSpec((rows, 2 * width), lambda k, s: (0, (s[base] >> 1) ^ (2 * group + k)))]
            + [whole] * 4
            + [pair] * len(before),
            out_specs=pair,
        ),
        compiler_params=params(),
        cost_estimate=cost(3 * rows * feats * columns, 2 * rows * columns),
        name="cross",
    )(scalars, targets, mine[2], mine[3], other[2], other[3], *before)


def unit_inverse(block):
    size, lanes = block.shape
    groups = size // 8
    lane = lax.broadcasted_iota(jnp.int32, (8, lanes), 1)
    sub = lax.broadcasted_iota(jnp.int32, (8, lanes), 0)

    def wide(column):
        return jnp.broadcast_to(column, (8, lanes))

    def turn(i, carry):
        rows, pivots = list(carry[0]), list(carry[1])
        before = list(rows)
        top_pivots = pivots[0]
        for j in range(0, 8, 2):
            pair = (lane == j) | (lane == j + 1)
            top = rows[0]
            col_a, col_b = wide(top[:, j : j + 1]), wide(top[:, j + 1 : j + 2])
            a, b, c = wide(col_a[j : j + 1]), wide(col_a[j + 1 : j + 2]), wide(col_b[j + 1 : j + 2])
            row_a, row_b = wide(top[j : j + 1]), wide(top[j + 1 : j + 2])
            inv_a = 1.0 / a
            inv_c = a * (1.0 / (a * c - b * b))
            link = b * inv_a
            use_a = jnp.where(lane == j, 1.0, jnp.where(lane == j + 1, 0.0, row_a))
            use_b = jnp.where(lane == j, -link, jnp.where(lane == j + 1, 1.0, row_b - link * row_a))
            m_a = jnp.where(sub > j, col_a * inv_a, 0.0)
            m_b = jnp.where(sub > j + 1, (col_b - m_a * b) * inv_c, 0.0)
            unit = jnp.where(pair & (lane == sub), 1.0, 0.0)
            rows[0] = jnp.where(pair, unit, top) - m_a * use_a - m_b * use_b
            top_pivots = jnp.where(sub == j, a, jnp.where(sub == j + 1, c - link * b, top_pivots))
            for g in range(1, groups):
                m_a = wide(rows[g][:, j : j + 1]) * inv_a
                m_b = (wide(rows[g][:, j + 1 : j + 2]) - m_a * b) * inv_c
                rows[g] = jnp.where(pair, 0.0, rows[g]) - m_a * use_a - m_b * use_b
        for g in range(1, groups):
            rows[g] = jnp.where(g < groups - i, rows[g], before[g])
        rows = [pltpu.roll(r, lanes - 8, 1) for r in rows]
        return tuple(rows[1:] + rows[:1]), tuple(pivots[1:] + [top_pivots])

    start = tuple(block[8 * g : 8 * g + 8] for g in range(groups))
    rows, pivots = lax.fori_loop(0, groups, turn, (start, start))
    scaled = [
        jnp.where(lane <= sub + 8 * g, rows[g] * lax.rsqrt(pivots[g]), 0.0) for g in range(groups)
    ]
    return jnp.concatenate(scaled, axis=0)


def eliminate(m_ref, start, size):
    total = m_ref.shape[0]
    here = slice(start, start + size)
    inverse = unit_inverse(m_ref[here, here])
    if start:
        m_ref[here, :start] = dot_full(inverse, m_ref[here, :start])
    if start + size < total:
        below = slice(start + size, total)
        panel = lax.dot_general(
            m_ref[below, here], inverse, (((1,), (1,)), ((), ())), precision=HIGHEST, preferred_element_type=F32
        )
        m_ref[here, below] = dot_full(inverse, m_ref[here, below])
        m_ref[below, here] = jnp.zeros((total - start - size, size), F32)
        m_ref[here, here] = inverse
        m_ref[below, :] = m_ref[below, :] - dot_full(panel, m_ref[here, :])
    else:
        m_ref[here, here] = inverse


def assemble_kernel(s_ref, g_ref, a_ref, side_ref):
    order = s_ref[ORDER_OWN]
    pieces, _, height, half = g_ref.shape
    for g in range(pieces):
        piece = g_ref[g ^ order]
        here = slice(g * height, (g + 1) * height)
        there = slice(half + g * height, half + (g + 1) * height)
        a_ref[here, :half] = piece[0]
        a_ref[there, :half] = piece[1]
        a_ref[there, half:] = piece[2]
        side_ref[here, :half] = piece[3]
        side_ref[here, half:] = piece[4]
    a_ref[:half, half:] = a_ref[half:, :half].T
    whole = a_ref[...]
    eye = lax.broadcasted_iota(jnp.int32, whole.shape, 0) == lax.broadcasted_iota(jnp.int32, whole.shape, 1)
    diagonal = jnp.where(eye, whole, 0.0)
    damping = 0.1 * jnp.sum(diagonal) / whole.shape[0]
    a_ref[...] = whole + jnp.where(eye, damping, 0.0)
    eliminate(a_ref, 0, whole.shape[0] // 4)


def assemble(order, pieces):
    half = pieces.shape[3]
    return pl.pallas_call(
        assemble_kernel,
        out_shape=[jax.ShapeDtypeStruct((2 * half, 2 * half), F32), jax.ShapeDtypeStruct((half, 2 * half), F32)],
        in_specs=[pl.BlockSpec(memory_space=pltpu.SMEM), pl.BlockSpec(memory_space=pltpu.VMEM)],
        out_specs=[pl.BlockSpec(memory_space=pltpu.VMEM)] * 2,
        compiler_params=params(),
        cost_estimate=cost(1e10, 4e6),
        name="assemble",
    )(order, pieces)


def factor_kernel(step, m_ref, out_ref):
    out_ref[...] = m_ref[...]
    eliminate(out_ref, step * (m_ref.shape[0] // 4), m_ref.shape[0] // 4)
    if step == 3:
        whole = out_ref[...]
        low = lax.broadcasted_iota(jnp.int32, whole.shape, 0) >= lax.broadcasted_iota(jnp.int32, whole.shape, 1)
        whole = jnp.where(low, whole, 0.0)
        out_ref[...] = dot_full(whole.T, whole)


def factor(step, matrix):
    return pl.pallas_call(
        functools.partial(factor_kernel, step),
        out_shape=jax.ShapeDtypeStruct(matrix.shape, F32),
        in_specs=[pl.BlockSpec(memory_space=pltpu.VMEM)],
        out_specs=pl.BlockSpec(memory_space=pltpu.VMEM),
        compiler_params=params(),
        cost_estimate=cost(1e10, 4e6),
        name="factor",
    )(matrix)


def couple_kernel(s_ref, own_ref, oth_ref, gown_ref, goth_ref, out_ref):
    core = s_ref[CORE]
    half = gown_ref.shape[0]
    second = jnp.where(core == 1, own_ref[...], oth_ref[...])
    top = jnp.where(core == 0, gown_ref[...], goth_ref[...])
    low = jnp.where(core == 0, goth_ref[...], gown_ref[...])
    out_ref[...] = dot_full(second[:, :half], top) + dot_full(second[:, half:], low)


def couple(core, own, oth, side_own, side_oth):
    return pl.pallas_call(
        couple_kernel,
        out_shape=jax.ShapeDtypeStruct(own.shape, F32),
        in_specs=[pl.BlockSpec(memory_space=pltpu.SMEM)] + [pl.BlockSpec(memory_space=pltpu.VMEM)] * 4,
        compiler_params=params(),
        name="couple",
    )(core, own, oth, side_own, side_oth)


def solve_kernel(s_ref, own_ref, oth_ref, b_ref, c_ref, out_ref, one_ref):
    core, far = s_ref[CORE], s_ref[FAR]
    feats = own_ref.shape[0]
    half = feats // 2
    width = c_ref.shape[2]

    def columns_of(step):
        start = pl.multiple_of((step ^ far) * feats, feats)
        return jnp.concatenate([c_ref[k, pl.ds(start, feats), :] for k in range(2)], axis=1)

    right = columns_of(0)

    def first(i, carry):
        here = pl.ds(pl.multiple_of(i * half, half), half)
        one = dot_full(jnp.where(core == 0, own_ref[here, :], oth_ref[here, :]), right)
        one_ref[here, :] = one
        for k in range(2):
            out_ref[k, here, :] = one[:, k * width : (k + 1) * width]
        return carry

    lax.fori_loop(0, 2, first, 0)
    right_two = jnp.concatenate([columns_of(1), one_ref[...]], axis=0)

    def second(i, carry):
        here = pl.ds(pl.multiple_of(i * half, half), half)
        there = pl.ds(pl.multiple_of(feats + i * half, half), half)
        left = jnp.where(core == 0, oth_ref[here, :], own_ref[here, :])
        two = dot_full(jnp.concatenate([left, -b_ref[here, :]], axis=1), right_two)
        for k in range(2):
            out_ref[k, there, :] = two[:, k * width : (k + 1) * width]
        return carry

    lax.fori_loop(0, 2, second, 0)


def solve(scalars, own, oth, coupling, crossed):
    count, height, width = crossed.shape
    feats = own.shape[0]
    whole = pl.BlockSpec((feats, feats), lambda k, s: (0, 0))
    pair = pl.BlockSpec((2, height, width), lambda k, s: (k, 0, 0))
    return pl.pallas_call(
        solve_kernel,
        out_shape=jax.ShapeDtypeStruct(crossed.shape, F32),
        grid_spec=pltpu.PrefetchScalarGridSpec(
            num_scalar_prefetch=1,
            grid=(count // 2,),
            in_specs=[whole] * 3 + [pair],
            out_specs=pair,
            scratch_shapes=[pltpu.VMEM((feats, 2 * width), F32)],
        ),
        compiler_params=params(),
        cost_estimate=cost(36 * feats * feats * count * width, 8 * count * height * width),
        name="solve",
    )(scalars, own, oth, coupling, crossed)


def residual_kernel(base, s_ref, t_ref, ah, al, bh, bl, w_in, *rest):
    r_ref, w_ref = rest[-2:]
    swap, core = s_ref[base] & 1, s_ref[CORE]
    rows, feats = ah.shape
    half = rows // 2

    def take(step):
        start = pl.multiple_of(step * feats, feats)
        return jnp.concatenate([w_in[i ^ swap, pl.ds(start, feats), :] for i in range(2)], axis=1)

    mine, other = take(core), take(1 - core)
    w_ref[core], w_ref[1 - core] = mine, other
    (mh, ml), (oh, ol) = split(mine), split(other)

    def body(i, carry):
        here = pl.ds(pl.multiple_of(i * half, half), half)
        fitted = dot3((ah[here, :], al[here, :]), (mh, ml)) + dot3((bh[here, :], bl[here, :]), (oh, ol))
        r_ref[here, :] = t_ref[here, :] - fitted
        return carry

    lax.fori_loop(0, 2, body, 0)


def residual_part(base, group, scalars, targets, mine, other, weights, before):
    rows, columns = targets.shape
    feats = mine[0].shape[1]
    _, height, width = weights.shape
    whole = pl.BlockSpec((rows, feats), lambda k, s: (0, 0))
    block = pl.BlockSpec((rows, 2 * width), lambda k, s: (0, (s[base] >> 1) ^ (2 * group + k)))
    anywhere = pl.BlockSpec(memory_space=pl.ANY)
    return pl.pallas_call(
        functools.partial(residual_kernel, base),
        out_shape=[
            jax.ShapeDtypeStruct((rows, columns), F32),
            jax.ShapeDtypeStruct((2, feats, columns), F32),
        ],
        grid_spec=pltpu.PrefetchScalarGridSpec(
            num_scalar_prefetch=1,
            grid=(2,),
            in_specs=[block]
            + [whole] * 4
            + [pl.BlockSpec((2, height, width), lambda k, s: (k, 0, 0))]
            + [anywhere] * len(before),
            out_specs=[
                block,
                pl.BlockSpec((2, feats, 2 * width), lambda k, s: (0, 0, (s[base] >> 1) ^ (2 * group + k))),
            ],
        ),
        input_output_aliases={7: 0, 8: 1} if before else {},
        compiler_params=params(),
        cost_estimate=cost(3 * rows * feats * columns, 3 * rows * columns),
        name="residual",
    )(scalars, targets, mine[0], mine[1], other[0], other[1], weights, *before)


def ints(*values):
    return jnp.stack([jnp.asarray(v, jnp.int32) for v in values])


def per_device(count, frames, targets, projection, phases, block_order):
    n_bits = count.bit_length() - 1
    device = lax.axis_index(ALL)
    bit = [(device >> k) & 1 for k in range(n_bits)]
    core = bit[0]
    one = jnp.where(core == 0, bit[1], bit[2])
    two = jnp.where(core == 0, bit[2], bit[1])
    near, far = bit[3], bit[4]
    more = [1 << k for k in range(5, n_bits)]

    def exchange(value, even, odd=None):
        odd = even if odd is None else odd
        pairs = [(i, i ^ (odd if i & 1 else even)) for i in range(count)]
        return lax.ppermute(value, ALL, pairs)

    def flood(value, masks):
        for mask in masks:
            value = value + exchange(value, mask)
        return value

    scalars = ints(
        core * 8 + one * 4 + two * 2 + near,
        (1 - core) * 8 + two * 4 + one * 2 + near,
        core,
        far,
        far ^ core,
        one * 8 + two * 4 + near * 2 + far,
        two * 8 + one * 4 + near * 2 + far,
        one * 2 + two,
        two * 2 + one,
        device,
    )

    projection_oth, phases_oth = exchange(projection, 1), exchange(phases, 1)
    padded = (projection.shape[1] // 8 + 1) * 8
    blocks = pack(scalars, block_order, projection, projection_oth, phases, phases_oth, padded)
    part = blocks[:2] + exchange(blocks[2:], 2, 4)
    part = part[:1] + exchange(part[1:], 4, 2)
    part = flood(part, [8, 16] + more)
    part = jnp.concatenate([part, exchange(part, 4, 2)])
    blocks = jnp.concatenate([part, exchange(part, 2, 4)])
    blocks_oth = exchange(blocks, 1)
    mine = features(QUARTER_OWN, scalars, frames.T, blocks)
    other = features(QUARTER_OTH, scalars, frames.T, blocks_oth)

    def after(done, sides):
        gated = lax.optimization_barrier([done, *sides[0], *sides[1]])
        return gated[1:5], gated[5:]

    sides = mine, other
    gram_sent = gram(False, scalars, other, mine)
    gram_came = exchange(gram_sent, 1)
    sides = after(gram_sent, sides)
    sent = cross(BASE_OTH, 1, scalars, targets, *sides)
    came_b = exchange(sent, 1)
    sides = after(sent, sides)
    pieces = gram(True, scalars, *sides) + gram_came
    sides = after(pieces, sides)
    sent = cross(BASE_OTH, 0, scalars, targets, *sides)
    came_a = exchange(sent, 1)
    sides = after(sent, sides)
    moving = cross(BASE_OWN, 1, scalars, targets, *sides, (came_b,))
    sides = after(moving, sides)
    staying = cross(BASE_OWN, 0, scalars, targets, *sides, (came_a,))

    moved = exchange(pieces[8:], 2, 4)
    pieces = pieces[:8] + moved
    pieces = pieces[:4] + exchange(pieces[4:], 4, 2)
    pieces, staying = lax.optimization_barrier([pieces, staying])
    pieces = pieces[:2] + exchange(pieces[2:], 8)
    pieces = pieces[:1] + exchange(pieces[1:], 16)
    pieces = flood(pieces, more)
    for masks in ((16,), (8,), (4, 2), (2, 4)):
        pieces = jnp.concatenate([pieces, exchange(pieces, *masks)])

    moved = exchange(moving, 2, 4)
    crossed = staying + moved
    crossed = crossed[:2] + exchange(crossed[2:], 4, 2)
    crossed = crossed[:1] + exchange(crossed[1:], 8)
    feats = crossed.shape[1] // 2
    crossed = crossed[:, :feats] + exchange(crossed[:, feats:], 16)
    crossed = flood(crossed, more)
    crossed = jnp.concatenate([crossed, exchange(crossed, 16)], axis=1)
    crossed = jnp.concatenate([crossed, exchange(crossed, 8)])
    crossed = jnp.concatenate([crossed, exchange(crossed, 4, 2)])

    matrix, side = assemble(scalars, pieces)
    side_oth = exchange(side, 1)
    for step in (1, 2, 3):
        matrix = factor(step, matrix)
    inverse = matrix
    inverse_oth = exchange(inverse, 1)
    coupling = couple(scalars, inverse, inverse_oth, side, side_oth)
    weights = solve(scalars, inverse, inverse_oth, coupling, crossed)
    weights_b = exchange(weights, 2, 4)
    outs = ()
    for group, part in ((0, weights), (1, weights_b)):
        part_oth = exchange(part, 1)
        for base, value in ((BASE_OWN, part), (BASE_OTH, part_oth)):
            outs = residual_part(base, group, scalars, targets, mine, other, value, tuple(outs))
    return tuple(outs)


def solution(mesh):
    count = math.prod(mesh.shape.values())

    def body(*arrays):
        return per_device(count, *arrays)

    return jax.shard_map(
        body,
        mesh=mesh,
        in_specs=(
            P(ALL, None),
            P(ALL, None),
            P(ALL, None, None),
            P(ALL, None),
            P(),
        ),
        out_specs=(P(ALL, None), P()),
        check_vma=False,
    )
```

profile of v0, /device:TPU:0, one launch (start us, length us, event | category | flops | bytes accessed | tf_op | source)
XLA Modules:
  0.0 293.0 jit_solution(8019275932393313116)
XLA Ops:
  1.4 2.1 collective-permute-done.1
  7.1 2.9 collective-permute-start.2
  10.0 6.5 %collective-permute-done.2 = f32[2,448,128]{2,1,0:T(8,128)S(1)} collective-permute-done((f32[2,448,128]{2,1,0:T(8,128)S(1)}, f32[2,448,128]{2,1,0:T(8,128)S(1)}, u32[]{:S(2)}, u32[]{:S(2)}) %collective-permute-start.2) | collective-permute-done | bytes 458784 | tf_op jit(solution)/shard_map/ppermute | solution.py:498
  16.6 2.1 collective-permute-start.3
  18.7 4.0 %collective-permute-done.3 = f32[1,448,128]{2,1,0:T(8,128)S(1)} collective-permute-done((f32[1,448,128]{2,1,0:T(8,128)S(1)}, f32[1,448,128]{2,1,0:T(8,128)S(1)}, u32[]{:S(2)}, u32[]{:S(2)}) %collective-permute-start.3) | collective-permute-done | bytes 229408 | tf_op jit(solution)/shard_map/ppermute | solution.py:498
  22.7 2.1 collective-permute-start.4
  24.9 4.2 %collective-permute-done.4 = f32[1,448,128]{2,1,0:T(8,128)S(1)} collective-permute-done((f32[1,448,128]{2,1,0:T(8,128)S(1)}, f32[1,448,128]{2,1,0:T(8,128)S(1)}, u32[]{:S(2)}, u32[]{:S(2)}) %collective-permute-start.4) | collective-permute-done | bytes 229408 | tf_op jit(solution)/shard_map/ppermute | solution.py:498
  29.1 3.1 %collective-permute-start.5 = (f32[1,448,128]{2,1,0:T(8,128)S(1)}, f32[1,448,128]{2,1,0:T(8,128)S(1)}, u32[]{:S(2)}, u32[]{:S(2)}) collective-permute-start(f32[1,448,128]{2,1,0:T(8,128)S(1)} %add.101), channel_id=1, source_target_pairs={{0,16},{1,17},{2,18},{3,19},{4,20},{5,21},{6,22},{7,23},{8,24},{9,... | collective-permute-start | bytes 688136 | tf_op jit(solution)/shard_map/ppermute | solution.py:498
  32.2 8.2 %collective-permute-done.5 = f32[1,448,128]{2,1,0:T(8,128)S(1)} collective-permute-done((f32[1,448,128]{2,1,0:T(8,128)S(1)}, f32[1,448,128]{2,1,0:T(8,128)S(1)}, u32[]{:S(2)}, u32[]{:S(2)}) %collective-permute-start.5) | collective-permute-done | bytes 229408 | tf_op jit(solution)/shard_map/ppermute | solution.py:498
  40.4 1.3 collective-permute-start.6
  41.6 4.8 %collective-permute-done.6 = f32[1,448,128]{2,1,0:T(8,128)S(1)} collective-permute-done((f32[1,448,128]{2,1,0:T(8,128)S(1)}, f32[1,448,128]{2,1,0:T(8,128)S(1)}, u32[]{:S(2)}, u32[]{:S(2)}) %collective-permute-start.6) | collective-permute-done | bytes 229408 | tf_op jit(solution)/shard_map/ppermute | solution.py:498
  47.7 7.3 %collective-permute-done.7 = f32[2,448,128]{2,1,0:T(8,128)S(1)} collective-permute-done((f32[2,448,128]{2,1,0:T(8,128)S(1)}, f32[2,448,128]{2,1,0:T(8,128)S(1)}, u32[]{:S(2)}, u32[]{:S(2)}) %collective-permute-start.7) | collective-permute-done | bytes 458784 | tf_op jit(solution)/shard_map/ppermute | solution.py:498
  55.2 7.8 %features.2 = (bf16[1024,512]{1,0:T(8,128)(2,1)S(1)}, bf16[1024,512]{1,0:T(8,128)(2,1)S(1)}, bf16[512,1024]{1,0:T(8,128)(2,1)S(1)}, bf16[512,1024]{1,0:T(8,128)(2,1)S(1)}) custom-call(s32[10]{0:T(128)S(1)} %stack.43.s_ref, f32[440,1024]{1,0:T(8,128)S(1)} %bitcast.17, f32[4,448,128]{2,1,0:T(8,128)S(1)} %pad_maximum_fusion.2.p_ref), custom_call_target="tpu_custom_call" | custom-call | flops 2768240640 | bytes 5996544 | tf_op jit(solution)/shard_map/features/pallas_call | solution.py:115
  63.1 7.8 %features.3 = (bf16[1024,512]{1,0:T(8,128)(2,1)S(1)}, bf16[1024,512]{1,0:T(8,128)(2,1)S(1)}, bf16[512,1024]{1,0:T(8,128)(2,1)S(1)}, bf16[512,1024]{1,0:T(8,128)(2,1)S(1)}) custom-call(s32[10]{0:T(128)S(1)} %stack.43.s_ref, f32[440,1024]{1,0:T(8,128)S(1)} %bitcast.18, f32[4,448,128]{2,1,0:T(8,128)S(1)} %collective-permute-done.8.p_ref), custom_call_target="tpu_custom_call" | custom-call | flops 2768240640 | bytes 5996544 | tf_op jit(solution)/shard_map/features/pallas_call | solution.py:115
  70.9 3.0 %gram.2 = f32[16,5,16,256]{3,2,1,0:T(8,128)S(1)} custom-call(s32[10]{0:T(128)S(1)} %stack.43.s_ref, bf16[1024,512]{1,0:T(8,128)(2,1)S(1)} %get-tuple-element.68.mh.oh.bh, bf16[1024,512]{1,0:T(8,128)(2,1)S(1)} %get-tuple-element.69.ml.ol.bl, bf16[512,1024]{1,0:T(8,128)(2,1)S(1)} %get-tuple-element.82.mth.bth.oth, ...), custom_call_target="tpu_custom_call" | custom-call | flops 2013265920 | bytes 8388608 | tf_op jit(solution)/shard_map/gram/pallas_call | solution.py:170
  74.4 6.0 %cross.4 = f32[4,1024,128]{2,1,0:T(8,128)S(1)} custom-call(s32[10]{0:T(128)S(1)} %stack.43.s_ref, f32[1024,2048]{1,0:T(8,128)S(1)} %bitcast.14, bf16[512,1024]{1,0:T(8,128)(2,1)S(1)} %get-tuple-element.80.oth.ath.mth, bf16[512,1024]{1,0:T(8,128)(2,1)S(1)} %get-tuple-element.81.otl.atl.mtl, bf16[512,1024]{1,0:T(8,128)(2,1)S(1)} %get-tuple-element.82.mth.bth.oth, ...), custom_call_target="tpu_custom_call" | custom-call | flops 3221225472 | bytes 4194304 | tf_op jit(solution)/shard_map/cross/pallas_call | solution.py:213
  80.5 3.1 %gram.3 = f32[16,5,16,256]{3,2,1,0:T(8,128)S(1)} custom-call(s32[10]{0:T(128)S(1)} %stack.43.s_ref, bf16[1024,512]{1,0:T(8,128)(2,1)S(1)} %get-tuple-element.64.oh.mh.ah, bf16[1024,512]{1,0:T(8,128)(2,1)S(1)} %get-tuple-element.65.ol.ml.al, bf16[512,1024]{1,0:T(8,128)(2,1)S(1)} %get-tuple-element.80.oth.ath.mth, ...), custom_call_target="tpu_custom_call" | custom-call | flops 2013265920 | bytes 8388608 | tf_op jit(solution)/shard_map/gram/pallas_call | solution.py:170
  83.9 5.9 %cross.5 = f32[4,1024,128]{2,1,0:T(8,128)S(1)} custom-call(s32[10]{0:T(128)S(1)} %stack.43.s_ref, f32[1024,2048]{1,0:T(8,128)S(1)} %bitcast.14, bf16[512,1024]{1,0:T(8,128)(2,1)S(1)} %get-tuple-element.80.oth.ath.mth, bf16[512,1024]{1,0:T(8,128)(2,1)S(1)} %get-tuple-element.81.otl.atl.mtl, bf16[512,1024]{1,0:T(8,128)(2,1)S(1)} %get-tuple-element.82.mth.bth.oth, ...), custom_call_target="tpu_custom_call" | custom-call | flops 3221225472 | bytes 4194304 | tf_op jit(solution)/shard_map/cross/pallas_call | solution.py:213
  91.7 9.4 %collective-permute-done.10 = f32[8,5,16,256]{3,2,1,0:T(8,128)S(1)} collective-permute-done((f32[8,5,16,256]{3,2,1,0:T(8,128)S(1)}, f32[8,5,16,256]{3,2,1,0:T(8,128)S(1)}, u32[]{:S(2)}, u32[]{:S(2)}) %collective-permute-start.10) | collective-permute-done | bytes 655392 | tf_op jit(solution)/shard_map/ppermute | solution.py:498
  102.5 6.0 %cross.6 = f32[4,1024,128]{2,1,0:T(8,128)S(1)} custom-call(s32[10]{0:T(128)S(1)} %stack.43.s_ref, f32[1024,2048]{1,0:T(8,128)S(1)} %bitcast.14, bf16[512,1024]{1,0:T(8,128)(2,1)S(1)} %get-tuple-element.80.oth.ath.mth, bf16[512,1024]{1,0:T(8,128)(2,1)S(1)} %get-tuple-element.81.otl.atl.mtl, bf16[512,1024]{1,0:T(8,128)(2,1)S(1)} %get-tuple-element.82.mth.bth.oth, ...), custom_call_target="tpu_custom_call" | custom-call | flops 3221225472 | bytes 4194304 | tf_op jit(solution)/shard_map/cross/pallas_call | solution.py:213
  108.5 1.6 collective-permute-start.22
  110.1 6.0 %cross.7 = f32[4,1024,128]{2,1,0:T(8,128)S(1)} custom-call(s32[10]{0:T(128)S(1)} %stack.43.s_ref, f32[1024,2048]{1,0:T(8,128)S(1)} %bitcast.14, bf16[512,1024]{1,0:T(8,128)(2,1)S(1)} %get-tuple-element.80.oth.ath.mth, bf16[512,1024]{1,0:T(8,128)(2,1)S(1)} %get-tuple-element.81.otl.atl.mtl, bf16[512,1024]{1,0:T(8,128)(2,1)S(1)} %get-tuple-element.82.mth.bth.oth, ...), custom_call_target="tpu_custom_call" | custom-call | flops 3221225472 | bytes 4194304 | tf_op jit(solution)/shard_map/cross/pallas_call | solution.py:213
  116.8 4.7 %collective-permute-done.14 = f32[2,5,16,256]{3,2,1,0:T(8,128)S(1)} collective-permute-done((f32[2,5,16,256]{3,2,1,0:T(8,128)S(1)}, f32[2,5,16,256]{3,2,1,0:T(8,128)S(1)}, u32[]{:S(2)}, u32[]{:S(2)}) %collective-permute-start.14) | collective-permute-done | bytes 163872 | tf_op jit(solution)/shard_map/ppermute | solution.py:498
  121.5 2.1 collective-permute-start.15
  123.6 4.4 %collective-permute-done.15 = f32[1,5,16,256]{3,2,1,0:T(8,128)S(1)} collective-permute-done((f32[1,5,16,256]{3,2,1,0:T(8,128)S(1)}, f32[1,5,16,256]{3,2,1,0:T(8,128)S(1)}, u32[]{:S(2)}, u32[]{:S(2)}) %collective-permute-start.15) | collective-permute-done | bytes 81952 | tf_op jit(solution)/shard_map/ppermute | solution.py:498
  129.1 4.5 %collective-permute-done.16 = f32[1,5,16,256]{3,2,1,0:T(8,128)S(1)} collective-permute-done((f32[1,5,16,256]{3,2,1,0:T(8,128)S(1)}, f32[1,5,16,256]{3,2,1,0:T(8,128)S(1)}, u32[]{:S(2)}, u32[]{:S(2)}) %collective-permute-start.16) | collective-permute-done | bytes 81952 | tf_op jit(solution)/shard_map/ppermute | solution.py:498
  133.6 2.3 collective-permute-start.17
  135.9 3.3 %collective-permute-done.17 = f32[2,5,16,256]{3,2,1,0:T(8,128)S(1)} collective-permute-done((f32[2,5,16,256]{3,2,1,0:T(8,128)S(1)}, f32[2,5,16,256]{3,2,1,0:T(8,128)S(1)}, u32[]{:S(2)}, u32[]{:S(2)}) %collective-permute-start.17) | collective-permute-done | bytes 163872 | tf_op jit(solution)/shard_map/ppermute | solution.py:498
  140.1 1.6 collective-permute-start.23
  141.7 7.6 %collective-permute-done.18 = f32[4,5,16,256]{3,2,1,0:T(8,128)S(1)} collective-permute-done((f32[4,5,16,256]{3,2,1,0:T(8,128)S(1)}, f32[4,5,16,256]{3,2,1,0:T(8,128)S(1)}, u32[]{:S(2)}, u32[]{:S(2)}) %collective-permute-start.18) | collective-permute-done | bytes 327712 | tf_op jit(solution)/shard_map/ppermute | solution.py:498
  149.9 10.1 %collective-permute-done.19 = f32[8,5,16,256]{3,2,1,0:T(8,128)S(1)} collective-permute-done((f32[8,5,16,256]{3,2,1,0:T(8,128)S(1)}, f32[8,5,16,256]{3,2,1,0:T(8,128)S(1)}, u32[]{:S(2)}, u32[]{:S(2)}) %collective-permute-start.19) | collective-permute-done | bytes 655392 | tf_op jit(solution)/shard_map/ppermute | solution.py:498
  160.0 4.6 %collective-permute-done.23 = f32[2,1024,128]{2,1,0:T(8,128)S(1)} collective-permute-done((f32[2,1024,128]{2,1,0:T(8,128)S(1)}, f32[2,1024,128]{2,1,0:T(8,128)S(1)}, u32[]{:S(2)}, u32[]{:S(2)}) %collective-permute-start.23) | collective-permute-done | bytes 1048608 | tf_op jit(solution)/shard_map/ppermute | solution.py:498
  164.8 1.3 collective-permute-start.24
  166.1 11.5 %assemble.1 = (f32[512,512]{1,0:T(8,128)S(1)}, f32[256,512]{1,0:T(8,128)S(1)}) custom-call(s32[10]{0:T(128)S(1)} %stack.43.s_ref, f32[16,5,16,256]{3,2,1,0:T(8,128)S(1)} %constant_dynamic-update-slice_fusion.g_ref), custom_call_target="tpu_custom_call" | custom-call | flops 10000000000 | bytes 4000000 | tf_op jit(solution)/shard_map/assemble/pallas_call | solution.py:318
  177.7 3.0 %collective-permute-start.25 = (f32[1,512,128]{2,1,0:T(8,128)S(1)}, f32[1,512,128]{2,1,0:T(8,128)S(1)}, u32[]{:S(2)}, u32[]{:S(2)}) collective-permute-start(f32[1,512,128]{2,1,0:T(8,128)S(1)} %slice.87), channel_id=1, source_target_pairs={{0,16},{1,17},{2,18},{3,19},{4,20},{5,21},{6,22},{7,23},{8,24},{9,... | collective-permute-start | bytes 786440 | tf_op jit(solution)/shard_map/ppermute | solution.py:498
  180.7 10.6 %factor.3.m_ref = f32[512,512]{1,0:T(8,128)S(1)} custom-call(f32[512,512]{1,0:T(8,128)S(1)} %get-tuple-element.85.m_ref), custom_call_target="tpu_custom_call" | custom-call | flops 10000000000 | bytes 4000000 | tf_op jit(solution)/shard_map/factor/pallas_call | solution.py:340
  192.0 10.4 %factor.4.m_ref = f32[512,512]{1,0:T(8,128)S(1)} custom-call(f32[512,512]{1,0:T(8,128)S(1)} %factor.3.m_ref), custom_call_target="tpu_custom_call" | custom-call | flops 10000000000 | bytes 4000000 | tf_op jit(solution)/shard_map/factor/pallas_call | solution.py:340
  202.5 3.0 %collective-permute-start.27 = (f32[1,1024,128]{2,1,0:T(8,128)S(1)}, f32[1,1024,128]{2,1,0:T(8,128)S(1)}, u32[]{:S(2)}, u32[]{:S(2)}) collective-permute-start(f32[1,1024,128]{2,1,0:T(8,128)S(1)} %pad_maximum_fusion.4), channel_id=1, source_target_pairs={{0,8},{1,9},{2,10},{3,11},{4,12},{5,13},{6,14},{7,15},{8,0},{9,1},... | collective-permute-start | bytes 1572872 | tf_op jit(solution)/shard_map/ppermute | solution.py:498
  205.5 11.8 %factor.5.own_ref = f32[512,512]{1,0:T(8,128)S(1)} custom-call(f32[512,512]{1,0:T(8,128)S(1)} %factor.4.m_ref), custom_call_target="tpu_custom_call" | custom-call | flops 10000000000 | bytes 4000000 | tf_op jit(solution)/shard_map/factor/pallas_call | solution.py:340
  218.3 2.5 collective-permute-done.21.goth_ref
  220.8 2.4 couple.1.b_ref
  223.2 9.1 %collective-permute-done.28 = f32[2,1024,128]{2,1,0:T(8,128)S(1)} collective-permute-done((f32[2,1024,128]{2,1,0:T(8,128)S(1)}, f32[2,1024,128]{2,1,0:T(8,128)S(1)}, u32[]{:S(2)}, u32[]{:S(2)}) %collective-permute-start.28) | collective-permute-done | bytes 1048608 | tf_op jit(solution)/shard_map/ppermute | solution.py:498
  232.5 8.2 %solve.1.w_in = f32[4,1024,128]{2,1,0:T(8,128)S(1)} custom-call(s32[10]{0:T(128)S(1)} %stack.43.s_ref, f32[512,512]{1,0:T(8,128)S(1)} %factor.5.own_ref, f32[512,512]{1,0:T(8,128)S(1)} %collective-permute-done.20.oth_ref, f32[512,512]{1,0:T(8,128)S(1)} %couple.1.b_ref, f32[4,1024,128]{2,1,0:T(8,128)S(1)} %pad_maximum_fusion.c_ref), custom_call_target="tpu_custom_call" | custom-call | flops 4831838208 | bytes 4194304 | tf_op jit(solution)/shard_map/solve/pallas_call | solution.py:410
  241.3 25.5 %collective-permute-done.29.w_in = f32[4,1024,128]{2,1,0:T(8,128)S(1)} collective-permute-done((f32[4,1024,128]{2,1,0:T(8,128)S(1)}, f32[4,1024,128]{2,1,0:T(8,128)S(1)}, u32[]{:S(2)}, u32[]{:S(2)}) %collective-permute-start.29) | collective-permute-done | bytes 2097184 | tf_op jit(solution)/shard_map/ppermute | solution.py:498
  266.8 6.5 %residual.4 = (f32[1024,2048]{1,0:T(8,128)}, f32[2,512,2048]{2,1,0:T(8,128)}) custom-call(s32[10]{0:T(128)S(1)} %stack.43.s_ref, f32[1024,2048]{1,0:T(8,128)S(1)} %bitcast.14, bf16[1024,512]{1,0:T(8,128)(2,1)S(1)} %get-tuple-element.64.oh.mh.ah, bf16[1024,512]{1,0:T(8,128)(2,1)S(1)} %get-tuple-element.65.ol.ml.al, ...), custom_call_target="tpu_custom_call" | custom-call | flops 3221225472 | bytes 6291456 | tf_op jit(solution)/shard_map/residual/pallas_call | solution.py:456
  273.3 6.5 %residual.5 = (f32[1024,2048]{1,0:T(8,128)}, f32[2,512,2048]{2,1,0:T(8,128)}) custom-call(s32[10]{0:T(128)S(1)} %stack.43.s_ref, f32[1024,2048]{1,0:T(8,128)S(1)} %bitcast.14, bf16[1024,512]{1,0:T(8,128)(2,1)S(1)} %get-tuple-element.64.oh.mh.ah, bf16[1024,512]{1,0:T(8,128)(2,1)S(1)} %get-tuple-element.65.ol.ml.al, ...), custom_call_target="tpu_custom_call", output_to_operand_aliasing={{0}: (7, {}), {1}: (8, {})} | custom-call | flops 3221225472 | bytes 6291456 | tf_op jit(solution)/shard_map/residual/pallas_call | solution.py:456
  279.9 6.6 %residual.6 = (f32[1024,2048]{1,0:T(8,128)}, f32[2,512,2048]{2,1,0:T(8,128)}) custom-call(s32[10]{0:T(128)S(1)} %stack.43.s_ref, f32[1024,2048]{1,0:T(8,128)S(1)} %bitcast.14, bf16[1024,512]{1,0:T(8,128)(2,1)S(1)} %get-tuple-element.64.oh.mh.ah, bf16[1024,512]{1,0:T(8,128)(2,1)S(1)} %get-tuple-element.65.ol.ml.al, ...), custom_call_target="tpu_custom_call", output_to_operand_aliasing={{0}: (7, {}), {1}: (8, {})} | custom-call | flops 3221225472 | bytes 6291456 | tf_op jit(solution)/shard_map/residual/pallas_call | solution.py:456
  286.4 6.6 %residual.7 = (f32[1024,2048]{1,0:T(8,128)}, f32[2,512,2048]{2,1,0:T(8,128)}) custom-call(s32[10]{0:T(128)S(1)} %stack.43.s_ref, f32[1024,2048]{1,0:T(8,128)S(1)} %bitcast.14, bf16[1024,512]{1,0:T(8,128)(2,1)S(1)} %get-tuple-element.64.oh.mh.ah, bf16[1024,512]{1,0:T(8,128)(2,1)S(1)} %get-tuple-element.65.ol.ml.al, ...), custom_call_target="tpu_custom_call", output_to_operand_aliasing={{0}: (7, {}), {1}: (8, {})} | custom-call | flops 3221225472 | bytes 6291456 | tf_op jit(solution)/shard_map/residual/pallas_call | solution.py:456
  (83 shorter events, 16.1 us)
Async XLA Ops:
  0.6 2.9 collective-permute-start
  1.2 2.3 collective-permute-start.1
  3.5 1.2 copy-start
  4.7 0.7 copy-start.1
  5.3 0.7 copy-start.2
  7.1 9.4 %collective-permute-start.2 = (f32[2,448,128]{2,1,0:T(8,128)S(1)}, f32[2,448,128]{2,1,0:T(8,128)S(1)}, u32[]{:S(2)}, u32[]{:S(2)}) collective-permute-start(f32[2,448,128]{2,1,0:T(8,128)S(1)} %slice.73), channel_id=1, source_target_pairs={{0,2},{1,5},{2,0},{3,7},{4,6},{5,1},{6,4},{7,3},{8,10},{9,13},{10,... | collective-permute-start | bytes 1376264 | tf_op jit(solution)/shard_map/ppermute | solution.py:498
  16.6 6.1 %collective-permute-start.3 = (f32[1,448,128]{2,1,0:T(8,128)S(1)}, f32[1,448,128]{2,1,0:T(8,128)S(1)}, u32[]{:S(2)}, u32[]{:S(2)}) collective-permute-start(f32[1,448,128]{2,1,0:T(8,128)S(1)} %slice.75), channel_id=1, source_target_pairs={{0,4},{1,3},{2,6},{3,1},{4,0},{5,7},{6,2},{7,5},{8,12},{9,11},{10,... | collective-permute-start | bytes 688136 | tf_op jit(solution)/shard_map/ppermute | solution.py:498
  22.7 32.5 %copy-start.3 = (f32[1024,440]{0,1:T(8,128)S(1)}, f32[1024,440]{0,1:T(8,128)}, u32[]{:S(2)}) copy-start(f32[1024,440]{0,1:T(8,128)} %param.5) | copy-start | bytes 5406724
  22.7 6.3 %collective-permute-start.4 = (f32[1,448,128]{2,1,0:T(8,128)S(1)}, f32[1,448,128]{2,1,0:T(8,128)S(1)}, u32[]{:S(2)}, u32[]{:S(2)}) collective-permute-start(f32[1,448,128]{2,1,0:T(8,128)S(1)} %slice_add_fusion.6), channel_id=1, source_target_pairs={{0,8},{1,9},{2,10},{3,11},{4,12},{5,13},{6,14},{7,15},{8,0},{9,1},... | collective-permute-start | bytes 688136 | tf_op jit(solution)/shard_map/ppermute | solution.py:498
  29.1 11.2 %collective-permute-start.5 = (f32[1,448,128]{2,1,0:T(8,128)S(1)}, f32[1,448,128]{2,1,0:T(8,128)S(1)}, u32[]{:S(2)}, u32[]{:S(2)}) collective-permute-start(f32[1,448,128]{2,1,0:T(8,128)S(1)} %add.101), channel_id=1, source_target_pairs={{0,16},{1,17},{2,18},{3,19},{4,20},{5,21},{6,22},{7,23},{8,24},{9,... | collective-permute-start | bytes 688136 | tf_op jit(solution)/shard_map/ppermute | solution.py:498
  40.4 6.1 %collective-permute-start.6 = (f32[1,448,128]{2,1,0:T(8,128)S(1)}, f32[1,448,128]{2,1,0:T(8,128)S(1)}, u32[]{:S(2)}, u32[]{:S(2)}) collective-permute-start(f32[1,448,128]{2,1,0:T(8,128)S(1)} %add.102), channel_id=1, source_target_pairs={{0,4},{1,3},{2,6},{3,1},{4,0},{5,7},{6,2},{7,5},{8,12},{9,11},{10,... | collective-permute-start | bytes 688136 | tf_op jit(solution)/shard_map/ppermute | solution.py:498
  46.5 8.5 %collective-permute-start.7 = (f32[2,448,128]{2,1,0:T(8,128)S(1)}, f32[2,448,128]{2,1,0:T(8,128)S(1)}, u32[]{:S(2)}, u32[]{:S(2)}) collective-permute-start(f32[2,448,128]{2,1,0:T(8,128)S(1)} %pad_maximum_fusion.5), channel_id=1, source_target_pairs={{0,2},{1,5},{2,0},{3,7},{4,6},{5,1},{6,4},{7,3},{8,10},{9,13},{10,... | collective-permute-start | bytes 1376264 | tf_op jit(solution)/shard_map/ppermute | solution.py:498
  55.1 8.0 %collective-permute-start.8 = (f32[4,448,128]{2,1,0:T(8,128)S(1)}, f32[4,448,128]{2,1,0:T(8,128)S(1)}, u32[]{:S(2)}, u32[]{:S(2)}) collective-permute-start(f32[4,448,128]{2,1,0:T(8,128)S(1)} %pad_maximum_fusion.2.p_ref), channel_id=1, source_target_pairs={{0,1},{1,0},{2,3},{3,2},{4,5},{5,4},{6,7},{7,6},{8,9},{9,8},{10,11... | collective-permute-start | bytes 2752520 | tf_op jit(solution)/shard_map/ppermute | solution.py:498
  55.2 19.2 %slice-start = ((s8[8388608]{0:T(1024)(128)(4,1)}), s8[4194304]{0:T(1024)(128)(4,1)S(1)}, s32[]{:S(2)}) async-start(s8[8388608]{0:T(1024)(128)(4,1)} %bitcast.13), calls=%async_computation | async-start | bytes 8388608
  63.1 11.4 %slice-start.1 = ((s8[8388608]{0:T(1024)(128)(4,1)}), s8[4194304]{0:T(1024)(128)(4,1)S(1)}, s32[]{:S(2)}) async-start(s8[8388608]{0:T(1024)(128)(4,1)} %bitcast.13), calls=%async_computation.1 | async-start | bytes 8388608
  73.9 9.7 %collective-permute-start.9 = (f32[16,5,16,256]{3,2,1,0:T(8,128)S(1)}, f32[16,5,16,256]{3,2,1,0:T(8,128)S(1)}, u32[]{:S(2)}, u32[]{:S(2)}) collective-permute-start(f32[16,5,16,256]{3,2,1,0:T(8,128)S(1)} %gram.2), channel_id=1, source_target_pairs={{0,1},{1,0},{2,3},{3,2},{4,5},{5,4},{6,7},{7,6},{8,9},{9,8},{10,11... | collective-permute-start | bytes 3932168 | tf_op jit(solution)/shard_map/ppermute | solution.py:498
  80.4 22.1 %collective-permute-start.12 = (f32[4,1024,128]{2,1,0:T(8,128)S(1)}, f32[4,1024,128]{2,1,0:T(8,128)S(1)}, u32[]{:S(2)}, u32[]{:S(2)}) collective-permute-start(f32[4,1024,128]{2,1,0:T(8,128)S(1)} %cross.4), channel_id=1, source_target_pairs={{0,1},{1,0},{2,3},{3,2},{4,5},{5,4},{6,7},{7,6},{8,9},{9,8},{10,11... | collective-permute-start | bytes 6291464 | tf_op jit(solution)/shard_map/ppermute | solution.py:498
  89.9 20.2 %collective-permute-start.13 = (f32[4,1024,128]{2,1,0:T(8,128)S(1)}, f32[4,1024,128]{2,1,0:T(8,128)S(1)}, u32[]{:S(2)}, u32[]{:S(2)}) collective-permute-start(f32[4,1024,128]{2,1,0:T(8,128)S(1)} %cross.5), channel_id=1, source_target_pairs={{0,1},{1,0},{2,3},{3,2},{4,5},{5,4},{6,7},{7,6},{8,9},{9,8},{10,11... | collective-permute-start | bytes 6291464 | tf_op jit(solution)/shard_map/ppermute | solution.py:498
  90.5 10.7 %collective-permute-start.10 = (f32[8,5,16,256]{3,2,1,0:T(8,128)S(1)}, f32[8,5,16,256]{3,2,1,0:T(8,128)S(1)}, u32[]{:S(2)}, u32[]{:S(2)}) collective-permute-start(f32[8,5,16,256]{3,2,1,0:T(8,128)S(1)} %slice.77), channel_id=1, source_target_pairs={{0,2},{1,5},{2,0},{3,7},{4,6},{5,1},{6,4},{7,3},{8,10},{9,13},{10,... | collective-permute-start | bytes 1966088 | tf_op jit(solution)/shard_map/ppermute | solution.py:498
  101.3 8.8 %collective-permute-start.11 = (f32[4,5,16,256]{3,2,1,0:T(8,128)S(1)}, f32[4,5,16,256]{3,2,1,0:T(8,128)S(1)}, u32[]{:S(2)}, u32[]{:S(2)}) collective-permute-start(f32[4,5,16,256]{3,2,1,0:T(8,128)S(1)} %slice.79), channel_id=1, source_target_pairs={{0,4},{1,3},{2,6},{3,1},{4,0},{5,7},{6,2},{7,5},{8,12},{9,11},{10,... | collective-permute-start | bytes 983048 | tf_op jit(solution)/shard_map/ppermute | solution.py:498
  108.5 31.3 %collective-permute-start.22 = (f32[4,1024,128]{2,1,0:T(8,128)S(1)}, f32[4,1024,128]{2,1,0:T(8,128)S(1)}, u32[]{:S(2)}, u32[]{:S(2)}) collective-permute-start(f32[4,1024,128]{2,1,0:T(8,128)S(1)} %cross.6), channel_id=1, source_target_pairs={{0,2},{1,5},{2,0},{3,7},{4,6},{5,1},{6,4},{7,3},{8,10},{9,13},{10,... | collective-permute-start | bytes 6291464 | tf_op jit(solution)/shard_map/ppermute | solution.py:498
  116.1 5.4 %collective-permute-start.14 = (f32[2,5,16,256]{3,2,1,0:T(8,128)S(1)}, f32[2,5,16,256]{3,2,1,0:T(8,128)S(1)}, u32[]{:S(2)}, u32[]{:S(2)}) collective-permute-start(f32[2,5,16,256]{3,2,1,0:T(8,128)S(1)} %slice.63), channel_id=1, source_target_pairs={{0,8},{1,9},{2,10},{3,11},{4,12},{5,13},{6,14},{7,15},{8,0},{9,1},... | collective-permute-start | bytes 491528 | tf_op jit(solution)/shard_map/ppermute | solution.py:498
  121.5 6.5 %collective-permute-start.15 = (f32[1,5,16,256]{3,2,1,0:T(8,128)S(1)}, f32[1,5,16,256]{3,2,1,0:T(8,128)S(1)}, u32[]{:S(2)}, u32[]{:S(2)}) collective-permute-start(f32[1,5,16,256]{3,2,1,0:T(8,128)S(1)} %slice.81), channel_id=1, source_target_pairs={{0,16},{1,17},{2,18},{3,19},{4,20},{5,21},{6,22},{7,23},{8,24},{9,... | collective-permute-start | bytes 245768 | tf_op jit(solution)/shard_map/ppermute | solution.py:498
  128.0 5.5 %collective-permute-start.16 = (f32[1,5,16,256]{3,2,1,0:T(8,128)S(1)}, f32[1,5,16,256]{3,2,1,0:T(8,128)S(1)}, u32[]{:S(2)}, u32[]{:S(2)}) collective-permute-start(f32[1,5,16,256]{3,2,1,0:T(8,128)S(1)} %get-tuple-element.95), channel_id=1, source_target_pairs={{0,16},{1,17},{2,18},{3,19},{4,20},{5,21},{6,22},{7,23},{8,24},{9,... | collective-permute-start | bytes 245768 | tf_op jit(solution)/shard_map/ppermute | solution.py:498
  133.6 5.6 %collective-permute-start.17 = (f32[2,5,16,256]{3,2,1,0:T(8,128)S(1)}, f32[2,5,16,256]{3,2,1,0:T(8,128)S(1)}, u32[]{:S(2)}, u32[]{:S(2)}) collective-permute-start(f32[2,5,16,256]{3,2,1,0:T(8,128)S(1)} %pad_maximum_fusion.7), channel_id=1, source_target_pairs={{0,8},{1,9},{2,10},{3,11},{4,12},{5,13},{6,14},{7,15},{8,0},{9,1},... | collective-permute-start | bytes 491528 | tf_op jit(solution)/shard_map/ppermute | solution.py:498
  139.2 10.1 %collective-permute-start.18 = (f32[4,5,16,256]{3,2,1,0:T(8,128)S(1)}, f32[4,5,16,256]{3,2,1,0:T(8,128)S(1)}, u32[]{:S(2)}, u32[]{:S(2)}) collective-permute-start(f32[4,5,16,256]{3,2,1,0:T(8,128)S(1)} %pad_maximum_fusion.6), channel_id=1, source_target_pairs={{0,4},{1,3},{2,6},{3,1},{4,0},{5,7},{6,2},{7,5},{8,12},{9,11},{10,... | collective-permute-start | bytes 983048 | tf_op jit(solution)/shard_map/ppermute | solution.py:498
  140.1 24.5 %collective-permute-start.23 = (f32[2,1024,128]{2,1,0:T(8,128)S(1)}, f32[2,1024,128]{2,1,0:T(8,128)S(1)}, u32[]{:S(2)}, u32[]{:S(2)}) collective-permute-start(f32[2,1024,128]{2,1,0:T(8,128)S(1)} %slice.83), channel_id=1, source_target_pairs={{0,4},{1,3},{2,6},{3,1},{4,0},{5,7},{6,2},{7,5},{8,12},{9,11},{10,... | collective-permute-start | bytes 3145736 | tf_op jit(solution)/shard_map/ppermute | solution.py:498
  149.3 10.7 %collective-permute-start.19 = (f32[8,5,16,256]{3,2,1,0:T(8,128)S(1)}, f32[8,5,16,256]{3,2,1,0:T(8,128)S(1)}, u32[]{:S(2)}, u32[]{:S(2)}) collective-permute-start(f32[8,5,16,256]{3,2,1,0:T(8,128)S(1)} %pad_maximum_fusion.3), channel_id=1, source_target_pairs={{0,2},{1,5},{2,0},{3,7},{4,6},{5,1},{6,4},{7,3},{8,10},{9,13},{10,... | collective-permute-start | bytes 1966088 | tf_op jit(solution)/shard_map/ppermute | solution.py:498
  164.8 12.8 %collective-permute-start.24 = (f32[1,1024,128]{2,1,0:T(8,128)S(1)}, f32[1,1024,128]{2,1,0:T(8,128)S(1)}, u32[]{:S(2)}, u32[]{:S(2)}) collective-permute-start(f32[1,1024,128]{2,1,0:T(8,128)S(1)} %slice.85), channel_id=1, source_target_pairs={{0,8},{1,9},{2,10},{3,11},{4,12},{5,13},{6,14},{7,15},{8,0},{9,1},... | collective-permute-start | bytes 1572872 | tf_op jit(solution)/shard_map/ppermute | solution.py:498
  177.7 14.2 %collective-permute-start.25 = (f32[1,512,128]{2,1,0:T(8,128)S(1)}, f32[1,512,128]{2,1,0:T(8,128)S(1)}, u32[]{:S(2)}, u32[]{:S(2)}) collective-permute-start(f32[1,512,128]{2,1,0:T(8,128)S(1)} %slice.87), channel_id=1, source_target_pairs={{0,16},{1,17},{2,18},{3,19},{4,20},{5,21},{6,22},{7,23},{8,24},{9,... | collective-permute-start | bytes 786440 | tf_op jit(solution)/shard_map/ppermute | solution.py:498
  192.0 10.5 %collective-permute-start.26 = (f32[1,512,128]{2,1,0:T(8,128)S(1)}, f32[1,512,128]{2,1,0:T(8,128)S(1)}, u32[]{:S(2)}, u32[]{:S(2)}) collective-permute-start(f32[1,512,128]{2,1,0:T(8,128)S(1)} %slice_add_fusion.5), channel_id=1, source_target_pairs={{0,16},{1,17},{2,18},{3,19},{4,20},{5,21},{6,22},{7,23},{8,24},{9,... | collective-permute-start | bytes 786440 | tf_op jit(solution)/shard_map/ppermute | solution.py:498
  202.5 14.9 %collective-permute-start.27 = (f32[1,1024,128]{2,1,0:T(8,128)S(1)}, f32[1,1024,128]{2,1,0:T(8,128)S(1)}, u32[]{:S(2)}, u32[]{:S(2)}) collective-permute-start(f32[1,1024,128]{2,1,0:T(8,128)S(1)} %pad_maximum_fusion.4), channel_id=1, source_target_pairs={{0,8},{1,9},{2,10},{3,11},{4,12},{5,13},{6,14},{7,15},{8,0},{9,1},... | collective-permute-start | bytes 1572872 | tf_op jit(solution)/shard_map/ppermute | solution.py:498
  217.3 3.5 %collective-permute-start.20 = (f32[512,512]{1,0:T(8,128)S(1)}, f32[512,512]{1,0:T(8,128)S(1)}, u32[]{:S(2)}, u32[]{:S(2)}) collective-permute-start(f32[512,512]{1,0:T(8,128)S(1)} %factor.5.own_ref), channel_id=1, source_target_pairs={{0,1},{1,0},{2,3},{3,2},{4,5},{5,4},{6,7},{7,6},{8,9},{9,8},{10,11... | collective-permute-start | bytes 3145736 | tf_op jit(solution)/shard_map/ppermute | solution.py:498
  217.5 14.9 %collective-permute-start.28 = (f32[2,1024,128]{2,1,0:T(8,128)S(1)}, f32[2,1024,128]{2,1,0:T(8,128)S(1)}, u32[]{:S(2)}, u32[]{:S(2)}) collective-permute-start(f32[2,1024,128]{2,1,0:T(8,128)S(1)} %pad_maximum_fusion.1), channel_id=1, source_target_pairs={{0,4},{1,3},{2,6},{3,1},{4,0},{5,7},{6,2},{7,5},{8,12},{9,11},{10,... | collective-permute-start | bytes 3145736 | tf_op jit(solution)/shard_map/ppermute | solution.py:498
  218.0 2.7 collective-permute-start.21
  240.7 26.1 %collective-permute-start.29 = (f32[4,1024,128]{2,1,0:T(8,128)S(1)}, f32[4,1024,128]{2,1,0:T(8,128)S(1)}, u32[]{:S(2)}, u32[]{:S(2)}) collective-permute-start(f32[4,1024,128]{2,1,0:T(8,128)S(1)} %solve.1.w_in), channel_id=1, source_target_pairs={{0,2},{1,5},{2,0},{3,7},{4,6},{5,1},{6,4},{7,3},{8,10},{9,13},{10,... | collective-permute-start | bytes 6291464 | tf_op jit(solution)/shard_map/ppermute | solution.py:498
  241.3 32.1 %collective-permute-start.31 = (f32[4,1024,128]{2,1,0:T(8,128)S(1)}, f32[4,1024,128]{2,1,0:T(8,128)S(1)}, u32[]{:S(2)}, u32[]{:S(2)}) collective-permute-start(f32[4,1024,128]{2,1,0:T(8,128)S(1)} %solve.1.w_in), channel_id=1, source_target_pairs={{0,1},{1,0},{2,3},{3,2},{4,5},{5,4},{6,7},{7,6},{8,9},{9,8},{10,11... | collective-permute-start | bytes 6291464 | tf_op jit(solution)/shard_map/ppermute | solution.py:498
  266.8 19.7 %collective-permute-start.30 = (f32[4,1024,128]{2,1,0:T(8,128)S(1)}, f32[4,1024,128]{2,1,0:T(8,128)S(1)}, u32[]{:S(2)}, u32[]{:S(2)}) collective-permute-start(f32[4,1024,128]{2,1,0:T(8,128)S(1)} %collective-permute-done.29.w_in), channel_id=1, source_target_pairs={{0,1},{1,0},{2,3},{3,2},{4,5},{5,4},{6,7},{7,6},{8,9},{9,8},{10,11... | collective-permute-start | bytes 6291464 | tf_op jit(solution)/shard_map/ppermute | solution.py:498
where the time goes:
time: 293 us
  Pallas kernels  128 us (44%)
  waiting for transfers between devices  123 us (42%)
  starting transfers between devices  36.4 us (12%)
  local copies, waits for them, and re-layouts  2.96 us (1%)
    ppermute x32, waiting for transfers between devices, exchange(): return lax.ppermute(value, ALL, pairs)  123 us
    ppermute x32, starting transfers between devices, exchange(): return lax.ppermute(value, ALL, pairs)  36.4 us
    pallas_call x3, Pallas kernels, factor(): pl.pallas_call(functools.partial(factor_kernel, step), out_shape=jax.Shap...  32.8 us
    pallas_call x4, Pallas kernels, residual_part(): pl.pallas_call(functools.partial(residual_kernel, base), out_shape=[jax.S...  26.2 us
    pallas_call x4, Pallas kernels, cross(): pl.pallas_call(functools.partial(cross_kernel, base), out_shape=jax.Shape...  23.8 us
    pallas_call x2, Pallas kernels, features(): pl.pallas_call(functools.partial(features_kernel, quarter), out_shape=[ja...  15.7 us
    pallas_call x1, Pallas kernels, assemble(): pl.pallas_call(assemble_kernel, out_shape=[jax.ShapeDtypeStruct((2 * half...  11.5 us
    pallas_call x1, Pallas kernels, solve(): pl.pallas_call(solve_kernel, out_shape=jax.ShapeDtypeStruct(crossed.shape...  8.18 us
  transfers between devices with their start and end apart: 32, of which 19 were waited for; matrix products, arithmetic and copies ran while one was open for 0% of the time, Pallas kernels for 35%

commit v1 on v0

--- a/solution.py
+++ b/solution.py
@@ -14,7 +14,7 @@
 HIGHEST = lax.Precision.HIGHEST
 
 
-BASE_OWN, BASE_OTH, CORE, FAR, PLACE, ORDER_OWN, ORDER_OTH, QUARTER_OWN, QUARTER_OTH, DEVICE = range(10)
+BASE_OWN, BASE_OTH, CORE, TURN, ORDER_OWN, ORDER_OTH, QUARTER_OWN, QUARTER_OTH, DEVICE = range(9)
 
 
 def params(mib=24):
@@ -180,17 +180,16 @@
 
 def cross_kernel(base, s_ref, t_ref, ath, atl, bth, btl, *rest):
     out_ref = rest[-1]
-    place, swap = s_ref[PLACE], s_ref[base] & 1
-    feats = ath.shape[0]
-    half = feats // 2
+    core, turn, swap = s_ref[CORE], s_ref[TURN], s_ref[base] & 1
+    half = ath.shape[0] // 2
     width = out_ref.shape[2]
     right = split(t_ref[...])
 
-    def rows_of(th, tl, start):
+    def rows_of(th, tl, step):
         def body(i, carry):
-            at = pl.multiple_of(i * half, half)
-            value = dot3((th[pl.ds(at, half), :], tl[pl.ds(at, half), :]), right)
-            to = pl.ds(pl.multiple_of(start + at, half), half)
+            at = pl.ds(pl.multiple_of(i * half, half), half)
+            value = dot3((th[at, :], tl[at, :]), right)
+            to = pl.ds(pl.multiple_of(((2 * step + i) ^ turn) * half, half), half)
             for k in range(2):
                 part = value[:, k * width : (k + 1) * width]
                 if len(rest) == 2:
@@ -200,8 +199,8 @@
 
         lax.fori_loop(0, 2, body, 0)
 
-    rows_of(ath, atl, place * feats)
-    rows_of(bth, btl, (1 - place) * feats)
+    rows_of(ath, atl, core)
+    rows_of(bth, btl, 1 - core)
 
 
 def cross(base, group, scalars, targets, mine, other, before=()):
@@ -216,7 +215,7 @@
         grid_spec=pltpu.PrefetchScalarGridSpec(
             num_scalar_prefetch=1,
             grid=(2,),
-            in_specs=[pl.BlockSpec((rows, 2 * width), lambda k, s: (0, (s[base] >> 1) ^ (2 * group + k)))]
+            in_specs=[pl.BlockSpec((rows, 2 * width), lambda k, s: (0, 4 * group + ((s[base] >> 1) ^ k)))]
             + [whole] * 4
             + [pair] * len(before),
             out_specs=pair,
@@ -233,40 +232,53 @@
     lane = lax.broadcasted_iota(jnp.int32, (8, lanes), 1)
     sub = lax.broadcasted_iota(jnp.int32, (8, lanes), 0)
 
-    def wide(column):
-        return jnp.broadcast_to(column, (8, lanes))
-
-    def turn(i, carry):
-        rows, pivots = list(carry[0]), list(carry[1])
-        before = list(rows)
-        top_pivots = pivots[0]
-        for j in range(0, 8, 2):
-            pair = (lane == j) | (lane == j + 1)
+    def wide(row):
+        return jnp.broadcast_to(row, (8, lanes))
+
+    def make(active):
+        def turn(i, carry):
+            rows, pivots = list(carry[0]), list(carry[1])
+            spots = [jnp.full((8, lanes), 8 * i + k, jnp.int32) for k in range(8)]
+            here = (lane >= 8 * i) & (lane < 8 * i + 8)
             top = rows[0]
-            col_a, col_b = wide(top[:, j : j + 1]), wide(top[:, j + 1 : j + 2])
-            a, b, c = wide(col_a[j : j + 1]), wide(col_a[j + 1 : j + 2]), wide(col_b[j + 1 : j + 2])
-            row_a, row_b = wide(top[j : j + 1]), wide(top[j + 1 : j + 2])
-            inv_a = 1.0 / a
-            inv_c = a * (1.0 / (a * c - b * b))
-            link = b * inv_a
-            use_a = jnp.where(lane == j, 1.0, jnp.where(lane == j + 1, 0.0, row_a))
-            use_b = jnp.where(lane == j, -link, jnp.where(lane == j + 1, 1.0, row_b - link * row_a))
-            m_a = jnp.where(sub > j, col_a * inv_a, 0.0)
-            m_b = jnp.where(sub > j + 1, (col_b - m_a * b) * inv_c, 0.0)
-            unit = jnp.where(pair & (lane == sub), 1.0, 0.0)
-            rows[0] = jnp.where(pair, unit, top) - m_a * use_a - m_b * use_b
-            top_pivots = jnp.where(sub == j, a, jnp.where(sub == j + 1, c - link * b, top_pivots))
-            for g in range(1, groups):
-                m_a = wide(rows[g][:, j : j + 1]) * inv_a
-                m_b = (wide(rows[g][:, j + 1 : j + 2]) - m_a * b) * inv_c
-                rows[g] = jnp.where(pair, 0.0, rows[g]) - m_a * use_a - m_b * use_b
-        for g in range(1, groups):
-            rows[g] = jnp.where(g < groups - i, rows[g], before[g])
-        rows = [pltpu.roll(r, lanes - 8, 1) for r in rows]
-        return tuple(rows[1:] + rows[:1]), tuple(pivots[1:] + [top_pivots])
+            cols = [jnp.take_along_axis(top, spot, axis=1) for spot in spots]
+            x = jnp.where(here, jnp.where(lane - 8 * i == sub, 1.0, 0.0), top)
+            diagonal, inverse = top, []
+            for j in range(0, 8, 2):
+                a, b, c = wide(cols[j][j : j + 1]), wide(cols[j][j + 1 : j + 2]), wide(cols[j + 1][j + 1 : j + 2])
+                inv_a = 1.0 / a
+                inv_c = a * (1.0 / (a * c - b * b))
+                link = b * inv_a
+                inverse += [inv_a, inv_c]
+                diagonal = jnp.where(sub == j, a, jnp.where(sub == j + 1, c - link * b, diagonal))
+                m_a = jnp.where(sub > j, cols[j] * inv_a, 0.0)
+                m_b = jnp.where(sub > j + 1, (cols[j + 1] - m_a * b) * inv_c, 0.0)
+
+                def swept(value):
+                    one = wide(value[j : j + 1])
+                    two = wide(value[j + 1 : j + 2]) - link * one
+                    return value - m_a * one - m_b * two
+
+                for k in range(j + 1, 8):
+                    cols[k] = swept(cols[k])
+                x = swept(x)
+            rest, z = x, [None] * 8
+            for j in range(7, -1, -1):
+                z[j] = wide(rest[j : j + 1]) * inverse[j]
+                if j:
+                    rest = rest - jnp.where(sub < j, cols[j], 0.0) * z[j]
+            for g in range(1, active):
+                parts = [jnp.take_along_axis(rows[g], spots[k], axis=1) * z[k] for k in range(8)]
+                total = ((parts[0] + parts[1]) + (parts[2] + parts[3])) + ((parts[4] + parts[5]) + (parts[6] + parts[7]))
+                rows[g] = jnp.where(g < groups - i, jnp.where(here, 0.0, rows[g]) - total, rows[g])
+            return tuple(rows[1:] + [x]), tuple(pivots[1:] + [diagonal])
+
+        return turn
 
     start = tuple(block[8 * g : 8 * g + 8] for g in range(groups))
-    rows, pivots = lax.fori_loop(0, groups, turn, (start, start))
+    state = (start, start)
+    state = lax.fori_loop(0, groups // 2, make(groups), state)
+    rows, pivots = lax.fori_loop(groups // 2, groups, make(groups // 2), state)
     scaled = [
         jnp.where(lane <= sub + 8 * g, rows[g] * lax.rsqrt(pivots[g]), 0.0) for g in range(groups)
     ]
@@ -368,14 +380,16 @@
 
 
 def solve_kernel(s_ref, own_ref, oth_ref, b_ref, c_ref, out_ref, one_ref):
-    core, far = s_ref[CORE], s_ref[FAR]
+    core, turn = s_ref[CORE], s_ref[TURN]
     feats = own_ref.shape[0]
     half = feats // 2
     width = c_ref.shape[2]
 
     def columns_of(step):
-        start = pl.multiple_of((step ^ far) * feats, feats)
-        return jnp.concatenate([c_ref[k, pl.ds(start, feats), :] for k in range(2)], axis=1)
+        starts = [pl.multiple_of(((2 * step + i) ^ turn) * half, half) for i in range(2)]
+        return jnp.concatenate(
+            [jnp.concatenate([c_ref[k, pl.ds(at, half), :] for k in range(2)], axis=1) for at in starts], axis=0
+        )
 
     right = columns_of(0)
 
@@ -423,15 +437,18 @@
     )(scalars, own, oth, coupling, crossed)
 
 
-def residual_kernel(base, s_ref, t_ref, ah, al, bh, bl, w_in, *rest):
+def residual_kernel(s_ref, t_ref, ah, al, bh, bl, wa_ref, wb_ref, *rest):
     r_ref, w_ref = rest[-2:]
-    swap, core = s_ref[base] & 1, s_ref[CORE]
+    own = pl.program_id(0) == 0
+    swap, core = jnp.where(own, s_ref[BASE_OWN], s_ref[BASE_OTH]) & 1, s_ref[CORE]
     rows, feats = ah.shape
     half = rows // 2
 
     def take(step):
-        start = pl.multiple_of(step * feats, feats)
-        return jnp.concatenate([w_in[i ^ swap, pl.ds(start, feats), :] for i in range(2)], axis=1)
+        here = pl.ds(pl.multiple_of(step * feats, feats), feats)
+        return jnp.concatenate(
+            [jnp.where(own, wa_ref[i ^ swap, here, :], wb_ref[i ^ swap, here, :]) for i in range(2)], axis=1
+        )
 
     mine, other = take(core), take(1 - core)
     w_ref[core], w_ref[1 - core] = mine, other
@@ -446,15 +463,20 @@
     lax.fori_loop(0, 2, body, 0)
 
 
-def residual_part(base, group, scalars, targets, mine, other, weights, before):
+def residual_part(group, pair, scalars, targets, mine, other, weights, weights_oth, before):
     rows, columns = targets.shape
     feats = mine[0].shape[1]
     _, height, width = weights.shape
     whole = pl.BlockSpec((rows, feats), lambda k, s: (0, 0))
-    block = pl.BlockSpec((rows, 2 * width), lambda k, s: (0, (s[base] >> 1) ^ (2 * group + k)))
+
+    def place(k, s):
+        return 4 * group + ((jnp.where(k == 0, s[BASE_OWN], s[BASE_OTH]) >> 1) ^ pair)
+
+    block = pl.BlockSpec((rows, 2 * width), lambda k, s: (0, place(k, s)))
+    both = pl.BlockSpec((2, height, width), lambda k, s: (0, 0, 0))
     anywhere = pl.BlockSpec(memory_space=pl.ANY)
     return pl.pallas_call(
-        functools.partial(residual_kernel, base),
+        residual_kernel,
         out_shape=[
             jax.ShapeDtypeStruct((rows, columns), F32),
             jax.ShapeDtypeStruct((2, feats, columns), F32),
@@ -462,20 +484,14 @@
         grid_spec=pltpu.PrefetchScalarGridSpec(
             num_scalar_prefetch=1,
             grid=(2,),
-            in_specs=[block]
-            + [whole] * 4
-            + [pl.BlockSpec((2, height, width), lambda k, s: (k, 0, 0))]
-            + [anywhere] * len(before),
-            out_specs=[
-                block,
-                pl.BlockSpec((2, feats, 2 * width), lambda k, s: (0, 0, (s[base] >> 1) ^ (2 * group + k))),
-            ],
+            in_specs=[block] + [whole] * 4 + [both] * 2 + [anywhere] * len(before),
+            out_specs=[block, pl.BlockSpec((2, feats, 2 * width), lambda k, s: (0, 0, place(k, s)))],
         ),
-        input_output_aliases={7: 0, 8: 1} if before else {},
+        input_output_aliases={8: 0, 9: 1} if before else {},
         compiler_params=params(),
         cost_estimate=cost(3 * rows * feats * columns, 3 * rows * columns),
         name="residual",
-    )(scalars, targets, mine[0], mine[1], other[0], other[1], weights, *before)
+    )(scalars, targets, mine[0], mine[1], other[0], other[1], weights, weights_oth, *before)
 
 
 def ints(*values):
@@ -503,11 +519,10 @@
         return value
 
     scalars = ints(
-        core * 8 + one * 4 + two * 2 + near,
-        (1 - core) * 8 + two * 4 + one * 2 + near,
+        core * 4 + one * 2 + two,
+        (1 - core) * 4 + two * 2 + one,
         core,
-        far,
-        far ^ core,
+        near * 2 + far,
         one * 8 + two * 4 + near * 2 + far,
         two * 8 + one * 4 + near * 2 + far,
         one * 2 + two,
@@ -535,38 +550,42 @@
     gram_sent = gram(False, scalars, other, mine)
     gram_came = exchange(gram_sent, 1)
     sides = after(gram_sent, sides)
-    sent = cross(BASE_OTH, 1, scalars, targets, *sides)
-    came_b = exchange(sent, 1)
+    sent = cross(BASE_OTH, 0, scalars, targets, *sides)
+    came = exchange(sent, 1)
     sides = after(sent, sides)
     pieces = gram(True, scalars, *sides) + gram_came
     sides = after(pieces, sides)
-    sent = cross(BASE_OTH, 0, scalars, targets, *sides)
-    came_a = exchange(sent, 1)
-    sides = after(sent, sides)
-    moving = cross(BASE_OWN, 1, scalars, targets, *sides, (came_b,))
-    sides = after(moving, sides)
-    staying = cross(BASE_OWN, 0, scalars, targets, *sides, (came_a,))
-
     moved = exchange(pieces[8:], 2, 4)
     pieces = pieces[:8] + moved
-    pieces = pieces[:4] + exchange(pieces[4:], 4, 2)
-    pieces, staying = lax.optimization_barrier([pieces, staying])
-    pieces = pieces[:2] + exchange(pieces[2:], 8)
+    kept = [cross(BASE_OWN, 0, scalars, targets, *sides, (came,))]
+    sides = after(kept[0], sides)
+    sent = cross(BASE_OTH, 1, scalars, targets, *sides)
+    came = exchange(sent, 1)
+    sides = after(sent, sides)
+    kept.append(cross(BASE_OWN, 1, scalars, targets, *sides, (came,)))
+
+    moved = exchange(pieces[4:], 4, 2)
+    pieces = pieces[:4] + moved
+    pieces, kept[1] = lax.optimization_barrier([pieces, kept[1]])
+    moved = exchange(pieces[2:], 8)
+    pieces = pieces[:2] + moved
     pieces = pieces[:1] + exchange(pieces[1:], 16)
     pieces = flood(pieces, more)
     for masks in ((16,), (8,), (4, 2), (2, 4)):
         pieces = jnp.concatenate([pieces, exchange(pieces, *masks)])
 
-    moved = exchange(moving, 2, 4)
-    crossed = staying + moved
-    crossed = crossed[:2] + exchange(crossed[2:], 4, 2)
-    crossed = crossed[:1] + exchange(crossed[1:], 8)
-    feats = crossed.shape[1] // 2
-    crossed = crossed[:, :feats] + exchange(crossed[:, feats:], 16)
-    crossed = flood(crossed, more)
-    crossed = jnp.concatenate([crossed, exchange(crossed, 16)], axis=1)
-    crossed = jnp.concatenate([crossed, exchange(crossed, 8)])
-    crossed = jnp.concatenate([crossed, exchange(crossed, 4, 2)])
+    crossed = []
+    for value in kept:
+        moved = exchange(value[2:], 2, 4)
+        value = value[:2] + moved
+        value = value[:1] + exchange(value[1:], 4, 2)
+        for mask in (8, 16):
+            middle = value.shape[1] // 2
+            value = value[:, :middle] + exchange(value[:, middle:], mask)
+        value = flood(value, more)
+        for mask in (16, 8):
+            value = jnp.concatenate([value, exchange(value, mask)], axis=1)
+        crossed.append(jnp.concatenate([value, exchange(value, 4, 2)]))
 
     matrix, side = assemble(scalars, pieces)
     side_oth = exchange(side, 1)
@@ -575,13 +594,16 @@
     inverse = matrix
     inverse_oth = exchange(inverse, 1)
     coupling = couple(scalars, inverse, inverse_oth, side, side_oth)
-    weights = solve(scalars, inverse, inverse_oth, coupling, crossed)
-    weights_b = exchange(weights, 2, 4)
+    parts = []
+    for value in crossed:
+        near_part = solve(scalars, inverse, inverse_oth, coupling, value)
+        parts.append((near_part, exchange(near_part, 2, 4)))
     outs = ()
-    for group, part in ((0, weights), (1, weights_b)):
-        part_oth = exchange(part, 1)
-        for base, value in ((BASE_OWN, part), (BASE_OTH, part_oth)):
-            outs = residual_part(base, group, scalars, targets, mine, other, value, tuple(outs))
+    for pair in range(2):
+        for group in range(2):
+            value = parts[group][pair]
+            value_oth = exchange(value, 1)
+            outs = residual_part(group, pair, scalars, targets, mine, other, value, value_oth, tuple(outs))
     return tuple(outs)
 
 

time: 293 us -> 292 us (level)
  starting transfers between devices: 36.4 us -> 58.2 us
  Pallas kernels: 128 us -> 112 us
  waiting for transfers between devices: 123 us -> 116 us
    ppermute x32 -> x42, starting transfers between devices: 36.4 us -> 58.2 us  [exchange(): return lax.ppermute(value, ALL, pairs)]
    pallas_call x3, Pallas kernels: 32.8 us -> 20.6 us  [factor(): pl.pallas_call(functools.partial(factor_kernel, step), out_shape=jax.Shap...]
    ppermute x32 -> x42, waiting for transfers between devices: 123 us -> 116 us  [exchange(): return lax.ppermute(value, ALL, pairs)]
    pallas_call x1, Pallas kernels: 11.5 us -> 7.48 us  [assemble(): pl.pallas_call(assemble_kernel, out_shape=[jax.ShapeDtypeStruct((2 * half...]
    pallas_call x1 -> x2, Pallas kernels: 8.18 us -> 8.69 us  [solve(): pl.pallas_call(solve_kernel, out_shape=jax.ShapeDtypeStruct(crossed.shape...]
  transfers between devices with their start and end apart: 32 -> 42, of which waited for: 19 -> 24; matrix products, arithmetic and copies ran while one was open for 0% -> 1% of each run, Pallas kernels for 35% -> 26%
where the time goes in v1:
time: 292 us; the launch traced here: 291 us
  waiting for transfers between devices  116 us (40%)
  Pallas kernels  112 us (38%)
  starting transfers between devices  58.2 us (20%)
  local copies, waits for them, and re-layouts  3.1 us (1%)
    ppermute x42, waiting for transfers between devices, exchange(): return lax.ppermute(value, ALL, pairs)  116 us
    ppermute x42, starting transfers between devices, exchange(): return lax.ppermute(value, ALL, pairs)  58.2 us
    pallas_call x4, Pallas kernels, residual_part(): pl.pallas_call(residual_kernel, out_shape=[jax.ShapeDtypeStruct((rows, co...  25.9 us
    pallas_call x4, Pallas kernels, cross(): pl.pallas_call(functools.partial(cross_kernel, base), out_shape=jax.Shape...  23.8 us
    pallas_call x3, Pallas kernels, factor(): pl.pallas_call(functools.partial(factor_kernel, step), out_shape=jax.Shap...  20.6 us
    pallas_call x2, Pallas kernels, features(): pl.pallas_call(functools.partial(features_kernel, quarter), out_shape=[ja...  15.7 us
    pallas_call x2, Pallas kernels, solve(): pl.pallas_call(solve_kernel, out_shape=jax.ShapeDtypeStruct(crossed.shape...  8.69 us
    pallas_call x1, Pallas kernels, assemble(): pl.pallas_call(assemble_kernel, out_shape=[jax.ShapeDtypeStruct((2 * half...  7.48 us
  transfers between devices with their start and end apart: 42, of which 24 were waited for; matrix products, arithmetic and copies ran while one was open for 1% of the time, Pallas kernels for 26%

profile of v1, /device:TPU:0, one launch (start us, length us, event | category | flops | bytes accessed | tf_op | source)
XLA Modules:
  0.0 291.3 jit_solution(13637688493519091220)
XLA Ops:
  1.4 2.1 collective-permute-done.1
  7.1 2.9 %collective-permute-start.2 = (f32[2,448,128]{2,1,0:T(8,128)S(1)}, f32[2,448,128]{2,1,0:T(8,128)S(1)}, u32[]{:S(2)}, u32[]{:S(2)}) collective-permute-start(f32[2,448,128]{2,1,0:T(8,128)S(1)} %slice.113), channel_id=1, source_target_pairs={{0,2},{1,5},{2,0},{3,7},{4,6},{5,1},{6,4},{7,3},{8,10},{9,13},{10,... | collective-permute-start | bytes 1376264 | tf_op jit(solution)/shard_map/ppermute | solution.py:514
  10.0 6.5 %collective-permute-done.2 = f32[2,448,128]{2,1,0:T(8,128)S(1)} collective-permute-done((f32[2,448,128]{2,1,0:T(8,128)S(1)}, f32[2,448,128]{2,1,0:T(8,128)S(1)}, u32[]{:S(2)}, u32[]{:S(2)}) %collective-permute-start.2) | collective-permute-done | bytes 458784 | tf_op jit(solution)/shard_map/ppermute | solution.py:514
  18.7 4.0 %collective-permute-done.3 = f32[1,448,128]{2,1,0:T(8,128)S(1)} collective-permute-done((f32[1,448,128]{2,1,0:T(8,128)S(1)}, f32[1,448,128]{2,1,0:T(8,128)S(1)}, u32[]{:S(2)}, u32[]{:S(2)}) %collective-permute-start.3) | collective-permute-done | bytes 229408 | tf_op jit(solution)/shard_map/ppermute | solution.py:514
  22.7 2.1 collective-permute-start.4
  24.9 4.2 %collective-permute-done.4 = f32[1,448,128]{2,1,0:T(8,128)S(1)} collective-permute-done((f32[1,448,128]{2,1,0:T(8,128)S(1)}, f32[1,448,128]{2,1,0:T(8,128)S(1)}, u32[]{:S(2)}, u32[]{:S(2)}) %collective-permute-start.4) | collective-permute-done | bytes 229408 | tf_op jit(solution)/shard_map/ppermute | solution.py:514
  29.1 3.1 %collective-permute-start.5 = (f32[1,448,128]{2,1,0:T(8,128)S(1)}, f32[1,448,128]{2,1,0:T(8,128)S(1)}, u32[]{:S(2)}, u32[]{:S(2)}) collective-permute-start(f32[1,448,128]{2,1,0:T(8,128)S(1)} %add.109), channel_id=1, source_target_pairs={{0,16},{1,17},{2,18},{3,19},{4,20},{5,21},{6,22},{7,23},{8,24},{9,... | collective-permute-start | bytes 688136 | tf_op jit(solution)/shard_map/ppermute | solution.py:514
  32.1 8.2 %collective-permute-done.5 = f32[1,448,128]{2,1,0:T(8,128)S(1)} collective-permute-done((f32[1,448,128]{2,1,0:T(8,128)S(1)}, f32[1,448,128]{2,1,0:T(8,128)S(1)}, u32[]{:S(2)}, u32[]{:S(2)}) %collective-permute-start.5) | collective-permute-done | bytes 229408 | tf_op jit(solution)/shard_map/ppermute | solution.py:514
  41.6 4.8 %collective-permute-done.6 = f32[1,448,128]{2,1,0:T(8,128)S(1)} collective-permute-done((f32[1,448,128]{2,1,0:T(8,128)S(1)}, f32[1,448,128]{2,1,0:T(8,128)S(1)}, u32[]{:S(2)}, u32[]{:S(2)}) %collective-permute-start.6) | collective-permute-done | bytes 229408 | tf_op jit(solution)/shard_map/ppermute | solution.py:514
  47.7 7.3 %collective-permute-done.7 = f32[2,448,128]{2,1,0:T(8,128)S(1)} collective-permute-done((f32[2,448,128]{2,1,0:T(8,128)S(1)}, f32[2,448,128]{2,1,0:T(8,128)S(1)}, u32[]{:S(2)}, u32[]{:S(2)}) %collective-permute-start.7) | collective-permute-done | bytes 458784 | tf_op jit(solution)/shard_map/ppermute | solution.py:514
  55.2 7.8 %features.2 = (bf16[1024,512]{1,0:T(8,128)(2,1)S(1)}, bf16[1024,512]{1,0:T(8,128)(2,1)S(1)}, bf16[512,1024]{1,0:T(8,128)(2,1)S(1)}, bf16[512,1024]{1,0:T(8,128)(2,1)S(1)}) custom-call(s32[9]{0:T(128)S(1)} %stack.39.s_ref, f32[440,1024]{1,0:T(8,128)S(1)} %bitcast.16, f32[4,448,128]{2,1,0:T(8,128)S(1)} %pad_maximum_fusion.2.p_ref), custom_call_target="tpu_custom_call" | custom-call | flops 2768240640 | bytes 5996544 | tf_op jit(solution)/shard_map/features/pallas_call | solution.py:115
  63.1 7.8 %features.3 = (bf16[1024,512]{1,0:T(8,128)(2,1)S(1)}, bf16[1024,512]{1,0:T(8,128)(2,1)S(1)}, bf16[512,1024]{1,0:T(8,128)(2,1)S(1)}, bf16[512,1024]{1,0:T(8,128)(2,1)S(1)}) custom-call(s32[9]{0:T(128)S(1)} %stack.39.s_ref, f32[440,1024]{1,0:T(8,128)S(1)} %bitcast.17, f32[4,448,128]{2,1,0:T(8,128)S(1)} %collective-permute-done.8.p_ref), custom_call_target="tpu_custom_call" | custom-call | flops 2768240640 | bytes 5996544 | tf_op jit(solution)/shard_map/features/pallas_call | solution.py:115
  70.9 3.0 %gram.2 = f32[16,5,16,256]{3,2,1,0:T(8,128)S(1)} custom-call(s32[9]{0:T(128)S(1)} %stack.39.s_ref, bf16[1024,512]{1,0:T(8,128)(2,1)S(1)} %get-tuple-element.68.mh.oh.bh, bf16[1024,512]{1,0:T(8,128)(2,1)S(1)} %get-tuple-element.69.ml.ol.bl, bf16[512,1024]{1,0:T(8,128)(2,1)S(1)} %get-tuple-element.82.mth.bth.oth, ...), custom_call_target="tpu_custom_call" | custom-call | flops 2013265920 | bytes 8388608 | tf_op jit(solution)/shard_map/gram/pallas_call | solution.py:170
  73.9 6.0 %cross.4 = f32[4,1024,128]{2,1,0:T(8,128)S(1)} custom-call(s32[9]{0:T(128)S(1)} %stack.39.s_ref, f32[1024,2048]{1,0:T(8,128)S(1)} %bitcast.13, bf16[512,1024]{1,0:T(8,128)(2,1)S(1)} %get-tuple-element.80.oth.ath.mth, bf16[512,1024]{1,0:T(8,128)(2,1)S(1)} %get-tuple-element.81.otl.atl.mtl, bf16[512,1024]{1,0:T(8,128)(2,1)S(1)} %get-tuple-element.82.mth.bth.oth, ...), custom_call_target="tpu_custom_call" | custom-call | flops 3221225472 | bytes 4194304 | tf_op jit(solution)/shard_map/cross/pallas_call | solution.py:212
  80.5 3.1 %gram.3 = f32[16,5,16,256]{3,2,1,0:T(8,128)S(1)} custom-call(s32[9]{0:T(128)S(1)} %stack.39.s_ref, bf16[1024,512]{1,0:T(8,128)(2,1)S(1)} %get-tuple-element.64.oh.mh.ah, bf16[1024,512]{1,0:T(8,128)(2,1)S(1)} %get-tuple-element.65.ol.ml.al, bf16[512,1024]{1,0:T(8,128)(2,1)S(1)} %get-tuple-element.80.oth.ath.mth, ...), custom_call_target="tpu_custom_call" | custom-call | flops 2013265920 | bytes 8388608 | tf_op jit(solution)/shard_map/gram/pallas_call | solution.py:170
  83.6 2.5 collective-permute-done.9
  86.4 6.0 %cross.5 = f32[4,1024,128]{2,1,0:T(8,128)S(1)} custom-call(s32[9]{0:T(128)S(1)} %stack.39.s_ref, f32[1024,2048]{1,0:T(8,128)S(1)} %bitcast.13, bf16[512,1024]{1,0:T(8,128)(2,1)S(1)} %get-tuple-element.80.oth.ath.mth, bf16[512,1024]{1,0:T(8,128)(2,1)S(1)} %get-tuple-element.81.otl.atl.mtl, bf16[512,1024]{1,0:T(8,128)(2,1)S(1)} %get-tuple-element.82.mth.bth.oth, ...), custom_call_target="tpu_custom_call" | custom-call | flops 3221225472 | bytes 4194304 | tf_op jit(solution)/shard_map/cross/pallas_call | solution.py:212
  92.3 6.0 %cross.6 = f32[4,1024,128]{2,1,0:T(8,128)S(1)} custom-call(s32[9]{0:T(128)S(1)} %stack.39.s_ref, f32[1024,2048]{1,0:T(8,128)S(1)} %bitcast.13, bf16[512,1024]{1,0:T(8,128)(2,1)S(1)} %get-tuple-element.80.oth.ath.mth, bf16[512,1024]{1,0:T(8,128)(2,1)S(1)} %get-tuple-element.81.otl.atl.mtl, bf16[512,1024]{1,0:T(8,128)(2,1)S(1)} %get-tuple-element.82.mth.bth.oth, ...), custom_call_target="tpu_custom_call" | custom-call | flops 3221225472 | bytes 4194304 | tf_op jit(solution)/shard_map/cross/pallas_call | solution.py:212
  101.0 8.4 %collective-permute-done.10 = f32[8,5,16,256]{3,2,1,0:T(8,128)S(1)} collective-permute-done((f32[8,5,16,256]{3,2,1,0:T(8,128)S(1)}, f32[8,5,16,256]{3,2,1,0:T(8,128)S(1)}, u32[]{:S(2)}, u32[]{:S(2)}) %collective-permute-start.10) | collective-permute-done | bytes 655392 | tf_op jit(solution)/shard_map/ppermute | solution.py:514
  110.8 9.4 %collective-permute-done.11 = f32[4,5,16,256]{3,2,1,0:T(8,128)S(1)} collective-permute-done((f32[4,5,16,256]{3,2,1,0:T(8,128)S(1)}, f32[4,5,16,256]{3,2,1,0:T(8,128)S(1)}, u32[]{:S(2)}, u32[]{:S(2)}) %collective-permute-start.11) | collective-permute-done | bytes 327712 | tf_op jit(solution)/shard_map/ppermute | solution.py:514
  120.3 3.9 %collective-permute-done.31 = f32[2,1024,128]{2,1,0:T(8,128)S(1)} collective-permute-done((f32[2,1024,128]{2,1,0:T(8,128)S(1)}, f32[2,1024,128]{2,1,0:T(8,128)S(1)}, u32[]{:S(2)}, u32[]{:S(2)}) %collective-permute-start.31) | collective-permute-done | bytes 1048608 | tf_op jit(solution)/shard_map/ppermute | solution.py:514
  125.6 6.0 %cross.7 = f32[4,1024,128]{2,1,0:T(8,128)S(1)} custom-call(s32[9]{0:T(128)S(1)} %stack.39.s_ref, f32[1024,2048]{1,0:T(8,128)S(1)} %bitcast.13, bf16[512,1024]{1,0:T(8,128)(2,1)S(1)} %get-tuple-element.80.oth.ath.mth, bf16[512,1024]{1,0:T(8,128)(2,1)S(1)} %get-tuple-element.81.otl.atl.mtl, bf16[512,1024]{1,0:T(8,128)(2,1)S(1)} %get-tuple-element.82.mth.bth.oth, ...), custom_call_target="tpu_custom_call" | custom-call | flops 3221225472 | bytes 4194304 | tf_op jit(solution)/shard_map/cross/pallas_call | solution.py:212
  132.3 4.6 %collective-permute-done.14 = f32[2,5,16,256]{3,2,1,0:T(8,128)S(1)} collective-permute-done((f32[2,5,16,256]{3,2,1,0:T(8,128)S(1)}, f32[2,5,16,256]{3,2,1,0:T(8,128)S(1)}, u32[]{:S(2)}, u32[]{:S(2)}) %collective-permute-start.14) | collective-permute-done | bytes 163872 | tf_op jit(solution)/shard_map/ppermute | solution.py:514
  137.0 2.1 collective-permute-start.15
  142.8 2.7 collective-permute-start.16
  148.3 2.4 collective-permute-start.17
  150.8 2.6 collective-permute-start.34
  154.1 2.4 collective-permute-start.18
  156.5 4.2 %collective-permute-done.34 = f32[1,256,128]{2,1,0:T(8,128)S(1)} collective-permute-done((f32[1,256,128]{2,1,0:T(8,128)S(1)}, f32[1,256,128]{2,1,0:T(8,128)S(1)}, u32[]{:S(2)}, u32[]{:S(2)}) %collective-permute-start.34) | collective-permute-done | bytes 131104 | tf_op jit(solution)/shard_map/ppermute | solution.py:514
  161.6 7.7 %collective-permute-start.19 = (f32[8,5,16,256]{3,2,1,0:T(8,128)S(1)}, f32[8,5,16,256]{3,2,1,0:T(8,128)S(1)}, u32[]{:S(2)}, u32[]{:S(2)}) collective-permute-start(f32[8,5,16,256]{3,2,1,0:T(8,128)S(1)} %pad_maximum_fusion.3), channel_id=1, source_target_pairs={{0,2},{1,5},{2,0},{3,7},{4,6},{5,1},{6,4},{7,3},{8,10},{9,13},{10,... | collective-permute-start | bytes 1966088 | tf_op jit(solution)/shard_map/ppermute | solution.py:514
  171.6 7.8 %collective-permute-done.19 = f32[8,5,16,256]{3,2,1,0:T(8,128)S(1)} collective-permute-done((f32[8,5,16,256]{3,2,1,0:T(8,128)S(1)}, f32[8,5,16,256]{3,2,1,0:T(8,128)S(1)}, u32[]{:S(2)}, u32[]{:S(2)}) %collective-permute-start.19) | collective-permute-done | bytes 655392 | tf_op jit(solution)/shard_map/ppermute | solution.py:514
  179.4 7.5 %assemble.1 = (f32[512,512]{1,0:T(8,128)S(1)}, f32[256,512]{1,0:T(8,128)S(1)}) custom-call(s32[9]{0:T(128)S(1)} %stack.39.s_ref, f32[16,5,16,256]{3,2,1,0:T(8,128)S(1)} %constant_dynamic-update-slice_fusion.g_ref), custom_call_target="tpu_custom_call" | custom-call | flops 10000000000 | bytes 4000000 | tf_op jit(solution)/shard_map/assemble/pallas_call | solution.py:330
  186.9 6.5 %factor.3.m_ref = f32[512,512]{1,0:T(8,128)S(1)} custom-call(f32[512,512]{1,0:T(8,128)S(1)} %get-tuple-element.85.m_ref), custom_call_target="tpu_custom_call" | custom-call | flops 10000000000 | bytes 4000000 | tf_op jit(solution)/shard_map/factor/pallas_call | solution.py:352
  194.5 6.3 %factor.4.m_ref = f32[512,512]{1,0:T(8,128)S(1)} custom-call(f32[512,512]{1,0:T(8,128)S(1)} %factor.3.m_ref), custom_call_target="tpu_custom_call" | custom-call | flops 10000000000 | bytes 4000000 | tf_op jit(solution)/shard_map/factor/pallas_call | solution.py:352
  201.0 4.7 %collective-permute-start.25 = (f32[1,256,128]{2,1,0:T(8,128)S(1)}, f32[1,256,128]{2,1,0:T(8,128)S(1)}, u32[]{:S(2)}, u32[]{:S(2)}) collective-permute-start(f32[1,256,128]{2,1,0:T(8,128)S(1)} %slice.127), channel_id=1, source_target_pairs={{0,16},{1,17},{2,18},{3,19},{4,20},{5,21},{6,22},{7,23},{8,24},{9,... | collective-permute-start | bytes 393224 | tf_op jit(solution)/shard_map/ppermute | solution.py:514
  205.7 7.8 %factor.5.own_ref = f32[512,512]{1,0:T(8,128)S(1)} custom-call(f32[512,512]{1,0:T(8,128)S(1)} %factor.4.m_ref), custom_call_target="tpu_custom_call" | custom-call | flops 10000000000 | bytes 4000000 | tf_op jit(solution)/shard_map/factor/pallas_call | solution.py:352
  213.6 9.0 %collective-permute-done.26 = f32[1,256,128]{2,1,0:T(8,128)S(1)} collective-permute-done((f32[1,256,128]{2,1,0:T(8,128)S(1)}, f32[1,256,128]{2,1,0:T(8,128)S(1)}, u32[]{:S(2)}, u32[]{:S(2)}) %collective-permute-start.26) | collective-permute-done | bytes 131104 | tf_op jit(solution)/shard_map/ppermute | solution.py:514
  225.0 6.1 %collective-permute-done.27 = f32[1,512,128]{2,1,0:T(8,128)S(1)} collective-permute-done((f32[1,512,128]{2,1,0:T(8,128)S(1)}, f32[1,512,128]{2,1,0:T(8,128)S(1)}, u32[]{:S(2)}, u32[]{:S(2)}) %collective-permute-start.27) | collective-permute-done | bytes 262176 | tf_op jit(solution)/shard_map/ppermute | solution.py:514
  232.2 2.4 couple.1.b_ref
  234.6 4.3 %solve.3.wa_ref = f32[2,1024,128]{2,1,0:T(8,128)S(1)} custom-call(s32[9]{0:T(128)S(1)} %stack.39.s_ref, f32[512,512]{1,0:T(8,128)S(1)} %factor.5.own_ref, f32[512,512]{1,0:T(8,128)S(1)} %collective-permute-done.20.oth_ref, f32[512,512]{1,0:T(8,128)S(1)} %couple.1.b_ref, f32[2,1024,128]{2,1,0:T(8,128)S(1)} %pad_maximum_fusion.1.c_ref), custom_call_target="tpu_custom_call" | custom-call | flops 2415919104 | bytes 2097152 | tf_op jit(solution)/shard_map/solve/pallas_call | solution.py:424
  239.0 2.4 collective-permute-start.38
  241.4 4.3 %solve.2.wa_ref = f32[2,1024,128]{2,1,0:T(8,128)S(1)} custom-call(s32[9]{0:T(128)S(1)} %stack.39.s_ref, f32[512,512]{1,0:T(8,128)S(1)} %factor.5.own_ref, f32[512,512]{1,0:T(8,128)S(1)} %collective-permute-done.20.oth_ref, f32[512,512]{1,0:T(8,128)S(1)} %couple.1.b_ref, f32[2,1024,128]{2,1,0:T(8,128)S(1)} %pad_maximum_fusion.c_ref), custom_call_target="tpu_custom_call" | custom-call | flops 2415919104 | bytes 2097152 | tf_op jit(solution)/shard_map/solve/pallas_call | solution.py:424
  247.7 6.5 %collective-permute-done.38.wa_ref = f32[2,1024,128]{2,1,0:T(8,128)S(1)} collective-permute-done((f32[2,1024,128]{2,1,0:T(8,128)S(1)}, f32[2,1024,128]{2,1,0:T(8,128)S(1)}, u32[]{:S(2)}, u32[]{:S(2)}) %collective-permute-start.38) | collective-permute-done | bytes 1048608 | tf_op jit(solution)/shard_map/ppermute | solution.py:514
  254.1 11.2 %collective-permute-done.29.wa_ref = f32[2,1024,128]{2,1,0:T(8,128)S(1)} collective-permute-done((f32[2,1024,128]{2,1,0:T(8,128)S(1)}, f32[2,1024,128]{2,1,0:T(8,128)S(1)}, u32[]{:S(2)}, u32[]{:S(2)}) %collective-permute-start.29) | collective-permute-done | bytes 1048608 | tf_op jit(solution)/shard_map/ppermute | solution.py:514
  265.4 6.5 %residual.4 = (f32[1024,2048]{1,0:T(8,128)}, f32[2,512,2048]{2,1,0:T(8,128)}) custom-call(s32[9]{0:T(128)S(1)} %stack.39.s_ref, f32[1024,2048]{1,0:T(8,128)S(1)} %bitcast.13, bf16[1024,512]{1,0:T(8,128)(2,1)S(1)} %get-tuple-element.64.oh.mh.ah, bf16[1024,512]{1,0:T(8,128)(2,1)S(1)} %get-tuple-element.65.ol.ml.al, ...), custom_call_target="tpu_custom_call" | custom-call | flops 3221225472 | bytes 6291456 | tf_op jit(solution)/shard_map/residual/pallas_call | solution.py:478
  271.9 6.5 %residual.5 = (f32[1024,2048]{1,0:T(8,128)}, f32[2,512,2048]{2,1,0:T(8,128)}) custom-call(s32[9]{0:T(128)S(1)} %stack.39.s_ref, f32[1024,2048]{1,0:T(8,128)S(1)} %bitcast.13, bf16[1024,512]{1,0:T(8,128)(2,1)S(1)} %get-tuple-element.64.oh.mh.ah, bf16[1024,512]{1,0:T(8,128)(2,1)S(1)} %get-tuple-element.65.ol.ml.al, ...), custom_call_target="tpu_custom_call", output_to_operand_aliasing={{0}: (8, {}), {1}: (9, {})} | custom-call | flops 3221225472 | bytes 6291456 | tf_op jit(solution)/shard_map/residual/pallas_call | solution.py:478
  278.3 6.5 %residual.6 = (f32[1024,2048]{1,0:T(8,128)}, f32[2,512,2048]{2,1,0:T(8,128)}) custom-call(s32[9]{0:T(128)S(1)} %stack.39.s_ref, f32[1024,2048]{1,0:T(8,128)S(1)} %bitcast.13, bf16[1024,512]{1,0:T(8,128)(2,1)S(1)} %get-tuple-element.64.oh.mh.ah, bf16[1024,512]{1,0:T(8,128)(2,1)S(1)} %get-tuple-element.65.ol.ml.al, ...), custom_call_target="tpu_custom_call", output_to_operand_aliasing={{0}: (8, {}), {1}: (9, {})} | custom-call | flops 3221225472 | bytes 6291456 | tf_op jit(solution)/shard_map/residual/pallas_call | solution.py:478
  284.8 6.5 %residual.7 = (f32[1024,2048]{1,0:T(8,128)}, f32[2,512,2048]{2,1,0:T(8,128)}) custom-call(s32[9]{0:T(128)S(1)} %stack.39.s_ref, f32[1024,2048]{1,0:T(8,128)S(1)} %bitcast.13, bf16[1024,512]{1,0:T(8,128)(2,1)S(1)} %get-tuple-element.64.oh.mh.ah, bf16[1024,512]{1,0:T(8,128)(2,1)S(1)} %get-tuple-element.65.ol.ml.al, ...), custom_call_target="tpu_custom_call", output_to_operand_aliasing={{0}: (8, {}), {1}: (9, {})} | custom-call | flops 3221225472 | bytes 6291456 | tf_op jit(solution)/shard_map/residual/pallas_call | solution.py:478
  (116 shorter events, 33.6 us)
Async XLA Ops:
  0.6 2.9 collective-permute-start
  1.2 2.3 collective-permute-start.1
  3.5 1.2 copy-start
  4.7 0.7 copy-start.1
  5.3 0.7 copy-start.2
  7.1 9.4 %collective-permute-start.2 = (f32[2,448,128]{2,1,0:T(8,128)S(1)}, f32[2,448,128]{2,1,0:T(8,128)S(1)}, u32[]{:S(2)}, u32[]{:S(2)}) collective-permute-start(f32[2,448,128]{2,1,0:T(8,128)S(1)} %slice.113), channel_id=1, source_target_pairs={{0,2},{1,5},{2,0},{3,7},{4,6},{5,1},{6,4},{7,3},{8,10},{9,13},{10,... | collective-permute-start | bytes 1376264 | tf_op jit(solution)/shard_map/ppermute | solution.py:514
  16.6 6.1 %collective-permute-start.3 = (f32[1,448,128]{2,1,0:T(8,128)S(1)}, f32[1,448,128]{2,1,0:T(8,128)S(1)}, u32[]{:S(2)}, u32[]{:S(2)}) collective-permute-start(f32[1,448,128]{2,1,0:T(8,128)S(1)} %slice.115), channel_id=1, source_target_pairs={{0,4},{1,3},{2,6},{3,1},{4,0},{5,7},{6,2},{7,5},{8,12},{9,11},{10,... | collective-permute-start | bytes 688136 | tf_op jit(solution)/shard_map/ppermute | solution.py:514
  22.7 6.3 %collective-permute-start.4 = (f32[1,448,128]{2,1,0:T(8,128)S(1)}, f32[1,448,128]{2,1,0:T(8,128)S(1)}, u32[]{:S(2)}, u32[]{:S(2)}) collective-permute-start(f32[1,448,128]{2,1,0:T(8,128)S(1)} %slice_add_fusion.9), channel_id=1, source_target_pairs={{0,8},{1,9},{2,10},{3,11},{4,12},{5,13},{6,14},{7,15},{8,0},{9,1},... | collective-permute-start | bytes 688136 | tf_op jit(solution)/shard_map/ppermute | solution.py:514
  29.1 11.2 %collective-permute-start.5 = (f32[1,448,128]{2,1,0:T(8,128)S(1)}, f32[1,448,128]{2,1,0:T(8,128)S(1)}, u32[]{:S(2)}, u32[]{:S(2)}) collective-permute-start(f32[1,448,128]{2,1,0:T(8,128)S(1)} %add.109), channel_id=1, source_target_pairs={{0,16},{1,17},{2,18},{3,19},{4,20},{5,21},{6,22},{7,23},{8,24},{9,... | collective-permute-start | bytes 688136 | tf_op jit(solution)/shard_map/ppermute | solution.py:514
  40.4 14.8 %copy-start.3 = (f32[1024,440]{0,1:T(8,128)S(1)}, f32[1024,440]{0,1:T(8,128)}, u32[]{:S(2)}) copy-start(f32[1024,440]{0,1:T(8,128)} %param.5) | copy-start | bytes 5406724
  40.4 6.1 %collective-permute-start.6 = (f32[1,448,128]{2,1,0:T(8,128)S(1)}, f32[1,448,128]{2,1,0:T(8,128)S(1)}, u32[]{:S(2)}, u32[]{:S(2)}) collective-permute-start(f32[1,448,128]{2,1,0:T(8,128)S(1)} %add.110), channel_id=1, source_target_pairs={{0,4},{1,3},{2,6},{3,1},{4,0},{5,7},{6,2},{7,5},{8,12},{9,11},{10,... | collective-permute-start | bytes 688136 | tf_op jit(solution)/shard_map/ppermute | solution.py:514
  46.5 8.5 %collective-permute-start.7 = (f32[2,448,128]{2,1,0:T(8,128)S(1)}, f32[2,448,128]{2,1,0:T(8,128)S(1)}, u32[]{:S(2)}, u32[]{:S(2)}) collective-permute-start(f32[2,448,128]{2,1,0:T(8,128)S(1)} %pad_maximum_fusion.6), channel_id=1, source_target_pairs={{0,2},{1,5},{2,0},{3,7},{4,6},{5,1},{6,4},{7,3},{8,10},{9,13},{10,... | collective-permute-start | bytes 1376264 | tf_op jit(solution)/shard_map/ppermute | solution.py:514
  55.1 8.0 %collective-permute-start.8 = (f32[4,448,128]{2,1,0:T(8,128)S(1)}, f32[4,448,128]{2,1,0:T(8,128)S(1)}, u32[]{:S(2)}, u32[]{:S(2)}) collective-permute-start(f32[4,448,128]{2,1,0:T(8,128)S(1)} %pad_maximum_fusion.2.p_ref), channel_id=1, source_target_pairs={{0,1},{1,0},{2,3},{3,2},{4,5},{5,4},{6,7},{7,6},{8,9},{9,8},{10,11... | collective-permute-start | bytes 2752520 | tf_op jit(solution)/shard_map/ppermute | solution.py:514
  55.2 18.7 %slice-start = ((s8[8388608]{0:T(1024)(128)(4,1)}), s8[4194304]{0:T(1024)(128)(4,1)S(1)}, s32[]{:S(2)}) async-start(s8[8388608]{0:T(1024)(128)(4,1)} %bitcast.12), calls=%async_computation | async-start | bytes 8388608
  63.1 10.9 %slice-start.1 = ((s8[8388608]{0:T(1024)(128)(4,1)}), s8[4194304]{0:T(1024)(128)(4,1)S(1)}, s32[]{:S(2)}) async-start(s8[8388608]{0:T(1024)(128)(4,1)} %bitcast.12), calls=%async_computation.1 | async-start | bytes 8388608
  79.9 6.5 %collective-permute-start.12 = (f32[4,1024,128]{2,1,0:T(8,128)S(1)}, f32[4,1024,128]{2,1,0:T(8,128)S(1)}, u32[]{:S(2)}, u32[]{:S(2)}) collective-permute-start(f32[4,1024,128]{2,1,0:T(8,128)S(1)} %cross.4), channel_id=1, source_target_pairs={{0,1},{1,0},{2,3},{3,2},{4,5},{5,4},{6,7},{7,6},{8,9},{9,8},{10,11... | collective-permute-start | bytes 6291464 | tf_op jit(solution)/shard_map/ppermute | solution.py:514
  80.4 5.7 %collective-permute-start.9 = (f32[16,5,16,256]{3,2,1,0:T(8,128)S(1)}, f32[16,5,16,256]{3,2,1,0:T(8,128)S(1)}, u32[]{:S(2)}, u32[]{:S(2)}) collective-permute-start(f32[16,5,16,256]{3,2,1,0:T(8,128)S(1)} %gram.2), channel_id=1, source_target_pairs={{0,1},{1,0},{2,3},{3,2},{4,5},{5,4},{6,7},{7,6},{8,9},{9,8},{10,11... | collective-permute-start | bytes 3932168 | tf_op jit(solution)/shard_map/ppermute | solution.py:514
  98.3 27.3 %collective-permute-start.13 = (f32[4,1024,128]{2,1,0:T(8,128)S(1)}, f32[4,1024,128]{2,1,0:T(8,128)S(1)}, u32[]{:S(2)}, u32[]{:S(2)}) collective-permute-start(f32[4,1024,128]{2,1,0:T(8,128)S(1)} %cross.6), channel_id=1, source_target_pairs={{0,1},{1,0},{2,3},{3,2},{4,5},{5,4},{6,7},{7,6},{8,9},{9,8},{10,11... | collective-permute-start | bytes 6291464 | tf_op jit(solution)/shard_map/ppermute | solution.py:514
  98.8 10.7 %collective-permute-start.10 = (f32[8,5,16,256]{3,2,1,0:T(8,128)S(1)}, f32[8,5,16,256]{3,2,1,0:T(8,128)S(1)}, u32[]{:S(2)}, u32[]{:S(2)}) collective-permute-start(f32[8,5,16,256]{3,2,1,0:T(8,128)S(1)} %slice.117), channel_id=1, source_target_pairs={{0,2},{1,5},{2,0},{3,7},{4,6},{5,1},{6,4},{7,3},{8,10},{9,13},{10,... | collective-permute-start | bytes 1966088 | tf_op jit(solution)/shard_map/ppermute | solution.py:514
  100.1 24.1 %collective-permute-start.31 = (f32[2,1024,128]{2,1,0:T(8,128)S(1)}, f32[2,1024,128]{2,1,0:T(8,128)S(1)}, u32[]{:S(2)}, u32[]{:S(2)}) collective-permute-start(f32[2,1024,128]{2,1,0:T(8,128)S(1)} %slice.129), channel_id=1, source_target_pairs={{0,2},{1,5},{2,0},{3,7},{4,6},{5,1},{6,4},{7,3},{8,10},{9,13},{10,... | collective-permute-start | bytes 3145736 | tf_op jit(solution)/shard_map/ppermute | solution.py:514
  109.6 10.6 %collective-permute-start.11 = (f32[4,5,16,256]{3,2,1,0:T(8,128)S(1)}, f32[4,5,16,256]{3,2,1,0:T(8,128)S(1)}, u32[]{:S(2)}, u32[]{:S(2)}) collective-permute-start(f32[4,5,16,256]{3,2,1,0:T(8,128)S(1)} %slice.119), channel_id=1, source_target_pairs={{0,4},{1,3},{2,6},{3,1},{4,0},{5,7},{6,2},{7,5},{8,12},{9,11},{10,... | collective-permute-start | bytes 983048 | tf_op jit(solution)/shard_map/ppermute | solution.py:514
  124.3 14.8 %collective-permute-start.32 = (f32[1,1024,128]{2,1,0:T(8,128)S(1)}, f32[1,1024,128]{2,1,0:T(8,128)S(1)}, u32[]{:S(2)}, u32[]{:S(2)}) collective-permute-start(f32[1,1024,128]{2,1,0:T(8,128)S(1)} %slice.131), channel_id=1, source_target_pairs={{0,4},{1,3},{2,6},{3,1},{4,0},{5,7},{6,2},{7,5},{8,12},{9,11},{10,... | collective-permute-start | bytes 1572872 | tf_op jit(solution)/shard_map/ppermute | solution.py:514
  131.6 5.4 %collective-permute-start.14 = (f32[2,5,16,256]{3,2,1,0:T(8,128)S(1)}, f32[2,5,16,256]{3,2,1,0:T(8,128)S(1)}, u32[]{:S(2)}, u32[]{:S(2)}) collective-permute-start(f32[2,5,16,256]{3,2,1,0:T(8,128)S(1)} %slice.93), channel_id=1, source_target_pairs={{0,8},{1,9},{2,10},{3,11},{4,12},{5,13},{6,14},{7,15},{8,0},{9,1},... | collective-permute-start | bytes 491528 | tf_op jit(solution)/shard_map/ppermute | solution.py:514
  137.0 5.7 %collective-permute-start.15 = (f32[1,5,16,256]{3,2,1,0:T(8,128)S(1)}, f32[1,5,16,256]{3,2,1,0:T(8,128)S(1)}, u32[]{:S(2)}, u32[]{:S(2)}) collective-permute-start(f32[1,5,16,256]{3,2,1,0:T(8,128)S(1)} %slice.121), channel_id=1, source_target_pairs={{0,16},{1,17},{2,18},{3,19},{4,20},{5,21},{6,22},{7,23},{8,24},{9,... | collective-permute-start | bytes 245768 | tf_op jit(solution)/shard_map/ppermute | solution.py:514
  139.2 11.5 %collective-permute-start.33 = (f32[1,512,128]{2,1,0:T(8,128)S(1)}, f32[1,512,128]{2,1,0:T(8,128)S(1)}, u32[]{:S(2)}, u32[]{:S(2)}) collective-permute-start(f32[1,512,128]{2,1,0:T(8,128)S(1)} %slice.133), channel_id=1, source_target_pairs={{0,8},{1,9},{2,10},{3,11},{4,12},{5,13},{6,14},{7,15},{8,0},{9,1},... | collective-permute-start | bytes 786440 | tf_op jit(solution)/shard_map/ppermute | solution.py:514
  142.8 5.5 %collective-permute-start.16 = (f32[1,5,16,256]{3,2,1,0:T(8,128)S(1)}, f32[1,5,16,256]{3,2,1,0:T(8,128)S(1)}, u32[]{:S(2)}, u32[]{:S(2)}) collective-permute-start(f32[1,5,16,256]{3,2,1,0:T(8,128)S(1)} %get-tuple-element.95), channel_id=1, source_target_pairs={{0,16},{1,17},{2,18},{3,19},{4,20},{5,21},{6,22},{7,23},{8,24},{9,... | collective-permute-start | bytes 245768 | tf_op jit(solution)/shard_map/ppermute | solution.py:514
  145.5 25.8 %collective-permute-start.22 = (f32[2,1024,128]{2,1,0:T(8,128)S(1)}, f32[2,1024,128]{2,1,0:T(8,128)S(1)}, u32[]{:S(2)}, u32[]{:S(2)}) collective-permute-start(f32[2,1024,128]{2,1,0:T(8,128)S(1)} %slice.97), channel_id=1, source_target_pairs={{0,2},{1,5},{2,0},{3,7},{4,6},{5,1},{6,4},{7,3},{8,10},{9,13},{10,... | collective-permute-start | bytes 3145736 | tf_op jit(solution)/shard_map/ppermute | solution.py:514
  148.3 5.7 %collective-permute-start.17 = (f32[2,5,16,256]{3,2,1,0:T(8,128)S(1)}, f32[2,5,16,256]{3,2,1,0:T(8,128)S(1)}, u32[]{:S(2)}, u32[]{:S(2)}) collective-permute-start(f32[2,5,16,256]{3,2,1,0:T(8,128)S(1)} %pad_maximum_fusion.10), channel_id=1, source_target_pairs={{0,8},{1,9},{2,10},{3,11},{4,12},{5,13},{6,14},{7,15},{8,0},{9,1},... | collective-permute-start | bytes 491528 | tf_op jit(solution)/shard_map/ppermute | solution.py:514
  150.8 9.9 %collective-permute-start.34 = (f32[1,256,128]{2,1,0:T(8,128)S(1)}, f32[1,256,128]{2,1,0:T(8,128)S(1)}, u32[]{:S(2)}, u32[]{:S(2)}) collective-permute-start(f32[1,256,128]{2,1,0:T(8,128)S(1)} %slice.135), channel_id=1, source_target_pairs={{0,16},{1,17},{2,18},{3,19},{4,20},{5,21},{6,22},{7,23},{8,24},{9,... | collective-permute-start | bytes 393224 | tf_op jit(solution)/shard_map/ppermute | solution.py:514
  154.1 7.5 %collective-permute-start.18 = (f32[4,5,16,256]{3,2,1,0:T(8,128)S(1)}, f32[4,5,16,256]{3,2,1,0:T(8,128)S(1)}, u32[]{:S(2)}, u32[]{:S(2)}) collective-permute-start(f32[4,5,16,256]{3,2,1,0:T(8,128)S(1)} %pad_maximum_fusion.7), channel_id=1, source_target_pairs={{0,4},{1,3},{2,6},{3,1},{4,0},{5,7},{6,2},{7,5},{8,12},{9,11},{10,... | collective-permute-start | bytes 983048 | tf_op jit(solution)/shard_map/ppermute | solution.py:514
  160.7 8.5 %collective-permute-start.35 = (f32[1,256,128]{2,1,0:T(8,128)S(1)}, f32[1,256,128]{2,1,0:T(8,128)S(1)}, u32[]{:S(2)}, u32[]{:S(2)}) collective-permute-start(f32[1,256,128]{2,1,0:T(8,128)S(1)} %slice_add_fusion.11), channel_id=1, source_target_pairs={{0,16},{1,17},{2,18},{3,19},{4,20},{5,21},{6,22},{7,23},{8,24},{9,... | collective-permute-start | bytes 393224 | tf_op jit(solution)/shard_map/ppermute | solution.py:514
  161.6 17.8 %collective-permute-start.19 = (f32[8,5,16,256]{3,2,1,0:T(8,128)S(1)}, f32[8,5,16,256]{3,2,1,0:T(8,128)S(1)}, u32[]{:S(2)}, u32[]{:S(2)}) collective-permute-start(f32[8,5,16,256]{3,2,1,0:T(8,128)S(1)} %pad_maximum_fusion.3), channel_id=1, source_target_pairs={{0,2},{1,5},{2,0},{3,7},{4,6},{5,1},{6,4},{7,3},{8,10},{9,13},{10,... | collective-permute-start | bytes 1966088 | tf_op jit(solution)/shard_map/ppermute | solution.py:514
  169.3 53.5 %collective-permute-start.36 = (f32[1,512,128]{2,1,0:T(8,128)S(1)}, f32[1,512,128]{2,1,0:T(8,128)S(1)}, u32[]{:S(2)}, u32[]{:S(2)}) collective-permute-start(f32[1,512,128]{2,1,0:T(8,128)S(1)} %pad_maximum_fusion.9), channel_id=1, source_target_pairs={{0,8},{1,9},{2,10},{3,11},{4,12},{5,13},{6,14},{7,15},{8,0},{9,1},... | collective-permute-start | bytes 786440 | tf_op jit(solution)/shard_map/ppermute | solution.py:514
  171.5 21.9 %collective-permute-start.23 = (f32[1,1024,128]{2,1,0:T(8,128)S(1)}, f32[1,1024,128]{2,1,0:T(8,128)S(1)}, u32[]{:S(2)}, u32[]{:S(2)}) collective-permute-start(f32[1,1024,128]{2,1,0:T(8,128)S(1)} %slice.123), channel_id=1, source_target_pairs={{0,4},{1,3},{2,6},{3,1},{4,0},{5,7},{6,2},{7,5},{8,12},{9,11},{10,... | collective-permute-start | bytes 1572872 | tf_op jit(solution)/shard_map/ppermute | solution.py:514
  193.5 7.5 %collective-permute-start.24 = (f32[1,512,128]{2,1,0:T(8,128)S(1)}, f32[1,512,128]{2,1,0:T(8,128)S(1)}, u32[]{:S(2)}, u32[]{:S(2)}) collective-permute-start(f32[1,512,128]{2,1,0:T(8,128)S(1)} %slice.125), channel_id=1, source_target_pairs={{0,8},{1,9},{2,10},{3,11},{4,12},{5,13},{6,14},{7,15},{8,0},{9,1},... | collective-permute-start | bytes 786440 | tf_op jit(solution)/shard_map/ppermute | solution.py:514
  201.0 12.5 %collective-permute-start.25 = (f32[1,256,128]{2,1,0:T(8,128)S(1)}, f32[1,256,128]{2,1,0:T(8,128)S(1)}, u32[]{:S(2)}, u32[]{:S(2)}) collective-permute-start(f32[1,256,128]{2,1,0:T(8,128)S(1)} %slice.127), channel_id=1, source_target_pairs={{0,16},{1,17},{2,18},{3,19},{4,20},{5,21},{6,22},{7,23},{8,24},{9,... | collective-permute-start | bytes 393224 | tf_op jit(solution)/shard_map/ppermute | solution.py:514
  213.5 18.7 %collective-permute-start.20 = (f32[512,512]{1,0:T(8,128)S(1)}, f32[512,512]{1,0:T(8,128)S(1)}, u32[]{:S(2)}, u32[]{:S(2)}) collective-permute-start(f32[512,512]{1,0:T(8,128)S(1)} %factor.5.own_ref), channel_id=1, source_target_pairs={{0,1},{1,0},{2,3},{3,2},{4,5},{5,4},{6,7},{7,6},{8,9},{9,8},{10,11... | collective-permute-start | bytes 3145736 | tf_op jit(solution)/shard_map/ppermute | solution.py:514
  213.6 9.1 %collective-permute-start.26 = (f32[1,256,128]{2,1,0:T(8,128)S(1)}, f32[1,256,128]{2,1,0:T(8,128)S(1)}, u32[]{:S(2)}, u32[]{:S(2)}) collective-permute-start(f32[1,256,128]{2,1,0:T(8,128)S(1)} %slice_add_fusion.12), channel_id=1, source_target_pairs={{0,16},{1,17},{2,18},{3,19},{4,20},{5,21},{6,22},{7,23},{8,24},{9,... | collective-permute-start | bytes 393224 | tf_op jit(solution)/shard_map/ppermute | solution.py:514
  222.7 8.3 %collective-permute-start.27 = (f32[1,512,128]{2,1,0:T(8,128)S(1)}, f32[1,512,128]{2,1,0:T(8,128)S(1)}, u32[]{:S(2)}, u32[]{:S(2)}) collective-permute-start(f32[1,512,128]{2,1,0:T(8,128)S(1)} %pad_maximum_fusion.8), channel_id=1, source_target_pairs={{0,8},{1,9},{2,10},{3,11},{4,12},{5,13},{6,14},{7,15},{8,0},{9,1},... | collective-permute-start | bytes 786440 | tf_op jit(solution)/shard_map/ppermute | solution.py:514
  222.9 9.2 %collective-permute-start.37 = (f32[1,1024,128]{2,1,0:T(8,128)S(1)}, f32[1,1024,128]{2,1,0:T(8,128)S(1)}, u32[]{:S(2)}, u32[]{:S(2)}) collective-permute-start(f32[1,1024,128]{2,1,0:T(8,128)S(1)} %pad_maximum_fusion.5), channel_id=1, source_target_pairs={{0,4},{1,3},{2,6},{3,1},{4,0},{5,7},{6,2},{7,5},{8,12},{9,11},{10,... | collective-permute-start | bytes 1572872 | tf_op jit(solution)/shard_map/ppermute | solution.py:514
  223.0 9.2 %collective-permute-start.21 = (f32[256,512]{1,0:T(8,128)S(1)}, f32[256,512]{1,0:T(8,128)S(1)}, u32[]{:S(2)}, u32[]{:S(2)}) collective-permute-start(f32[256,512]{1,0:T(8,128)S(1)} %get-tuple-element.86.gown_ref), channel_id=1, source_target_pairs={{0,1},{1,0},{2,3},{3,2},{4,5},{5,4},{6,7},{7,6},{8,9},{9,8},{10,11... | collective-permute-start | bytes 1572872 | tf_op jit(solution)/shard_map/ppermute | solution.py:514
  231.1 10.2 %collective-permute-start.28 = (f32[1,1024,128]{2,1,0:T(8,128)S(1)}, f32[1,1024,128]{2,1,0:T(8,128)S(1)}, u32[]{:S(2)}, u32[]{:S(2)}) collective-permute-start(f32[1,1024,128]{2,1,0:T(8,128)S(1)} %pad_maximum_fusion.4), channel_id=1, source_target_pairs={{0,4},{1,3},{2,6},{3,1},{4,0},{5,7},{6,2},{7,5},{8,12},{9,11},{10,... | collective-permute-start | bytes 1572872 | tf_op jit(solution)/shard_map/ppermute | solution.py:514
  239.0 15.1 %collective-permute-start.38 = (f32[2,1024,128]{2,1,0:T(8,128)S(1)}, f32[2,1024,128]{2,1,0:T(8,128)S(1)}, u32[]{:S(2)}, u32[]{:S(2)}) collective-permute-start(f32[2,1024,128]{2,1,0:T(8,128)S(1)} %solve.3.wa_ref), channel_id=1, source_target_pairs={{0,2},{1,5},{2,0},{3,7},{4,6},{5,1},{6,4},{7,3},{8,10},{9,13},{10,... | collective-permute-start | bytes 3145736 | tf_op jit(solution)/shard_map/ppermute | solution.py:514
  245.8 19.6 %collective-permute-start.29 = (f32[2,1024,128]{2,1,0:T(8,128)S(1)}, f32[2,1024,128]{2,1,0:T(8,128)S(1)}, u32[]{:S(2)}, u32[]{:S(2)}) collective-permute-start(f32[2,1024,128]{2,1,0:T(8,128)S(1)} %solve.2.wa_ref), channel_id=1, source_target_pairs={{0,2},{1,5},{2,0},{3,7},{4,6},{5,1},{6,4},{7,3},{8,10},{9,13},{10,... | collective-permute-start | bytes 3145736 | tf_op jit(solution)/shard_map/ppermute | solution.py:514
  247.1 18.2 %collective-permute-start.41 = (f32[2,1024,128]{2,1,0:T(8,128)S(1)}, f32[2,1024,128]{2,1,0:T(8,128)S(1)}, u32[]{:S(2)}, u32[]{:S(2)}) collective-permute-start(f32[2,1024,128]{2,1,0:T(8,128)S(1)} %solve.3.wa_ref), channel_id=1, source_target_pairs={{0,1},{1,0},{2,3},{3,2},{4,5},{5,4},{6,7},{7,6},{8,9},{9,8},{10,11... | collective-permute-start | bytes 3145736 | tf_op jit(solution)/shard_map/ppermute | solution.py:514
  247.1 24.7 %collective-permute-start.40 = (f32[2,1024,128]{2,1,0:T(8,128)S(1)}, f32[2,1024,128]{2,1,0:T(8,128)S(1)}, u32[]{:S(2)}, u32[]{:S(2)}) collective-permute-start(f32[2,1024,128]{2,1,0:T(8,128)S(1)} %solve.2.wa_ref), channel_id=1, source_target_pairs={{0,1},{1,0},{2,3},{3,2},{4,5},{5,4},{6,7},{7,6},{8,9},{9,8},{10,11... | collective-permute-start | bytes 3145736 | tf_op jit(solution)/shard_map/ppermute | solution.py:514
  254.1 24.2 %collective-permute-start.39 = (f32[2,1024,128]{2,1,0:T(8,128)S(1)}, f32[2,1024,128]{2,1,0:T(8,128)S(1)}, u32[]{:S(2)}, u32[]{:S(2)}) collective-permute-start(f32[2,1024,128]{2,1,0:T(8,128)S(1)} %collective-permute-done.38.wa_ref), channel_id=1, source_target_pairs={{0,1},{1,0},{2,3},{3,2},{4,5},{5,4},{6,7},{7,6},{8,9},{9,8},{10,11... | collective-permute-start | bytes 3145736 | tf_op jit(solution)/shard_map/ppermute | solution.py:514
  265.4 19.5 %collective-permute-start.30 = (f32[2,1024,128]{2,1,0:T(8,128)S(1)}, f32[2,1024,128]{2,1,0:T(8,128)S(1)}, u32[]{:S(2)}, u32[]{:S(2)}) collective-permute-start(f32[2,1024,128]{2,1,0:T(8,128)S(1)} %collective-permute-done.29.wa_ref), channel_id=1, source_target_pairs={{0,1},{1,0},{2,3},{3,2},{4,5},{5,4},{6,7},{7,6},{8,9},{9,8},{10,11... | collective-permute-start | bytes 3145736 | tf_op jit(solution)/shard_map/ppermute | solution.py:514

commit v2 on v1

--- a/solution.py
+++ b/solution.py
@@ -183,6 +183,7 @@
     core, turn, swap = s_ref[CORE], s_ref[TURN], s_ref[base] & 1
     half = ath.shape[0] // 2
     width = out_ref.shape[2]
+    first = 2 * pl.program_id(0)
     right = split(t_ref[...])
 
     def rows_of(th, tl, step):
@@ -193,8 +194,8 @@
             for k in range(2):
                 part = value[:, k * width : (k + 1) * width]
                 if len(rest) == 2:
-                    part = part + rest[0][k ^ swap, to, :]
-                out_ref[k ^ swap, to, :] = part
+                    part = part + rest[0][first + (k ^ swap), to, :]
+                out_ref[first + (k ^ swap), to, :] = part
             return carry
 
         lax.fori_loop(0, 2, body, 0)
@@ -207,8 +208,7 @@
     rows, columns = targets.shape
     feats = mine[2].shape[0]
     width = columns // 16
-    whole = pl.BlockSpec((feats, rows), lambda k, s: (0, 0))
-    pair = pl.BlockSpec((2, 2 * feats, width), lambda k, s: (k, 0, 0))
+    whole = pl.BlockSpec(memory_space=pltpu.VMEM)
     return pl.pallas_call(
         functools.partial(cross_kernel, base),
         out_shape=jax.ShapeDtypeStruct((4, 2 * feats, width), F32),
@@ -216,9 +216,8 @@
             num_scalar_prefetch=1,
             grid=(2,),
             in_specs=[pl.BlockSpec((rows, 2 * width), lambda k, s: (0, 4 * group + ((s[base] >> 1) ^ k)))]
-            + [whole] * 4
-            + [pair] * len(before),
-            out_specs=pair,
+            + [whole] * (4 + len(before)),
+            out_specs=whole,
         ),
         compiler_params=params(),
         cost_estimate=cost(3 * rows * feats * columns, 2 * rows * columns),
@@ -440,9 +439,9 @@
 def residual_kernel(s_ref, t_ref, ah, al, bh, bl, wa_ref, wb_ref, *rest):
     r_ref, w_ref = rest[-2:]
     own = pl.program_id(0) == 0
+    half = t_ref.shape[0]
     swap, core = jnp.where(own, s_ref[BASE_OWN], s_ref[BASE_OTH]) & 1, s_ref[CORE]
-    rows, feats = ah.shape
-    half = rows // 2
+    feats = ah.shape[1]
 
     def take(step):
         here = pl.ds(pl.multiple_of(step * feats, feats), feats)
@@ -452,28 +451,21 @@
 
     mine, other = take(core), take(1 - core)
     w_ref[core], w_ref[1 - core] = mine, other
-    (mh, ml), (oh, ol) = split(mine), split(other)
-
-    def body(i, carry):
-        here = pl.ds(pl.multiple_of(i * half, half), half)
-        fitted = dot3((ah[here, :], al[here, :]), (mh, ml)) + dot3((bh[here, :], bl[here, :]), (oh, ol))
-        r_ref[here, :] = t_ref[here, :] - fitted
-        return carry
-
-    lax.fori_loop(0, 2, body, 0)
+    here = pl.ds(pl.multiple_of(pl.program_id(1) * half, half), half)
+    fitted = dot3((ah[here, :], al[here, :]), split(mine)) + dot3((bh[here, :], bl[here, :]), split(other))
+    r_ref[...] = t_ref[...] - fitted
 
 
 def residual_part(group, pair, scalars, targets, mine, other, weights, weights_oth, before):
     rows, columns = targets.shape
     feats = mine[0].shape[1]
-    _, height, width = weights.shape
-    whole = pl.BlockSpec((rows, feats), lambda k, s: (0, 0))
+    _, _, width = weights.shape
+    whole = pl.BlockSpec(memory_space=pltpu.VMEM)
 
     def place(k, s):
         return 4 * group + ((jnp.where(k == 0, s[BASE_OWN], s[BASE_OTH]) >> 1) ^ pair)
 
-    block = pl.BlockSpec((rows, 2 * width), lambda k, s: (0, place(k, s)))
-    both = pl.BlockSpec((2, height, width), lambda k, s: (0, 0, 0))
+    block = pl.BlockSpec((rows // 2, 2 * width), lambda k, i, s: (i, place(k, s)))
     anywhere = pl.BlockSpec(memory_space=pl.ANY)
     return pl.pallas_call(
         residual_kernel,
@@ -483,9 +475,9 @@
         ],
         grid_spec=pltpu.PrefetchScalarGridSpec(
             num_scalar_prefetch=1,
-            grid=(2,),
-            in_specs=[block] + [whole] * 4 + [both] * 2 + [anywhere] * len(before),
-            out_specs=[block, pl.BlockSpec((2, feats, 2 * width), lambda k, s: (0, 0, place(k, s)))],
+            grid=(2, 2),
+            in_specs=[block] + [whole] * 6 + [anywhere] * len(before),
+            out_specs=[block, pl.BlockSpec((2, feats, 2 * width), lambda k, i, s: (0, 0, place(k, s)))],
         ),
         input_output_aliases={8: 0, 9: 1} if before else {},
         compiler_params=params(),
@@ -564,11 +556,9 @@
     sides = after(sent, sides)
     kept.append(cross(BASE_OWN, 1, scalars, targets, *sides, (came,)))
 
-    moved = exchange(pieces[4:], 4, 2)
-    pieces = pieces[:4] + moved
+    pieces = pieces[:4] + exchange(pieces[4:], 4, 2)
     pieces, kept[1] = lax.optimization_barrier([pieces, kept[1]])
-    moved = exchange(pieces[2:], 8)
-    pieces = pieces[:2] + moved
+    pieces = pieces[:2] + exchange(pieces[2:], 8)
     pieces = pieces[:1] + exchange(pieces[1:], 16)
     pieces = flood(pieces, more)
     for masks in ((16,), (8,), (4, 2), (2, 4)):
@@ -576,8 +566,7 @@
 
     crossed = []
     for value in kept:
-        moved = exchange(value[2:], 2, 4)
-        value = value[:2] + moved
+        value = value[:2] + exchange(value[2:], 2, 4)
         value = value[:1] + exchange(value[1:], 4, 2)
         for mask in (8, 16):
             middle = value.shape[1] // 2

time: 292 us -> 290 us (level)
  no operation moved by 1% of the time
where the time goes in v2:
time: 290 us
  waiting for transfers between devices  116 us (40%)
  Pallas kernels  110 us (38%)
  starting transfers between devices  58.2 us (20%)
  local copies, waits for them, and re-layouts  3.1 us (1%)
    ppermute x42, waiting for transfers between devices, exchange(): return lax.ppermute(value, ALL, pairs)  116 us
    ppermute x42, starting transfers between devices, exchange(): return lax.ppermute(value, ALL, pairs)  58.2 us
    pallas_call x4, Pallas kernels, residual_part(): pl.pallas_call(residual_kernel, out_shape=[jax.ShapeDtypeStruct((rows, co...  24.5 us
    pallas_call x4, Pallas kernels, cross(): pl.pallas_call(functools.partial(cross_kernel, base), out_shape=jax.Shape...  23.8 us
    pallas_call x3, Pallas kernels, factor(): pl.pallas_call(functools.partial(factor_kernel, step), out_shape=jax.Shap...  20.6 us
    pallas_call x2, Pallas kernels, features(): pl.pallas_call(functools.partial(features_kernel, quarter), out_shape=[ja...  15.7 us
    pallas_call x2, Pallas kernels, solve(): pl.pallas_call(solve_kernel, out_shape=jax.ShapeDtypeStruct(crossed.shape...  8.69 us
    pallas_call x1, Pallas kernels, assemble(): pl.pallas_call(assemble_kernel, out_shape=[jax.ShapeDtypeStruct((2 * half...  7.48 us
  transfers between devices with their start and end apart: 42, of which 24 were waited for; matrix products, arithmetic and copies ran while one was open for 1% of the time, Pallas kernels for 26%

profile of v2, /device:TPU:0, one launch (start us, length us, event | category | flops | bytes accessed | tf_op | source)
XLA Modules:
  0.0 289.8 jit_solution(12365748438399611938)
XLA Ops:
  1.4 2.1 collective-permute-done.1
  7.1 2.9 %collective-permute-start.2 = (f32[2,448,128]{2,1,0:T(8,128)S(1)}, f32[2,448,128]{2,1,0:T(8,128)S(1)}, u32[]{:S(2)}, u32[]{:S(2)}) collective-permute-start(f32[2,448,128]{2,1,0:T(8,128)S(1)} %slice.113), channel_id=1, source_target_pairs={{0,2},{1,5},{2,0},{3,7},{4,6},{5,1},{6,4},{7,3},{8,10},{9,13},{10,... | collective-permute-start | bytes 1376264 | tf_op jit(solution)/shard_map/ppermute | solution.py:506
  10.0 6.5 %collective-permute-done.2 = f32[2,448,128]{2,1,0:T(8,128)S(1)} collective-permute-done((f32[2,448,128]{2,1,0:T(8,128)S(1)}, f32[2,448,128]{2,1,0:T(8,128)S(1)}, u32[]{:S(2)}, u32[]{:S(2)}) %collective-permute-start.2) | collective-permute-done | bytes 458784 | tf_op jit(solution)/shard_map/ppermute | solution.py:506
  18.7 4.0 %collective-permute-done.3 = f32[1,448,128]{2,1,0:T(8,128)S(1)} collective-permute-done((f32[1,448,128]{2,1,0:T(8,128)S(1)}, f32[1,448,128]{2,1,0:T(8,128)S(1)}, u32[]{:S(2)}, u32[]{:S(2)}) %collective-permute-start.3) | collective-permute-done | bytes 229408 | tf_op jit(solution)/shard_map/ppermute | solution.py:506
  22.7 2.1 collective-permute-start.4
  24.9 4.2 %collective-permute-done.4 = f32[1,448,128]{2,1,0:T(8,128)S(1)} collective-permute-done((f32[1,448,128]{2,1,0:T(8,128)S(1)}, f32[1,448,128]{2,1,0:T(8,128)S(1)}, u32[]{:S(2)}, u32[]{:S(2)}) %collective-permute-start.4) | collective-permute-done | bytes 229408 | tf_op jit(solution)/shard_map/ppermute | solution.py:506
  29.1 3.1 %collective-permute-start.5 = (f32[1,448,128]{2,1,0:T(8,128)S(1)}, f32[1,448,128]{2,1,0:T(8,128)S(1)}, u32[]{:S(2)}, u32[]{:S(2)}) collective-permute-start(f32[1,448,128]{2,1,0:T(8,128)S(1)} %add.109), channel_id=1, source_target_pairs={{0,16},{1,17},{2,18},{3,19},{4,20},{5,21},{6,22},{7,23},{8,24},{9,... | collective-permute-start | bytes 688136 | tf_op jit(solution)/shard_map/ppermute | solution.py:506
  32.1 8.2 %collective-permute-done.5 = f32[1,448,128]{2,1,0:T(8,128)S(1)} collective-permute-done((f32[1,448,128]{2,1,0:T(8,128)S(1)}, f32[1,448,128]{2,1,0:T(8,128)S(1)}, u32[]{:S(2)}, u32[]{:S(2)}) %collective-permute-start.5) | collective-permute-done | bytes 229408 | tf_op jit(solution)/shard_map/ppermute | solution.py:506
  41.6 4.8 %collective-permute-done.6 = f32[1,448,128]{2,1,0:T(8,128)S(1)} collective-permute-done((f32[1,448,128]{2,1,0:T(8,128)S(1)}, f32[1,448,128]{2,1,0:T(8,128)S(1)}, u32[]{:S(2)}, u32[]{:S(2)}) %collective-permute-start.6) | collective-permute-done | bytes 229408 | tf_op jit(solution)/shard_map/ppermute | solution.py:506
  47.7 7.3 %collective-permute-done.7 = f32[2,448,128]{2,1,0:T(8,128)S(1)} collective-permute-done((f32[2,448,128]{2,1,0:T(8,128)S(1)}, f32[2,448,128]{2,1,0:T(8,128)S(1)}, u32[]{:S(2)}, u32[]{:S(2)}) %collective-permute-start.7) | collective-permute-done | bytes 458784 | tf_op jit(solution)/shard_map/ppermute | solution.py:506
  55.2 7.8 %features.2 = (bf16[1024,512]{1,0:T(8,128)(2,1)S(1)}, bf16[1024,512]{1,0:T(8,128)(2,1)S(1)}, bf16[512,1024]{1,0:T(8,128)(2,1)S(1)}, bf16[512,1024]{1,0:T(8,128)(2,1)S(1)}) custom-call(s32[9]{0:T(128)S(1)} %stack.39.s_ref, f32[440,1024]{1,0:T(8,128)S(1)} %bitcast.16, f32[4,448,128]{2,1,0:T(8,128)S(1)} %pad_maximum_fusion.2.p_ref), custom_call_target="tpu_custom_call" | custom-call | flops 2768240640 | bytes 5996544 | tf_op jit(solution)/shard_map/features/pallas_call | solution.py:115
  63.1 7.8 %features.3 = (bf16[1024,512]{1,0:T(8,128)(2,1)S(1)}, bf16[1024,512]{1,0:T(8,128)(2,1)S(1)}, bf16[512,1024]{1,0:T(8,128)(2,1)S(1)}, bf16[512,1024]{1,0:T(8,128)(2,1)S(1)}) custom-call(s32[9]{0:T(128)S(1)} %stack.39.s_ref, f32[440,1024]{1,0:T(8,128)S(1)} %bitcast.17, f32[4,448,128]{2,1,0:T(8,128)S(1)} %collective-permute-done.8.p_ref), custom_call_target="tpu_custom_call" | custom-call | flops 2768240640 | bytes 5996544 | tf_op jit(solution)/shard_map/features/pallas_call | solution.py:115
  70.9 3.0 %gram.2 = f32[16,5,16,256]{3,2,1,0:T(8,128)S(1)} custom-call(s32[9]{0:T(128)S(1)} %stack.39.s_ref, bf16[1024,512]{1,0:T(8,128)(2,1)S(1)} %get-tuple-element.68.mh.oh.bh, bf16[1024,512]{1,0:T(8,128)(2,1)S(1)} %get-tuple-element.69.ml.ol.bl, bf16[512,1024]{1,0:T(8,128)(2,1)S(1)} %get-tuple-element.82.mth.bth.oth, ...), custom_call_target="tpu_custom_call" | custom-call | flops 2013265920 | bytes 8388608 | tf_op jit(solution)/shard_map/gram/pallas_call | solution.py:170
  73.9 5.9 %cross.4 = f32[4,1024,128]{2,1,0:T(8,128)S(1)} custom-call(s32[9]{0:T(128)S(1)} %stack.39.s_ref, f32[1024,2048]{1,0:T(8,128)S(1)} %bitcast.13, bf16[512,1024]{1,0:T(8,128)(2,1)S(1)} %get-tuple-element.80.oth.ath.mth, bf16[512,1024]{1,0:T(8,128)(2,1)S(1)} %get-tuple-element.81.otl.atl.mtl, bf16[512,1024]{1,0:T(8,128)(2,1)S(1)} %get-tuple-element.82.mth.bth.oth, ...), custom_call_target="tpu_custom_call" | custom-call | flops 3221225472 | bytes 4194304 | tf_op jit(solution)/shard_map/cross/pallas_call | solution.py:212
  80.5 3.1 %gram.3 = f32[16,5,16,256]{3,2,1,0:T(8,128)S(1)} custom-call(s32[9]{0:T(128)S(1)} %stack.39.s_ref, bf16[1024,512]{1,0:T(8,128)(2,1)S(1)} %get-tuple-element.64.oh.mh.ah, bf16[1024,512]{1,0:T(8,128)(2,1)S(1)} %get-tuple-element.65.ol.ml.al, bf16[512,1024]{1,0:T(8,128)(2,1)S(1)} %get-tuple-element.80.oth.ath.mth, ...), custom_call_target="tpu_custom_call" | custom-call | flops 2013265920 | bytes 8388608 | tf_op jit(solution)/shard_map/gram/pallas_call | solution.py:170
  83.6 2.5 collective-permute-done.9
  86.4 6.0 %cross.5 = f32[4,1024,128]{2,1,0:T(8,128)S(1)} custom-call(s32[9]{0:T(128)S(1)} %stack.39.s_ref, f32[1024,2048]{1,0:T(8,128)S(1)} %bitcast.13, bf16[512,1024]{1,0:T(8,128)(2,1)S(1)} %get-tuple-element.80.oth.ath.mth, bf16[512,1024]{1,0:T(8,128)(2,1)S(1)} %get-tuple-element.81.otl.atl.mtl, bf16[512,1024]{1,0:T(8,128)(2,1)S(1)} %get-tuple-element.82.mth.bth.oth, ...), custom_call_target="tpu_custom_call" | custom-call | flops 3221225472 | bytes 4194304 | tf_op jit(solution)/shard_map/cross/pallas_call | solution.py:212
  92.3 6.0 %cross.6 = f32[4,1024,128]{2,1,0:T(8,128)S(1)} custom-call(s32[9]{0:T(128)S(1)} %stack.39.s_ref, f32[1024,2048]{1,0:T(8,128)S(1)} %bitcast.13, bf16[512,1024]{1,0:T(8,128)(2,1)S(1)} %get-tuple-element.80.oth.ath.mth, bf16[512,1024]{1,0:T(8,128)(2,1)S(1)} %get-tuple-element.81.otl.atl.mtl, bf16[512,1024]{1,0:T(8,128)(2,1)S(1)} %get-tuple-element.82.mth.bth.oth, ...), custom_call_target="tpu_custom_call" | custom-call | flops 3221225472 | bytes 4194304 | tf_op jit(solution)/shard_map/cross/pallas_call | solution.py:212
  101.0 8.4 %collective-permute-done.10 = f32[8,5,16,256]{3,2,1,0:T(8,128)S(1)} collective-permute-done((f32[8,5,16,256]{3,2,1,0:T(8,128)S(1)}, f32[8,5,16,256]{3,2,1,0:T(8,128)S(1)}, u32[]{:S(2)}, u32[]{:S(2)}) %collective-permute-start.10) | collective-permute-done | bytes 655392 | tf_op jit(solution)/shard_map/ppermute | solution.py:506
  110.8 9.4 %collective-permute-done.11 = f32[4,5,16,256]{3,2,1,0:T(8,128)S(1)} collective-permute-done((f32[4,5,16,256]{3,2,1,0:T(8,128)S(1)}, f32[4,5,16,256]{3,2,1,0:T(8,128)S(1)}, u32[]{:S(2)}, u32[]{:S(2)}) %collective-permute-start.11) | collective-permute-done | bytes 327712 | tf_op jit(solution)/shard_map/ppermute | solution.py:506
  120.3 3.9 %collective-permute-done.31 = f32[2,1024,128]{2,1,0:T(8,128)S(1)} collective-permute-done((f32[2,1024,128]{2,1,0:T(8,128)S(1)}, f32[2,1024,128]{2,1,0:T(8,128)S(1)}, u32[]{:S(2)}, u32[]{:S(2)}) %collective-permute-start.31) | collective-permute-done | bytes 1048608 | tf_op jit(solution)/shard_map/ppermute | solution.py:506
  125.6 6.0 %cross.7 = f32[4,1024,128]{2,1,0:T(8,128)S(1)} custom-call(s32[9]{0:T(128)S(1)} %stack.39.s_ref, f32[1024,2048]{1,0:T(8,128)S(1)} %bitcast.13, bf16[512,1024]{1,0:T(8,128)(2,1)S(1)} %get-tuple-element.80.oth.ath.mth, bf16[512,1024]{1,0:T(8,128)(2,1)S(1)} %get-tuple-element.81.otl.atl.mtl, bf16[512,1024]{1,0:T(8,128)(2,1)S(1)} %get-tuple-element.82.mth.bth.oth, ...), custom_call_target="tpu_custom_call" | custom-call | flops 3221225472 | bytes 4194304 | tf_op jit(solution)/shard_map/cross/pallas_call | solution.py:212
  132.3 4.6 %collective-permute-done.14 = f32[2,5,16,256]{3,2,1,0:T(8,128)S(1)} collective-permute-done((f32[2,5,16,256]{3,2,1,0:T(8,128)S(1)}, f32[2,5,16,256]{3,2,1,0:T(8,128)S(1)}, u32[]{:S(2)}, u32[]{:S(2)}) %collective-permute-start.14) | collective-permute-done | bytes 163872 | tf_op jit(solution)/shard_map/ppermute | solution.py:506
  137.0 2.1 collective-permute-start.15
  142.7 2.7 collective-permute-start.16
  148.2 2.5 collective-permute-start.17
  150.7 2.7 collective-permute-start.34
  154.0 2.4 collective-permute-start.18
  156.4 4.3 %collective-permute-done.34 = f32[1,256,128]{2,1,0:T(8,128)S(1)} collective-permute-done((f32[1,256,128]{2,1,0:T(8,128)S(1)}, f32[1,256,128]{2,1,0:T(8,128)S(1)}, u32[]{:S(2)}, u32[]{:S(2)}) %collective-permute-start.34) | collective-permute-done | bytes 131104 | tf_op jit(solution)/shard_map/ppermute | solution.py:506
  161.5 7.6 %collective-permute-start.19 = (f32[8,5,16,256]{3,2,1,0:T(8,128)S(1)}, f32[8,5,16,256]{3,2,1,0:T(8,128)S(1)}, u32[]{:S(2)}, u32[]{:S(2)}) collective-permute-start(f32[8,5,16,256]{3,2,1,0:T(8,128)S(1)} %pad_maximum_fusion.3), channel_id=1, source_target_pairs={{0,2},{1,5},{2,0},{3,7},{4,6},{5,1},{6,4},{7,3},{8,10},{9,13},{10,... | collective-permute-start | bytes 1966088 | tf_op jit(solution)/shard_map/ppermute | solution.py:506
  171.5 7.8 %collective-permute-done.19 = f32[8,5,16,256]{3,2,1,0:T(8,128)S(1)} collective-permute-done((f32[8,5,16,256]{3,2,1,0:T(8,128)S(1)}, f32[8,5,16,256]{3,2,1,0:T(8,128)S(1)}, u32[]{:S(2)}, u32[]{:S(2)}) %collective-permute-start.19) | collective-permute-done | bytes 655392 | tf_op jit(solution)/shard_map/ppermute | solution.py:506
  179.4 7.5 %assemble.1 = (f32[512,512]{1,0:T(8,128)S(1)}, f32[256,512]{1,0:T(8,128)S(1)}) custom-call(s32[9]{0:T(128)S(1)} %stack.39.s_ref, f32[16,5,16,256]{3,2,1,0:T(8,128)S(1)} %constant_dynamic-update-slice_fusion.g_ref), custom_call_target="tpu_custom_call" | custom-call | flops 10000000000 | bytes 4000000 | tf_op jit(solution)/shard_map/assemble/pallas_call | solution.py:329
  186.8 6.5 %factor.3.m_ref = f32[512,512]{1,0:T(8,128)S(1)} custom-call(f32[512,512]{1,0:T(8,128)S(1)} %get-tuple-element.85.m_ref), custom_call_target="tpu_custom_call" | custom-call | flops 10000000000 | bytes 4000000 | tf_op jit(solution)/shard_map/factor/pallas_call | solution.py:351
  194.4 6.3 %factor.4.m_ref = f32[512,512]{1,0:T(8,128)S(1)} custom-call(f32[512,512]{1,0:T(8,128)S(1)} %factor.3.m_ref), custom_call_target="tpu_custom_call" | custom-call | flops 10000000000 | bytes 4000000 | tf_op jit(solution)/shard_map/factor/pallas_call | solution.py:351
  201.0 4.7 %collective-permute-start.25 = (f32[1,256,128]{2,1,0:T(8,128)S(1)}, f32[1,256,128]{2,1,0:T(8,128)S(1)}, u32[]{:S(2)}, u32[]{:S(2)}) collective-permute-start(f32[1,256,128]{2,1,0:T(8,128)S(1)} %slice.127), channel_id=1, source_target_pairs={{0,16},{1,17},{2,18},{3,19},{4,20},{5,21},{6,22},{7,23},{8,24},{9,... | collective-permute-start | bytes 393224 | tf_op jit(solution)/shard_map/ppermute | solution.py:506
  205.6 7.8 %factor.5.own_ref = f32[512,512]{1,0:T(8,128)S(1)} custom-call(f32[512,512]{1,0:T(8,128)S(1)} %factor.4.m_ref), custom_call_target="tpu_custom_call" | custom-call | flops 10000000000 | bytes 4000000 | tf_op jit(solution)/shard_map/factor/pallas_call | solution.py:351
  213.6 9.1 %collective-permute-done.26 = f32[1,256,128]{2,1,0:T(8,128)S(1)} collective-permute-done((f32[1,256,128]{2,1,0:T(8,128)S(1)}, f32[1,256,128]{2,1,0:T(8,128)S(1)}, u32[]{:S(2)}, u32[]{:S(2)}) %collective-permute-start.26) | collective-permute-done | bytes 131104 | tf_op jit(solution)/shard_map/ppermute | solution.py:506
  225.0 6.1 %collective-permute-done.27 = f32[1,512,128]{2,1,0:T(8,128)S(1)} collective-permute-done((f32[1,512,128]{2,1,0:T(8,128)S(1)}, f32[1,512,128]{2,1,0:T(8,128)S(1)}, u32[]{:S(2)}, u32[]{:S(2)}) %collective-permute-start.27) | collective-permute-done | bytes 262176 | tf_op jit(solution)/shard_map/ppermute | solution.py:506
  232.1 2.4 couple.1.b_ref
  234.6 4.3 %solve.3.wa_ref = f32[2,1024,128]{2,1,0:T(8,128)S(1)} custom-call(s32[9]{0:T(128)S(1)} %stack.39.s_ref, f32[512,512]{1,0:T(8,128)S(1)} %factor.5.own_ref, f32[512,512]{1,0:T(8,128)S(1)} %collective-permute-done.20.oth_ref, f32[512,512]{1,0:T(8,128)S(1)} %couple.1.b_ref, f32[2,1024,128]{2,1,0:T(8,128)S(1)} %pad_maximum_fusion.1.c_ref), custom_call_target="tpu_custom_call" | custom-call | flops 2415919104 | bytes 2097152 | tf_op jit(solution)/shard_map/solve/pallas_call | solution.py:423
  238.9 2.4 collective-permute-start.38
  241.4 4.3 %solve.2.wa_ref = f32[2,1024,128]{2,1,0:T(8,128)S(1)} custom-call(s32[9]{0:T(128)S(1)} %stack.39.s_ref, f32[512,512]{1,0:T(8,128)S(1)} %factor.5.own_ref, f32[512,512]{1,0:T(8,128)S(1)} %collective-permute-done.20.oth_ref, f32[512,512]{1,0:T(8,128)S(1)} %couple.1.b_ref, f32[2,1024,128]{2,1,0:T(8,128)S(1)} %pad_maximum_fusion.c_ref), custom_call_target="tpu_custom_call" | custom-call | flops 2415919104 | bytes 2097152 | tf_op jit(solution)/shard_map/solve/pallas_call | solution.py:423
  247.6 6.5 %collective-permute-done.38.wa_ref = f32[2,1024,128]{2,1,0:T(8,128)S(1)} collective-permute-done((f32[2,1024,128]{2,1,0:T(8,128)S(1)}, f32[2,1024,128]{2,1,0:T(8,128)S(1)}, u32[]{:S(2)}, u32[]{:S(2)}) %collective-permute-start.38) | collective-permute-done | bytes 1048608 | tf_op jit(solution)/shard_map/ppermute | solution.py:506
  254.1 11.2 %collective-permute-done.29.wa_ref = f32[2,1024,128]{2,1,0:T(8,128)S(1)} collective-permute-done((f32[2,1024,128]{2,1,0:T(8,128)S(1)}, f32[2,1024,128]{2,1,0:T(8,128)S(1)}, u32[]{:S(2)}, u32[]{:S(2)}) %collective-permute-start.29) | collective-permute-done | bytes 1048608 | tf_op jit(solution)/shard_map/ppermute | solution.py:506
  265.3 6.1 %residual.4 = (f32[1024,2048]{1,0:T(8,128)}, f32[2,512,2048]{2,1,0:T(8,128)}) custom-call(s32[9]{0:T(128)S(1)} %stack.39.s_ref, f32[1024,2048]{1,0:T(8,128)S(1)} %bitcast.13, bf16[1024,512]{1,0:T(8,128)(2,1)S(1)} %get-tuple-element.64.oh.mh.ah, bf16[1024,512]{1,0:T(8,128)(2,1)S(1)} %get-tuple-element.65.ol.ml.al, ...), custom_call_target="tpu_custom_call" | custom-call | flops 3221225472 | bytes 6291456 | tf_op jit(solution)/shard_map/residual/pallas_call | solution.py:470
  271.4 6.1 %residual.5 = (f32[1024,2048]{1,0:T(8,128)}, f32[2,512,2048]{2,1,0:T(8,128)}) custom-call(s32[9]{0:T(128)S(1)} %stack.39.s_ref, f32[1024,2048]{1,0:T(8,128)S(1)} %bitcast.13, bf16[1024,512]{1,0:T(8,128)(2,1)S(1)} %get-tuple-element.64.oh.mh.ah, bf16[1024,512]{1,0:T(8,128)(2,1)S(1)} %get-tuple-element.65.ol.ml.al, ...), custom_call_target="tpu_custom_call", output_to_operand_aliasing={{0}: (8, {}), {1}: (9, {})} | custom-call | flops 3221225472 | bytes 6291456 | tf_op jit(solution)/shard_map/residual/pallas_call | solution.py:470
  277.5 6.1 %residual.6 = (f32[1024,2048]{1,0:T(8,128)}, f32[2,512,2048]{2,1,0:T(8,128)}) custom-call(s32[9]{0:T(128)S(1)} %stack.39.s_ref, f32[1024,2048]{1,0:T(8,128)S(1)} %bitcast.13, bf16[1024,512]{1,0:T(8,128)(2,1)S(1)} %get-tuple-element.64.oh.mh.ah, bf16[1024,512]{1,0:T(8,128)(2,1)S(1)} %get-tuple-element.65.ol.ml.al, ...), custom_call_target="tpu_custom_call", output_to_operand_aliasing={{0}: (8, {}), {1}: (9, {})} | custom-call | flops 3221225472 | bytes 6291456 | tf_op jit(solution)/shard_map/residual/pallas_call | solution.py:470
  283.7 6.1 %residual.7 = (f32[1024,2048]{1,0:T(8,128)}, f32[2,512,2048]{2,1,0:T(8,128)}) custom-call(s32[9]{0:T(128)S(1)} %stack.39.s_ref, f32[1024,2048]{1,0:T(8,128)S(1)} %bitcast.13, bf16[1024,512]{1,0:T(8,128)(2,1)S(1)} %get-tuple-element.64.oh.mh.ah, bf16[1024,512]{1,0:T(8,128)(2,1)S(1)} %get-tuple-element.65.ol.ml.al, ...), custom_call_target="tpu_custom_call", output_to_operand_aliasing={{0}: (8, {}), {1}: (9, {})} | custom-call | flops 3221225472 | bytes 6291456 | tf_op jit(solution)/shard_map/residual/pallas_call | solution.py:470
  (116 shorter events, 33.4 us)
Async XLA Ops:
  0.6 2.9 collective-permute-start
  1.2 2.3 collective-permute-start.1
  3.5 1.2 copy-start
  4.7 0.7 copy-start.1
  5.3 0.7 copy-start.2
  7.1 9.4 %collective-permute-start.2 = (f32[2,448,128]{2,1,0:T(8,128)S(1)}, f32[2,448,128]{2,1,0:T(8,128)S(1)}, u32[]{:S(2)}, u32[]{:S(2)}) collective-permute-start(f32[2,448,128]{2,1,0:T(8,128)S(1)} %slice.113), channel_id=1, source_target_pairs={{0,2},{1,5},{2,0},{3,7},{4,6},{5,1},{6,4},{7,3},{8,10},{9,13},{10,... | collective-permute-start | bytes 1376264 | tf_op jit(solution)/shard_map/ppermute | solution.py:506
  16.6 6.1 %collective-permute-start.3 = (f32[1,448,128]{2,1,0:T(8,128)S(1)}, f32[1,448,128]{2,1,0:T(8,128)S(1)}, u32[]{:S(2)}, u32[]{:S(2)}) collective-permute-start(f32[1,448,128]{2,1,0:T(8,128)S(1)} %slice.115), channel_id=1, source_target_pairs={{0,4},{1,3},{2,6},{3,1},{4,0},{5,7},{6,2},{7,5},{8,12},{9,11},{10,... | collective-permute-start | bytes 688136 | tf_op jit(solution)/shard_map/ppermute | solution.py:506
  22.7 6.3 %collective-permute-start.4 = (f32[1,448,128]{2,1,0:T(8,128)S(1)}, f32[1,448,128]{2,1,0:T(8,128)S(1)}, u32[]{:S(2)}, u32[]{:S(2)}) collective-permute-start(f32[1,448,128]{2,1,0:T(8,128)S(1)} %slice_add_fusion.9), channel_id=1, source_target_pairs={{0,8},{1,9},{2,10},{3,11},{4,12},{5,13},{6,14},{7,15},{8,0},{9,1},... | collective-permute-start | bytes 688136 | tf_op jit(solution)/shard_map/ppermute | solution.py:506
  29.1 11.2 %collective-permute-start.5 = (f32[1,448,128]{2,1,0:T(8,128)S(1)}, f32[1,448,128]{2,1,0:T(8,128)S(1)}, u32[]{:S(2)}, u32[]{:S(2)}) collective-permute-start(f32[1,448,128]{2,1,0:T(8,128)S(1)} %add.109), channel_id=1, source_target_pairs={{0,16},{1,17},{2,18},{3,19},{4,20},{5,21},{6,22},{7,23},{8,24},{9,... | collective-permute-start | bytes 688136 | tf_op jit(solution)/shard_map/ppermute | solution.py:506
  40.4 14.8 %copy-start.3 = (f32[1024,440]{0,1:T(8,128)S(1)}, f32[1024,440]{0,1:T(8,128)}, u32[]{:S(2)}) copy-start(f32[1024,440]{0,1:T(8,128)} %param.5) | copy-start | bytes 5406724
  40.4 6.1 %collective-permute-start.6 = (f32[1,448,128]{2,1,0:T(8,128)S(1)}, f32[1,448,128]{2,1,0:T(8,128)S(1)}, u32[]{:S(2)}, u32[]{:S(2)}) collective-permute-start(f32[1,448,128]{2,1,0:T(8,128)S(1)} %add.110), channel_id=1, source_target_pairs={{0,4},{1,3},{2,6},{3,1},{4,0},{5,7},{6,2},{7,5},{8,12},{9,11},{10,... | collective-permute-start | bytes 688136 | tf_op jit(solution)/shard_map/ppermute | solution.py:506
  46.5 8.5 %collective-permute-start.7 = (f32[2,448,128]{2,1,0:T(8,128)S(1)}, f32[2,448,128]{2,1,0:T(8,128)S(1)}, u32[]{:S(2)}, u32[]{:S(2)}) collective-permute-start(f32[2,448,128]{2,1,0:T(8,128)S(1)} %pad_maximum_fusion.6), channel_id=1, source_target_pairs={{0,2},{1,5},{2,0},{3,7},{4,6},{5,1},{6,4},{7,3},{8,10},{9,13},{10,... | collective-permute-start | bytes 1376264 | tf_op jit(solution)/shard_map/ppermute | solution.py:506
  55.1 8.0 %collective-permute-start.8 = (f32[4,448,128]{2,1,0:T(8,128)S(1)}, f32[4,448,128]{2,1,0:T(8,128)S(1)}, u32[]{:S(2)}, u32[]{:S(2)}) collective-permute-start(f32[4,448,128]{2,1,0:T(8,128)S(1)} %pad_maximum_fusion.2.p_ref), channel_id=1, source_target_pairs={{0,1},{1,0},{2,3},{3,2},{4,5},{5,4},{6,7},{7,6},{8,9},{9,8},{10,11... | collective-permute-start | bytes 2752520 | tf_op jit(solution)/shard_map/ppermute | solution.py:506
  55.2 18.7 %slice-start = ((s8[8388608]{0:T(1024)(128)(4,1)}), s8[4194304]{0:T(1024)(128)(4,1)S(1)}, s32[]{:S(2)}) async-start(s8[8388608]{0:T(1024)(128)(4,1)} %bitcast.12), calls=%async_computation | async-start | bytes 8388608
  63.1 10.9 %slice-start.1 = ((s8[8388608]{0:T(1024)(128)(4,1)}), s8[4194304]{0:T(1024)(128)(4,1)S(1)}, s32[]{:S(2)}) async-start(s8[8388608]{0:T(1024)(128)(4,1)} %bitcast.12), calls=%async_computation.1 | async-start | bytes 8388608
  79.9 6.5 %collective-permute-start.12 = (f32[4,1024,128]{2,1,0:T(8,128)S(1)}, f32[4,1024,128]{2,1,0:T(8,128)S(1)}, u32[]{:S(2)}, u32[]{:S(2)}) collective-permute-start(f32[4,1024,128]{2,1,0:T(8,128)S(1)} %cross.4), channel_id=1, source_target_pairs={{0,1},{1,0},{2,3},{3,2},{4,5},{5,4},{6,7},{7,6},{8,9},{9,8},{10,11... | collective-permute-start | bytes 6291464 | tf_op jit(solution)/shard_map/ppermute | solution.py:506
  80.4 5.7 %collective-permute-start.9 = (f32[16,5,16,256]{3,2,1,0:T(8,128)S(1)}, f32[16,5,16,256]{3,2,1,0:T(8,128)S(1)}, u32[]{:S(2)}, u32[]{:S(2)}) collective-permute-start(f32[16,5,16,256]{3,2,1,0:T(8,128)S(1)} %gram.2), channel_id=1, source_target_pairs={{0,1},{1,0},{2,3},{3,2},{4,5},{5,4},{6,7},{7,6},{8,9},{9,8},{10,11... | collective-permute-start | bytes 3932168 | tf_op jit(solution)/shard_map/ppermute | solution.py:506
  98.3 27.3 %collective-permute-start.13 = (f32[4,1024,128]{2,1,0:T(8,128)S(1)}, f32[4,1024,128]{2,1,0:T(8,128)S(1)}, u32[]{:S(2)}, u32[]{:S(2)}) collective-permute-start(f32[4,1024,128]{2,1,0:T(8,128)S(1)} %cross.6), channel_id=1, source_target_pairs={{0,1},{1,0},{2,3},{3,2},{4,5},{5,4},{6,7},{7,6},{8,9},{9,8},{10,11... | collective-permute-start | bytes 6291464 | tf_op jit(solution)/shard_map/ppermute | solution.py:506
  98.8 10.7 %collective-permute-start.10 = (f32[8,5,16,256]{3,2,1,0:T(8,128)S(1)}, f32[8,5,16,256]{3,2,1,0:T(8,128)S(1)}, u32[]{:S(2)}, u32[]{:S(2)}) collective-permute-start(f32[8,5,16,256]{3,2,1,0:T(8,128)S(1)} %slice.117), channel_id=1, source_target_pairs={{0,2},{1,5},{2,0},{3,7},{4,6},{5,1},{6,4},{7,3},{8,10},{9,13},{10,... | collective-permute-start | bytes 1966088 | tf_op jit(solution)/shard_map/ppermute | solution.py:506
  100.1 24.1 %collective-permute-start.31 = (f32[2,1024,128]{2,1,0:T(8,128)S(1)}, f32[2,1024,128]{2,1,0:T(8,128)S(1)}, u32[]{:S(2)}, u32[]{:S(2)}) collective-permute-start(f32[2,1024,128]{2,1,0:T(8,128)S(1)} %slice.129), channel_id=1, source_target_pairs={{0,2},{1,5},{2,0},{3,7},{4,6},{5,1},{6,4},{7,3},{8,10},{9,13},{10,... | collective-permute-start | bytes 3145736 | tf_op jit(solution)/shard_map/ppermute | solution.py:506
  109.6 10.6 %collective-permute-start.11 = (f32[4,5,16,256]{3,2,1,0:T(8,128)S(1)}, f32[4,5,16,256]{3,2,1,0:T(8,128)S(1)}, u32[]{:S(2)}, u32[]{:S(2)}) collective-permute-start(f32[4,5,16,256]{3,2,1,0:T(8,128)S(1)} %slice.119), channel_id=1, source_target_pairs={{0,4},{1,3},{2,6},{3,1},{4,0},{5,7},{6,2},{7,5},{8,12},{9,11},{10,... | collective-permute-start | bytes 983048 | tf_op jit(solution)/shard_map/ppermute | solution.py:506
  124.3 14.8 %collective-permute-start.32 = (f32[1,1024,128]{2,1,0:T(8,128)S(1)}, f32[1,1024,128]{2,1,0:T(8,128)S(1)}, u32[]{:S(2)}, u32[]{:S(2)}) collective-permute-start(f32[1,1024,128]{2,1,0:T(8,128)S(1)} %slice.131), channel_id=1, source_target_pairs={{0,4},{1,3},{2,6},{3,1},{4,0},{5,7},{6,2},{7,5},{8,12},{9,11},{10,... | collective-permute-start | bytes 1572872 | tf_op jit(solution)/shard_map/ppermute | solution.py:506
  131.6 5.4 %collective-permute-start.14 = (f32[2,5,16,256]{3,2,1,0:T(8,128)S(1)}, f32[2,5,16,256]{3,2,1,0:T(8,128)S(1)}, u32[]{:S(2)}, u32[]{:S(2)}) collective-permute-start(f32[2,5,16,256]{3,2,1,0:T(8,128)S(1)} %slice.93), channel_id=1, source_target_pairs={{0,8},{1,9},{2,10},{3,11},{4,12},{5,13},{6,14},{7,15},{8,0},{9,1},... | collective-permute-start | bytes 491528 | tf_op jit(solution)/shard_map/ppermute | solution.py:506
  137.0 5.7 %collective-permute-start.15 = (f32[1,5,16,256]{3,2,1,0:T(8,128)S(1)}, f32[1,5,16,256]{3,2,1,0:T(8,128)S(1)}, u32[]{:S(2)}, u32[]{:S(2)}) collective-permute-start(f32[1,5,16,256]{3,2,1,0:T(8,128)S(1)} %slice.121), channel_id=1, source_target_pairs={{0,16},{1,17},{2,18},{3,19},{4,20},{5,21},{6,22},{7,23},{8,24},{9,... | collective-permute-start | bytes 245768 | tf_op jit(solution)/shard_map/ppermute | solution.py:506
  139.2 11.5 %collective-permute-start.33 = (f32[1,512,128]{2,1,0:T(8,128)S(1)}, f32[1,512,128]{2,1,0:T(8,128)S(1)}, u32[]{:S(2)}, u32[]{:S(2)}) collective-permute-start(f32[1,512,128]{2,1,0:T(8,128)S(1)} %slice.133), channel_id=1, source_target_pairs={{0,8},{1,9},{2,10},{3,11},{4,12},{5,13},{6,14},{7,15},{8,0},{9,1},... | collective-permute-start | bytes 786440 | tf_op jit(solution)/shard_map/ppermute | solution.py:506
  142.7 5.5 %collective-permute-start.16 = (f32[1,5,16,256]{3,2,1,0:T(8,128)S(1)}, f32[1,5,16,256]{3,2,1,0:T(8,128)S(1)}, u32[]{:S(2)}, u32[]{:S(2)}) collective-permute-start(f32[1,5,16,256]{3,2,1,0:T(8,128)S(1)} %get-tuple-element.95), channel_id=1, source_target_pairs={{0,16},{1,17},{2,18},{3,19},{4,20},{5,21},{6,22},{7,23},{8,24},{9,... | collective-permute-start | bytes 245768 | tf_op jit(solution)/shard_map/ppermute | solution.py:506
  145.5 25.7 %collective-permute-start.22 = (f32[2,1024,128]{2,1,0:T(8,128)S(1)}, f32[2,1024,128]{2,1,0:T(8,128)S(1)}, u32[]{:S(2)}, u32[]{:S(2)}) collective-permute-start(f32[2,1024,128]{2,1,0:T(8,128)S(1)} %slice.97), channel_id=1, source_target_pairs={{0,2},{1,5},{2,0},{3,7},{4,6},{5,1},{6,4},{7,3},{8,10},{9,13},{10,... | collective-permute-start | bytes 3145736 | tf_op jit(solution)/shard_map/ppermute | solution.py:506
  148.2 5.8 %collective-permute-start.17 = (f32[2,5,16,256]{3,2,1,0:T(8,128)S(1)}, f32[2,5,16,256]{3,2,1,0:T(8,128)S(1)}, u32[]{:S(2)}, u32[]{:S(2)}) collective-permute-start(f32[2,5,16,256]{3,2,1,0:T(8,128)S(1)} %pad_maximum_fusion.10), channel_id=1, source_target_pairs={{0,8},{1,9},{2,10},{3,11},{4,12},{5,13},{6,14},{7,15},{8,0},{9,1},... | collective-permute-start | bytes 491528 | tf_op jit(solution)/shard_map/ppermute | solution.py:506
  150.7 10.0 %collective-permute-start.34 = (f32[1,256,128]{2,1,0:T(8,128)S(1)}, f32[1,256,128]{2,1,0:T(8,128)S(1)}, u32[]{:S(2)}, u32[]{:S(2)}) collective-permute-start(f32[1,256,128]{2,1,0:T(8,128)S(1)} %slice.135), channel_id=1, source_target_pairs={{0,16},{1,17},{2,18},{3,19},{4,20},{5,21},{6,22},{7,23},{8,24},{9,... | collective-permute-start | bytes 393224 | tf_op jit(solution)/shard_map/ppermute | solution.py:506
  154.0 7.5 %collective-permute-start.18 = (f32[4,5,16,256]{3,2,1,0:T(8,128)S(1)}, f32[4,5,16,256]{3,2,1,0:T(8,128)S(1)}, u32[]{:S(2)}, u32[]{:S(2)}) collective-permute-start(f32[4,5,16,256]{3,2,1,0:T(8,128)S(1)} %pad_maximum_fusion.7), channel_id=1, source_target_pairs={{0,4},{1,3},{2,6},{3,1},{4,0},{5,7},{6,2},{7,5},{8,12},{9,11},{10,... | collective-permute-start | bytes 983048 | tf_op jit(solution)/shard_map/ppermute | solution.py:506
  160.7 8.4 %collective-permute-start.35 = (f32[1,256,128]{2,1,0:T(8,128)S(1)}, f32[1,256,128]{2,1,0:T(8,128)S(1)}, u32[]{:S(2)}, u32[]{:S(2)}) collective-permute-start(f32[1,256,128]{2,1,0:T(8,128)S(1)} %slice_add_fusion.11), channel_id=1, source_target_pairs={{0,16},{1,17},{2,18},{3,19},{4,20},{5,21},{6,22},{7,23},{8,24},{9,... | collective-permute-start | bytes 393224 | tf_op jit(solution)/shard_map/ppermute | solution.py:506
  161.5 17.8 %collective-permute-start.19 = (f32[8,5,16,256]{3,2,1,0:T(8,128)S(1)}, f32[8,5,16,256]{3,2,1,0:T(8,128)S(1)}, u32[]{:S(2)}, u32[]{:S(2)}) collective-permute-start(f32[8,5,16,256]{3,2,1,0:T(8,128)S(1)} %pad_maximum_fusion.3), channel_id=1, source_target_pairs={{0,2},{1,5},{2,0},{3,7},{4,6},{5,1},{6,4},{7,3},{8,10},{9,13},{10,... | collective-permute-start | bytes 1966088 | tf_op jit(solution)/shard_map/ppermute | solution.py:506
  169.2 53.6 %collective-permute-start.36 = (f32[1,512,128]{2,1,0:T(8,128)S(1)}, f32[1,512,128]{2,1,0:T(8,128)S(1)}, u32[]{:S(2)}, u32[]{:S(2)}) collective-permute-start(f32[1,512,128]{2,1,0:T(8,128)S(1)} %pad_maximum_fusion.9), channel_id=1, source_target_pairs={{0,8},{1,9},{2,10},{3,11},{4,12},{5,13},{6,14},{7,15},{8,0},{9,1},... | collective-permute-start | bytes 786440 | tf_op jit(solution)/shard_map/ppermute | solution.py:506
  171.4 22.0 %collective-permute-start.23 = (f32[1,1024,128]{2,1,0:T(8,128)S(1)}, f32[1,1024,128]{2,1,0:T(8,128)S(1)}, u32[]{:S(2)}, u32[]{:S(2)}) collective-permute-start(f32[1,1024,128]{2,1,0:T(8,128)S(1)} %slice.123), channel_id=1, source_target_pairs={{0,4},{1,3},{2,6},{3,1},{4,0},{5,7},{6,2},{7,5},{8,12},{9,11},{10,... | collective-permute-start | bytes 1572872 | tf_op jit(solution)/shard_map/ppermute | solution.py:506
  193.5 7.4 %collective-permute-start.24 = (f32[1,512,128]{2,1,0:T(8,128)S(1)}, f32[1,512,128]{2,1,0:T(8,128)S(1)}, u32[]{:S(2)}, u32[]{:S(2)}) collective-permute-start(f32[1,512,128]{2,1,0:T(8,128)S(1)} %slice.125), channel_id=1, source_target_pairs={{0,8},{1,9},{2,10},{3,11},{4,12},{5,13},{6,14},{7,15},{8,0},{9,1},... | collective-permute-start | bytes 786440 | tf_op jit(solution)/shard_map/ppermute | solution.py:506
  201.0 12.5 %collective-permute-start.25 = (f32[1,256,128]{2,1,0:T(8,128)S(1)}, f32[1,256,128]{2,1,0:T(8,128)S(1)}, u32[]{:S(2)}, u32[]{:S(2)}) collective-permute-start(f32[1,256,128]{2,1,0:T(8,128)S(1)} %slice.127), channel_id=1, source_target_pairs={{0,16},{1,17},{2,18},{3,19},{4,20},{5,21},{6,22},{7,23},{8,24},{9,... | collective-permute-start | bytes 393224 | tf_op jit(solution)/shard_map/ppermute | solution.py:506
  213.4 18.7 %collective-permute-start.20 = (f32[512,512]{1,0:T(8,128)S(1)}, f32[512,512]{1,0:T(8,128)S(1)}, u32[]{:S(2)}, u32[]{:S(2)}) collective-permute-start(f32[512,512]{1,0:T(8,128)S(1)} %factor.5.own_ref), channel_id=1, source_target_pairs={{0,1},{1,0},{2,3},{3,2},{4,5},{5,4},{6,7},{7,6},{8,9},{9,8},{10,11... | collective-permute-start | bytes 3145736 | tf_op jit(solution)/shard_map/ppermute | solution.py:506
  213.5 9.1 %collective-permute-start.26 = (f32[1,256,128]{2,1,0:T(8,128)S(1)}, f32[1,256,128]{2,1,0:T(8,128)S(1)}, u32[]{:S(2)}, u32[]{:S(2)}) collective-permute-start(f32[1,256,128]{2,1,0:T(8,128)S(1)} %slice_add_fusion.12), channel_id=1, source_target_pairs={{0,16},{1,17},{2,18},{3,19},{4,20},{5,21},{6,22},{7,23},{8,24},{9,... | collective-permute-start | bytes 393224 | tf_op jit(solution)/shard_map/ppermute | solution.py:506
  222.7 8.3 %collective-permute-start.27 = (f32[1,512,128]{2,1,0:T(8,128)S(1)}, f32[1,512,128]{2,1,0:T(8,128)S(1)}, u32[]{:S(2)}, u32[]{:S(2)}) collective-permute-start(f32[1,512,128]{2,1,0:T(8,128)S(1)} %pad_maximum_fusion.8), channel_id=1, source_target_pairs={{0,8},{1,9},{2,10},{3,11},{4,12},{5,13},{6,14},{7,15},{8,0},{9,1},... | collective-permute-start | bytes 786440 | tf_op jit(solution)/shard_map/ppermute | solution.py:506
  222.8 9.2 %collective-permute-start.37 = (f32[1,1024,128]{2,1,0:T(8,128)S(1)}, f32[1,1024,128]{2,1,0:T(8,128)S(1)}, u32[]{:S(2)}, u32[]{:S(2)}) collective-permute-start(f32[1,1024,128]{2,1,0:T(8,128)S(1)} %pad_maximum_fusion.5), channel_id=1, source_target_pairs={{0,4},{1,3},{2,6},{3,1},{4,0},{5,7},{6,2},{7,5},{8,12},{9,11},{10,... | collective-permute-start | bytes 1572872 | tf_op jit(solution)/shard_map/ppermute | solution.py:506
  222.9 9.2 %collective-permute-start.21 = (f32[256,512]{1,0:T(8,128)S(1)}, f32[256,512]{1,0:T(8,128)S(1)}, u32[]{:S(2)}, u32[]{:S(2)}) collective-permute-start(f32[256,512]{1,0:T(8,128)S(1)} %get-tuple-element.86.gown_ref), channel_id=1, source_target_pairs={{0,1},{1,0},{2,3},{3,2},{4,5},{5,4},{6,7},{7,6},{8,9},{9,8},{10,11... | collective-permute-start | bytes 1572872 | tf_op jit(solution)/shard_map/ppermute | solution.py:506
  231.0 10.2 %collective-permute-start.28 = (f32[1,1024,128]{2,1,0:T(8,128)S(1)}, f32[1,1024,128]{2,1,0:T(8,128)S(1)}, u32[]{:S(2)}, u32[]{:S(2)}) collective-permute-start(f32[1,1024,128]{2,1,0:T(8,128)S(1)} %pad_maximum_fusion.4), channel_id=1, source_target_pairs={{0,4},{1,3},{2,6},{3,1},{4,0},{5,7},{6,2},{7,5},{8,12},{9,11},{10,... | collective-permute-start | bytes 1572872 | tf_op jit(solution)/shard_map/ppermute | solution.py:506
  238.9 15.2 %collective-permute-start.38 = (f32[2,1024,128]{2,1,0:T(8,128)S(1)}, f32[2,1024,128]{2,1,0:T(8,128)S(1)}, u32[]{:S(2)}, u32[]{:S(2)}) collective-permute-start(f32[2,1024,128]{2,1,0:T(8,128)S(1)} %solve.3.wa_ref), channel_id=1, source_target_pairs={{0,2},{1,5},{2,0},{3,7},{4,6},{5,1},{6,4},{7,3},{8,10},{9,13},{10,... | collective-permute-start | bytes 3145736 | tf_op jit(solution)/shard_map/ppermute | solution.py:506
  245.7 19.6 %collective-permute-start.29 = (f32[2,1024,128]{2,1,0:T(8,128)S(1)}, f32[2,1024,128]{2,1,0:T(8,128)S(1)}, u32[]{:S(2)}, u32[]{:S(2)}) collective-permute-start(f32[2,1024,128]{2,1,0:T(8,128)S(1)} %solve.2.wa_ref), channel_id=1, source_target_pairs={{0,2},{1,5},{2,0},{3,7},{4,6},{5,1},{6,4},{7,3},{8,10},{9,13},{10,... | collective-permute-start | bytes 3145736 | tf_op jit(solution)/shard_map/ppermute | solution.py:506
  247.1 18.2 %collective-permute-start.41 = (f32[2,1024,128]{2,1,0:T(8,128)S(1)}, f32[2,1024,128]{2,1,0:T(8,128)S(1)}, u32[]{:S(2)}, u32[]{:S(2)}) collective-permute-start(f32[2,1024,128]{2,1,0:T(8,128)S(1)} %solve.3.wa_ref), channel_id=1, source_target_pairs={{0,1},{1,0},{2,3},{3,2},{4,5},{5,4},{6,7},{7,6},{8,9},{9,8},{10,11... | collective-permute-start | bytes 3145736 | tf_op jit(solution)/shard_map/ppermute | solution.py:506
  247.1 24.3 %collective-permute-start.40 = (f32[2,1024,128]{2,1,0:T(8,128)S(1)}, f32[2,1024,128]{2,1,0:T(8,128)S(1)}, u32[]{:S(2)}, u32[]{:S(2)}) collective-permute-start(f32[2,1024,128]{2,1,0:T(8,128)S(1)} %solve.2.wa_ref), channel_id=1, source_target_pairs={{0,1},{1,0},{2,3},{3,2},{4,5},{5,4},{6,7},{7,6},{8,9},{9,8},{10,11... | collective-permute-start | bytes 3145736 | tf_op jit(solution)/shard_map/ppermute | solution.py:506
  254.1 23.5 %collective-permute-start.39 = (f32[2,1024,128]{2,1,0:T(8,128)S(1)}, f32[2,1024,128]{2,1,0:T(8,128)S(1)}, u32[]{:S(2)}, u32[]{:S(2)}) collective-permute-start(f32[2,1024,128]{2,1,0:T(8,128)S(1)} %collective-permute-done.38.wa_ref), channel_id=1, source_target_pairs={{0,1},{1,0},{2,3},{3,2},{4,5},{5,4},{6,7},{7,6},{8,9},{9,8},{10,11... | collective-permute-start | bytes 3145736 | tf_op jit(solution)/shard_map/ppermute | solution.py:506
  265.3 18.4 %collective-permute-start.30 = (f32[2,1024,128]{2,1,0:T(8,128)S(1)}, f32[2,1024,128]{2,1,0:T(8,128)S(1)}, u32[]{:S(2)}, u32[]{:S(2)}) collective-permute-start(f32[2,1024,128]{2,1,0:T(8,128)S(1)} %collective-permute-done.29.wa_ref), channel_id=1, source_target_pairs={{0,1},{1,0},{2,3},{3,2},{4,5},{5,4},{6,7},{7,6},{8,9},{9,8},{10,11... | collective-permute-start | bytes 3145736 | tf_op jit(solution)/shard_map/ppermute | solution.py:506

commit v3 on v2

--- a/solution.py
+++ b/solution.py
@@ -96,7 +96,8 @@
     )(scalars, block_order, own, oth, phase_own[:, None, :], phase_oth[:, None, :])
 
 
-def features_kernel(quarter, s_ref, x_ref, p_ref, fh_ref, fl_ref, th_ref, tl_ref):
+def features_kernel(quarter, s_ref, x_ref, p_ref, *rest):
+    fh_ref, fl_ref, th_ref, tl_ref = rest[-4:]
     depth = x_ref.shape[0]
     order = s_ref[quarter]
     turned = jnp.concatenate([p_ref[i ^ order] for i in range(4)], axis=1).T
@@ -106,35 +107,39 @@
     fh_ref[...], fl_ref[...] = split(feats.T)
 
 
-def features(quarter, scalars, frames_turned, blocks):
+def features(quarter, slot, scalars, frames_turned, blocks, before=()):
     depth, rows = frames_turned.shape
     feats = blocks.shape[0] * blocks.shape[2]
     tile = 256
     flat = pl.BlockSpec((tile, feats), lambda i, s: (i, 0))
-    turned = pl.BlockSpec((feats, tile), lambda i, s: (0, i))
+    turned = pl.BlockSpec((feats, tile), lambda i, s: (slot, i))
     return pl.pallas_call(
         functools.partial(features_kernel, quarter),
-        out_shape=[jax.ShapeDtypeStruct((rows, feats), BF16)] * 2 + [jax.ShapeDtypeStruct((feats, rows), BF16)] * 2,
+        out_shape=[jax.ShapeDtypeStruct((rows, feats), BF16)] * 2 + [jax.ShapeDtypeStruct((2 * feats, rows), BF16)] * 2,
         grid_spec=pltpu.PrefetchScalarGridSpec(
             num_scalar_prefetch=1,
             grid=(rows // tile,),
             in_specs=[
                 pl.BlockSpec((depth, tile), lambda i, s: (0, i)),
                 pl.BlockSpec(blocks.shape, lambda i, s: (0, 0, 0)),
-            ],
+            ]
+            + [pl.BlockSpec(memory_space=pl.ANY)] * len(before),
             out_specs=[flat, flat, turned, turned],
         ),
+        input_output_aliases={3: 2, 4: 3} if before else {},
         compiler_params=params(),
         cost_estimate=cost(12 * rows * depth * feats, 4 * rows * depth + 8 * rows * feats),
         name="features",
-    )(scalars, frames_turned, blocks)
-
-
-def gram_kernel(kept, s_ref, mh, ml, mth, mtl, oh, ol, oth, otl, out_ref):
+    )(scalars, frames_turned, blocks, *before)
+
+
+def gram_kernel(kept, s_ref, ah, al, bh, bl, th, tl, out_ref):
     order = s_ref[ORDER_OWN if kept else ORDER_OTH]
     half_row = s_ref[CORE] if kept else 1 - s_ref[CORE]
     m_is_second = half_row
-    feats, _ = mth.shape
+    feats = th.shape[0] // 2
+    mh, ml, oh, ol = (ah, al, bh, bl) if kept else (bh, bl, ah, al)
+    m_at, o_at = (0, feats) if kept else (feats, 0)
     half = feats // 2
     pieces, _, height, _ = out_ref.shape
 
@@ -142,71 +147,69 @@
         for g in range(pieces):
             out_ref[g ^ order, tile] = value[g * height : (g + 1) * height]
 
-    top = (mth[:half], mtl[:half])
-    low = (mth[half:], mtl[half:])
+    top = tuple(r[m_at : m_at + half] for r in (th, tl))
+    low = tuple(r[m_at + half : m_at + feats] for r in (th, tl))
     left = (mh[:, :half], ml[:, :half])
     right = (mh[:, half:], ml[:, half:])
     put(0, dot3(top, left))
     put(1, dot3(low, left))
     put(2, dot3(low, right))
 
-    def cross(th, tl, h, l):
-        start = pl.multiple_of(half_row * half, half)
+    def cross(at, h, l):
+        start = pl.multiple_of(at + half_row * half, half)
         side = (th[pl.ds(start, half)], tl[pl.ds(start, half)])
         put(3, dot3(side, (h[:, :half], l[:, :half])))
         put(4, dot3(side, (h[:, half:], l[:, half:])))
 
     @pl.when(m_is_second == 1)
     def _():
-        cross(mth, mtl, oh, ol)
+        cross(m_at, oh, ol)
 
     @pl.when(m_is_second == 0)
     def _():
-        cross(oth, otl, mh, ml)
-
-
-def gram(kept, scalars, mine, other):
-    rows, feats = mine[0].shape
+        cross(o_at, mh, ml)
+
+
+def gram(kept, scalars, flat, turned):
+    rows, feats = flat[0].shape
     return pl.pallas_call(
         functools.partial(gram_kernel, kept),
         out_shape=jax.ShapeDtypeStruct((16, 5, feats // 32, feats // 2), F32),
-        in_specs=[pl.BlockSpec(memory_space=pltpu.SMEM)] + [pl.BlockSpec(memory_space=pltpu.VMEM)] * 8,
+        in_specs=[pl.BlockSpec(memory_space=pltpu.SMEM)] + [pl.BlockSpec(memory_space=pltpu.VMEM)] * 6,
         out_specs=pl.BlockSpec(memory_space=pltpu.VMEM),
         compiler_params=params(),
         cost_estimate=cost(6 * rows * feats * feats * 1.25, 16 * rows * feats),
         name="gram",
-    )(scalars, *mine, *other)
-
-
-def cross_kernel(base, s_ref, t_ref, ath, atl, bth, btl, *rest):
+    )(scalars, *flat, *turned)
+
+
+def cross_kernel(base, s_ref, t_ref, th, tl, *rest):
     out_ref = rest[-1]
     core, turn, swap = s_ref[CORE], s_ref[TURN], s_ref[base] & 1
-    half = ath.shape[0] // 2
+    feats = th.shape[0] // 2
+    half = feats // 2
     width = out_ref.shape[2]
     first = 2 * pl.program_id(0)
     right = split(t_ref[...])
 
-    def rows_of(th, tl, step):
-        def body(i, carry):
-            at = pl.ds(pl.multiple_of(i * half, half), half)
-            value = dot3((th[at, :], tl[at, :]), right)
-            to = pl.ds(pl.multiple_of(((2 * step + i) ^ turn) * half, half), half)
+    def body(slot, carry):
+        at = pl.ds(pl.multiple_of(slot * feats, feats), feats)
+        value = dot3((th[at, :], tl[at, :]), right)
+        for i in range(2):
+            to = pl.ds(pl.multiple_of(((2 * (core ^ slot) + i) ^ turn) * half, half), half)
             for k in range(2):
-                part = value[:, k * width : (k + 1) * width]
+                part = value[i * half : (i + 1) * half, k * width : (k + 1) * width]
                 if len(rest) == 2:
                     part = part + rest[0][first + (k ^ swap), to, :]
                 out_ref[first + (k ^ swap), to, :] = part
-            return carry
-
-        lax.fori_loop(0, 2, body, 0)
-
-    rows_of(ath, atl, core)
-    rows_of(bth, btl, 1 - core)
-
-
-def cross(base, group, scalars, targets, mine, other, before=()):
+        return carry
+
+    lax.fori_loop(0, 2, body, 0)
+
+
+def cross(base, group, scalars, targets, turned, before=()):
     rows, columns = targets.shape
-    feats = mine[2].shape[0]
+    feats = turned[0].shape[0] // 2
     width = columns // 16
     whole = pl.BlockSpec(memory_space=pltpu.VMEM)
     return pl.pallas_call(
@@ -216,13 +219,13 @@
             num_scalar_prefetch=1,
             grid=(2,),
             in_specs=[pl.BlockSpec((rows, 2 * width), lambda k, s: (0, 4 * group + ((s[base] >> 1) ^ k)))]
-            + [whole] * (4 + len(before)),
+            + [whole] * (2 + len(before)),
             out_specs=whole,
         ),
         compiler_params=params(),
         cost_estimate=cost(3 * rows * feats * columns, 2 * rows * columns),
         name="cross",
-    )(scalars, targets, mine[2], mine[3], other[2], other[3], *before)
+    )(scalars, targets, *turned, *before)
 
 
 def unit_inverse(block):
@@ -531,30 +534,31 @@
     part = jnp.concatenate([part, exchange(part, 4, 2)])
     blocks = jnp.concatenate([part, exchange(part, 2, 4)])
     blocks_oth = exchange(blocks, 1)
-    mine = features(QUARTER_OWN, scalars, frames.T, blocks)
-    other = features(QUARTER_OTH, scalars, frames.T, blocks_oth)
-
-    def after(done, sides):
-        gated = lax.optimization_barrier([done, *sides[0], *sides[1]])
-        return gated[1:5], gated[5:]
-
-    sides = mine, other
-    gram_sent = gram(False, scalars, other, mine)
+    *mine, high, low = features(QUARTER_OWN, 0, scalars, frames.T, blocks)
+    *other, high, low = features(QUARTER_OTH, 1, scalars, frames.T, blocks_oth, (high, low))
+
+    flat = mine + other
+
+    def after(done, turned):
+        return lax.optimization_barrier([done, *turned])[1:]
+
+    sides = [high, low]
+    gram_sent = gram(False, scalars, flat, sides)
     gram_came = exchange(gram_sent, 1)
     sides = after(gram_sent, sides)
-    sent = cross(BASE_OTH, 0, scalars, targets, *sides)
+    sent = cross(BASE_OTH, 0, scalars, targets, sides)
     came = exchange(sent, 1)
     sides = after(sent, sides)
-    pieces = gram(True, scalars, *sides) + gram_came
+    pieces = gram(True, scalars, flat, sides) + gram_came
     sides = after(pieces, sides)
     moved = exchange(pieces[8:], 2, 4)
     pieces = pieces[:8] + moved
-    kept = [cross(BASE_OWN, 0, scalars, targets, *sides, (came,))]
+    kept = [cross(BASE_OWN, 0, scalars, targets, sides, (came,))]
     sides = after(kept[0], sides)
-    sent = cross(BASE_OTH, 1, scalars, targets, *sides)
+    sent = cross(BASE_OTH, 1, scalars, targets, sides)
     came = exchange(sent, 1)
     sides = after(sent, sides)
-    kept.append(cross(BASE_OWN, 1, scalars, targets, *sides, (came,)))
+    kept.append(cross(BASE_OWN, 1, scalars, targets, sides, (came,)))
 
     pieces = pieces[:4] + exchange(pieces[4:], 4, 2)
     pieces, kept[1] = lax.optimization_barrier([pieces, kept[1]])

time: 290 us -> 286 us (0.986)
  Pallas kernels: 110 us -> 107 us
    pallas_call x4, Pallas kernels: 23.8 us -> 20.5 us  [cross(): pl.pallas_call(functools.partial(cross_kernel, base), out_shape=jax.Shape...]
where the time goes in v3:
time: 286 us
  waiting for transfers between devices  115 us (40%)
  Pallas kernels  107 us (37%)
  starting transfers between devices  57.9 us (20%)
  local copies, waits for them, and re-layouts  3.1 us (1%)
    ppermute x42, waiting for transfers between devices, exchange(): return lax.ppermute(value, ALL, pairs)  115 us
    ppermute x42, starting transfers between devices, exchange(): return lax.ppermute(value, ALL, pairs)  57.9 us
    pallas_call x4, Pallas kernels, residual_part(): pl.pallas_call(residual_kernel, out_shape=[jax.ShapeDtypeStruct((rows, co...  24.5 us
    pallas_call x3, Pallas kernels, factor(): pl.pallas_call(functools.partial(factor_kernel, step), out_shape=jax.Shap...  20.6 us
    pallas_call x4, Pallas kernels, cross(): pl.pallas_call(functools.partial(cross_kernel, base), out_shape=jax.Shape...  20.5 us
    pallas_call x2, Pallas kernels, features(): pl.pallas_call(functools.partial(features_kernel, quarter), out_shape=[ja...  15.7 us
    pallas_call x2, Pallas kernels, solve(): pl.pallas_call(solve_kernel, out_shape=jax.ShapeDtypeStruct(crossed.shape...  8.69 us
    pallas_call x1, Pallas kernels, assemble(): pl.pallas_call(assemble_kernel, out_shape=[jax.ShapeDtypeStruct((2 * half...  7.47 us
  transfers between devices with their start and end apart: 42, of which 24 were waited for; matrix products, arithmetic and copies ran while one was open for 1% of the time, Pallas kernels for 26%

profile of v3, /device:TPU:0, one launch (start us, length us, event | category | flops | bytes accessed | tf_op | source)
XLA Modules:
  0.0 285.7 jit_solution(14980197530104434706)
XLA Ops:
  1.4 2.1 collective-permute-done.1
  7.1 2.9 %collective-permute-start.2 = (f32[2,448,128]{2,1,0:T(8,128)S(1)}, f32[2,448,128]{2,1,0:T(8,128)S(1)}, u32[]{:S(2)}, u32[]{:S(2)}) collective-permute-start(f32[2,448,128]{2,1,0:T(8,128)S(1)} %slice.113), channel_id=1, source_target_pairs={{0,2},{1,5},{2,0},{3,7},{4,6},{5,1},{6,4},{7,3},{8,10},{9,13},{10,... | collective-permute-start | bytes 1376264 | tf_op jit(solution)/shard_map/ppermute | solution.py:509
  10.0 6.5 %collective-permute-done.2 = f32[2,448,128]{2,1,0:T(8,128)S(1)} collective-permute-done((f32[2,448,128]{2,1,0:T(8,128)S(1)}, f32[2,448,128]{2,1,0:T(8,128)S(1)}, u32[]{:S(2)}, u32[]{:S(2)}) %collective-permute-start.2) | collective-permute-done | bytes 458784 | tf_op jit(solution)/shard_map/ppermute | solution.py:509
  18.7 4.0 %collective-permute-done.3 = f32[1,448,128]{2,1,0:T(8,128)S(1)} collective-permute-done((f32[1,448,128]{2,1,0:T(8,128)S(1)}, f32[1,448,128]{2,1,0:T(8,128)S(1)}, u32[]{:S(2)}, u32[]{:S(2)}) %collective-permute-start.3) | collective-permute-done | bytes 229408 | tf_op jit(solution)/shard_map/ppermute | solution.py:509
  22.7 2.1 collective-permute-start.4
  24.9 4.2 %collective-permute-done.4 = f32[1,448,128]{2,1,0:T(8,128)S(1)} collective-permute-done((f32[1,448,128]{2,1,0:T(8,128)S(1)}, f32[1,448,128]{2,1,0:T(8,128)S(1)}, u32[]{:S(2)}, u32[]{:S(2)}) %collective-permute-start.4) | collective-permute-done | bytes 229408 | tf_op jit(solution)/shard_map/ppermute | solution.py:509
  29.1 3.1 %collective-permute-start.5 = (f32[1,448,128]{2,1,0:T(8,128)S(1)}, f32[1,448,128]{2,1,0:T(8,128)S(1)}, u32[]{:S(2)}, u32[]{:S(2)}) collective-permute-start(f32[1,448,128]{2,1,0:T(8,128)S(1)} %add.109), channel_id=1, source_target_pairs={{0,16},{1,17},{2,18},{3,19},{4,20},{5,21},{6,22},{7,23},{8,24},{9,... | collective-permute-start | bytes 688136 | tf_op jit(solution)/shard_map/ppermute | solution.py:509
  32.2 8.2 %collective-permute-done.5 = f32[1,448,128]{2,1,0:T(8,128)S(1)} collective-permute-done((f32[1,448,128]{2,1,0:T(8,128)S(1)}, f32[1,448,128]{2,1,0:T(8,128)S(1)}, u32[]{:S(2)}, u32[]{:S(2)}) %collective-permute-start.5) | collective-permute-done | bytes 229408 | tf_op jit(solution)/shard_map/ppermute | solution.py:509
  41.6 4.8 %collective-permute-done.6 = f32[1,448,128]{2,1,0:T(8,128)S(1)} collective-permute-done((f32[1,448,128]{2,1,0:T(8,128)S(1)}, f32[1,448,128]{2,1,0:T(8,128)S(1)}, u32[]{:S(2)}, u32[]{:S(2)}) %collective-permute-start.6) | collective-permute-done | bytes 229408 | tf_op jit(solution)/shard_map/ppermute | solution.py:509
  47.7 7.3 %collective-permute-done.7 = f32[2,448,128]{2,1,0:T(8,128)S(1)} collective-permute-done((f32[2,448,128]{2,1,0:T(8,128)S(1)}, f32[2,448,128]{2,1,0:T(8,128)S(1)}, u32[]{:S(2)}, u32[]{:S(2)}) %collective-permute-start.7) | collective-permute-done | bytes 458784 | tf_op jit(solution)/shard_map/ppermute | solution.py:509
  55.2 7.8 %features.2 = (bf16[1024,512]{1,0:T(8,128)(2,1)S(1)}, bf16[1024,512]{1,0:T(8,128)(2,1)S(1)}, bf16[1024,1024]{1,0:T(8,128)(2,1)S(1)}, bf16[1024,1024]{1,0:T(8,128)(2,1)S(1)}) custom-call(s32[9]{0:T(128)S(1)} %stack.39.s_ref, f32[440,1024]{1,0:T(8,128)S(1)} %bitcast.16, f32[4,448,128]{2,1,0:T(8,128)S(1)} %pad_maximum_fusion.2.p_ref), custom_call_target="tpu_custom_call" | custom-call | flops 2768240640 | bytes 5996544 | tf_op jit(solution)/shard_map/features/pallas_call | solution.py:116
  63.1 7.8 %features.3 = (bf16[1024,512]{1,0:T(8,128)(2,1)S(1)}, bf16[1024,512]{1,0:T(8,128)(2,1)S(1)}, bf16[1024,1024]{1,0:T(8,128)(2,1)S(1)}, bf16[1024,1024]{1,0:T(8,128)(2,1)S(1)}) custom-call(s32[9]{0:T(128)S(1)} %stack.39.s_ref, f32[440,1024]{1,0:T(8,128)S(1)} %bitcast.17, ...), custom_call_target="tpu_custom_call", output_to_operand_aliasing={{2}: (3, {}), {3}: (4, {})} | custom-call | flops 2768240640 | bytes 5996544 | tf_op jit(solution)/shard_map/features/pallas_call | solution.py:116
  70.9 2.9 %gram.2 = f32[16,5,16,256]{3,2,1,0:T(8,128)S(1)} custom-call(s32[9]{0:T(128)S(1)} %stack.39.s_ref, bf16[1024,512]{1,0:T(8,128)(2,1)S(1)} %get-tuple-element.30.ah, bf16[1024,512]{1,0:T(8,128)(2,1)S(1)} %get-tuple-element.31.al, bf16[1024,512]{1,0:T(8,128)(2,1)S(1)} %get-tuple-element.34.bh, bf16[1024,512]{1,0:T(8,128)(2,1)S(1)} %get-tuple-element.35.bl, ...), custom_call_target="tpu_custom_call" | custom-call | flops 2013265920 | bytes 8388608 | tf_op jit(solution)/shard_map/gram/pallas_call | solution.py:175
  73.9 5.1 %cross.4 = f32[4,1024,128]{2,1,0:T(8,128)S(1)} custom-call(s32[9]{0:T(128)S(1)} %stack.39.s_ref, f32[1024,2048]{1,0:T(8,128)S(1)} %bitcast.13, bf16[1024,1024]{1,0:T(8,128)(2,1)S(1)} %get-tuple-element.46.th, bf16[1024,1024]{1,0:T(8,128)(2,1)S(1)} %get-tuple-element.47.tl), custom_call_target="tpu_custom_call" | custom-call | flops 3221225472 | bytes 4194304 | tf_op jit(solution)/shard_map/cross/pallas_call | solution.py:215
  79.6 3.1 %gram.3 = f32[16,5,16,256]{3,2,1,0:T(8,128)S(1)} custom-call(s32[9]{0:T(128)S(1)} %stack.39.s_ref, bf16[1024,512]{1,0:T(8,128)(2,1)S(1)} %get-tuple-element.30.ah, bf16[1024,512]{1,0:T(8,128)(2,1)S(1)} %get-tuple-element.31.al, bf16[1024,512]{1,0:T(8,128)(2,1)S(1)} %get-tuple-element.34.bh, bf16[1024,512]{1,0:T(8,128)(2,1)S(1)} %get-tuple-element.35.bl, ...), custom_call_target="tpu_custom_call" | custom-call | flops 2013265920 | bytes 8388608 | tf_op jit(solution)/shard_map/gram/pallas_call | solution.py:175
  82.8 2.5 collective-permute-done.9
  85.5 5.1 %cross.5 = f32[4,1024,128]{2,1,0:T(8,128)S(1)} custom-call(s32[9]{0:T(128)S(1)} %stack.39.s_ref, f32[1024,2048]{1,0:T(8,128)S(1)} %bitcast.13, bf16[1024,1024]{1,0:T(8,128)(2,1)S(1)} %get-tuple-element.46.th, bf16[1024,1024]{1,0:T(8,128)(2,1)S(1)} %get-tuple-element.47.tl, f32[4,1024,128]{2,1,0:T(8,128)S(1)} %collective-permute-done.12.rest_0_), custom_call_target="tpu_custom_call" | custom-call | flops 3221225472 | bytes 4194304 | tf_op jit(solution)/shard_map/cross/pallas_call | solution.py:215
  90.6 5.1 %cross.6 = f32[4,1024,128]{2,1,0:T(8,128)S(1)} custom-call(s32[9]{0:T(128)S(1)} %stack.39.s_ref, f32[1024,2048]{1,0:T(8,128)S(1)} %bitcast.13, bf16[1024,1024]{1,0:T(8,128)(2,1)S(1)} %get-tuple-element.46.th, bf16[1024,1024]{1,0:T(8,128)(2,1)S(1)} %get-tuple-element.47.tl), custom_call_target="tpu_custom_call" | custom-call | flops 3221225472 | bytes 4194304 | tf_op jit(solution)/shard_map/cross/pallas_call | solution.py:215
  98.5 8.4 %collective-permute-done.10 = f32[8,5,16,256]{3,2,1,0:T(8,128)S(1)} collective-permute-done((f32[8,5,16,256]{3,2,1,0:T(8,128)S(1)}, f32[8,5,16,256]{3,2,1,0:T(8,128)S(1)}, u32[]{:S(2)}, u32[]{:S(2)}) %collective-permute-start.10) | collective-permute-done | bytes 655392 | tf_op jit(solution)/shard_map/ppermute | solution.py:509
  108.3 9.4 %collective-permute-done.11 = f32[4,5,16,256]{3,2,1,0:T(8,128)S(1)} collective-permute-done((f32[4,5,16,256]{3,2,1,0:T(8,128)S(1)}, f32[4,5,16,256]{3,2,1,0:T(8,128)S(1)}, u32[]{:S(2)}, u32[]{:S(2)}) %collective-permute-start.11) | collective-permute-done | bytes 327712 | tf_op jit(solution)/shard_map/ppermute | solution.py:509
  117.7 3.9 %collective-permute-done.31 = f32[2,1024,128]{2,1,0:T(8,128)S(1)} collective-permute-done((f32[2,1024,128]{2,1,0:T(8,128)S(1)}, f32[2,1024,128]{2,1,0:T(8,128)S(1)}, u32[]{:S(2)}, u32[]{:S(2)}) %collective-permute-start.31) | collective-permute-done | bytes 1048608 | tf_op jit(solution)/shard_map/ppermute | solution.py:509
  123.1 5.1 %cross.7 = f32[4,1024,128]{2,1,0:T(8,128)S(1)} custom-call(s32[9]{0:T(128)S(1)} %stack.39.s_ref, f32[1024,2048]{1,0:T(8,128)S(1)} %bitcast.13, bf16[1024,1024]{1,0:T(8,128)(2,1)S(1)} %get-tuple-element.46.th, bf16[1024,1024]{1,0:T(8,128)(2,1)S(1)} %get-tuple-element.47.tl, f32[4,1024,128]{2,1,0:T(8,128)S(1)} %collective-permute-done.13.rest_0_), custom_call_target="tpu_custom_call" | custom-call | flops 3221225472 | bytes 4194304 | tf_op jit(solution)/shard_map/cross/pallas_call | solution.py:215
  129.0 4.7 %collective-permute-done.14 = f32[2,5,16,256]{3,2,1,0:T(8,128)S(1)} collective-permute-done((f32[2,5,16,256]{3,2,1,0:T(8,128)S(1)}, f32[2,5,16,256]{3,2,1,0:T(8,128)S(1)}, u32[]{:S(2)}, u32[]{:S(2)}) %collective-permute-start.14) | collective-permute-done | bytes 163872 | tf_op jit(solution)/shard_map/ppermute | solution.py:509
  133.6 2.1 collective-permute-start.15
  139.4 2.7 collective-permute-start.16
  146.9 3.2 %collective-permute-start.34 = (f32[1,256,128]{2,1,0:T(8,128)S(1)}, f32[1,256,128]{2,1,0:T(8,128)S(1)}, u32[]{:S(2)}, u32[]{:S(2)}) collective-permute-start(f32[1,256,128]{2,1,0:T(8,128)S(1)} %slice.135), channel_id=1, source_target_pairs={{0,16},{1,17},{2,18},{3,19},{4,20},{5,21},{6,22},{7,23},{8,24},{9,... | collective-permute-start | bytes 393224 | tf_op jit(solution)/shard_map/ppermute | solution.py:509
  150.3 2.7 collective-permute-start.18
  153.1 3.2 %collective-permute-done.34 = f32[1,256,128]{2,1,0:T(8,128)S(1)} collective-permute-done((f32[1,256,128]{2,1,0:T(8,128)S(1)}, f32[1,256,128]{2,1,0:T(8,128)S(1)}, u32[]{:S(2)}, u32[]{:S(2)}) %collective-permute-start.34) | collective-permute-done | bytes 131104 | tf_op jit(solution)/shard_map/ppermute | solution.py:509
  158.2 5.9 %collective-permute-start.19 = (f32[8,5,16,256]{3,2,1,0:T(8,128)S(1)}, f32[8,5,16,256]{3,2,1,0:T(8,128)S(1)}, u32[]{:S(2)}, u32[]{:S(2)}) collective-permute-start(f32[8,5,16,256]{3,2,1,0:T(8,128)S(1)} %pad_maximum_fusion.3), channel_id=1, source_target_pairs={{0,2},{1,5},{2,0},{3,7},{4,6},{5,1},{6,4},{7,3},{8,10},{9,13},{10,... | collective-permute-start | bytes 1966088 | tf_op jit(solution)/shard_map/ppermute | solution.py:509
  164.1 3.2 %collective-permute-start.36 = (f32[1,512,128]{2,1,0:T(8,128)S(1)}, f32[1,512,128]{2,1,0:T(8,128)S(1)}, u32[]{:S(2)}, u32[]{:S(2)}) collective-permute-start(f32[1,512,128]{2,1,0:T(8,128)S(1)} %pad_maximum_fusion.9), channel_id=1, source_target_pairs={{0,8},{1,9},{2,10},{3,11},{4,12},{5,13},{6,14},{7,15},{8,0},{9,1},... | collective-permute-start | bytes 786440 | tf_op jit(solution)/shard_map/ppermute | solution.py:509
  167.7 8.3 %collective-permute-done.19 = f32[8,5,16,256]{3,2,1,0:T(8,128)S(1)} collective-permute-done((f32[8,5,16,256]{3,2,1,0:T(8,128)S(1)}, f32[8,5,16,256]{3,2,1,0:T(8,128)S(1)}, u32[]{:S(2)}, u32[]{:S(2)}) %collective-permute-start.19) | collective-permute-done | bytes 655392 | tf_op jit(solution)/shard_map/ppermute | solution.py:509
  176.0 7.5 %assemble.1 = (f32[512,512]{1,0:T(8,128)S(1)}, f32[256,512]{1,0:T(8,128)S(1)}) custom-call(s32[9]{0:T(128)S(1)} %stack.39.s_ref, f32[16,5,16,256]{3,2,1,0:T(8,128)S(1)} %constant_dynamic-update-slice_fusion.g_ref), custom_call_target="tpu_custom_call" | custom-call | flops 10000000000 | bytes 4000000 | tf_op jit(solution)/shard_map/assemble/pallas_call | solution.py:332
  183.5 6.5 %factor.3.m_ref = f32[512,512]{1,0:T(8,128)S(1)} custom-call(f32[512,512]{1,0:T(8,128)S(1)} %get-tuple-element.49.m_ref), custom_call_target="tpu_custom_call" | custom-call | flops 10000000000 | bytes 4000000 | tf_op jit(solution)/shard_map/factor/pallas_call | solution.py:354
  191.1 6.3 %factor.4.m_ref = f32[512,512]{1,0:T(8,128)S(1)} custom-call(f32[512,512]{1,0:T(8,128)S(1)} %factor.3.m_ref), custom_call_target="tpu_custom_call" | custom-call | flops 10000000000 | bytes 4000000 | tf_op jit(solution)/shard_map/factor/pallas_call | solution.py:354
  197.6 4.0 %collective-permute-start.25 = (f32[1,256,128]{2,1,0:T(8,128)S(1)}, f32[1,256,128]{2,1,0:T(8,128)S(1)}, u32[]{:S(2)}, u32[]{:S(2)}) collective-permute-start(f32[1,256,128]{2,1,0:T(8,128)S(1)} %slice.127), channel_id=1, source_target_pairs={{0,16},{1,17},{2,18},{3,19},{4,20},{5,21},{6,22},{7,23},{8,24},{9,... | collective-permute-start | bytes 393224 | tf_op jit(solution)/shard_map/ppermute | solution.py:509
  201.7 7.8 %factor.5.own_ref = f32[512,512]{1,0:T(8,128)S(1)} custom-call(f32[512,512]{1,0:T(8,128)S(1)} %factor.4.m_ref), custom_call_target="tpu_custom_call" | custom-call | flops 10000000000 | bytes 4000000 | tf_op jit(solution)/shard_map/factor/pallas_call | solution.py:354
  209.6 9.1 %collective-permute-done.26 = f32[1,256,128]{2,1,0:T(8,128)S(1)} collective-permute-done((f32[1,256,128]{2,1,0:T(8,128)S(1)}, f32[1,256,128]{2,1,0:T(8,128)S(1)}, u32[]{:S(2)}, u32[]{:S(2)}) %collective-permute-start.26) | collective-permute-done | bytes 131104 | tf_op jit(solution)/shard_map/ppermute | solution.py:509
  220.9 6.1 %collective-permute-done.27 = f32[1,512,128]{2,1,0:T(8,128)S(1)} collective-permute-done((f32[1,512,128]{2,1,0:T(8,128)S(1)}, f32[1,512,128]{2,1,0:T(8,128)S(1)}, u32[]{:S(2)}, u32[]{:S(2)}) %collective-permute-start.27) | collective-permute-done | bytes 262176 | tf_op jit(solution)/shard_map/ppermute | solution.py:509
  228.2 2.4 couple.1.b_ref
  230.6 4.3 %solve.3.wa_ref = f32[2,1024,128]{2,1,0:T(8,128)S(1)} custom-call(s32[9]{0:T(128)S(1)} %stack.39.s_ref, f32[512,512]{1,0:T(8,128)S(1)} %factor.5.own_ref, f32[512,512]{1,0:T(8,128)S(1)} %collective-permute-done.20.oth_ref, f32[512,512]{1,0:T(8,128)S(1)} %couple.1.b_ref, f32[2,1024,128]{2,1,0:T(8,128)S(1)} %pad_maximum_fusion.1.c_ref), custom_call_target="tpu_custom_call" | custom-call | flops 2415919104 | bytes 2097152 | tf_op jit(solution)/shard_map/solve/pallas_call | solution.py:426
  235.0 2.3 collective-permute-start.38
  237.3 4.3 %solve.2.wa_ref = f32[2,1024,128]{2,1,0:T(8,128)S(1)} custom-call(s32[9]{0:T(128)S(1)} %stack.39.s_ref, f32[512,512]{1,0:T(8,128)S(1)} %factor.5.own_ref, f32[512,512]{1,0:T(8,128)S(1)} %collective-permute-done.20.oth_ref, f32[512,512]{1,0:T(8,128)S(1)} %couple.1.b_ref, f32[2,1024,128]{2,1,0:T(8,128)S(1)} %pad_maximum_fusion.c_ref), custom_call_target="tpu_custom_call" | custom-call | flops 2415919104 | bytes 2097152 | tf_op jit(solution)/shard_map/solve/pallas_call | solution.py:426
  243.6 6.5 %collective-permute-done.38.wa_ref = f32[2,1024,128]{2,1,0:T(8,128)S(1)} collective-permute-done((f32[2,1024,128]{2,1,0:T(8,128)S(1)}, f32[2,1024,128]{2,1,0:T(8,128)S(1)}, u32[]{:S(2)}, u32[]{:S(2)}) %collective-permute-start.38) | collective-permute-done | bytes 1048608 | tf_op jit(solution)/shard_map/ppermute | solution.py:509
  250.0 11.2 %collective-permute-done.29.wa_ref = f32[2,1024,128]{2,1,0:T(8,128)S(1)} collective-permute-done((f32[2,1024,128]{2,1,0:T(8,128)S(1)}, f32[2,1024,128]{2,1,0:T(8,128)S(1)}, u32[]{:S(2)}, u32[]{:S(2)}) %collective-permute-start.29) | collective-permute-done | bytes 1048608 | tf_op jit(solution)/shard_map/ppermute | solution.py:509
  261.3 6.1 %residual.4 = (f32[1024,2048]{1,0:T(8,128)}, f32[2,512,2048]{2,1,0:T(8,128)}) custom-call(s32[9]{0:T(128)S(1)} %stack.39.s_ref, f32[1024,2048]{1,0:T(8,128)S(1)} %bitcast.13, bf16[1024,512]{1,0:T(8,128)(2,1)S(1)} %get-tuple-element.30.ah, bf16[1024,512]{1,0:T(8,128)(2,1)S(1)} %get-tuple-element.31.al, bf16[1024,512]{1,0:T(8,128)(2,1)S(1)} %get-tuple-element.34.bh, ...), custom_call_target="tpu_custom_call" | custom-call | flops 3221225472 | bytes 6291456 | tf_op jit(solution)/shard_map/residual/pallas_call | solution.py:473
  267.4 6.1 %residual.5 = (f32[1024,2048]{1,0:T(8,128)}, f32[2,512,2048]{2,1,0:T(8,128)}) custom-call(s32[9]{0:T(128)S(1)} %stack.39.s_ref, f32[1024,2048]{1,0:T(8,128)S(1)} %bitcast.13, bf16[1024,512]{1,0:T(8,128)(2,1)S(1)} %get-tuple-element.30.ah, bf16[1024,512]{1,0:T(8,128)(2,1)S(1)} %get-tuple-element.31.al, ...), custom_call_target="tpu_custom_call", output_to_operand_aliasing={{0}: (8, {}), {1}: (9, {})} | custom-call | flops 3221225472 | bytes 6291456 | tf_op jit(solution)/shard_map/residual/pallas_call | solution.py:473
  273.5 6.1 %residual.6 = (f32[1024,2048]{1,0:T(8,128)}, f32[2,512,2048]{2,1,0:T(8,128)}) custom-call(s32[9]{0:T(128)S(1)} %stack.39.s_ref, f32[1024,2048]{1,0:T(8,128)S(1)} %bitcast.13, bf16[1024,512]{1,0:T(8,128)(2,1)S(1)} %get-tuple-element.30.ah, bf16[1024,512]{1,0:T(8,128)(2,1)S(1)} %get-tuple-element.31.al, ...), custom_call_target="tpu_custom_call", output_to_operand_aliasing={{0}: (8, {}), {1}: (9, {})} | custom-call | flops 3221225472 | bytes 6291456 | tf_op jit(solution)/shard_map/residual/pallas_call | solution.py:473
  279.6 6.1 %residual.7 = (f32[1024,2048]{1,0:T(8,128)}, f32[2,512,2048]{2,1,0:T(8,128)}) custom-call(s32[9]{0:T(128)S(1)} %stack.39.s_ref, f32[1024,2048]{1,0:T(8,128)S(1)} %bitcast.13, bf16[1024,512]{1,0:T(8,128)(2,1)S(1)} %get-tuple-element.30.ah, bf16[1024,512]{1,0:T(8,128)(2,1)S(1)} %get-tuple-element.31.al, ...), custom_call_target="tpu_custom_call", output_to_operand_aliasing={{0}: (8, {}), {1}: (9, {})} | custom-call | flops 3221225472 | bytes 6291456 | tf_op jit(solution)/shard_map/residual/pallas_call | solution.py:473
  (116 shorter events, 34.1 us)
Async XLA Ops:
  0.6 2.9 collective-permute-start
  1.2 2.3 collective-permute-start.1
  3.5 1.2 copy-start
  4.7 0.7 copy-start.1
  5.3 0.7 copy-start.2
  7.1 9.4 %collective-permute-start.2 = (f32[2,448,128]{2,1,0:T(8,128)S(1)}, f32[2,448,128]{2,1,0:T(8,128)S(1)}, u32[]{:S(2)}, u32[]{:S(2)}) collective-permute-start(f32[2,448,128]{2,1,0:T(8,128)S(1)} %slice.113), channel_id=1, source_target_pairs={{0,2},{1,5},{2,0},{3,7},{4,6},{5,1},{6,4},{7,3},{8,10},{9,13},{10,... | collective-permute-start | bytes 1376264 | tf_op jit(solution)/shard_map/ppermute | solution.py:509
  16.6 6.1 %collective-permute-start.3 = (f32[1,448,128]{2,1,0:T(8,128)S(1)}, f32[1,448,128]{2,1,0:T(8,128)S(1)}, u32[]{:S(2)}, u32[]{:S(2)}) collective-permute-start(f32[1,448,128]{2,1,0:T(8,128)S(1)} %slice.115), channel_id=1, source_target_pairs={{0,4},{1,3},{2,6},{3,1},{4,0},{5,7},{6,2},{7,5},{8,12},{9,11},{10,... | collective-permute-start | bytes 688136 | tf_op jit(solution)/shard_map/ppermute | solution.py:509
  22.7 32.5 %copy-start.3 = (f32[1024,440]{0,1:T(8,128)S(1)}, f32[1024,440]{0,1:T(8,128)}, u32[]{:S(2)}) copy-start(f32[1024,440]{0,1:T(8,128)} %param.5) | copy-start | bytes 5406724
  22.7 6.3 %collective-permute-start.4 = (f32[1,448,128]{2,1,0:T(8,128)S(1)}, f32[1,448,128]{2,1,0:T(8,128)S(1)}, u32[]{:S(2)}, u32[]{:S(2)}) collective-permute-start(f32[1,448,128]{2,1,0:T(8,128)S(1)} %slice_add_fusion.9), channel_id=1, source_target_pairs={{0,8},{1,9},{2,10},{3,11},{4,12},{5,13},{6,14},{7,15},{8,0},{9,1},... | collective-permute-start | bytes 688136 | tf_op jit(solution)/shard_map/ppermute | solution.py:509
  29.1 11.2 %collective-permute-start.5 = (f32[1,448,128]{2,1,0:T(8,128)S(1)}, f32[1,448,128]{2,1,0:T(8,128)S(1)}, u32[]{:S(2)}, u32[]{:S(2)}) collective-permute-start(f32[1,448,128]{2,1,0:T(8,128)S(1)} %add.109), channel_id=1, source_target_pairs={{0,16},{1,17},{2,18},{3,19},{4,20},{5,21},{6,22},{7,23},{8,24},{9,... | collective-permute-start | bytes 688136 | tf_op jit(solution)/shard_map/ppermute | solution.py:509
  40.4 6.1 %collective-permute-start.6 = (f32[1,448,128]{2,1,0:T(8,128)S(1)}, f32[1,448,128]{2,1,0:T(8,128)S(1)}, u32[]{:S(2)}, u32[]{:S(2)}) collective-permute-start(f32[1,448,128]{2,1,0:T(8,128)S(1)} %add.110), channel_id=1, source_target_pairs={{0,4},{1,3},{2,6},{3,1},{4,0},{5,7},{6,2},{7,5},{8,12},{9,11},{10,... | collective-permute-start | bytes 688136 | tf_op jit(solution)/shard_map/ppermute | solution.py:509
  46.5 8.5 %collective-permute-start.7 = (f32[2,448,128]{2,1,0:T(8,128)S(1)}, f32[2,448,128]{2,1,0:T(8,128)S(1)}, u32[]{:S(2)}, u32[]{:S(2)}) collective-permute-start(f32[2,448,128]{2,1,0:T(8,128)S(1)} %pad_maximum_fusion.6), channel_id=1, source_target_pairs={{0,2},{1,5},{2,0},{3,7},{4,6},{5,1},{6,4},{7,3},{8,10},{9,13},{10,... | collective-permute-start | bytes 1376264 | tf_op jit(solution)/shard_map/ppermute | solution.py:509
  55.1 8.0 %collective-permute-start.8 = (f32[4,448,128]{2,1,0:T(8,128)S(1)}, f32[4,448,128]{2,1,0:T(8,128)S(1)}, u32[]{:S(2)}, u32[]{:S(2)}) collective-permute-start(f32[4,448,128]{2,1,0:T(8,128)S(1)} %pad_maximum_fusion.2.p_ref), channel_id=1, source_target_pairs={{0,1},{1,0},{2,3},{3,2},{4,5},{5,4},{6,7},{7,6},{8,9},{9,8},{10,11... | collective-permute-start | bytes 2752520 | tf_op jit(solution)/shard_map/ppermute | solution.py:509
  55.2 18.7 %slice-start = ((s8[8388608]{0:T(1024)(128)(4,1)}), s8[4194304]{0:T(1024)(128)(4,1)S(1)}, s32[]{:S(2)}) async-start(s8[8388608]{0:T(1024)(128)(4,1)} %bitcast.12), calls=%async_computation | async-start | bytes 8388608
  63.1 10.8 %slice-start.1 = ((s8[8388608]{0:T(1024)(128)(4,1)}), s8[4194304]{0:T(1024)(128)(4,1)S(1)}, s32[]{:S(2)}) async-start(s8[8388608]{0:T(1024)(128)(4,1)} %bitcast.12), calls=%async_computation.1 | async-start | bytes 8388608
  79.0 6.5 %collective-permute-start.12 = (f32[4,1024,128]{2,1,0:T(8,128)S(1)}, f32[4,1024,128]{2,1,0:T(8,128)S(1)}, u32[]{:S(2)}, u32[]{:S(2)}) collective-permute-start(f32[4,1024,128]{2,1,0:T(8,128)S(1)} %cross.4), channel_id=1, source_target_pairs={{0,1},{1,0},{2,3},{3,2},{4,5},{5,4},{6,7},{7,6},{8,9},{9,8},{10,11... | collective-permute-start | bytes 6291464 | tf_op jit(solution)/shard_map/ppermute | solution.py:509
  79.6 5.7 %collective-permute-start.9 = (f32[16,5,16,256]{3,2,1,0:T(8,128)S(1)}, f32[16,5,16,256]{3,2,1,0:T(8,128)S(1)}, u32[]{:S(2)}, u32[]{:S(2)}) collective-permute-start(f32[16,5,16,256]{3,2,1,0:T(8,128)S(1)} %gram.2), channel_id=1, source_target_pairs={{0,1},{1,0},{2,3},{3,2},{4,5},{5,4},{6,7},{7,6},{8,9},{9,8},{10,11... | collective-permute-start | bytes 3932168 | tf_op jit(solution)/shard_map/ppermute | solution.py:509
  95.8 27.3 %collective-permute-start.13 = (f32[4,1024,128]{2,1,0:T(8,128)S(1)}, f32[4,1024,128]{2,1,0:T(8,128)S(1)}, u32[]{:S(2)}, u32[]{:S(2)}) collective-permute-start(f32[4,1024,128]{2,1,0:T(8,128)S(1)} %cross.6), channel_id=1, source_target_pairs={{0,1},{1,0},{2,3},{3,2},{4,5},{5,4},{6,7},{7,6},{8,9},{9,8},{10,11... | collective-permute-start | bytes 6291464 | tf_op jit(solution)/shard_map/ppermute | solution.py:509
  96.3 10.7 %collective-permute-start.10 = (f32[8,5,16,256]{3,2,1,0:T(8,128)S(1)}, f32[8,5,16,256]{3,2,1,0:T(8,128)S(1)}, u32[]{:S(2)}, u32[]{:S(2)}) collective-permute-start(f32[8,5,16,256]{3,2,1,0:T(8,128)S(1)} %slice.117), channel_id=1, source_target_pairs={{0,2},{1,5},{2,0},{3,7},{4,6},{5,1},{6,4},{7,3},{8,10},{9,13},{10,... | collective-permute-start | bytes 1966088 | tf_op jit(solution)/shard_map/ppermute | solution.py:509
  97.6 24.1 %collective-permute-start.31 = (f32[2,1024,128]{2,1,0:T(8,128)S(1)}, f32[2,1024,128]{2,1,0:T(8,128)S(1)}, u32[]{:S(2)}, u32[]{:S(2)}) collective-permute-start(f32[2,1024,128]{2,1,0:T(8,128)S(1)} %slice.129), channel_id=1, source_target_pairs={{0,2},{1,5},{2,0},{3,7},{4,6},{5,1},{6,4},{7,3},{8,10},{9,13},{10,... | collective-permute-start | bytes 3145736 | tf_op jit(solution)/shard_map/ppermute | solution.py:509
  107.1 10.6 %collective-permute-start.11 = (f32[4,5,16,256]{3,2,1,0:T(8,128)S(1)}, f32[4,5,16,256]{3,2,1,0:T(8,128)S(1)}, u32[]{:S(2)}, u32[]{:S(2)}) collective-permute-start(f32[4,5,16,256]{3,2,1,0:T(8,128)S(1)} %slice.119), channel_id=1, source_target_pairs={{0,4},{1,3},{2,6},{3,1},{4,0},{5,7},{6,2},{7,5},{8,12},{9,11},{10,... | collective-permute-start | bytes 983048 | tf_op jit(solution)/shard_map/ppermute | solution.py:509
  121.8 14.0 %collective-permute-start.32 = (f32[1,1024,128]{2,1,0:T(8,128)S(1)}, f32[1,1024,128]{2,1,0:T(8,128)S(1)}, u32[]{:S(2)}, u32[]{:S(2)}) collective-permute-start(f32[1,1024,128]{2,1,0:T(8,128)S(1)} %slice.131), channel_id=1, source_target_pairs={{0,4},{1,3},{2,6},{3,1},{4,0},{5,7},{6,2},{7,5},{8,12},{9,11},{10,... | collective-permute-start | bytes 1572872 | tf_op jit(solution)/shard_map/ppermute | solution.py:509
  128.2 5.4 %collective-permute-start.14 = (f32[2,5,16,256]{3,2,1,0:T(8,128)S(1)}, f32[2,5,16,256]{3,2,1,0:T(8,128)S(1)}, u32[]{:S(2)}, u32[]{:S(2)}) collective-permute-start(f32[2,5,16,256]{3,2,1,0:T(8,128)S(1)} %slice.93), channel_id=1, source_target_pairs={{0,8},{1,9},{2,10},{3,11},{4,12},{5,13},{6,14},{7,15},{8,0},{9,1},... | collective-permute-start | bytes 491528 | tf_op jit(solution)/shard_map/ppermute | solution.py:509
  133.6 5.7 %collective-permute-start.15 = (f32[1,5,16,256]{3,2,1,0:T(8,128)S(1)}, f32[1,5,16,256]{3,2,1,0:T(8,128)S(1)}, u32[]{:S(2)}, u32[]{:S(2)}) collective-permute-start(f32[1,5,16,256]{3,2,1,0:T(8,128)S(1)} %slice.121), channel_id=1, source_target_pairs={{0,16},{1,17},{2,18},{3,19},{4,20},{5,21},{6,22},{7,23},{8,24},{9,... | collective-permute-start | bytes 245768 | tf_op jit(solution)/shard_map/ppermute | solution.py:509
  135.9 10.9 %collective-permute-start.33 = (f32[1,512,128]{2,1,0:T(8,128)S(1)}, f32[1,512,128]{2,1,0:T(8,128)S(1)}, u32[]{:S(2)}, u32[]{:S(2)}) collective-permute-start(f32[1,512,128]{2,1,0:T(8,128)S(1)} %slice.133), channel_id=1, source_target_pairs={{0,8},{1,9},{2,10},{3,11},{4,12},{5,13},{6,14},{7,15},{8,0},{9,1},... | collective-permute-start | bytes 786440 | tf_op jit(solution)/shard_map/ppermute | solution.py:509
  139.4 5.5 %collective-permute-start.16 = (f32[1,5,16,256]{3,2,1,0:T(8,128)S(1)}, f32[1,5,16,256]{3,2,1,0:T(8,128)S(1)}, u32[]{:S(2)}, u32[]{:S(2)}) collective-permute-start(f32[1,5,16,256]{3,2,1,0:T(8,128)S(1)} %get-tuple-element.59), channel_id=1, source_target_pairs={{0,16},{1,17},{2,18},{3,19},{4,20},{5,21},{6,22},{7,23},{8,24},{9,... | collective-permute-start | bytes 245768 | tf_op jit(solution)/shard_map/ppermute | solution.py:509
  142.2 25.2 %collective-permute-start.22 = (f32[2,1024,128]{2,1,0:T(8,128)S(1)}, f32[2,1024,128]{2,1,0:T(8,128)S(1)}, u32[]{:S(2)}, u32[]{:S(2)}) collective-permute-start(f32[2,1024,128]{2,1,0:T(8,128)S(1)} %slice.97), channel_id=1, source_target_pairs={{0,2},{1,5},{2,0},{3,7},{4,6},{5,1},{6,4},{7,3},{8,10},{9,13},{10,... | collective-permute-start | bytes 3145736 | tf_op jit(solution)/shard_map/ppermute | solution.py:509
  144.9 5.4 %collective-permute-start.17 = (f32[2,5,16,256]{3,2,1,0:T(8,128)S(1)}, f32[2,5,16,256]{3,2,1,0:T(8,128)S(1)}, u32[]{:S(2)}, u32[]{:S(2)}) collective-permute-start(f32[2,5,16,256]{3,2,1,0:T(8,128)S(1)} %pad_maximum_fusion.10), channel_id=1, source_target_pairs={{0,8},{1,9},{2,10},{3,11},{4,12},{5,13},{6,14},{7,15},{8,0},{9,1},... | collective-permute-start | bytes 491528 | tf_op jit(solution)/shard_map/ppermute | solution.py:509
  146.9 9.3 %collective-permute-start.34 = (f32[1,256,128]{2,1,0:T(8,128)S(1)}, f32[1,256,128]{2,1,0:T(8,128)S(1)}, u32[]{:S(2)}, u32[]{:S(2)}) collective-permute-start(f32[1,256,128]{2,1,0:T(8,128)S(1)} %slice.135), channel_id=1, source_target_pairs={{0,16},{1,17},{2,18},{3,19},{4,20},{5,21},{6,22},{7,23},{8,24},{9,... | collective-permute-start | bytes 393224 | tf_op jit(solution)/shard_map/ppermute | solution.py:509
  150.3 7.8 %collective-permute-start.18 = (f32[4,5,16,256]{3,2,1,0:T(8,128)S(1)}, f32[4,5,16,256]{3,2,1,0:T(8,128)S(1)}, u32[]{:S(2)}, u32[]{:S(2)}) collective-permute-start(f32[4,5,16,256]{3,2,1,0:T(8,128)S(1)} %pad_maximum_fusion.7), channel_id=1, source_target_pairs={{0,4},{1,3},{2,6},{3,1},{4,0},{5,7},{6,2},{7,5},{8,12},{9,11},{10,... | collective-permute-start | bytes 983048 | tf_op jit(solution)/shard_map/ppermute | solution.py:509
  156.2 7.8 %collective-permute-start.35 = (f32[1,256,128]{2,1,0:T(8,128)S(1)}, f32[1,256,128]{2,1,0:T(8,128)S(1)}, u32[]{:S(2)}, u32[]{:S(2)}) collective-permute-start(f32[1,256,128]{2,1,0:T(8,128)S(1)} %slice_add_fusion.11), channel_id=1, source_target_pairs={{0,16},{1,17},{2,18},{3,19},{4,20},{5,21},{6,22},{7,23},{8,24},{9,... | collective-permute-start | bytes 393224 | tf_op jit(solution)/shard_map/ppermute | solution.py:509
  158.2 17.8 %collective-permute-start.19 = (f32[8,5,16,256]{3,2,1,0:T(8,128)S(1)}, f32[8,5,16,256]{3,2,1,0:T(8,128)S(1)}, u32[]{:S(2)}, u32[]{:S(2)}) collective-permute-start(f32[8,5,16,256]{3,2,1,0:T(8,128)S(1)} %pad_maximum_fusion.3), channel_id=1, source_target_pairs={{0,2},{1,5},{2,0},{3,7},{4,6},{5,1},{6,4},{7,3},{8,10},{9,13},{10,... | collective-permute-start | bytes 1966088 | tf_op jit(solution)/shard_map/ppermute | solution.py:509
  164.1 54.7 %collective-permute-start.36 = (f32[1,512,128]{2,1,0:T(8,128)S(1)}, f32[1,512,128]{2,1,0:T(8,128)S(1)}, u32[]{:S(2)}, u32[]{:S(2)}) collective-permute-start(f32[1,512,128]{2,1,0:T(8,128)S(1)} %pad_maximum_fusion.9), channel_id=1, source_target_pairs={{0,8},{1,9},{2,10},{3,11},{4,12},{5,13},{6,14},{7,15},{8,0},{9,1},... | collective-permute-start | bytes 786440 | tf_op jit(solution)/shard_map/ppermute | solution.py:509
  167.6 22.4 %collective-permute-start.23 = (f32[1,1024,128]{2,1,0:T(8,128)S(1)}, f32[1,1024,128]{2,1,0:T(8,128)S(1)}, u32[]{:S(2)}, u32[]{:S(2)}) collective-permute-start(f32[1,1024,128]{2,1,0:T(8,128)S(1)} %slice.123), channel_id=1, source_target_pairs={{0,4},{1,3},{2,6},{3,1},{4,0},{5,7},{6,2},{7,5},{8,12},{9,11},{10,... | collective-permute-start | bytes 1572872 | tf_op jit(solution)/shard_map/ppermute | solution.py:509
  190.1 7.5 %collective-permute-start.24 = (f32[1,512,128]{2,1,0:T(8,128)S(1)}, f32[1,512,128]{2,1,0:T(8,128)S(1)}, u32[]{:S(2)}, u32[]{:S(2)}) collective-permute-start(f32[1,512,128]{2,1,0:T(8,128)S(1)} %slice.125), channel_id=1, source_target_pairs={{0,8},{1,9},{2,10},{3,11},{4,12},{5,13},{6,14},{7,15},{8,0},{9,1},... | collective-permute-start | bytes 786440 | tf_op jit(solution)/shard_map/ppermute | solution.py:509
  197.6 11.9 %collective-permute-start.25 = (f32[1,256,128]{2,1,0:T(8,128)S(1)}, f32[1,256,128]{2,1,0:T(8,128)S(1)}, u32[]{:S(2)}, u32[]{:S(2)}) collective-permute-start(f32[1,256,128]{2,1,0:T(8,128)S(1)} %slice.127), channel_id=1, source_target_pairs={{0,16},{1,17},{2,18},{3,19},{4,20},{5,21},{6,22},{7,23},{8,24},{9,... | collective-permute-start | bytes 393224 | tf_op jit(solution)/shard_map/ppermute | solution.py:509
  209.4 18.7 %collective-permute-start.20 = (f32[512,512]{1,0:T(8,128)S(1)}, f32[512,512]{1,0:T(8,128)S(1)}, u32[]{:S(2)}, u32[]{:S(2)}) collective-permute-start(f32[512,512]{1,0:T(8,128)S(1)} %factor.5.own_ref), channel_id=1, source_target_pairs={{0,1},{1,0},{2,3},{3,2},{4,5},{5,4},{6,7},{7,6},{8,9},{9,8},{10,11... | collective-permute-start | bytes 3145736 | tf_op jit(solution)/shard_map/ppermute | solution.py:509
  209.5 9.1 %collective-permute-start.26 = (f32[1,256,128]{2,1,0:T(8,128)S(1)}, f32[1,256,128]{2,1,0:T(8,128)S(1)}, u32[]{:S(2)}, u32[]{:S(2)}) collective-permute-start(f32[1,256,128]{2,1,0:T(8,128)S(1)} %slice_add_fusion.12), channel_id=1, source_target_pairs={{0,16},{1,17},{2,18},{3,19},{4,20},{5,21},{6,22},{7,23},{8,24},{9,... | collective-permute-start | bytes 393224 | tf_op jit(solution)/shard_map/ppermute | solution.py:509
  218.7 8.3 %collective-permute-start.27 = (f32[1,512,128]{2,1,0:T(8,128)S(1)}, f32[1,512,128]{2,1,0:T(8,128)S(1)}, u32[]{:S(2)}, u32[]{:S(2)}) collective-permute-start(f32[1,512,128]{2,1,0:T(8,128)S(1)} %pad_maximum_fusion.8), channel_id=1, source_target_pairs={{0,8},{1,9},{2,10},{3,11},{4,12},{5,13},{6,14},{7,15},{8,0},{9,1},... | collective-permute-start | bytes 786440 | tf_op jit(solution)/shard_map/ppermute | solution.py:509
  218.8 9.2 %collective-permute-start.37 = (f32[1,1024,128]{2,1,0:T(8,128)S(1)}, f32[1,1024,128]{2,1,0:T(8,128)S(1)}, u32[]{:S(2)}, u32[]{:S(2)}) collective-permute-start(f32[1,1024,128]{2,1,0:T(8,128)S(1)} %pad_maximum_fusion.5), channel_id=1, source_target_pairs={{0,4},{1,3},{2,6},{3,1},{4,0},{5,7},{6,2},{7,5},{8,12},{9,11},{10,... | collective-permute-start | bytes 1572872 | tf_op jit(solution)/shard_map/ppermute | solution.py:509
  219.0 9.2 %collective-permute-start.21 = (f32[256,512]{1,0:T(8,128)S(1)}, f32[256,512]{1,0:T(8,128)S(1)}, u32[]{:S(2)}, u32[]{:S(2)}) collective-permute-start(f32[256,512]{1,0:T(8,128)S(1)} %get-tuple-element.50.gown_ref), channel_id=1, source_target_pairs={{0,1},{1,0},{2,3},{3,2},{4,5},{5,4},{6,7},{7,6},{8,9},{9,8},{10,11... | collective-permute-start | bytes 1572872 | tf_op jit(solution)/shard_map/ppermute | solution.py:509
  227.1 10.2 %collective-permute-start.28 = (f32[1,1024,128]{2,1,0:T(8,128)S(1)}, f32[1,1024,128]{2,1,0:T(8,128)S(1)}, u32[]{:S(2)}, u32[]{:S(2)}) collective-permute-start(f32[1,1024,128]{2,1,0:T(8,128)S(1)} %pad_maximum_fusion.4), channel_id=1, source_target_pairs={{0,4},{1,3},{2,6},{3,1},{4,0},{5,7},{6,2},{7,5},{8,12},{9,11},{10,... | collective-permute-start | bytes 1572872 | tf_op jit(solution)/shard_map/ppermute | solution.py:509
  235.0 15.1 %collective-permute-start.38 = (f32[2,1024,128]{2,1,0:T(8,128)S(1)}, f32[2,1024,128]{2,1,0:T(8,128)S(1)}, u32[]{:S(2)}, u32[]{:S(2)}) collective-permute-start(f32[2,1024,128]{2,1,0:T(8,128)S(1)} %solve.3.wa_ref), channel_id=1, source_target_pairs={{0,2},{1,5},{2,0},{3,7},{4,6},{5,1},{6,4},{7,3},{8,10},{9,13},{10,... | collective-permute-start | bytes 3145736 | tf_op jit(solution)/shard_map/ppermute | solution.py:509
  241.7 19.6 %collective-permute-start.29 = (f32[2,1024,128]{2,1,0:T(8,128)S(1)}, f32[2,1024,128]{2,1,0:T(8,128)S(1)}, u32[]{:S(2)}, u32[]{:S(2)}) collective-permute-start(f32[2,1024,128]{2,1,0:T(8,128)S(1)} %solve.2.wa_ref), channel_id=1, source_target_pairs={{0,2},{1,5},{2,0},{3,7},{4,6},{5,1},{6,4},{7,3},{8,10},{9,13},{10,... | collective-permute-start | bytes 3145736 | tf_op jit(solution)/shard_map/ppermute | solution.py:509
  243.1 18.2 %collective-permute-start.41 = (f32[2,1024,128]{2,1,0:T(8,128)S(1)}, f32[2,1024,128]{2,1,0:T(8,128)S(1)}, u32[]{:S(2)}, u32[]{:S(2)}) collective-permute-start(f32[2,1024,128]{2,1,0:T(8,128)S(1)} %solve.3.wa_ref), channel_id=1, source_target_pairs={{0,1},{1,0},{2,3},{3,2},{4,5},{5,4},{6,7},{7,6},{8,9},{9,8},{10,11... | collective-permute-start | bytes 3145736 | tf_op jit(solution)/shard_map/ppermute | solution.py:509
  243.1 24.3 %collective-permute-start.40 = (f32[2,1024,128]{2,1,0:T(8,128)S(1)}, f32[2,1024,128]{2,1,0:T(8,128)S(1)}, u32[]{:S(2)}, u32[]{:S(2)}) collective-permute-start(f32[2,1024,128]{2,1,0:T(8,128)S(1)} %solve.2.wa_ref), channel_id=1, source_target_pairs={{0,1},{1,0},{2,3},{3,2},{4,5},{5,4},{6,7},{7,6},{8,9},{9,8},{10,11... | collective-permute-start | bytes 3145736 | tf_op jit(solution)/shard_map/ppermute | solution.py:509
  250.0 23.5 %collective-permute-start.39 = (f32[2,1024,128]{2,1,0:T(8,128)S(1)}, f32[2,1024,128]{2,1,0:T(8,128)S(1)}, u32[]{:S(2)}, u32[]{:S(2)}) collective-permute-start(f32[2,1024,128]{2,1,0:T(8,128)S(1)} %collective-permute-done.38.wa_ref), channel_id=1, source_target_pairs={{0,1},{1,0},{2,3},{3,2},{4,5},{5,4},{6,7},{7,6},{8,9},{9,8},{10,11... | collective-permute-start | bytes 3145736 | tf_op jit(solution)/shard_map/ppermute | solution.py:509
  261.3 18.4 %collective-permute-start.30 = (f32[2,1024,128]{2,1,0:T(8,128)S(1)}, f32[2,1024,128]{2,1,0:T(8,128)S(1)}, u32[]{:S(2)}, u32[]{:S(2)}) collective-permute-start(f32[2,1024,128]{2,1,0:T(8,128)S(1)} %collective-permute-done.29.wa_ref), channel_id=1, source_target_pairs={{0,1},{1,0},{2,3},{3,2},{4,5},{5,4},{6,7},{7,6},{8,9},{9,8},{10,11... | collective-permute-start | bytes 3145736 | tf_op jit(solution)/shard_map/ppermute | solution.py:509

commit v4 on v3

--- a/solution.py
+++ b/solution.py
@@ -99,23 +99,30 @@
 def features_kernel(quarter, s_ref, x_ref, p_ref, *rest):
     fh_ref, fl_ref, th_ref, tl_ref = rest[-4:]
     depth = x_ref.shape[0]
-    order = s_ref[quarter]
-    turned = jnp.concatenate([p_ref[i ^ order] for i in range(4)], axis=1).T
+    swap = s_ref[quarter] & 1
+    turned = jnp.concatenate([p_ref[i ^ swap] for i in range(2)], axis=1).T
     inner = dot_full(turned[:, :depth], x_ref[...]) + turned[:, depth : depth + 1]
-    feats = math.sqrt(2.0 / turned.shape[0]) * cosine(inner)
+    feats = math.sqrt(1.0 / turned.shape[0]) * cosine(inner)
     th_ref[...], tl_ref[...] = split(feats)
     fh_ref[...], fl_ref[...] = split(feats.T)
 
 
-def features(quarter, slot, scalars, frames_turned, blocks, before=()):
+def features(quarter, slot, part, scalars, frames_turned, blocks, flat=(), stacked=()):
     depth, rows = frames_turned.shape
-    feats = blocks.shape[0] * blocks.shape[2]
+    half = blocks.shape[0] * blocks.shape[2]
     tile = 256
-    flat = pl.BlockSpec((tile, feats), lambda i, s: (i, 0))
-    turned = pl.BlockSpec((feats, tile), lambda i, s: (slot, i))
+    before = tuple(flat) + tuple(stacked)
+    n_flat = len(flat)
+    aliases = {3 + k: k for k in range(n_flat)}
+    aliases.update({3 + n_flat + k: 2 + k for k in range(len(stacked))})
+
+    def pair(s):
+        return part ^ (s[quarter] >> 1)
+
     return pl.pallas_call(
         functools.partial(features_kernel, quarter),
-        out_shape=[jax.ShapeDtypeStruct((rows, feats), BF16)] * 2 + [jax.ShapeDtypeStruct((2 * feats, rows), BF16)] * 2,
+        out_shape=[jax.ShapeDtypeStruct((rows, 2 * half), BF16)] * 2
+        + [jax.ShapeDtypeStruct((4 * half, rows), BF16)] * 2,
         grid_spec=pltpu.PrefetchScalarGridSpec(
             num_scalar_prefetch=1,
             grid=(rows // tile,),
@@ -124,11 +131,12 @@
                 pl.BlockSpec(blocks.shape, lambda i, s: (0, 0, 0)),
             ]
             + [pl.BlockSpec(memory_space=pl.ANY)] * len(before),
-            out_specs=[flat, flat, turned, turned],
+            out_specs=[pl.BlockSpec((tile, half), lambda i, s: (i, pair(s)))] * 2
+            + [pl.BlockSpec((half, tile), lambda i, s: (2 * slot + pair(s), i))] * 2,
         ),
-        input_output_aliases={3: 2, 4: 3} if before else {},
-        compiler_params=params(),
-        cost_estimate=cost(12 * rows * depth * feats, 4 * rows * depth + 8 * rows * feats),
+        input_output_aliases=aliases,
+        compiler_params=params(),
+        cost_estimate=cost(12 * rows * depth * half, 4 * rows * depth + 8 * rows * half),
         name="features",
     )(scalars, frames_turned, blocks, *before)
 
@@ -532,11 +540,13 @@
     part = part[:1] + exchange(part[1:], 4, 2)
     part = flood(part, [8, 16] + more)
     part = jnp.concatenate([part, exchange(part, 4, 2)])
-    blocks = jnp.concatenate([part, exchange(part, 2, 4)])
-    blocks_oth = exchange(blocks, 1)
-    *mine, high, low = features(QUARTER_OWN, 0, scalars, frames.T, blocks)
-    *other, high, low = features(QUARTER_OTH, 1, scalars, frames.T, blocks_oth, (high, low))
-
+    part_b = exchange(part, 2, 4)
+    mine, other, stacked = (), (), ()
+    for half, value in enumerate((part, part_b)):
+        value_oth = exchange(value, 1)
+        *mine, high, low = features(QUARTER_OWN, 0, half, scalars, frames.T, value, mine, stacked)
+        *other, high, low = features(QUARTER_OTH, 1, half, scalars, frames.T, value_oth, other, (high, low))
+        stacked = (high, low)
     flat = mine + other
 
     def after(done, turned):

time: 286 us -> 291 us (1.017)
  Pallas kernels: 107 us -> 111 us
    pallas_call x2 -> x4, Pallas kernels: 15.7 us -> 20.2 us  [features(): pl.pallas_call(functools.partial(features_kernel, quarter), out_shape=[ja...]
    ppermute x42 -> x43, waiting for transfers between devices: 115 us -> 115 us  [exchange(): return lax.ppermute(value, ALL, pairs)]
    ppermute x42 -> x43, starting transfers between devices: 57.9 us -> 57.9 us  [exchange(): return lax.ppermute(value, ALL, pairs)]
  transfers between devices with their start and end apart: 42 -> 43, of which waited for: 24 -> 24; matrix products, arithmetic and copies ran while one was open for 1% -> 1% of each run, Pallas kernels for 26% -> 28%
where the time goes in v4:
time: 291 us; the launch traced here: 290 us
  waiting for transfers between devices  115 us (40%)
  Pallas kernels  111 us (38%)
  starting transfers between devices  57.9 us (20%)
  local copies, waits for them, and re-layouts  3.11 us (1%)
    ppermute x43, waiting for transfers between devices, exchange(): return lax.ppermute(value, ALL, pairs)  115 us
    ppermute x43, starting transfers between devices, exchange(): return lax.ppermute(value, ALL, pairs)  57.9 us
    pallas_call x4, Pallas kernels, residual_part(): pl.pallas_call(residual_kernel, out_shape=[jax.ShapeDtypeStruct((rows, co...  24.5 us
    pallas_call x3, Pallas kernels, factor(): pl.pallas_call(functools.partial(factor_kernel, step), out_shape=jax.Shap...  20.6 us
    pallas_call x4, Pallas kernels, cross(): pl.pallas_call(functools.partial(cross_kernel, base), out_shape=jax.Shape...  20.5 us
    pallas_call x4, Pallas kernels, features(): pl.pallas_call(functools.partial(features_kernel, quarter), out_shape=[ja...  20.2 us
    pallas_call x2, Pallas kernels, solve(): pl.pallas_call(solve_kernel, out_shape=jax.ShapeDtypeStruct(crossed.shape...  8.69 us
    pallas_call x1, Pallas kernels, assemble(): pl.pallas_call(assemble_kernel, out_shape=[jax.ShapeDtypeStruct((2 * half...  7.48 us
  transfers between devices with their start and end apart: 43, of which 24 were waited for; matrix products, arithmetic and copies ran while one was open for 1% of the time, Pallas kernels for 28%

profile of v4, /device:TPU:0, one launch (start us, length us, event | category | flops | bytes accessed | tf_op | source)
XLA Modules:
  0.0 290.2 jit_solution(13297579714209029085)
XLA Ops:
  7.1 2.9 %collective-permute-start.2 = (f32[2,448,128]{2,1,0:T(8,128)S(1)}, f32[2,448,128]{2,1,0:T(8,128)S(1)}, u32[]{:S(2)}, u32[]{:S(2)}) collective-permute-start(f32[2,448,128]{2,1,0:T(8,128)S(1)} %slice.113), channel_id=1, source_target_pairs={{0,2},{1,5},{2,0},{3,7},{4,6},{5,1},{6,4},{7,3},{8,10},{9,13},{10,... | collective-permute-start | bytes 1376264 | tf_op jit(solution)/shard_map/ppermute | solution.py:517
  10.0 6.5 %collective-permute-done.2 = f32[2,448,128]{2,1,0:T(8,128)S(1)} collective-permute-done((f32[2,448,128]{2,1,0:T(8,128)S(1)}, f32[2,448,128]{2,1,0:T(8,128)S(1)}, u32[]{:S(2)}, u32[]{:S(2)}) %collective-permute-start.2) | collective-permute-done | bytes 458784 | tf_op jit(solution)/shard_map/ppermute | solution.py:517
  18.7 4.0 %collective-permute-done.3 = f32[1,448,128]{2,1,0:T(8,128)S(1)} collective-permute-done((f32[1,448,128]{2,1,0:T(8,128)S(1)}, f32[1,448,128]{2,1,0:T(8,128)S(1)}, u32[]{:S(2)}, u32[]{:S(2)}) %collective-permute-start.3) | collective-permute-done | bytes 229408 | tf_op jit(solution)/shard_map/ppermute | solution.py:517
  24.9 4.2 %collective-permute-done.4 = f32[1,448,128]{2,1,0:T(8,128)S(1)} collective-permute-done((f32[1,448,128]{2,1,0:T(8,128)S(1)}, f32[1,448,128]{2,1,0:T(8,128)S(1)}, u32[]{:S(2)}, u32[]{:S(2)}) %collective-permute-start.4) | collective-permute-done | bytes 229408 | tf_op jit(solution)/shard_map/ppermute | solution.py:517
  29.1 3.1 %collective-permute-start.5 = (f32[1,448,128]{2,1,0:T(8,128)S(1)}, f32[1,448,128]{2,1,0:T(8,128)S(1)}, u32[]{:S(2)}, u32[]{:S(2)}) collective-permute-start(f32[1,448,128]{2,1,0:T(8,128)S(1)} %add.109), channel_id=1, source_target_pairs={{0,16},{1,17},{2,18},{3,19},{4,20},{5,21},{6,22},{7,23},{8,24},{9,... | collective-permute-start | bytes 688136 | tf_op jit(solution)/shard_map/ppermute | solution.py:517
  32.1 8.2 %collective-permute-done.5 = f32[1,448,128]{2,1,0:T(8,128)S(1)} collective-permute-done((f32[1,448,128]{2,1,0:T(8,128)S(1)}, f32[1,448,128]{2,1,0:T(8,128)S(1)}, u32[]{:S(2)}, u32[]{:S(2)}) %collective-permute-start.5) | collective-permute-done | bytes 229408 | tf_op jit(solution)/shard_map/ppermute | solution.py:517
  41.6 4.8 %collective-permute-done.6 = f32[1,448,128]{2,1,0:T(8,128)S(1)} collective-permute-done((f32[1,448,128]{2,1,0:T(8,128)S(1)}, f32[1,448,128]{2,1,0:T(8,128)S(1)}, u32[]{:S(2)}, u32[]{:S(2)}) %collective-permute-start.6) | collective-permute-done | bytes 229408 | tf_op jit(solution)/shard_map/ppermute | solution.py:517
  47.7 7.3 %collective-permute-done.7.p_ref = f32[2,448,128]{2,1,0:T(8,128)S(1)} collective-permute-done((f32[2,448,128]{2,1,0:T(8,128)S(1)}, f32[2,448,128]{2,1,0:T(8,128)S(1)}, u32[]{:S(2)}, u32[]{:S(2)}) %collective-permute-start.7) | collective-permute-done | bytes 458784 | tf_op jit(solution)/shard_map/ppermute | solution.py:517
  55.0 5.0 %features.4 = (bf16[1024,512]{1,0:T(8,128)(2,1)S(1)}, bf16[1024,512]{1,0:T(8,128)(2,1)S(1)}, bf16[1024,1024]{1,0:T(8,128)(2,1)S(1)}, bf16[1024,1024]{1,0:T(8,128)(2,1)S(1)}) custom-call(s32[9]{0:T(128)S(1)} %stack.39.s_ref, f32[440,1024]{1,0:T(8,128)S(1)} %bitcast.14, f32[2,448,128]{2,1,0:T(8,128)S(1)} %pad_maximum_fusion.5.p_ref), custom_call_target="tpu_custom_call" | custom-call | flops 1384120320 | bytes 3899392 | tf_op jit(solution)/shard_map/features/pallas_call | solution.py:122
  60.1 5.1 %features.5 = (bf16[1024,512]{1,0:T(8,128)(2,1)S(1)}, bf16[1024,512]{1,0:T(8,128)(2,1)S(1)}, bf16[1024,1024]{1,0:T(8,128)(2,1)S(1)}, bf16[1024,1024]{1,0:T(8,128)(2,1)S(1)}) custom-call(s32[9]{0:T(128)S(1)} %stack.39.s_ref, f32[440,1024]{1,0:T(8,128)S(1)} %bitcast.15, ...), custom_call_target="tpu_custom_call", output_to_operand_aliasing={{2}: (3, {}), {3}: (4, {})} | custom-call | flops 1384120320 | bytes 3899392 | tf_op jit(solution)/shard_map/features/pallas_call | solution.py:122
  65.1 5.0 %features.6 = (bf16[1024,512]{1,0:T(8,128)(2,1)S(1)}, bf16[1024,512]{1,0:T(8,128)(2,1)S(1)}, bf16[1024,1024]{1,0:T(8,128)(2,1)S(1)}, bf16[1024,1024]{1,0:T(8,128)(2,1)S(1)}) custom-call(s32[9]{0:T(128)S(1)} %stack.39.s_ref, f32[440,1024]{1,0:T(8,128)S(1)} %bitcast.16, ...), custom_call_target="tpu_custom_call", output_to_operand_aliasing={{0}: (3, {}), {1}: (4, {}), {2}: (5, {}), {3}: (6, {})} | custom-call | flops 1384120320 | bytes 3899392 | tf_op jit(solution)/shard_map/features/pallas_call | solution.py:122
  70.2 5.1 %features.7 = (bf16[1024,512]{1,0:T(8,128)(2,1)S(1)}, bf16[1024,512]{1,0:T(8,128)(2,1)S(1)}, bf16[1024,1024]{1,0:T(8,128)(2,1)S(1)}, bf16[1024,1024]{1,0:T(8,128)(2,1)S(1)}) custom-call(s32[9]{0:T(128)S(1)} %stack.39.s_ref, f32[440,1024]{1,0:T(8,128)S(1)} %bitcast.17, ...), custom_call_target="tpu_custom_call", output_to_operand_aliasing={{0}: (3, {}), {1}: (4, {}), {2}: (5, {}), {3}: (6, {})} | custom-call | flops 1384120320 | bytes 3899392 | tf_op jit(solution)/shard_map/features/pallas_call | solution.py:122
  75.3 2.9 %gram.2 = f32[16,5,16,256]{3,2,1,0:T(8,128)S(1)} custom-call(s32[9]{0:T(128)S(1)} %stack.39.s_ref, bf16[1024,512]{1,0:T(8,128)(2,1)S(1)} %get-tuple-element.44.ah, bf16[1024,512]{1,0:T(8,128)(2,1)S(1)} %get-tuple-element.45.al, bf16[1024,512]{1,0:T(8,128)(2,1)S(1)} %get-tuple-element.50.bh, bf16[1024,512]{1,0:T(8,128)(2,1)S(1)} %get-tuple-element.51.bl, ...), custom_call_target="tpu_custom_call" | custom-call | flops 2013265920 | bytes 8388608 | tf_op jit(solution)/shard_map/gram/pallas_call | solution.py:183
  78.3 5.1 %cross.4 = f32[4,1024,128]{2,1,0:T(8,128)S(1)} custom-call(s32[9]{0:T(128)S(1)} %stack.39.s_ref, f32[1024,2048]{1,0:T(8,128)S(1)} %bitcast.13, bf16[1024,1024]{1,0:T(8,128)(2,1)S(1)} %get-tuple-element.62.th, bf16[1024,1024]{1,0:T(8,128)(2,1)S(1)} %get-tuple-element.63.tl), custom_call_target="tpu_custom_call" | custom-call | flops 3221225472 | bytes 4194304 | tf_op jit(solution)/shard_map/cross/pallas_call | solution.py:223
  84.0 3.1 %gram.3 = f32[16,5,16,256]{3,2,1,0:T(8,128)S(1)} custom-call(s32[9]{0:T(128)S(1)} %stack.39.s_ref, bf16[1024,512]{1,0:T(8,128)(2,1)S(1)} %get-tuple-element.44.ah, bf16[1024,512]{1,0:T(8,128)(2,1)S(1)} %get-tuple-element.45.al, bf16[1024,512]{1,0:T(8,128)(2,1)S(1)} %get-tuple-element.50.bh, bf16[1024,512]{1,0:T(8,128)(2,1)S(1)} %get-tuple-element.51.bl, ...), custom_call_target="tpu_custom_call" | custom-call | flops 2013265920 | bytes 8388608 | tf_op jit(solution)/shard_map/gram/pallas_call | solution.py:183
  87.2 2.5 collective-permute-done.10
  89.9 5.1 %cross.5 = f32[4,1024,128]{2,1,0:T(8,128)S(1)} custom-call(s32[9]{0:T(128)S(1)} %stack.39.s_ref, f32[1024,2048]{1,0:T(8,128)S(1)} %bitcast.13, bf16[1024,1024]{1,0:T(8,128)(2,1)S(1)} %get-tuple-element.62.th, bf16[1024,1024]{1,0:T(8,128)(2,1)S(1)} %get-tuple-element.63.tl, f32[4,1024,128]{2,1,0:T(8,128)S(1)} %collective-permute-done.13.rest_0_), custom_call_target="tpu_custom_call" | custom-call | flops 3221225472 | bytes 4194304 | tf_op jit(solution)/shard_map/cross/pallas_call | solution.py:223
  95.0 5.1 %cross.6 = f32[4,1024,128]{2,1,0:T(8,128)S(1)} custom-call(s32[9]{0:T(128)S(1)} %stack.39.s_ref, f32[1024,2048]{1,0:T(8,128)S(1)} %bitcast.13, bf16[1024,1024]{1,0:T(8,128)(2,1)S(1)} %get-tuple-element.62.th, bf16[1024,1024]{1,0:T(8,128)(2,1)S(1)} %get-tuple-element.63.tl), custom_call_target="tpu_custom_call" | custom-call | flops 3221225472 | bytes 4194304 | tf_op jit(solution)/shard_map/cross/pallas_call | solution.py:223
  102.9 8.4 %collective-permute-done.11 = f32[8,5,16,256]{3,2,1,0:T(8,128)S(1)} collective-permute-done((f32[8,5,16,256]{3,2,1,0:T(8,128)S(1)}, f32[8,5,16,256]{3,2,1,0:T(8,128)S(1)}, u32[]{:S(2)}, u32[]{:S(2)}) %collective-permute-start.11) | collective-permute-done | bytes 655392 | tf_op jit(solution)/shard_map/ppermute | solution.py:517
  112.7 9.4 %collective-permute-done.12 = f32[4,5,16,256]{3,2,1,0:T(8,128)S(1)} collective-permute-done((f32[4,5,16,256]{3,2,1,0:T(8,128)S(1)}, f32[4,5,16,256]{3,2,1,0:T(8,128)S(1)}, u32[]{:S(2)}, u32[]{:S(2)}) %collective-permute-start.12) | collective-permute-done | bytes 327712 | tf_op jit(solution)/shard_map/ppermute | solution.py:517
  122.1 3.9 %collective-permute-done.32 = f32[2,1024,128]{2,1,0:T(8,128)S(1)} collective-permute-done((f32[2,1024,128]{2,1,0:T(8,128)S(1)}, f32[2,1024,128]{2,1,0:T(8,128)S(1)}, u32[]{:S(2)}, u32[]{:S(2)}) %collective-permute-start.32) | collective-permute-done | bytes 1048608 | tf_op jit(solution)/shard_map/ppermute | solution.py:517
  127.5 5.1 %cross.7 = f32[4,1024,128]{2,1,0:T(8,128)S(1)} custom-call(s32[9]{0:T(128)S(1)} %stack.39.s_ref, f32[1024,2048]{1,0:T(8,128)S(1)} %bitcast.13, bf16[1024,1024]{1,0:T(8,128)(2,1)S(1)} %get-tuple-element.62.th, bf16[1024,1024]{1,0:T(8,128)(2,1)S(1)} %get-tuple-element.63.tl, f32[4,1024,128]{2,1,0:T(8,128)S(1)} %collective-permute-done.14.rest_0_), custom_call_target="tpu_custom_call" | custom-call | flops 3221225472 | bytes 4194304 | tf_op jit(solution)/shard_map/cross/pallas_call | solution.py:223
  133.4 4.6 %collective-permute-done.15 = f32[2,5,16,256]{3,2,1,0:T(8,128)S(1)} collective-permute-done((f32[2,5,16,256]{3,2,1,0:T(8,128)S(1)}, f32[2,5,16,256]{3,2,1,0:T(8,128)S(1)}, u32[]{:S(2)}, u32[]{:S(2)}) %collective-permute-start.15) | collective-permute-done | bytes 163872 | tf_op jit(solution)/shard_map/ppermute | solution.py:517
  138.0 2.1 collective-permute-start.16
  143.8 2.7 collective-permute-start.17
  151.3 3.2 %collective-permute-start.35 = (f32[1,256,128]{2,1,0:T(8,128)S(1)}, f32[1,256,128]{2,1,0:T(8,128)S(1)}, u32[]{:S(2)}, u32[]{:S(2)}) collective-permute-start(f32[1,256,128]{2,1,0:T(8,128)S(1)} %slice.135), channel_id=1, source_target_pairs={{0,16},{1,17},{2,18},{3,19},{4,20},{5,21},{6,22},{7,23},{8,24},{9,... | collective-permute-start | bytes 393224 | tf_op jit(solution)/shard_map/ppermute | solution.py:517
  154.7 2.9 collective-permute-start.19
  157.5 3.1 %collective-permute-done.35 = f32[1,256,128]{2,1,0:T(8,128)S(1)} collective-permute-done((f32[1,256,128]{2,1,0:T(8,128)S(1)}, f32[1,256,128]{2,1,0:T(8,128)S(1)}, u32[]{:S(2)}, u32[]{:S(2)}) %collective-permute-start.35) | collective-permute-done | bytes 131104 | tf_op jit(solution)/shard_map/ppermute | solution.py:517
  162.6 5.9 %collective-permute-start.20 = (f32[8,5,16,256]{3,2,1,0:T(8,128)S(1)}, f32[8,5,16,256]{3,2,1,0:T(8,128)S(1)}, u32[]{:S(2)}, u32[]{:S(2)}) collective-permute-start(f32[8,5,16,256]{3,2,1,0:T(8,128)S(1)} %pad_maximum_fusion.2), channel_id=1, source_target_pairs={{0,2},{1,5},{2,0},{3,7},{4,6},{5,1},{6,4},{7,3},{8,10},{9,13},{10,... | collective-permute-start | bytes 1966088 | tf_op jit(solution)/shard_map/ppermute | solution.py:517
  168.6 3.1 %collective-permute-start.37 = (f32[1,512,128]{2,1,0:T(8,128)S(1)}, f32[1,512,128]{2,1,0:T(8,128)S(1)}, u32[]{:S(2)}, u32[]{:S(2)}) collective-permute-start(f32[1,512,128]{2,1,0:T(8,128)S(1)} %pad_maximum_fusion.8), channel_id=1, source_target_pairs={{0,8},{1,9},{2,10},{3,11},{4,12},{5,13},{6,14},{7,15},{8,0},{9,1},... | collective-permute-start | bytes 786440 | tf_op jit(solution)/shard_map/ppermute | solution.py:517
  172.0 8.4 %collective-permute-done.20 = f32[8,5,16,256]{3,2,1,0:T(8,128)S(1)} collective-permute-done((f32[8,5,16,256]{3,2,1,0:T(8,128)S(1)}, f32[8,5,16,256]{3,2,1,0:T(8,128)S(1)}, u32[]{:S(2)}, u32[]{:S(2)}) %collective-permute-start.20) | collective-permute-done | bytes 655392 | tf_op jit(solution)/shard_map/ppermute | solution.py:517
  180.4 7.5 %assemble.1 = (f32[512,512]{1,0:T(8,128)S(1)}, f32[256,512]{1,0:T(8,128)S(1)}) custom-call(s32[9]{0:T(128)S(1)} %stack.39.s_ref, f32[16,5,16,256]{3,2,1,0:T(8,128)S(1)} %constant_dynamic-update-slice_fusion.g_ref), custom_call_target="tpu_custom_call" | custom-call | flops 10000000000 | bytes 4000000 | tf_op jit(solution)/shard_map/assemble/pallas_call | solution.py:340
  187.9 6.5 %factor.3.m_ref = f32[512,512]{1,0:T(8,128)S(1)} custom-call(f32[512,512]{1,0:T(8,128)S(1)} %get-tuple-element.65.m_ref), custom_call_target="tpu_custom_call" | custom-call | flops 10000000000 | bytes 4000000 | tf_op jit(solution)/shard_map/factor/pallas_call | solution.py:362
  195.5 6.3 %factor.4.m_ref = f32[512,512]{1,0:T(8,128)S(1)} custom-call(f32[512,512]{1,0:T(8,128)S(1)} %factor.3.m_ref), custom_call_target="tpu_custom_call" | custom-call | flops 10000000000 | bytes 4000000 | tf_op jit(solution)/shard_map/factor/pallas_call | solution.py:362
  202.0 4.2 %collective-permute-start.26 = (f32[1,256,128]{2,1,0:T(8,128)S(1)}, f32[1,256,128]{2,1,0:T(8,128)S(1)}, u32[]{:S(2)}, u32[]{:S(2)}) collective-permute-start(f32[1,256,128]{2,1,0:T(8,128)S(1)} %slice.127), channel_id=1, source_target_pairs={{0,16},{1,17},{2,18},{3,19},{4,20},{5,21},{6,22},{7,23},{8,24},{9,... | collective-permute-start | bytes 393224 | tf_op jit(solution)/shard_map/ppermute | solution.py:517
  206.1 7.8 %factor.5.own_ref = f32[512,512]{1,0:T(8,128)S(1)} custom-call(f32[512,512]{1,0:T(8,128)S(1)} %factor.4.m_ref), custom_call_target="tpu_custom_call" | custom-call | flops 10000000000 | bytes 4000000 | tf_op jit(solution)/shard_map/factor/pallas_call | solution.py:362
  214.1 9.0 %collective-permute-done.27 = f32[1,256,128]{2,1,0:T(8,128)S(1)} collective-permute-done((f32[1,256,128]{2,1,0:T(8,128)S(1)}, f32[1,256,128]{2,1,0:T(8,128)S(1)}, u32[]{:S(2)}, u32[]{:S(2)}) %collective-permute-start.27) | collective-permute-done | bytes 131104 | tf_op jit(solution)/shard_map/ppermute | solution.py:517
  225.3 6.2 %collective-permute-done.28 = f32[1,512,128]{2,1,0:T(8,128)S(1)} collective-permute-done((f32[1,512,128]{2,1,0:T(8,128)S(1)}, f32[1,512,128]{2,1,0:T(8,128)S(1)}, u32[]{:S(2)}, u32[]{:S(2)}) %collective-permute-start.28) | collective-permute-done | bytes 262176 | tf_op jit(solution)/shard_map/ppermute | solution.py:517
  232.7 2.4 couple.1.b_ref
  235.1 4.3 %solve.3.wa_ref = f32[2,1024,128]{2,1,0:T(8,128)S(1)} custom-call(s32[9]{0:T(128)S(1)} %stack.39.s_ref, f32[512,512]{1,0:T(8,128)S(1)} %factor.5.own_ref, f32[512,512]{1,0:T(8,128)S(1)} %collective-permute-done.21.oth_ref, f32[512,512]{1,0:T(8,128)S(1)} %couple.1.b_ref, f32[2,1024,128]{2,1,0:T(8,128)S(1)} %pad_maximum_fusion.1.c_ref), custom_call_target="tpu_custom_call" | custom-call | flops 2415919104 | bytes 2097152 | tf_op jit(solution)/shard_map/solve/pallas_call | solution.py:434
  239.4 2.2 collective-permute-start.39
  241.8 4.3 %solve.2.wa_ref = f32[2,1024,128]{2,1,0:T(8,128)S(1)} custom-call(s32[9]{0:T(128)S(1)} %stack.39.s_ref, f32[512,512]{1,0:T(8,128)S(1)} %factor.5.own_ref, f32[512,512]{1,0:T(8,128)S(1)} %collective-permute-done.21.oth_ref, f32[512,512]{1,0:T(8,128)S(1)} %couple.1.b_ref, f32[2,1024,128]{2,1,0:T(8,128)S(1)} %pad_maximum_fusion.c_ref), custom_call_target="tpu_custom_call" | custom-call | flops 2415919104 | bytes 2097152 | tf_op jit(solution)/shard_map/solve/pallas_call | solution.py:434
  248.0 6.5 %collective-permute-done.39.wa_ref = f32[2,1024,128]{2,1,0:T(8,128)S(1)} collective-permute-done((f32[2,1024,128]{2,1,0:T(8,128)S(1)}, f32[2,1024,128]{2,1,0:T(8,128)S(1)}, u32[]{:S(2)}, u32[]{:S(2)}) %collective-permute-start.39) | collective-permute-done | bytes 1048608 | tf_op jit(solution)/shard_map/ppermute | solution.py:517
  254.5 11.2 %collective-permute-done.30.wa_ref = f32[2,1024,128]{2,1,0:T(8,128)S(1)} collective-permute-done((f32[2,1024,128]{2,1,0:T(8,128)S(1)}, f32[2,1024,128]{2,1,0:T(8,128)S(1)}, u32[]{:S(2)}, u32[]{:S(2)}) %collective-permute-start.30) | collective-permute-done | bytes 1048608 | tf_op jit(solution)/shard_map/ppermute | solution.py:517
  265.7 6.1 %residual.4 = (f32[1024,2048]{1,0:T(8,128)}, f32[2,512,2048]{2,1,0:T(8,128)}) custom-call(s32[9]{0:T(128)S(1)} %stack.39.s_ref, f32[1024,2048]{1,0:T(8,128)S(1)} %bitcast.13, bf16[1024,512]{1,0:T(8,128)(2,1)S(1)} %get-tuple-element.44.ah, bf16[1024,512]{1,0:T(8,128)(2,1)S(1)} %get-tuple-element.45.al, bf16[1024,512]{1,0:T(8,128)(2,1)S(1)} %get-tuple-element.50.bh, ...), custom_call_target="tpu_custom_call" | custom-call | flops 3221225472 | bytes 6291456 | tf_op jit(solution)/shard_map/residual/pallas_call | solution.py:481
  271.8 6.1 %residual.5 = (f32[1024,2048]{1,0:T(8,128)}, f32[2,512,2048]{2,1,0:T(8,128)}) custom-call(s32[9]{0:T(128)S(1)} %stack.39.s_ref, f32[1024,2048]{1,0:T(8,128)S(1)} %bitcast.13, bf16[1024,512]{1,0:T(8,128)(2,1)S(1)} %get-tuple-element.44.ah, bf16[1024,512]{1,0:T(8,128)(2,1)S(1)} %get-tuple-element.45.al, ...), custom_call_target="tpu_custom_call", output_to_operand_aliasing={{0}: (8, {}), {1}: (9, {})} | custom-call | flops 3221225472 | bytes 6291456 | tf_op jit(solution)/shard_map/residual/pallas_call | solution.py:481
  277.9 6.1 %residual.6 = (f32[1024,2048]{1,0:T(8,128)}, f32[2,512,2048]{2,1,0:T(8,128)}) custom-call(s32[9]{0:T(128)S(1)} %stack.39.s_ref, f32[1024,2048]{1,0:T(8,128)S(1)} %bitcast.13, bf16[1024,512]{1,0:T(8,128)(2,1)S(1)} %get-tuple-element.44.ah, bf16[1024,512]{1,0:T(8,128)(2,1)S(1)} %get-tuple-element.45.al, ...), custom_call_target="tpu_custom_call", output_to_operand_aliasing={{0}: (8, {}), {1}: (9, {})} | custom-call | flops 3221225472 | bytes 6291456 | tf_op jit(solution)/shard_map/residual/pallas_call | solution.py:481
  284.1 6.1 %residual.7 = (f32[1024,2048]{1,0:T(8,128)}, f32[2,512,2048]{2,1,0:T(8,128)}) custom-call(s32[9]{0:T(128)S(1)} %stack.39.s_ref, f32[1024,2048]{1,0:T(8,128)S(1)} %bitcast.13, bf16[1024,512]{1,0:T(8,128)(2,1)S(1)} %get-tuple-element.44.ah, bf16[1024,512]{1,0:T(8,128)(2,1)S(1)} %get-tuple-element.45.al, ...), custom_call_target="tpu_custom_call", output_to_operand_aliasing={{0}: (8, {}), {1}: (9, {})} | custom-call | flops 3221225472 | bytes 6291456 | tf_op jit(solution)/shard_map/residual/pallas_call | solution.py:481
  (119 shorter events, 38.1 us)
Async XLA Ops:
  0.6 2.9 collective-permute-start
  1.2 2.3 collective-permute-start.1
  3.5 1.2 copy-start.1
  4.7 0.7 copy-start.2
  7.1 47.9 %copy-start = (f32[1024,440]{0,1:T(8,128)S(1)}, f32[1024,440]{0,1:T(8,128)}, u32[]{:S(2)}) copy-start(f32[1024,440]{0,1:T(8,128)} %param.5) | copy-start | bytes 5406724
  7.1 9.4 %collective-permute-start.2 = (f32[2,448,128]{2,1,0:T(8,128)S(1)}, f32[2,448,128]{2,1,0:T(8,128)S(1)}, u32[]{:S(2)}, u32[]{:S(2)}) collective-permute-start(f32[2,448,128]{2,1,0:T(8,128)S(1)} %slice.113), channel_id=1, source_target_pairs={{0,2},{1,5},{2,0},{3,7},{4,6},{5,1},{6,4},{7,3},{8,10},{9,13},{10,... | collective-permute-start | bytes 1376264 | tf_op jit(solution)/shard_map/ppermute | solution.py:517
  16.6 6.1 %collective-permute-start.3 = (f32[1,448,128]{2,1,0:T(8,128)S(1)}, f32[1,448,128]{2,1,0:T(8,128)S(1)}, u32[]{:S(2)}, u32[]{:S(2)}) collective-permute-start(f32[1,448,128]{2,1,0:T(8,128)S(1)} %slice.115), channel_id=1, source_target_pairs={{0,4},{1,3},{2,6},{3,1},{4,0},{5,7},{6,2},{7,5},{8,12},{9,11},{10,... | collective-permute-start | bytes 688136 | tf_op jit(solution)/shard_map/ppermute | solution.py:517
  22.7 6.3 %collective-permute-start.4 = (f32[1,448,128]{2,1,0:T(8,128)S(1)}, f32[1,448,128]{2,1,0:T(8,128)S(1)}, u32[]{:S(2)}, u32[]{:S(2)}) collective-permute-start(f32[1,448,128]{2,1,0:T(8,128)S(1)} %slice_add_fusion.9), channel_id=1, source_target_pairs={{0,8},{1,9},{2,10},{3,11},{4,12},{5,13},{6,14},{7,15},{8,0},{9,1},... | collective-permute-start | bytes 688136 | tf_op jit(solution)/shard_map/ppermute | solution.py:517
  29.1 11.2 %collective-permute-start.5 = (f32[1,448,128]{2,1,0:T(8,128)S(1)}, f32[1,448,128]{2,1,0:T(8,128)S(1)}, u32[]{:S(2)}, u32[]{:S(2)}) collective-permute-start(f32[1,448,128]{2,1,0:T(8,128)S(1)} %add.109), channel_id=1, source_target_pairs={{0,16},{1,17},{2,18},{3,19},{4,20},{5,21},{6,22},{7,23},{8,24},{9,... | collective-permute-start | bytes 688136 | tf_op jit(solution)/shard_map/ppermute | solution.py:517
  40.3 6.1 %collective-permute-start.6 = (f32[1,448,128]{2,1,0:T(8,128)S(1)}, f32[1,448,128]{2,1,0:T(8,128)S(1)}, u32[]{:S(2)}, u32[]{:S(2)}) collective-permute-start(f32[1,448,128]{2,1,0:T(8,128)S(1)} %add.110), channel_id=1, source_target_pairs={{0,4},{1,3},{2,6},{3,1},{4,0},{5,7},{6,2},{7,5},{8,12},{9,11},{10,... | collective-permute-start | bytes 688136 | tf_op jit(solution)/shard_map/ppermute | solution.py:517
  46.5 8.5 %collective-permute-start.7 = (f32[2,448,128]{2,1,0:T(8,128)S(1)}, f32[2,448,128]{2,1,0:T(8,128)S(1)}, u32[]{:S(2)}, u32[]{:S(2)}) collective-permute-start(f32[2,448,128]{2,1,0:T(8,128)S(1)} %pad_maximum_fusion.5.p_ref), channel_id=1, source_target_pairs={{0,2},{1,5},{2,0},{3,7},{4,6},{5,1},{6,4},{7,3},{8,10},{9,13},{10,... | collective-permute-start | bytes 1376264 | tf_op jit(solution)/shard_map/ppermute | solution.py:517
  47.7 12.4 %collective-permute-start.8 = (f32[2,448,128]{2,1,0:T(8,128)S(1)}, f32[2,448,128]{2,1,0:T(8,128)S(1)}, u32[]{:S(2)}, u32[]{:S(2)}) collective-permute-start(f32[2,448,128]{2,1,0:T(8,128)S(1)} %pad_maximum_fusion.5.p_ref), channel_id=1, source_target_pairs={{0,1},{1,0},{2,3},{3,2},{4,5},{5,4},{6,7},{7,6},{8,9},{9,8},{10,11... | collective-permute-start | bytes 1376264 | tf_op jit(solution)/shard_map/ppermute | solution.py:517
  55.0 15.2 %collective-permute-start.9 = (f32[2,448,128]{2,1,0:T(8,128)S(1)}, f32[2,448,128]{2,1,0:T(8,128)S(1)}, u32[]{:S(2)}, u32[]{:S(2)}) collective-permute-start(f32[2,448,128]{2,1,0:T(8,128)S(1)} %collective-permute-done.7.p_ref), channel_id=1, source_target_pairs={{0,1},{1,0},{2,3},{3,2},{4,5},{5,4},{6,7},{7,6},{8,9},{9,8},{10,11... | collective-permute-start | bytes 1376264 | tf_op jit(solution)/shard_map/ppermute | solution.py:517
  70.2 8.0 %slice-start = ((s8[8388608]{0:T(1024)(128)(4,1)}), s8[4194304]{0:T(1024)(128)(4,1)S(1)}, s32[]{:S(2)}) async-start(s8[8388608]{0:T(1024)(128)(4,1)} %bitcast.12), calls=%async_computation | async-start | bytes 8388608
  75.3 3.0 %slice-start.1 = ((s8[8388608]{0:T(1024)(128)(4,1)}), s8[4194304]{0:T(1024)(128)(4,1)S(1)}, s32[]{:S(2)}) async-start(s8[8388608]{0:T(1024)(128)(4,1)} %bitcast.12), calls=%async_computation.1 | async-start | bytes 8388608
  83.4 6.5 %collective-permute-start.13 = (f32[4,1024,128]{2,1,0:T(8,128)S(1)}, f32[4,1024,128]{2,1,0:T(8,128)S(1)}, u32[]{:S(2)}, u32[]{:S(2)}) collective-permute-start(f32[4,1024,128]{2,1,0:T(8,128)S(1)} %cross.4), channel_id=1, source_target_pairs={{0,1},{1,0},{2,3},{3,2},{4,5},{5,4},{6,7},{7,6},{8,9},{9,8},{10,11... | collective-permute-start | bytes 6291464 | tf_op jit(solution)/shard_map/ppermute | solution.py:517
  84.0 5.7 %collective-permute-start.10 = (f32[16,5,16,256]{3,2,1,0:T(8,128)S(1)}, f32[16,5,16,256]{3,2,1,0:T(8,128)S(1)}, u32[]{:S(2)}, u32[]{:S(2)}) collective-permute-start(f32[16,5,16,256]{3,2,1,0:T(8,128)S(1)} %gram.2), channel_id=1, source_target_pairs={{0,1},{1,0},{2,3},{3,2},{4,5},{5,4},{6,7},{7,6},{8,9},{9,8},{10,11... | collective-permute-start | bytes 3932168 | tf_op jit(solution)/shard_map/ppermute | solution.py:517
  100.2 27.3 %collective-permute-start.14 = (f32[4,1024,128]{2,1,0:T(8,128)S(1)}, f32[4,1024,128]{2,1,0:T(8,128)S(1)}, u32[]{:S(2)}, u32[]{:S(2)}) collective-permute-start(f32[4,1024,128]{2,1,0:T(8,128)S(1)} %cross.6), channel_id=1, source_target_pairs={{0,1},{1,0},{2,3},{3,2},{4,5},{5,4},{6,7},{7,6},{8,9},{9,8},{10,11... | collective-permute-start | bytes 6291464 | tf_op jit(solution)/shard_map/ppermute | solution.py:517
  100.7 10.7 %collective-permute-start.11 = (f32[8,5,16,256]{3,2,1,0:T(8,128)S(1)}, f32[8,5,16,256]{3,2,1,0:T(8,128)S(1)}, u32[]{:S(2)}, u32[]{:S(2)}) collective-permute-start(f32[8,5,16,256]{3,2,1,0:T(8,128)S(1)} %slice.117), channel_id=1, source_target_pairs={{0,2},{1,5},{2,0},{3,7},{4,6},{5,1},{6,4},{7,3},{8,10},{9,13},{10,... | collective-permute-start | bytes 1966088 | tf_op jit(solution)/shard_map/ppermute | solution.py:517
  102.0 24.1 %collective-permute-start.32 = (f32[2,1024,128]{2,1,0:T(8,128)S(1)}, f32[2,1024,128]{2,1,0:T(8,128)S(1)}, u32[]{:S(2)}, u32[]{:S(2)}) collective-permute-start(f32[2,1024,128]{2,1,0:T(8,128)S(1)} %slice.129), channel_id=1, source_target_pairs={{0,2},{1,5},{2,0},{3,7},{4,6},{5,1},{6,4},{7,3},{8,10},{9,13},{10,... | collective-permute-start | bytes 3145736 | tf_op jit(solution)/shard_map/ppermute | solution.py:517
  111.4 10.6 %collective-permute-start.12 = (f32[4,5,16,256]{3,2,1,0:T(8,128)S(1)}, f32[4,5,16,256]{3,2,1,0:T(8,128)S(1)}, u32[]{:S(2)}, u32[]{:S(2)}) collective-permute-start(f32[4,5,16,256]{3,2,1,0:T(8,128)S(1)} %slice.119), channel_id=1, source_target_pairs={{0,4},{1,3},{2,6},{3,1},{4,0},{5,7},{6,2},{7,5},{8,12},{9,11},{10,... | collective-permute-start | bytes 983048 | tf_op jit(solution)/shard_map/ppermute | solution.py:517
  126.2 14.0 %collective-permute-start.33 = (f32[1,1024,128]{2,1,0:T(8,128)S(1)}, f32[1,1024,128]{2,1,0:T(8,128)S(1)}, u32[]{:S(2)}, u32[]{:S(2)}) collective-permute-start(f32[1,1024,128]{2,1,0:T(8,128)S(1)} %slice.131), channel_id=1, source_target_pairs={{0,4},{1,3},{2,6},{3,1},{4,0},{5,7},{6,2},{7,5},{8,12},{9,11},{10,... | collective-permute-start | bytes 1572872 | tf_op jit(solution)/shard_map/ppermute | solution.py:517
  132.6 5.4 %collective-permute-start.15 = (f32[2,5,16,256]{3,2,1,0:T(8,128)S(1)}, f32[2,5,16,256]{3,2,1,0:T(8,128)S(1)}, u32[]{:S(2)}, u32[]{:S(2)}) collective-permute-start(f32[2,5,16,256]{3,2,1,0:T(8,128)S(1)} %slice.93), channel_id=1, source_target_pairs={{0,8},{1,9},{2,10},{3,11},{4,12},{5,13},{6,14},{7,15},{8,0},{9,1},... | collective-permute-start | bytes 491528 | tf_op jit(solution)/shard_map/ppermute | solution.py:517
  138.0 5.7 %collective-permute-start.16 = (f32[1,5,16,256]{3,2,1,0:T(8,128)S(1)}, f32[1,5,16,256]{3,2,1,0:T(8,128)S(1)}, u32[]{:S(2)}, u32[]{:S(2)}) collective-permute-start(f32[1,5,16,256]{3,2,1,0:T(8,128)S(1)} %slice.121), channel_id=1, source_target_pairs={{0,16},{1,17},{2,18},{3,19},{4,20},{5,21},{6,22},{7,23},{8,24},{9,... | collective-permute-start | bytes 245768 | tf_op jit(solution)/shard_map/ppermute | solution.py:517
  140.3 11.0 %collective-permute-start.34 = (f32[1,512,128]{2,1,0:T(8,128)S(1)}, f32[1,512,128]{2,1,0:T(8,128)S(1)}, u32[]{:S(2)}, u32[]{:S(2)}) collective-permute-start(f32[1,512,128]{2,1,0:T(8,128)S(1)} %slice.133), channel_id=1, source_target_pairs={{0,8},{1,9},{2,10},{3,11},{4,12},{5,13},{6,14},{7,15},{8,0},{9,1},... | collective-permute-start | bytes 786440 | tf_op jit(solution)/shard_map/ppermute | solution.py:517
  143.8 5.5 %collective-permute-start.17 = (f32[1,5,16,256]{3,2,1,0:T(8,128)S(1)}, f32[1,5,16,256]{3,2,1,0:T(8,128)S(1)}, u32[]{:S(2)}, u32[]{:S(2)}) collective-permute-start(f32[1,5,16,256]{3,2,1,0:T(8,128)S(1)} %get-tuple-element.75), channel_id=1, source_target_pairs={{0,16},{1,17},{2,18},{3,19},{4,20},{5,21},{6,22},{7,23},{8,24},{9,... | collective-permute-start | bytes 245768 | tf_op jit(solution)/shard_map/ppermute | solution.py:517
  146.6 25.2 %collective-permute-start.23 = (f32[2,1024,128]{2,1,0:T(8,128)S(1)}, f32[2,1024,128]{2,1,0:T(8,128)S(1)}, u32[]{:S(2)}, u32[]{:S(2)}) collective-permute-start(f32[2,1024,128]{2,1,0:T(8,128)S(1)} %slice.97), channel_id=1, source_target_pairs={{0,2},{1,5},{2,0},{3,7},{4,6},{5,1},{6,4},{7,3},{8,10},{9,13},{10,... | collective-permute-start | bytes 3145736 | tf_op jit(solution)/shard_map/ppermute | solution.py:517
  149.3 5.4 %collective-permute-start.18 = (f32[2,5,16,256]{3,2,1,0:T(8,128)S(1)}, f32[2,5,16,256]{3,2,1,0:T(8,128)S(1)}, u32[]{:S(2)}, u32[]{:S(2)}) collective-permute-start(f32[2,5,16,256]{3,2,1,0:T(8,128)S(1)} %pad_maximum_fusion.9), channel_id=1, source_target_pairs={{0,8},{1,9},{2,10},{3,11},{4,12},{5,13},{6,14},{7,15},{8,0},{9,1},... | collective-permute-start | bytes 491528 | tf_op jit(solution)/shard_map/ppermute | solution.py:517
  151.3 9.3 %collective-permute-start.35 = (f32[1,256,128]{2,1,0:T(8,128)S(1)}, f32[1,256,128]{2,1,0:T(8,128)S(1)}, u32[]{:S(2)}, u32[]{:S(2)}) collective-permute-start(f32[1,256,128]{2,1,0:T(8,128)S(1)} %slice.135), channel_id=1, source_target_pairs={{0,16},{1,17},{2,18},{3,19},{4,20},{5,21},{6,22},{7,23},{8,24},{9,... | collective-permute-start | bytes 393224 | tf_op jit(solution)/shard_map/ppermute | solution.py:517
  154.7 7.9 %collective-permute-start.19 = (f32[4,5,16,256]{3,2,1,0:T(8,128)S(1)}, f32[4,5,16,256]{3,2,1,0:T(8,128)S(1)}, u32[]{:S(2)}, u32[]{:S(2)}) collective-permute-start(f32[4,5,16,256]{3,2,1,0:T(8,128)S(1)} %pad_maximum_fusion.6), channel_id=1, source_target_pairs={{0,4},{1,3},{2,6},{3,1},{4,0},{5,7},{6,2},{7,5},{8,12},{9,11},{10,... | collective-permute-start | bytes 983048 | tf_op jit(solution)/shard_map/ppermute | solution.py:517
  160.6 7.9 %collective-permute-start.36 = (f32[1,256,128]{2,1,0:T(8,128)S(1)}, f32[1,256,128]{2,1,0:T(8,128)S(1)}, u32[]{:S(2)}, u32[]{:S(2)}) collective-permute-start(f32[1,256,128]{2,1,0:T(8,128)S(1)} %slice_add_fusion.11), channel_id=1, source_target_pairs={{0,16},{1,17},{2,18},{3,19},{4,20},{5,21},{6,22},{7,23},{8,24},{9,... | collective-permute-start | bytes 393224 | tf_op jit(solution)/shard_map/ppermute | solution.py:517
  162.6 17.8 %collective-permute-start.20 = (f32[8,5,16,256]{3,2,1,0:T(8,128)S(1)}, f32[8,5,16,256]{3,2,1,0:T(8,128)S(1)}, u32[]{:S(2)}, u32[]{:S(2)}) collective-permute-start(f32[8,5,16,256]{3,2,1,0:T(8,128)S(1)} %pad_maximum_fusion.2), channel_id=1, source_target_pairs={{0,2},{1,5},{2,0},{3,7},{4,6},{5,1},{6,4},{7,3},{8,10},{9,13},{10,... | collective-permute-start | bytes 1966088 | tf_op jit(solution)/shard_map/ppermute | solution.py:517
  168.6 54.7 %collective-permute-start.37 = (f32[1,512,128]{2,1,0:T(8,128)S(1)}, f32[1,512,128]{2,1,0:T(8,128)S(1)}, u32[]{:S(2)}, u32[]{:S(2)}) collective-permute-start(f32[1,512,128]{2,1,0:T(8,128)S(1)} %pad_maximum_fusion.8), channel_id=1, source_target_pairs={{0,8},{1,9},{2,10},{3,11},{4,12},{5,13},{6,14},{7,15},{8,0},{9,1},... | collective-permute-start | bytes 786440 | tf_op jit(solution)/shard_map/ppermute | solution.py:517
  171.9 22.6 %collective-permute-start.24 = (f32[1,1024,128]{2,1,0:T(8,128)S(1)}, f32[1,1024,128]{2,1,0:T(8,128)S(1)}, u32[]{:S(2)}, u32[]{:S(2)}) collective-permute-start(f32[1,1024,128]{2,1,0:T(8,128)S(1)} %slice.123), channel_id=1, source_target_pairs={{0,4},{1,3},{2,6},{3,1},{4,0},{5,7},{6,2},{7,5},{8,12},{9,11},{10,... | collective-permute-start | bytes 1572872 | tf_op jit(solution)/shard_map/ppermute | solution.py:517
  194.6 7.4 %collective-permute-start.25 = (f32[1,512,128]{2,1,0:T(8,128)S(1)}, f32[1,512,128]{2,1,0:T(8,128)S(1)}, u32[]{:S(2)}, u32[]{:S(2)}) collective-permute-start(f32[1,512,128]{2,1,0:T(8,128)S(1)} %slice.125), channel_id=1, source_target_pairs={{0,8},{1,9},{2,10},{3,11},{4,12},{5,13},{6,14},{7,15},{8,0},{9,1},... | collective-permute-start | bytes 786440 | tf_op jit(solution)/shard_map/ppermute | solution.py:517
  202.0 12.0 %collective-permute-start.26 = (f32[1,256,128]{2,1,0:T(8,128)S(1)}, f32[1,256,128]{2,1,0:T(8,128)S(1)}, u32[]{:S(2)}, u32[]{:S(2)}) collective-permute-start(f32[1,256,128]{2,1,0:T(8,128)S(1)} %slice.127), channel_id=1, source_target_pairs={{0,16},{1,17},{2,18},{3,19},{4,20},{5,21},{6,22},{7,23},{8,24},{9,... | collective-permute-start | bytes 393224 | tf_op jit(solution)/shard_map/ppermute | solution.py:517
  213.9 18.7 %collective-permute-start.21 = (f32[512,512]{1,0:T(8,128)S(1)}, f32[512,512]{1,0:T(8,128)S(1)}, u32[]{:S(2)}, u32[]{:S(2)}) collective-permute-start(f32[512,512]{1,0:T(8,128)S(1)} %factor.5.own_ref), channel_id=1, source_target_pairs={{0,1},{1,0},{2,3},{3,2},{4,5},{5,4},{6,7},{7,6},{8,9},{9,8},{10,11... | collective-permute-start | bytes 3145736 | tf_op jit(solution)/shard_map/ppermute | solution.py:517
  214.0 9.1 %collective-permute-start.27 = (f32[1,256,128]{2,1,0:T(8,128)S(1)}, f32[1,256,128]{2,1,0:T(8,128)S(1)}, u32[]{:S(2)}, u32[]{:S(2)}) collective-permute-start(f32[1,256,128]{2,1,0:T(8,128)S(1)} %slice_add_fusion.12), channel_id=1, source_target_pairs={{0,16},{1,17},{2,18},{3,19},{4,20},{5,21},{6,22},{7,23},{8,24},{9,... | collective-permute-start | bytes 393224 | tf_op jit(solution)/shard_map/ppermute | solution.py:517
  223.2 8.3 %collective-permute-start.28 = (f32[1,512,128]{2,1,0:T(8,128)S(1)}, f32[1,512,128]{2,1,0:T(8,128)S(1)}, u32[]{:S(2)}, u32[]{:S(2)}) collective-permute-start(f32[1,512,128]{2,1,0:T(8,128)S(1)} %pad_maximum_fusion.7), channel_id=1, source_target_pairs={{0,8},{1,9},{2,10},{3,11},{4,12},{5,13},{6,14},{7,15},{8,0},{9,1},... | collective-permute-start | bytes 786440 | tf_op jit(solution)/shard_map/ppermute | solution.py:517
  223.3 9.2 %collective-permute-start.38 = (f32[1,1024,128]{2,1,0:T(8,128)S(1)}, f32[1,1024,128]{2,1,0:T(8,128)S(1)}, u32[]{:S(2)}, u32[]{:S(2)}) collective-permute-start(f32[1,1024,128]{2,1,0:T(8,128)S(1)} %pad_maximum_fusion.4), channel_id=1, source_target_pairs={{0,4},{1,3},{2,6},{3,1},{4,0},{5,7},{6,2},{7,5},{8,12},{9,11},{10,... | collective-permute-start | bytes 1572872 | tf_op jit(solution)/shard_map/ppermute | solution.py:517
  223.4 9.2 %collective-permute-start.22 = (f32[256,512]{1,0:T(8,128)S(1)}, f32[256,512]{1,0:T(8,128)S(1)}, u32[]{:S(2)}, u32[]{:S(2)}) collective-permute-start(f32[256,512]{1,0:T(8,128)S(1)} %get-tuple-element.66.gown_ref), channel_id=1, source_target_pairs={{0,1},{1,0},{2,3},{3,2},{4,5},{5,4},{6,7},{7,6},{8,9},{9,8},{10,11... | collective-permute-start | bytes 1572872 | tf_op jit(solution)/shard_map/ppermute | solution.py:517
  231.6 10.1 %collective-permute-start.29 = (f32[1,1024,128]{2,1,0:T(8,128)S(1)}, f32[1,1024,128]{2,1,0:T(8,128)S(1)}, u32[]{:S(2)}, u32[]{:S(2)}) collective-permute-start(f32[1,1024,128]{2,1,0:T(8,128)S(1)} %pad_maximum_fusion.3), channel_id=1, source_target_pairs={{0,4},{1,3},{2,6},{3,1},{4,0},{5,7},{6,2},{7,5},{8,12},{9,11},{10,... | collective-permute-start | bytes 1572872 | tf_op jit(solution)/shard_map/ppermute | solution.py:517
  239.4 15.0 %collective-permute-start.39 = (f32[2,1024,128]{2,1,0:T(8,128)S(1)}, f32[2,1024,128]{2,1,0:T(8,128)S(1)}, u32[]{:S(2)}, u32[]{:S(2)}) collective-permute-start(f32[2,1024,128]{2,1,0:T(8,128)S(1)} %solve.3.wa_ref), channel_id=1, source_target_pairs={{0,2},{1,5},{2,0},{3,7},{4,6},{5,1},{6,4},{7,3},{8,10},{9,13},{10,... | collective-permute-start | bytes 3145736 | tf_op jit(solution)/shard_map/ppermute | solution.py:517
  246.1 19.6 %collective-permute-start.30 = (f32[2,1024,128]{2,1,0:T(8,128)S(1)}, f32[2,1024,128]{2,1,0:T(8,128)S(1)}, u32[]{:S(2)}, u32[]{:S(2)}) collective-permute-start(f32[2,1024,128]{2,1,0:T(8,128)S(1)} %solve.2.wa_ref), channel_id=1, source_target_pairs={{0,2},{1,5},{2,0},{3,7},{4,6},{5,1},{6,4},{7,3},{8,10},{9,13},{10,... | collective-permute-start | bytes 3145736 | tf_op jit(solution)/shard_map/ppermute | solution.py:517
  247.5 18.2 %collective-permute-start.42 = (f32[2,1024,128]{2,1,0:T(8,128)S(1)}, f32[2,1024,128]{2,1,0:T(8,128)S(1)}, u32[]{:S(2)}, u32[]{:S(2)}) collective-permute-start(f32[2,1024,128]{2,1,0:T(8,128)S(1)} %solve.3.wa_ref), channel_id=1, source_target_pairs={{0,1},{1,0},{2,3},{3,2},{4,5},{5,4},{6,7},{7,6},{8,9},{9,8},{10,11... | collective-permute-start | bytes 3145736 | tf_op jit(solution)/shard_map/ppermute | solution.py:517
  247.5 24.4 %collective-permute-start.41 = (f32[2,1024,128]{2,1,0:T(8,128)S(1)}, f32[2,1024,128]{2,1,0:T(8,128)S(1)}, u32[]{:S(2)}, u32[]{:S(2)}) collective-permute-start(f32[2,1024,128]{2,1,0:T(8,128)S(1)} %solve.2.wa_ref), channel_id=1, source_target_pairs={{0,1},{1,0},{2,3},{3,2},{4,5},{5,4},{6,7},{7,6},{8,9},{9,8},{10,11... | collective-permute-start | bytes 3145736 | tf_op jit(solution)/shard_map/ppermute | solution.py:517
  254.5 23.5 %collective-permute-start.40 = (f32[2,1024,128]{2,1,0:T(8,128)S(1)}, f32[2,1024,128]{2,1,0:T(8,128)S(1)}, u32[]{:S(2)}, u32[]{:S(2)}) collective-permute-start(f32[2,1024,128]{2,1,0:T(8,128)S(1)} %collective-permute-done.39.wa_ref), channel_id=1, source_target_pairs={{0,1},{1,0},{2,3},{3,2},{4,5},{5,4},{6,7},{7,6},{8,9},{9,8},{10,11... | collective-permute-start | bytes 3145736 | tf_op jit(solution)/shard_map/ppermute | solution.py:517
  265.7 18.4 %collective-permute-start.31 = (f32[2,1024,128]{2,1,0:T(8,128)S(1)}, f32[2,1024,128]{2,1,0:T(8,128)S(1)}, u32[]{:S(2)}, u32[]{:S(2)}) collective-permute-start(f32[2,1024,128]{2,1,0:T(8,128)S(1)} %collective-permute-done.30.wa_ref), channel_id=1, source_target_pairs={{0,1},{1,0},{2,3},{3,2},{4,5},{5,4},{6,7},{7,6},{8,9},{9,8},{10,11... | collective-permute-start | bytes 3145736 | tf_op jit(solution)/shard_map/ppermute | solution.py:517
  (1 other events, 0.7 us)

commit v5 on v4

--- a/solution.py
+++ b/solution.py
@@ -96,44 +96,41 @@
     )(scalars, block_order, own, oth, phase_own[:, None, :], phase_oth[:, None, :])
 
 
-def features_kernel(quarter, s_ref, x_ref, p_ref, *rest):
+def features_kernel(quarter, slot, part, s_ref, x_ref, p_ref, *rest):
     fh_ref, fl_ref, th_ref, tl_ref = rest[-4:]
-    depth = x_ref.shape[0]
-    swap = s_ref[quarter] & 1
+    depth, rows = x_ref.shape
+    swap, pair = s_ref[quarter] & 1, part ^ (s_ref[quarter] >> 1)
     turned = jnp.concatenate([p_ref[i ^ swap] for i in range(2)], axis=1).T
-    inner = dot_full(turned[:, :depth], x_ref[...]) + turned[:, depth : depth + 1]
-    feats = math.sqrt(1.0 / turned.shape[0]) * cosine(inner)
-    th_ref[...], tl_ref[...] = split(feats)
-    fh_ref[...], fl_ref[...] = split(feats.T)
+    half = turned.shape[0]
+    weights, phase = turned[:, :depth], turned[:, depth : depth + 1]
+    across = pl.ds(pl.multiple_of(pair * half, half), half)
+    down = pl.ds(pl.multiple_of((2 * slot + pair) * half, half), half)
+    tile = 256
+
+    def body(i, carry):
+        at = pl.ds(pl.multiple_of(i * tile, tile), tile)
+        feats = math.sqrt(1.0 / half) * cosine(dot_full(weights, x_ref[:, at]) + phase)
+        th_ref[down, at], tl_ref[down, at] = split(feats)
+        fh_ref[at, across], fl_ref[at, across] = split(feats.T)
+        return carry
+
+    lax.fori_loop(0, rows // tile, body, 0)
 
 
 def features(quarter, slot, part, scalars, frames_turned, blocks, flat=(), stacked=()):
     depth, rows = frames_turned.shape
     half = blocks.shape[0] * blocks.shape[2]
-    tile = 256
     before = tuple(flat) + tuple(stacked)
     n_flat = len(flat)
     aliases = {3 + k: k for k in range(n_flat)}
     aliases.update({3 + n_flat + k: 2 + k for k in range(len(stacked))})
-
-    def pair(s):
-        return part ^ (s[quarter] >> 1)
-
-    return pl.pallas_call(
-        functools.partial(features_kernel, quarter),
+    whole = pl.BlockSpec(memory_space=pltpu.VMEM)
+    return pl.pallas_call(
+        functools.partial(features_kernel, quarter, slot, part),
         out_shape=[jax.ShapeDtypeStruct((rows, 2 * half), BF16)] * 2
         + [jax.ShapeDtypeStruct((4 * half, rows), BF16)] * 2,
-        grid_spec=pltpu.PrefetchScalarGridSpec(
-            num_scalar_prefetch=1,
-            grid=(rows // tile,),
-            in_specs=[
-                pl.BlockSpec((depth, tile), lambda i, s: (0, i)),
-                pl.BlockSpec(blocks.shape, lambda i, s: (0, 0, 0)),
-            ]
-            + [pl.BlockSpec(memory_space=pl.ANY)] * len(before),
-            out_specs=[pl.BlockSpec((tile, half), lambda i, s: (i, pair(s)))] * 2
-            + [pl.BlockSpec((half, tile), lambda i, s: (2 * slot + pair(s), i))] * 2,
-        ),
+        in_specs=[pl.BlockSpec(memory_space=pltpu.SMEM)] + [whole] * (2 + len(before)),
+        out_specs=[whole] * 4,
         input_output_aliases=aliases,
         compiler_params=params(),
         cost_estimate=cost(12 * rows * depth * half, 4 * rows * depth + 8 * rows * half),

time: 291 us -> 288 us (0.990)
  no operation moved by 1% of the time
where the time goes in v5:
time: 288 us
  waiting for transfers between devices  115 us (40%)
  Pallas kernels  109 us (38%)
  starting transfers between devices  57.7 us (20%)
  local copies, waits for them, and re-layouts  3.11 us (1%)
    ppermute x43, waiting for transfers between devices, exchange(): return lax.ppermute(value, ALL, pairs)  115 us
    ppermute x43, starting transfers between devices, exchange(): return lax.ppermute(value, ALL, pairs)  57.7 us
    pallas_call x4, Pallas kernels, residual_part(): pl.pallas_call(residual_kernel, out_shape=[jax.ShapeDtypeStruct((rows, co...  24.5 us
    pallas_call x3, Pallas kernels, factor(): pl.pallas_call(functools.partial(factor_kernel, step), out_shape=jax.Shap...  20.6 us
    pallas_call x4, Pallas kernels, cross(): pl.pallas_call(functools.partial(cross_kernel, base), out_shape=jax.Shape...  20.5 us
    pallas_call x4, Pallas kernels, features(): pl.pallas_call(functools.partial(features_kernel, quarter, slot, part), o...  18.2 us
    pallas_call x2, Pallas kernels, solve(): pl.pallas_call(solve_kernel, out_shape=jax.ShapeDtypeStruct(crossed.shape...  8.69 us
    pallas_call x1, Pallas kernels, assemble(): pl.pallas_call(assemble_kernel, out_shape=[jax.ShapeDtypeStruct((2 * half...  7.47 us
  transfers between devices with their start and end apart: 43, of which 24 were waited for; matrix products, arithmetic and copies ran while one was open for 1% of the time, Pallas kernels for 28%

profile of v5, /device:TPU:0, one launch (start us, length us, event | category | flops | bytes accessed | tf_op | source)
XLA Modules:
  0.0 288.1 jit_solution(17137482192413069403)
XLA Ops:
  7.1 2.9 %collective-permute-start.2 = (f32[2,448,128]{2,1,0:T(8,128)S(1)}, f32[2,448,128]{2,1,0:T(8,128)S(1)}, u32[]{:S(2)}, u32[]{:S(2)}) collective-permute-start(f32[2,448,128]{2,1,0:T(8,128)S(1)} %slice.113), channel_id=1, source_target_pairs={{0,2},{1,5},{2,0},{3,7},{4,6},{5,1},{6,4},{7,3},{8,10},{9,13},{10,... | collective-permute-start | bytes 1376264 | tf_op jit(solution)/shard_map/ppermute | solution.py:514
  10.0 6.5 %collective-permute-done.2 = f32[2,448,128]{2,1,0:T(8,128)S(1)} collective-permute-done((f32[2,448,128]{2,1,0:T(8,128)S(1)}, f32[2,448,128]{2,1,0:T(8,128)S(1)}, u32[]{:S(2)}, u32[]{:S(2)}) %collective-permute-start.2) | collective-permute-done | bytes 458784 | tf_op jit(solution)/shard_map/ppermute | solution.py:514
  18.7 4.0 %collective-permute-done.3 = f32[1,448,128]{2,1,0:T(8,128)S(1)} collective-permute-done((f32[1,448,128]{2,1,0:T(8,128)S(1)}, f32[1,448,128]{2,1,0:T(8,128)S(1)}, u32[]{:S(2)}, u32[]{:S(2)}) %collective-permute-start.3) | collective-permute-done | bytes 229408 | tf_op jit(solution)/shard_map/ppermute | solution.py:514
  22.7 2.1 collective-permute-start.4
  24.9 4.2 %collective-permute-done.4 = f32[1,448,128]{2,1,0:T(8,128)S(1)} collective-permute-done((f32[1,448,128]{2,1,0:T(8,128)S(1)}, f32[1,448,128]{2,1,0:T(8,128)S(1)}, u32[]{:S(2)}, u32[]{:S(2)}) %collective-permute-start.4) | collective-permute-done | bytes 229408 | tf_op jit(solution)/shard_map/ppermute | solution.py:514
  29.1 3.1 %collective-permute-start.5 = (f32[1,448,128]{2,1,0:T(8,128)S(1)}, f32[1,448,128]{2,1,0:T(8,128)S(1)}, u32[]{:S(2)}, u32[]{:S(2)}) collective-permute-start(f32[1,448,128]{2,1,0:T(8,128)S(1)} %add.109), channel_id=1, source_target_pairs={{0,16},{1,17},{2,18},{3,19},{4,20},{5,21},{6,22},{7,23},{8,24},{9,... | collective-permute-start | bytes 688136 | tf_op jit(solution)/shard_map/ppermute | solution.py:514
  32.1 8.2 %collective-permute-done.5 = f32[1,448,128]{2,1,0:T(8,128)S(1)} collective-permute-done((f32[1,448,128]{2,1,0:T(8,128)S(1)}, f32[1,448,128]{2,1,0:T(8,128)S(1)}, u32[]{:S(2)}, u32[]{:S(2)}) %collective-permute-start.5) | collective-permute-done | bytes 229408 | tf_op jit(solution)/shard_map/ppermute | solution.py:514
  41.6 4.8 %collective-permute-done.6 = f32[1,448,128]{2,1,0:T(8,128)S(1)} collective-permute-done((f32[1,448,128]{2,1,0:T(8,128)S(1)}, f32[1,448,128]{2,1,0:T(8,128)S(1)}, u32[]{:S(2)}, u32[]{:S(2)}) %collective-permute-start.6) | collective-permute-done | bytes 229408 | tf_op jit(solution)/shard_map/ppermute | solution.py:514
  47.7 7.3 %collective-permute-done.7.p_ref = f32[2,448,128]{2,1,0:T(8,128)S(1)} collective-permute-done((f32[2,448,128]{2,1,0:T(8,128)S(1)}, f32[2,448,128]{2,1,0:T(8,128)S(1)}, u32[]{:S(2)}, u32[]{:S(2)}) %collective-permute-start.7) | collective-permute-done | bytes 458784 | tf_op jit(solution)/shard_map/ppermute | solution.py:514
  55.0 4.5 %features.4 = (bf16[1024,512]{1,0:T(8,128)(2,1)S(1)}, bf16[1024,512]{1,0:T(8,128)(2,1)S(1)}, bf16[1024,1024]{1,0:T(8,128)(2,1)S(1)}, bf16[1024,1024]{1,0:T(8,128)(2,1)S(1)}) custom-call(s32[9]{0:T(128)S(1)} %stack.39.s_ref, f32[440,1024]{1,0:T(8,128)S(1)} %bitcast.14, f32[2,448,128]{2,1,0:T(8,128)S(1)} %pad_maximum_fusion.5.p_ref), custom_call_target="tpu_custom_call" | custom-call | flops 1384120320 | bytes 3899392 | tf_op jit(solution)/shard_map/features/pallas_call | solution.py:128
  59.6 4.5 %features.5 = (bf16[1024,512]{1,0:T(8,128)(2,1)S(1)}, bf16[1024,512]{1,0:T(8,128)(2,1)S(1)}, bf16[1024,1024]{1,0:T(8,128)(2,1)S(1)}, bf16[1024,1024]{1,0:T(8,128)(2,1)S(1)}) custom-call(s32[9]{0:T(128)S(1)} %stack.39.s_ref, f32[440,1024]{1,0:T(8,128)S(1)} %bitcast.15, ...), custom_call_target="tpu_custom_call", output_to_operand_aliasing={{2}: (3, {}), {3}: (4, {})} | custom-call | flops 1384120320 | bytes 3899392 | tf_op jit(solution)/shard_map/features/pallas_call | solution.py:128
  64.1 4.5 %features.6 = (bf16[1024,512]{1,0:T(8,128)(2,1)S(1)}, bf16[1024,512]{1,0:T(8,128)(2,1)S(1)}, bf16[1024,1024]{1,0:T(8,128)(2,1)S(1)}, bf16[1024,1024]{1,0:T(8,128)(2,1)S(1)}) custom-call(s32[9]{0:T(128)S(1)} %stack.39.s_ref, f32[440,1024]{1,0:T(8,128)S(1)} %bitcast.16, ...), custom_call_target="tpu_custom_call", output_to_operand_aliasing={{0}: (3, {}), {1}: (4, {}), {2}: (5, {}), {3}: (6, {})} | custom-call | flops 1384120320 | bytes 3899392 | tf_op jit(solution)/shard_map/features/pallas_call | solution.py:128
  68.7 4.5 %features.7 = (bf16[1024,512]{1,0:T(8,128)(2,1)S(1)}, bf16[1024,512]{1,0:T(8,128)(2,1)S(1)}, bf16[1024,1024]{1,0:T(8,128)(2,1)S(1)}, bf16[1024,1024]{1,0:T(8,128)(2,1)S(1)}) custom-call(s32[9]{0:T(128)S(1)} %stack.39.s_ref, f32[440,1024]{1,0:T(8,128)S(1)} %bitcast.17, ...), custom_call_target="tpu_custom_call", output_to_operand_aliasing={{0}: (3, {}), {1}: (4, {}), {2}: (5, {}), {3}: (6, {})} | custom-call | flops 1384120320 | bytes 3899392 | tf_op jit(solution)/shard_map/features/pallas_call | solution.py:128
  73.3 3.0 %gram.2 = f32[16,5,16,256]{3,2,1,0:T(8,128)S(1)} custom-call(s32[9]{0:T(128)S(1)} %stack.39.s_ref, bf16[1024,512]{1,0:T(8,128)(2,1)S(1)} %get-tuple-element.44.ah, bf16[1024,512]{1,0:T(8,128)(2,1)S(1)} %get-tuple-element.45.al, bf16[1024,512]{1,0:T(8,128)(2,1)S(1)} %get-tuple-element.50.bh, bf16[1024,512]{1,0:T(8,128)(2,1)S(1)} %get-tuple-element.51.bl, ...), custom_call_target="tpu_custom_call" | custom-call | flops 2013265920 | bytes 8388608 | tf_op jit(solution)/shard_map/gram/pallas_call | solution.py:180
  76.3 5.1 %cross.4 = f32[4,1024,128]{2,1,0:T(8,128)S(1)} custom-call(s32[9]{0:T(128)S(1)} %stack.39.s_ref, f32[1024,2048]{1,0:T(8,128)S(1)} %bitcast.13, bf16[1024,1024]{1,0:T(8,128)(2,1)S(1)} %get-tuple-element.62.th, bf16[1024,1024]{1,0:T(8,128)(2,1)S(1)} %get-tuple-element.63.tl), custom_call_target="tpu_custom_call" | custom-call | flops 3221225472 | bytes 4194304 | tf_op jit(solution)/shard_map/cross/pallas_call | solution.py:220
  82.0 3.1 %gram.3 = f32[16,5,16,256]{3,2,1,0:T(8,128)S(1)} custom-call(s32[9]{0:T(128)S(1)} %stack.39.s_ref, bf16[1024,512]{1,0:T(8,128)(2,1)S(1)} %get-tuple-element.44.ah, bf16[1024,512]{1,0:T(8,128)(2,1)S(1)} %get-tuple-element.45.al, bf16[1024,512]{1,0:T(8,128)(2,1)S(1)} %get-tuple-element.50.bh, bf16[1024,512]{1,0:T(8,128)(2,1)S(1)} %get-tuple-element.51.bl, ...), custom_call_target="tpu_custom_call" | custom-call | flops 2013265920 | bytes 8388608 | tf_op jit(solution)/shard_map/gram/pallas_call | solution.py:180
  85.2 2.5 collective-permute-done.10
  87.9 5.1 %cross.5 = f32[4,1024,128]{2,1,0:T(8,128)S(1)} custom-call(s32[9]{0:T(128)S(1)} %stack.39.s_ref, f32[1024,2048]{1,0:T(8,128)S(1)} %bitcast.13, bf16[1024,1024]{1,0:T(8,128)(2,1)S(1)} %get-tuple-element.62.th, bf16[1024,1024]{1,0:T(8,128)(2,1)S(1)} %get-tuple-element.63.tl, f32[4,1024,128]{2,1,0:T(8,128)S(1)} %collective-permute-done.13.rest_0_), custom_call_target="tpu_custom_call" | custom-call | flops 3221225472 | bytes 4194304 | tf_op jit(solution)/shard_map/cross/pallas_call | solution.py:220
  93.0 5.1 %cross.6 = f32[4,1024,128]{2,1,0:T(8,128)S(1)} custom-call(s32[9]{0:T(128)S(1)} %stack.39.s_ref, f32[1024,2048]{1,0:T(8,128)S(1)} %bitcast.13, bf16[1024,1024]{1,0:T(8,128)(2,1)S(1)} %get-tuple-element.62.th, bf16[1024,1024]{1,0:T(8,128)(2,1)S(1)} %get-tuple-element.63.tl), custom_call_target="tpu_custom_call" | custom-call | flops 3221225472 | bytes 4194304 | tf_op jit(solution)/shard_map/cross/pallas_call | solution.py:220
  100.9 8.4 %collective-permute-done.11 = f32[8,5,16,256]{3,2,1,0:T(8,128)S(1)} collective-permute-done((f32[8,5,16,256]{3,2,1,0:T(8,128)S(1)}, f32[8,5,16,256]{3,2,1,0:T(8,128)S(1)}, u32[]{:S(2)}, u32[]{:S(2)}) %collective-permute-start.11) | collective-permute-done | bytes 655392 | tf_op jit(solution)/shard_map/ppermute | solution.py:514
  110.7 9.4 %collective-permute-done.12 = f32[4,5,16,256]{3,2,1,0:T(8,128)S(1)} collective-permute-done((f32[4,5,16,256]{3,2,1,0:T(8,128)S(1)}, f32[4,5,16,256]{3,2,1,0:T(8,128)S(1)}, u32[]{:S(2)}, u32[]{:S(2)}) %collective-permute-start.12) | collective-permute-done | bytes 327712 | tf_op jit(solution)/shard_map/ppermute | solution.py:514
  120.1 3.9 %collective-permute-done.32 = f32[2,1024,128]{2,1,0:T(8,128)S(1)} collective-permute-done((f32[2,1024,128]{2,1,0:T(8,128)S(1)}, f32[2,1024,128]{2,1,0:T(8,128)S(1)}, u32[]{:S(2)}, u32[]{:S(2)}) %collective-permute-start.32) | collective-permute-done | bytes 1048608 | tf_op jit(solution)/shard_map/ppermute | solution.py:514
  125.5 5.1 %cross.7 = f32[4,1024,128]{2,1,0:T(8,128)S(1)} custom-call(s32[9]{0:T(128)S(1)} %stack.39.s_ref, f32[1024,2048]{1,0:T(8,128)S(1)} %bitcast.13, bf16[1024,1024]{1,0:T(8,128)(2,1)S(1)} %get-tuple-element.62.th, bf16[1024,1024]{1,0:T(8,128)(2,1)S(1)} %get-tuple-element.63.tl, f32[4,1024,128]{2,1,0:T(8,128)S(1)} %collective-permute-done.14.rest_0_), custom_call_target="tpu_custom_call" | custom-call | flops 3221225472 | bytes 4194304 | tf_op jit(solution)/shard_map/cross/pallas_call | solution.py:220
  131.4 4.6 %collective-permute-done.15 = f32[2,5,16,256]{3,2,1,0:T(8,128)S(1)} collective-permute-done((f32[2,5,16,256]{3,2,1,0:T(8,128)S(1)}, f32[2,5,16,256]{3,2,1,0:T(8,128)S(1)}, u32[]{:S(2)}, u32[]{:S(2)}) %collective-permute-start.15) | collective-permute-done | bytes 163872 | tf_op jit(solution)/shard_map/ppermute | solution.py:514
  141.8 2.7 collective-permute-start.17
  149.3 3.2 %collective-permute-start.35 = (f32[1,256,128]{2,1,0:T(8,128)S(1)}, f32[1,256,128]{2,1,0:T(8,128)S(1)}, u32[]{:S(2)}, u32[]{:S(2)}) collective-permute-start(f32[1,256,128]{2,1,0:T(8,128)S(1)} %slice.135), channel_id=1, source_target_pairs={{0,16},{1,17},{2,18},{3,19},{4,20},{5,21},{6,22},{7,23},{8,24},{9,... | collective-permute-start | bytes 393224 | tf_op jit(solution)/shard_map/ppermute | solution.py:514
  152.7 2.8 collective-permute-start.19
  155.5 3.1 %collective-permute-done.35 = f32[1,256,128]{2,1,0:T(8,128)S(1)} collective-permute-done((f32[1,256,128]{2,1,0:T(8,128)S(1)}, f32[1,256,128]{2,1,0:T(8,128)S(1)}, u32[]{:S(2)}, u32[]{:S(2)}) %collective-permute-start.35) | collective-permute-done | bytes 131104 | tf_op jit(solution)/shard_map/ppermute | solution.py:514
  160.6 5.9 %collective-permute-start.20 = (f32[8,5,16,256]{3,2,1,0:T(8,128)S(1)}, f32[8,5,16,256]{3,2,1,0:T(8,128)S(1)}, u32[]{:S(2)}, u32[]{:S(2)}) collective-permute-start(f32[8,5,16,256]{3,2,1,0:T(8,128)S(1)} %pad_maximum_fusion.2), channel_id=1, source_target_pairs={{0,2},{1,5},{2,0},{3,7},{4,6},{5,1},{6,4},{7,3},{8,10},{9,13},{10,... | collective-permute-start | bytes 1966088 | tf_op jit(solution)/shard_map/ppermute | solution.py:514
  166.5 3.1 %collective-permute-start.37 = (f32[1,512,128]{2,1,0:T(8,128)S(1)}, f32[1,512,128]{2,1,0:T(8,128)S(1)}, u32[]{:S(2)}, u32[]{:S(2)}) collective-permute-start(f32[1,512,128]{2,1,0:T(8,128)S(1)} %pad_maximum_fusion.8), channel_id=1, source_target_pairs={{0,8},{1,9},{2,10},{3,11},{4,12},{5,13},{6,14},{7,15},{8,0},{9,1},... | collective-permute-start | bytes 786440 | tf_op jit(solution)/shard_map/ppermute | solution.py:514
  170.0 8.4 %collective-permute-done.20 = f32[8,5,16,256]{3,2,1,0:T(8,128)S(1)} collective-permute-done((f32[8,5,16,256]{3,2,1,0:T(8,128)S(1)}, f32[8,5,16,256]{3,2,1,0:T(8,128)S(1)}, u32[]{:S(2)}, u32[]{:S(2)}) %collective-permute-start.20) | collective-permute-done | bytes 655392 | tf_op jit(solution)/shard_map/ppermute | solution.py:514
  178.4 7.5 %assemble.1 = (f32[512,512]{1,0:T(8,128)S(1)}, f32[256,512]{1,0:T(8,128)S(1)}) custom-call(s32[9]{0:T(128)S(1)} %stack.39.s_ref, f32[16,5,16,256]{3,2,1,0:T(8,128)S(1)} %constant_dynamic-update-slice_fusion.g_ref), custom_call_target="tpu_custom_call" | custom-call | flops 10000000000 | bytes 4000000 | tf_op jit(solution)/shard_map/assemble/pallas_call | solution.py:337
  185.9 6.5 %factor.3.m_ref = f32[512,512]{1,0:T(8,128)S(1)} custom-call(f32[512,512]{1,0:T(8,128)S(1)} %get-tuple-element.65.m_ref), custom_call_target="tpu_custom_call" | custom-call | flops 10000000000 | bytes 4000000 | tf_op jit(solution)/shard_map/factor/pallas_call | solution.py:359
  193.5 6.3 %factor.4.m_ref = f32[512,512]{1,0:T(8,128)S(1)} custom-call(f32[512,512]{1,0:T(8,128)S(1)} %factor.3.m_ref), custom_call_target="tpu_custom_call" | custom-call | flops 10000000000 | bytes 4000000 | tf_op jit(solution)/shard_map/factor/pallas_call | solution.py:359
  200.0 4.1 %collective-permute-start.26 = (f32[1,256,128]{2,1,0:T(8,128)S(1)}, f32[1,256,128]{2,1,0:T(8,128)S(1)}, u32[]{:S(2)}, u32[]{:S(2)}) collective-permute-start(f32[1,256,128]{2,1,0:T(8,128)S(1)} %slice.127), channel_id=1, source_target_pairs={{0,16},{1,17},{2,18},{3,19},{4,20},{5,21},{6,22},{7,23},{8,24},{9,... | collective-permute-start | bytes 393224 | tf_op jit(solution)/shard_map/ppermute | solution.py:514
  204.1 7.8 %factor.5.own_ref = f32[512,512]{1,0:T(8,128)S(1)} custom-call(f32[512,512]{1,0:T(8,128)S(1)} %factor.4.m_ref), custom_call_target="tpu_custom_call" | custom-call | flops 10000000000 | bytes 4000000 | tf_op jit(solution)/shard_map/factor/pallas_call | solution.py:359
  212.1 9.0 %collective-permute-done.27 = f32[1,256,128]{2,1,0:T(8,128)S(1)} collective-permute-done((f32[1,256,128]{2,1,0:T(8,128)S(1)}, f32[1,256,128]{2,1,0:T(8,128)S(1)}, u32[]{:S(2)}, u32[]{:S(2)}) %collective-permute-start.27) | collective-permute-done | bytes 131104 | tf_op jit(solution)/shard_map/ppermute | solution.py:514
  223.3 6.2 %collective-permute-done.28 = f32[1,512,128]{2,1,0:T(8,128)S(1)} collective-permute-done((f32[1,512,128]{2,1,0:T(8,128)S(1)}, f32[1,512,128]{2,1,0:T(8,128)S(1)}, u32[]{:S(2)}, u32[]{:S(2)}) %collective-permute-start.28) | collective-permute-done | bytes 262176 | tf_op jit(solution)/shard_map/ppermute | solution.py:514
  230.6 2.4 couple.1.b_ref
  233.1 4.3 %solve.3.wa_ref = f32[2,1024,128]{2,1,0:T(8,128)S(1)} custom-call(s32[9]{0:T(128)S(1)} %stack.39.s_ref, f32[512,512]{1,0:T(8,128)S(1)} %factor.5.own_ref, f32[512,512]{1,0:T(8,128)S(1)} %collective-permute-done.21.oth_ref, f32[512,512]{1,0:T(8,128)S(1)} %couple.1.b_ref, f32[2,1024,128]{2,1,0:T(8,128)S(1)} %pad_maximum_fusion.1.c_ref), custom_call_target="tpu_custom_call" | custom-call | flops 2415919104 | bytes 2097152 | tf_op jit(solution)/shard_map/solve/pallas_call | solution.py:431
  237.4 2.2 collective-permute-start.39
  239.7 4.3 %solve.2.wa_ref = f32[2,1024,128]{2,1,0:T(8,128)S(1)} custom-call(s32[9]{0:T(128)S(1)} %stack.39.s_ref, f32[512,512]{1,0:T(8,128)S(1)} %factor.5.own_ref, f32[512,512]{1,0:T(8,128)S(1)} %collective-permute-done.21.oth_ref, f32[512,512]{1,0:T(8,128)S(1)} %couple.1.b_ref, f32[2,1024,128]{2,1,0:T(8,128)S(1)} %pad_maximum_fusion.c_ref), custom_call_target="tpu_custom_call" | custom-call | flops 2415919104 | bytes 2097152 | tf_op jit(solution)/shard_map/solve/pallas_call | solution.py:431
  245.9 6.5 %collective-permute-done.39.wa_ref = f32[2,1024,128]{2,1,0:T(8,128)S(1)} collective-permute-done((f32[2,1024,128]{2,1,0:T(8,128)S(1)}, f32[2,1024,128]{2,1,0:T(8,128)S(1)}, u32[]{:S(2)}, u32[]{:S(2)}) %collective-permute-start.39) | collective-permute-done | bytes 1048608 | tf_op jit(solution)/shard_map/ppermute | solution.py:514
  252.4 11.2 %collective-permute-done.30.wa_ref = f32[2,1024,128]{2,1,0:T(8,128)S(1)} collective-permute-done((f32[2,1024,128]{2,1,0:T(8,128)S(1)}, f32[2,1024,128]{2,1,0:T(8,128)S(1)}, u32[]{:S(2)}, u32[]{:S(2)}) %collective-permute-start.30) | collective-permute-done | bytes 1048608 | tf_op jit(solution)/shard_map/ppermute | solution.py:514
  263.7 6.1 %residual.4 = (f32[1024,2048]{1,0:T(8,128)}, f32[2,512,2048]{2,1,0:T(8,128)}) custom-call(s32[9]{0:T(128)S(1)} %stack.39.s_ref, f32[1024,2048]{1,0:T(8,128)S(1)} %bitcast.13, bf16[1024,512]{1,0:T(8,128)(2,1)S(1)} %get-tuple-element.44.ah, bf16[1024,512]{1,0:T(8,128)(2,1)S(1)} %get-tuple-element.45.al, bf16[1024,512]{1,0:T(8,128)(2,1)S(1)} %get-tuple-element.50.bh, ...), custom_call_target="tpu_custom_call" | custom-call | flops 3221225472 | bytes 6291456 | tf_op jit(solution)/shard_map/residual/pallas_call | solution.py:478
  269.8 6.1 %residual.5 = (f32[1024,2048]{1,0:T(8,128)}, f32[2,512,2048]{2,1,0:T(8,128)}) custom-call(s32[9]{0:T(128)S(1)} %stack.39.s_ref, f32[1024,2048]{1,0:T(8,128)S(1)} %bitcast.13, bf16[1024,512]{1,0:T(8,128)(2,1)S(1)} %get-tuple-element.44.ah, bf16[1024,512]{1,0:T(8,128)(2,1)S(1)} %get-tuple-element.45.al, ...), custom_call_target="tpu_custom_call", output_to_operand_aliasing={{0}: (8, {}), {1}: (9, {})} | custom-call | flops 3221225472 | bytes 6291456 | tf_op jit(solution)/shard_map/residual/pallas_call | solution.py:478
  275.9 6.1 %residual.6 = (f32[1024,2048]{1,0:T(8,128)}, f32[2,512,2048]{2,1,0:T(8,128)}) custom-call(s32[9]{0:T(128)S(1)} %stack.39.s_ref, f32[1024,2048]{1,0:T(8,128)S(1)} %bitcast.13, bf16[1024,512]{1,0:T(8,128)(2,1)S(1)} %get-tuple-element.44.ah, bf16[1024,512]{1,0:T(8,128)(2,1)S(1)} %get-tuple-element.45.al, ...), custom_call_target="tpu_custom_call", output_to_operand_aliasing={{0}: (8, {}), {1}: (9, {})} | custom-call | flops 3221225472 | bytes 6291456 | tf_op jit(solution)/shard_map/residual/pallas_call | solution.py:478
  282.0 6.1 %residual.7 = (f32[1024,2048]{1,0:T(8,128)}, f32[2,512,2048]{2,1,0:T(8,128)}) custom-call(s32[9]{0:T(128)S(1)} %stack.39.s_ref, f32[1024,2048]{1,0:T(8,128)S(1)} %bitcast.13, bf16[1024,512]{1,0:T(8,128)(2,1)S(1)} %get-tuple-element.44.ah, bf16[1024,512]{1,0:T(8,128)(2,1)S(1)} %get-tuple-element.45.al, ...), custom_call_target="tpu_custom_call", output_to_operand_aliasing={{0}: (8, {}), {1}: (9, {})} | custom-call | flops 3221225472 | bytes 6291456 | tf_op jit(solution)/shard_map/residual/pallas_call | solution.py:478
  (119 shorter events, 38.1 us)
Async XLA Ops:
  0.6 2.9 collective-permute-start
  1.2 2.3 collective-permute-start.1
  3.5 1.2 copy-start.1
  4.7 0.7 copy-start.2
  7.1 47.9 %copy-start = (f32[1024,440]{0,1:T(8,128)S(1)}, f32[1024,440]{0,1:T(8,128)}, u32[]{:S(2)}) copy-start(f32[1024,440]{0,1:T(8,128)} %param.5) | copy-start | bytes 5406724
  7.1 9.4 %collective-permute-start.2 = (f32[2,448,128]{2,1,0:T(8,128)S(1)}, f32[2,448,128]{2,1,0:T(8,128)S(1)}, u32[]{:S(2)}, u32[]{:S(2)}) collective-permute-start(f32[2,448,128]{2,1,0:T(8,128)S(1)} %slice.113), channel_id=1, source_target_pairs={{0,2},{1,5},{2,0},{3,7},{4,6},{5,1},{6,4},{7,3},{8,10},{9,13},{10,... | collective-permute-start | bytes 1376264 | tf_op jit(solution)/shard_map/ppermute | solution.py:514
  16.6 6.1 %collective-permute-start.3 = (f32[1,448,128]{2,1,0:T(8,128)S(1)}, f32[1,448,128]{2,1,0:T(8,128)S(1)}, u32[]{:S(2)}, u32[]{:S(2)}) collective-permute-start(f32[1,448,128]{2,1,0:T(8,128)S(1)} %slice.115), channel_id=1, source_target_pairs={{0,4},{1,3},{2,6},{3,1},{4,0},{5,7},{6,2},{7,5},{8,12},{9,11},{10,... | collective-permute-start | bytes 688136 | tf_op jit(solution)/shard_map/ppermute | solution.py:514
  22.7 6.3 %collective-permute-start.4 = (f32[1,448,128]{2,1,0:T(8,128)S(1)}, f32[1,448,128]{2,1,0:T(8,128)S(1)}, u32[]{:S(2)}, u32[]{:S(2)}) collective-permute-start(f32[1,448,128]{2,1,0:T(8,128)S(1)} %slice_add_fusion.9), channel_id=1, source_target_pairs={{0,8},{1,9},{2,10},{3,11},{4,12},{5,13},{6,14},{7,15},{8,0},{9,1},... | collective-permute-start | bytes 688136 | tf_op jit(solution)/shard_map/ppermute | solution.py:514
  29.1 11.2 %collective-permute-start.5 = (f32[1,448,128]{2,1,0:T(8,128)S(1)}, f32[1,448,128]{2,1,0:T(8,128)S(1)}, u32[]{:S(2)}, u32[]{:S(2)}) collective-permute-start(f32[1,448,128]{2,1,0:T(8,128)S(1)} %add.109), channel_id=1, source_target_pairs={{0,16},{1,17},{2,18},{3,19},{4,20},{5,21},{6,22},{7,23},{8,24},{9,... | collective-permute-start | bytes 688136 | tf_op jit(solution)/shard_map/ppermute | solution.py:514
  40.3 6.1 %collective-permute-start.6 = (f32[1,448,128]{2,1,0:T(8,128)S(1)}, f32[1,448,128]{2,1,0:T(8,128)S(1)}, u32[]{:S(2)}, u32[]{:S(2)}) collective-permute-start(f32[1,448,128]{2,1,0:T(8,128)S(1)} %add.110), channel_id=1, source_target_pairs={{0,4},{1,3},{2,6},{3,1},{4,0},{5,7},{6,2},{7,5},{8,12},{9,11},{10,... | collective-permute-start | bytes 688136 | tf_op jit(solution)/shard_map/ppermute | solution.py:514
  46.5 8.5 %collective-permute-start.7 = (f32[2,448,128]{2,1,0:T(8,128)S(1)}, f32[2,448,128]{2,1,0:T(8,128)S(1)}, u32[]{:S(2)}, u32[]{:S(2)}) collective-permute-start(f32[2,448,128]{2,1,0:T(8,128)S(1)} %pad_maximum_fusion.5.p_ref), channel_id=1, source_target_pairs={{0,2},{1,5},{2,0},{3,7},{4,6},{5,1},{6,4},{7,3},{8,10},{9,13},{10,... | collective-permute-start | bytes 1376264 | tf_op jit(solution)/shard_map/ppermute | solution.py:514
  47.7 11.9 %collective-permute-start.8 = (f32[2,448,128]{2,1,0:T(8,128)S(1)}, f32[2,448,128]{2,1,0:T(8,128)S(1)}, u32[]{:S(2)}, u32[]{:S(2)}) collective-permute-start(f32[2,448,128]{2,1,0:T(8,128)S(1)} %pad_maximum_fusion.5.p_ref), channel_id=1, source_target_pairs={{0,1},{1,0},{2,3},{3,2},{4,5},{5,4},{6,7},{7,6},{8,9},{9,8},{10,11... | collective-permute-start | bytes 1376264 | tf_op jit(solution)/shard_map/ppermute | solution.py:514
  55.0 13.7 %collective-permute-start.9 = (f32[2,448,128]{2,1,0:T(8,128)S(1)}, f32[2,448,128]{2,1,0:T(8,128)S(1)}, u32[]{:S(2)}, u32[]{:S(2)}) collective-permute-start(f32[2,448,128]{2,1,0:T(8,128)S(1)} %collective-permute-done.7.p_ref), channel_id=1, source_target_pairs={{0,1},{1,0},{2,3},{3,2},{4,5},{5,4},{6,7},{7,6},{8,9},{9,8},{10,11... | collective-permute-start | bytes 1376264 | tf_op jit(solution)/shard_map/ppermute | solution.py:514
  68.7 7.5 %slice-start = ((s8[8388608]{0:T(1024)(128)(4,1)}), s8[4194304]{0:T(1024)(128)(4,1)S(1)}, s32[]{:S(2)}) async-start(s8[8388608]{0:T(1024)(128)(4,1)} %bitcast.12), calls=%async_computation | async-start | bytes 8388608
  73.3 3.0 %slice-start.1 = ((s8[8388608]{0:T(1024)(128)(4,1)}), s8[4194304]{0:T(1024)(128)(4,1)S(1)}, s32[]{:S(2)}) async-start(s8[8388608]{0:T(1024)(128)(4,1)} %bitcast.12), calls=%async_computation.1 | async-start | bytes 8388608
  81.4 6.5 %collective-permute-start.13 = (f32[4,1024,128]{2,1,0:T(8,128)S(1)}, f32[4,1024,128]{2,1,0:T(8,128)S(1)}, u32[]{:S(2)}, u32[]{:S(2)}) collective-permute-start(f32[4,1024,128]{2,1,0:T(8,128)S(1)} %cross.4), channel_id=1, source_target_pairs={{0,1},{1,0},{2,3},{3,2},{4,5},{5,4},{6,7},{7,6},{8,9},{9,8},{10,11... | collective-permute-start | bytes 6291464 | tf_op jit(solution)/shard_map/ppermute | solution.py:514
  82.0 5.7 %collective-permute-start.10 = (f32[16,5,16,256]{3,2,1,0:T(8,128)S(1)}, f32[16,5,16,256]{3,2,1,0:T(8,128)S(1)}, u32[]{:S(2)}, u32[]{:S(2)}) collective-permute-start(f32[16,5,16,256]{3,2,1,0:T(8,128)S(1)} %gram.2), channel_id=1, source_target_pairs={{0,1},{1,0},{2,3},{3,2},{4,5},{5,4},{6,7},{7,6},{8,9},{9,8},{10,11... | collective-permute-start | bytes 3932168 | tf_op jit(solution)/shard_map/ppermute | solution.py:514
  98.2 27.3 %collective-permute-start.14 = (f32[4,1024,128]{2,1,0:T(8,128)S(1)}, f32[4,1024,128]{2,1,0:T(8,128)S(1)}, u32[]{:S(2)}, u32[]{:S(2)}) collective-permute-start(f32[4,1024,128]{2,1,0:T(8,128)S(1)} %cross.6), channel_id=1, source_target_pairs={{0,1},{1,0},{2,3},{3,2},{4,5},{5,4},{6,7},{7,6},{8,9},{9,8},{10,11... | collective-permute-start | bytes 6291464 | tf_op jit(solution)/shard_map/ppermute | solution.py:514
  98.6 10.7 %collective-permute-start.11 = (f32[8,5,16,256]{3,2,1,0:T(8,128)S(1)}, f32[8,5,16,256]{3,2,1,0:T(8,128)S(1)}, u32[]{:S(2)}, u32[]{:S(2)}) collective-permute-start(f32[8,5,16,256]{3,2,1,0:T(8,128)S(1)} %slice.117), channel_id=1, source_target_pairs={{0,2},{1,5},{2,0},{3,7},{4,6},{5,1},{6,4},{7,3},{8,10},{9,13},{10,... | collective-permute-start | bytes 1966088 | tf_op jit(solution)/shard_map/ppermute | solution.py:514
  100.0 24.1 %collective-permute-start.32 = (f32[2,1024,128]{2,1,0:T(8,128)S(1)}, f32[2,1024,128]{2,1,0:T(8,128)S(1)}, u32[]{:S(2)}, u32[]{:S(2)}) collective-permute-start(f32[2,1024,128]{2,1,0:T(8,128)S(1)} %slice.129), channel_id=1, source_target_pairs={{0,2},{1,5},{2,0},{3,7},{4,6},{5,1},{6,4},{7,3},{8,10},{9,13},{10,... | collective-permute-start | bytes 3145736 | tf_op jit(solution)/shard_map/ppermute | solution.py:514
  109.4 10.6 %collective-permute-start.12 = (f32[4,5,16,256]{3,2,1,0:T(8,128)S(1)}, f32[4,5,16,256]{3,2,1,0:T(8,128)S(1)}, u32[]{:S(2)}, u32[]{:S(2)}) collective-permute-start(f32[4,5,16,256]{3,2,1,0:T(8,128)S(1)} %slice.119), channel_id=1, source_target_pairs={{0,4},{1,3},{2,6},{3,1},{4,0},{5,7},{6,2},{7,5},{8,12},{9,11},{10,... | collective-permute-start | bytes 983048 | tf_op jit(solution)/shard_map/ppermute | solution.py:514
  124.2 14.0 %collective-permute-start.33 = (f32[1,1024,128]{2,1,0:T(8,128)S(1)}, f32[1,1024,128]{2,1,0:T(8,128)S(1)}, u32[]{:S(2)}, u32[]{:S(2)}) collective-permute-start(f32[1,1024,128]{2,1,0:T(8,128)S(1)} %slice.131), channel_id=1, source_target_pairs={{0,4},{1,3},{2,6},{3,1},{4,0},{5,7},{6,2},{7,5},{8,12},{9,11},{10,... | collective-permute-start | bytes 1572872 | tf_op jit(solution)/shard_map/ppermute | solution.py:514
  130.6 5.4 %collective-permute-start.15 = (f32[2,5,16,256]{3,2,1,0:T(8,128)S(1)}, f32[2,5,16,256]{3,2,1,0:T(8,128)S(1)}, u32[]{:S(2)}, u32[]{:S(2)}) collective-permute-start(f32[2,5,16,256]{3,2,1,0:T(8,128)S(1)} %slice.93), channel_id=1, source_target_pairs={{0,8},{1,9},{2,10},{3,11},{4,12},{5,13},{6,14},{7,15},{8,0},{9,1},... | collective-permute-start | bytes 491528 | tf_op jit(solution)/shard_map/ppermute | solution.py:514
  136.1 5.7 %collective-permute-start.16 = (f32[1,5,16,256]{3,2,1,0:T(8,128)S(1)}, f32[1,5,16,256]{3,2,1,0:T(8,128)S(1)}, u32[]{:S(2)}, u32[]{:S(2)}) collective-permute-start(f32[1,5,16,256]{3,2,1,0:T(8,128)S(1)} %slice.121), channel_id=1, source_target_pairs={{0,16},{1,17},{2,18},{3,19},{4,20},{5,21},{6,22},{7,23},{8,24},{9,... | collective-permute-start | bytes 245768 | tf_op jit(solution)/shard_map/ppermute | solution.py:514
  138.3 10.9 %collective-permute-start.34 = (f32[1,512,128]{2,1,0:T(8,128)S(1)}, f32[1,512,128]{2,1,0:T(8,128)S(1)}, u32[]{:S(2)}, u32[]{:S(2)}) collective-permute-start(f32[1,512,128]{2,1,0:T(8,128)S(1)} %slice.133), channel_id=1, source_target_pairs={{0,8},{1,9},{2,10},{3,11},{4,12},{5,13},{6,14},{7,15},{8,0},{9,1},... | collective-permute-start | bytes 786440 | tf_op jit(solution)/shard_map/ppermute | solution.py:514
  141.8 5.5 %collective-permute-start.17 = (f32[1,5,16,256]{3,2,1,0:T(8,128)S(1)}, f32[1,5,16,256]{3,2,1,0:T(8,128)S(1)}, u32[]{:S(2)}, u32[]{:S(2)}) collective-permute-start(f32[1,5,16,256]{3,2,1,0:T(8,128)S(1)} %get-tuple-element.75), channel_id=1, source_target_pairs={{0,16},{1,17},{2,18},{3,19},{4,20},{5,21},{6,22},{7,23},{8,24},{9,... | collective-permute-start | bytes 245768 | tf_op jit(solution)/shard_map/ppermute | solution.py:514
  144.6 25.2 %collective-permute-start.23 = (f32[2,1024,128]{2,1,0:T(8,128)S(1)}, f32[2,1024,128]{2,1,0:T(8,128)S(1)}, u32[]{:S(2)}, u32[]{:S(2)}) collective-permute-start(f32[2,1024,128]{2,1,0:T(8,128)S(1)} %slice.97), channel_id=1, source_target_pairs={{0,2},{1,5},{2,0},{3,7},{4,6},{5,1},{6,4},{7,3},{8,10},{9,13},{10,... | collective-permute-start | bytes 3145736 | tf_op jit(solution)/shard_map/ppermute | solution.py:514
  147.3 5.4 %collective-permute-start.18 = (f32[2,5,16,256]{3,2,1,0:T(8,128)S(1)}, f32[2,5,16,256]{3,2,1,0:T(8,128)S(1)}, u32[]{:S(2)}, u32[]{:S(2)}) collective-permute-start(f32[2,5,16,256]{3,2,1,0:T(8,128)S(1)} %pad_maximum_fusion.9), channel_id=1, source_target_pairs={{0,8},{1,9},{2,10},{3,11},{4,12},{5,13},{6,14},{7,15},{8,0},{9,1},... | collective-permute-start | bytes 491528 | tf_op jit(solution)/shard_map/ppermute | solution.py:514
  149.3 9.3 %collective-permute-start.35 = (f32[1,256,128]{2,1,0:T(8,128)S(1)}, f32[1,256,128]{2,1,0:T(8,128)S(1)}, u32[]{:S(2)}, u32[]{:S(2)}) collective-permute-start(f32[1,256,128]{2,1,0:T(8,128)S(1)} %slice.135), channel_id=1, source_target_pairs={{0,16},{1,17},{2,18},{3,19},{4,20},{5,21},{6,22},{7,23},{8,24},{9,... | collective-permute-start | bytes 393224 | tf_op jit(solution)/shard_map/ppermute | solution.py:514
  152.7 7.8 %collective-permute-start.19 = (f32[4,5,16,256]{3,2,1,0:T(8,128)S(1)}, f32[4,5,16,256]{3,2,1,0:T(8,128)S(1)}, u32[]{:S(2)}, u32[]{:S(2)}) collective-permute-start(f32[4,5,16,256]{3,2,1,0:T(8,128)S(1)} %pad_maximum_fusion.6), channel_id=1, source_target_pairs={{0,4},{1,3},{2,6},{3,1},{4,0},{5,7},{6,2},{7,5},{8,12},{9,11},{10,... | collective-permute-start | bytes 983048 | tf_op jit(solution)/shard_map/ppermute | solution.py:514
  158.6 7.9 %collective-permute-start.36 = (f32[1,256,128]{2,1,0:T(8,128)S(1)}, f32[1,256,128]{2,1,0:T(8,128)S(1)}, u32[]{:S(2)}, u32[]{:S(2)}) collective-permute-start(f32[1,256,128]{2,1,0:T(8,128)S(1)} %slice_add_fusion.11), channel_id=1, source_target_pairs={{0,16},{1,17},{2,18},{3,19},{4,20},{5,21},{6,22},{7,23},{8,24},{9,... | collective-permute-start | bytes 393224 | tf_op jit(solution)/shard_map/ppermute | solution.py:514
  160.6 17.8 %collective-permute-start.20 = (f32[8,5,16,256]{3,2,1,0:T(8,128)S(1)}, f32[8,5,16,256]{3,2,1,0:T(8,128)S(1)}, u32[]{:S(2)}, u32[]{:S(2)}) collective-permute-start(f32[8,5,16,256]{3,2,1,0:T(8,128)S(1)} %pad_maximum_fusion.2), channel_id=1, source_target_pairs={{0,2},{1,5},{2,0},{3,7},{4,6},{5,1},{6,4},{7,3},{8,10},{9,13},{10,... | collective-permute-start | bytes 1966088 | tf_op jit(solution)/shard_map/ppermute | solution.py:514
  166.5 54.7 %collective-permute-start.37 = (f32[1,512,128]{2,1,0:T(8,128)S(1)}, f32[1,512,128]{2,1,0:T(8,128)S(1)}, u32[]{:S(2)}, u32[]{:S(2)}) collective-permute-start(f32[1,512,128]{2,1,0:T(8,128)S(1)} %pad_maximum_fusion.8), channel_id=1, source_target_pairs={{0,8},{1,9},{2,10},{3,11},{4,12},{5,13},{6,14},{7,15},{8,0},{9,1},... | collective-permute-start | bytes 786440 | tf_op jit(solution)/shard_map/ppermute | solution.py:514
  169.9 22.5 %collective-permute-start.24 = (f32[1,1024,128]{2,1,0:T(8,128)S(1)}, f32[1,1024,128]{2,1,0:T(8,128)S(1)}, u32[]{:S(2)}, u32[]{:S(2)}) collective-permute-start(f32[1,1024,128]{2,1,0:T(8,128)S(1)} %slice.123), channel_id=1, source_target_pairs={{0,4},{1,3},{2,6},{3,1},{4,0},{5,7},{6,2},{7,5},{8,12},{9,11},{10,... | collective-permute-start | bytes 1572872 | tf_op jit(solution)/shard_map/ppermute | solution.py:514
  192.5 7.4 %collective-permute-start.25 = (f32[1,512,128]{2,1,0:T(8,128)S(1)}, f32[1,512,128]{2,1,0:T(8,128)S(1)}, u32[]{:S(2)}, u32[]{:S(2)}) collective-permute-start(f32[1,512,128]{2,1,0:T(8,128)S(1)} %slice.125), channel_id=1, source_target_pairs={{0,8},{1,9},{2,10},{3,11},{4,12},{5,13},{6,14},{7,15},{8,0},{9,1},... | collective-permute-start | bytes 786440 | tf_op jit(solution)/shard_map/ppermute | solution.py:514
  200.0 12.0 %collective-permute-start.26 = (f32[1,256,128]{2,1,0:T(8,128)S(1)}, f32[1,256,128]{2,1,0:T(8,128)S(1)}, u32[]{:S(2)}, u32[]{:S(2)}) collective-permute-start(f32[1,256,128]{2,1,0:T(8,128)S(1)} %slice.127), channel_id=1, source_target_pairs={{0,16},{1,17},{2,18},{3,19},{4,20},{5,21},{6,22},{7,23},{8,24},{9,... | collective-permute-start | bytes 393224 | tf_op jit(solution)/shard_map/ppermute | solution.py:514
  211.9 18.7 %collective-permute-start.21 = (f32[512,512]{1,0:T(8,128)S(1)}, f32[512,512]{1,0:T(8,128)S(1)}, u32[]{:S(2)}, u32[]{:S(2)}) collective-permute-start(f32[512,512]{1,0:T(8,128)S(1)} %factor.5.own_ref), channel_id=1, source_target_pairs={{0,1},{1,0},{2,3},{3,2},{4,5},{5,4},{6,7},{7,6},{8,9},{9,8},{10,11... | collective-permute-start | bytes 3145736 | tf_op jit(solution)/shard_map/ppermute | solution.py:514
  212.0 9.1 %collective-permute-start.27 = (f32[1,256,128]{2,1,0:T(8,128)S(1)}, f32[1,256,128]{2,1,0:T(8,128)S(1)}, u32[]{:S(2)}, u32[]{:S(2)}) collective-permute-start(f32[1,256,128]{2,1,0:T(8,128)S(1)} %slice_add_fusion.12), channel_id=1, source_target_pairs={{0,16},{1,17},{2,18},{3,19},{4,20},{5,21},{6,22},{7,23},{8,24},{9,... | collective-permute-start | bytes 393224 | tf_op jit(solution)/shard_map/ppermute | solution.py:514
  221.1 8.3 %collective-permute-start.28 = (f32[1,512,128]{2,1,0:T(8,128)S(1)}, f32[1,512,128]{2,1,0:T(8,128)S(1)}, u32[]{:S(2)}, u32[]{:S(2)}) collective-permute-start(f32[1,512,128]{2,1,0:T(8,128)S(1)} %pad_maximum_fusion.7), channel_id=1, source_target_pairs={{0,8},{1,9},{2,10},{3,11},{4,12},{5,13},{6,14},{7,15},{8,0},{9,1},... | collective-permute-start | bytes 786440 | tf_op jit(solution)/shard_map/ppermute | solution.py:514
  221.3 9.2 %collective-permute-start.38 = (f32[1,1024,128]{2,1,0:T(8,128)S(1)}, f32[1,1024,128]{2,1,0:T(8,128)S(1)}, u32[]{:S(2)}, u32[]{:S(2)}) collective-permute-start(f32[1,1024,128]{2,1,0:T(8,128)S(1)} %pad_maximum_fusion.4), channel_id=1, source_target_pairs={{0,4},{1,3},{2,6},{3,1},{4,0},{5,7},{6,2},{7,5},{8,12},{9,11},{10,... | collective-permute-start | bytes 1572872 | tf_op jit(solution)/shard_map/ppermute | solution.py:514
  221.4 9.2 %collective-permute-start.22 = (f32[256,512]{1,0:T(8,128)S(1)}, f32[256,512]{1,0:T(8,128)S(1)}, u32[]{:S(2)}, u32[]{:S(2)}) collective-permute-start(f32[256,512]{1,0:T(8,128)S(1)} %get-tuple-element.66.gown_ref), channel_id=1, source_target_pairs={{0,1},{1,0},{2,3},{3,2},{4,5},{5,4},{6,7},{7,6},{8,9},{9,8},{10,11... | collective-permute-start | bytes 1572872 | tf_op jit(solution)/shard_map/ppermute | solution.py:514
  229.5 10.1 %collective-permute-start.29 = (f32[1,1024,128]{2,1,0:T(8,128)S(1)}, f32[1,1024,128]{2,1,0:T(8,128)S(1)}, u32[]{:S(2)}, u32[]{:S(2)}) collective-permute-start(f32[1,1024,128]{2,1,0:T(8,128)S(1)} %pad_maximum_fusion.3), channel_id=1, source_target_pairs={{0,4},{1,3},{2,6},{3,1},{4,0},{5,7},{6,2},{7,5},{8,12},{9,11},{10,... | collective-permute-start | bytes 1572872 | tf_op jit(solution)/shard_map/ppermute | solution.py:514
  237.4 15.0 %collective-permute-start.39 = (f32[2,1024,128]{2,1,0:T(8,128)S(1)}, f32[2,1024,128]{2,1,0:T(8,128)S(1)}, u32[]{:S(2)}, u32[]{:S(2)}) collective-permute-start(f32[2,1024,128]{2,1,0:T(8,128)S(1)} %solve.3.wa_ref), channel_id=1, source_target_pairs={{0,2},{1,5},{2,0},{3,7},{4,6},{5,1},{6,4},{7,3},{8,10},{9,13},{10,... | collective-permute-start | bytes 3145736 | tf_op jit(solution)/shard_map/ppermute | solution.py:514
  244.1 19.6 %collective-permute-start.30 = (f32[2,1024,128]{2,1,0:T(8,128)S(1)}, f32[2,1024,128]{2,1,0:T(8,128)S(1)}, u32[]{:S(2)}, u32[]{:S(2)}) collective-permute-start(f32[2,1024,128]{2,1,0:T(8,128)S(1)} %solve.2.wa_ref), channel_id=1, source_target_pairs={{0,2},{1,5},{2,0},{3,7},{4,6},{5,1},{6,4},{7,3},{8,10},{9,13},{10,... | collective-permute-start | bytes 3145736 | tf_op jit(solution)/shard_map/ppermute | solution.py:514
  245.4 18.2 %collective-permute-start.42 = (f32[2,1024,128]{2,1,0:T(8,128)S(1)}, f32[2,1024,128]{2,1,0:T(8,128)S(1)}, u32[]{:S(2)}, u32[]{:S(2)}) collective-permute-start(f32[2,1024,128]{2,1,0:T(8,128)S(1)} %solve.3.wa_ref), channel_id=1, source_target_pairs={{0,1},{1,0},{2,3},{3,2},{4,5},{5,4},{6,7},{7,6},{8,9},{9,8},{10,11... | collective-permute-start | bytes 3145736 | tf_op jit(solution)/shard_map/ppermute | solution.py:514
  245.4 24.4 %collective-permute-start.41 = (f32[2,1024,128]{2,1,0:T(8,128)S(1)}, f32[2,1024,128]{2,1,0:T(8,128)S(1)}, u32[]{:S(2)}, u32[]{:S(2)}) collective-permute-start(f32[2,1024,128]{2,1,0:T(8,128)S(1)} %solve.2.wa_ref), channel_id=1, source_target_pairs={{0,1},{1,0},{2,3},{3,2},{4,5},{5,4},{6,7},{7,6},{8,9},{9,8},{10,11... | collective-permute-start | bytes 3145736 | tf_op jit(solution)/shard_map/ppermute | solution.py:514
  252.4 23.5 %collective-permute-start.40 = (f32[2,1024,128]{2,1,0:T(8,128)S(1)}, f32[2,1024,128]{2,1,0:T(8,128)S(1)}, u32[]{:S(2)}, u32[]{:S(2)}) collective-permute-start(f32[2,1024,128]{2,1,0:T(8,128)S(1)} %collective-permute-done.39.wa_ref), channel_id=1, source_target_pairs={{0,1},{1,0},{2,3},{3,2},{4,5},{5,4},{6,7},{7,6},{8,9},{9,8},{10,11... | collective-permute-start | bytes 3145736 | tf_op jit(solution)/shard_map/ppermute | solution.py:514
  263.7 18.4 %collective-permute-start.31 = (f32[2,1024,128]{2,1,0:T(8,128)S(1)}, f32[2,1024,128]{2,1,0:T(8,128)S(1)}, u32[]{:S(2)}, u32[]{:S(2)}) collective-permute-start(f32[2,1024,128]{2,1,0:T(8,128)S(1)} %collective-permute-done.30.wa_ref), channel_id=1, source_target_pairs={{0,1},{1,0},{2,3},{3,2},{4,5},{5,4},{6,7},{7,6},{8,9},{9,8},{10,11... | collective-permute-start | bytes 3145736 | tf_op jit(solution)/shard_map/ppermute | solution.py:514
  (1 other events, 0.7 us)

commit v6 on v5

--- a/solution.py
+++ b/solution.py
@@ -367,26 +367,7 @@
     )(matrix)
 
 
-def couple_kernel(s_ref, own_ref, oth_ref, gown_ref, goth_ref, out_ref):
-    core = s_ref[CORE]
-    half = gown_ref.shape[0]
-    second = jnp.where(core == 1, own_ref[...], oth_ref[...])
-    top = jnp.where(core == 0, gown_ref[...], goth_ref[...])
-    low = jnp.where(core == 0, goth_ref[...], gown_ref[...])
-    out_ref[...] = dot_full(second[:, :half], top) + dot_full(second[:, half:], low)
-
-
-def couple(core, own, oth, side_own, side_oth):
-    return pl.pallas_call(
-        couple_kernel,
-        out_shape=jax.ShapeDtypeStruct(own.shape, F32),
-        in_specs=[pl.BlockSpec(memory_space=pltpu.SMEM)] + [pl.BlockSpec(memory_space=pltpu.VMEM)] * 4,
-        compiler_params=params(),
-        name="couple",
-    )(core, own, oth, side_own, side_oth)
-
-
-def solve_kernel(s_ref, own_ref, oth_ref, b_ref, c_ref, out_ref, one_ref):
+def solve_kernel(s_ref, own_ref, oth_ref, gown_ref, goth_ref, c_ref, out_ref, one_ref, two_ref):
     core, turn = s_ref[CORE], s_ref[TURN]
     feats = own_ref.shape[0]
     half = feats // 2
@@ -409,13 +390,20 @@
         return carry
 
     lax.fori_loop(0, 2, first, 0)
-    right_two = jnp.concatenate([columns_of(1), one_ref[...]], axis=0)
+    two_ref[...] = columns_of(1)
+
+    def couple(i, carry):
+        here = pl.ds(pl.multiple_of(i * half, half), half)
+        side = jnp.where((core ^ i) == 0, gown_ref[...], goth_ref[...])
+        two_ref[here, :] = two_ref[here, :] - dot_full(side, one_ref[...])
+        return carry
+
+    lax.fori_loop(0, 2, couple, 0)
 
     def second(i, carry):
         here = pl.ds(pl.multiple_of(i * half, half), half)
         there = pl.ds(pl.multiple_of(feats + i * half, half), half)
-        left = jnp.where(core == 0, oth_ref[here, :], own_ref[here, :])
-        two = dot_full(jnp.concatenate([left, -b_ref[here, :]], axis=1), right_two)
+        two = dot_full(jnp.where(core == 0, oth_ref[here, :], own_ref[here, :]), two_ref[...])
         for k in range(2):
             out_ref[k, there, :] = two[:, k * width : (k + 1) * width]
         return carry
@@ -423,10 +411,10 @@
     lax.fori_loop(0, 2, second, 0)
 
 
-def solve(scalars, own, oth, coupling, crossed):
+def solve(scalars, own, oth, side, side_oth, crossed):
     count, height, width = crossed.shape
     feats = own.shape[0]
-    whole = pl.BlockSpec((feats, feats), lambda k, s: (0, 0))
+    whole = pl.BlockSpec(memory_space=pltpu.VMEM)
     pair = pl.BlockSpec((2, height, width), lambda k, s: (k, 0, 0))
     return pl.pallas_call(
         solve_kernel,
@@ -434,19 +422,19 @@
         grid_spec=pltpu.PrefetchScalarGridSpec(
             num_scalar_prefetch=1,
             grid=(count // 2,),
-            in_specs=[whole] * 3 + [pair],
+            in_specs=[whole] * 4 + [pair],
             out_specs=pair,
-            scratch_shapes=[pltpu.VMEM((feats, 2 * width), F32)],
+            scratch_shapes=[pltpu.VMEM((feats, 2 * width), F32)] * 2,
         ),
         compiler_params=params(),
         cost_estimate=cost(36 * feats * feats * count * width, 8 * count * height * width),
         name="solve",
-    )(scalars, own, oth, coupling, crossed)
-
-
-def residual_kernel(s_ref, t_ref, ah, al, bh, bl, wa_ref, wb_ref, *rest):
+    )(scalars, own, oth, side, side_oth, crossed)
+
+
+def residual_kernel(only, s_ref, t_ref, ah, al, bh, bl, wa_ref, wb_ref, *rest):
     r_ref, w_ref = rest[-2:]
-    own = pl.program_id(0) == 0
+    own = pl.program_id(0) + only == 0
     half = t_ref.shape[0]
     swap, core = jnp.where(own, s_ref[BASE_OWN], s_ref[BASE_OTH]) & 1, s_ref[CORE]
     feats = ah.shape[1]
@@ -464,26 +452,26 @@
     r_ref[...] = t_ref[...] - fitted
 
 
-def residual_part(group, pair, scalars, targets, mine, other, weights, weights_oth, before):
+def residual_part(group, pair, sides, scalars, targets, mine, other, weights, weights_oth, before):
     rows, columns = targets.shape
     feats = mine[0].shape[1]
     _, _, width = weights.shape
     whole = pl.BlockSpec(memory_space=pltpu.VMEM)
 
     def place(k, s):
-        return 4 * group + ((jnp.where(k == 0, s[BASE_OWN], s[BASE_OTH]) >> 1) ^ pair)
+        return 4 * group + ((jnp.where(k + sides[0] == 0, s[BASE_OWN], s[BASE_OTH]) >> 1) ^ pair)
 
     block = pl.BlockSpec((rows // 2, 2 * width), lambda k, i, s: (i, place(k, s)))
     anywhere = pl.BlockSpec(memory_space=pl.ANY)
     return pl.pallas_call(
-        residual_kernel,
+        functools.partial(residual_kernel, sides[0]),
         out_shape=[
             jax.ShapeDtypeStruct((rows, columns), F32),
             jax.ShapeDtypeStruct((2, feats, columns), F32),
         ],
         grid_spec=pltpu.PrefetchScalarGridSpec(
             num_scalar_prefetch=1,
-            grid=(2, 2),
+            grid=(len(sides), 2),
             in_specs=[block] + [whole] * 6 + [anywhere] * len(before),
             out_specs=[block, pl.BlockSpec((2, feats, 2 * width), lambda k, i, s: (0, 0, place(k, s)))],
         ),
@@ -593,17 +581,19 @@
         matrix = factor(step, matrix)
     inverse = matrix
     inverse_oth = exchange(inverse, 1)
-    coupling = couple(scalars, inverse, inverse_oth, side, side_oth)
     parts = []
     for value in crossed:
-        near_part = solve(scalars, inverse, inverse_oth, coupling, value)
+        near_part = solve(scalars, inverse, inverse_oth, side, side_oth, value)
         parts.append((near_part, exchange(near_part, 2, 4)))
     outs = ()
     for pair in range(2):
         for group in range(2):
             value = parts[group][pair]
             value_oth = exchange(value, 1)
-            outs = residual_part(group, pair, scalars, targets, mine, other, value, value_oth, tuple(outs))
+            last = group + pair == 2
+            for sides in ((0,), (1,)) if last else ((0, 1),):
+                held = value if sides == (0,) else value_oth
+                outs = residual_part(group, pair, sides, scalars, targets, mine, other, value, held, tuple(outs))
     return tuple(outs)
 
 

time: 288 us -> 287 us (level)
  no operation moved by 1% of the time
where the time goes in v6:
time: 287 us
  waiting for transfers between devices  113 us (39%)
  Pallas kernels  109 us (38%)
  starting transfers between devices  59.4 us (21%)
  local copies, waits for them, and re-layouts  3.11 us (1%)
    ppermute x43, waiting for transfers between devices, exchange(): return lax.ppermute(value, ALL, pairs)  113 us
    ppermute x43, starting transfers between devices, exchange(): return lax.ppermute(value, ALL, pairs)  59.4 us
    pallas_call x5, Pallas kernels, residual_part(): pl.pallas_call(functools.partial(residual_kernel, sides[0]), out_shape=[j...  25.7 us
    pallas_call x3, Pallas kernels, factor(): pl.pallas_call(functools.partial(factor_kernel, step), out_shape=jax.Shap...  20.6 us
    pallas_call x4, Pallas kernels, cross(): pl.pallas_call(functools.partial(cross_kernel, base), out_shape=jax.Shape...  20.5 us
    pallas_call x4, Pallas kernels, features(): pl.pallas_call(functools.partial(features_kernel, quarter, slot, part), o...  18.2 us
    pallas_call x2, Pallas kernels, solve(): pl.pallas_call(solve_kernel, out_shape=jax.ShapeDtypeStruct(crossed.shape...  9.42 us
    pallas_call x1, Pallas kernels, assemble(): pl.pallas_call(assemble_kernel, out_shape=[jax.ShapeDtypeStruct((2 * half...  7.47 us
  transfers between devices with their start and end apart: 43, of which 24 were waited for; matrix products, arithmetic and copies ran while one was open for 1% of the time, Pallas kernels for 28%

profile of v6, /device:TPU:0, one launch (start us, length us, event | category | flops | bytes accessed | tf_op | source)
XLA Modules:
  0.0 286.9 jit_solution(2344378804368778141)
XLA Ops:
  7.1 2.9 %collective-permute-start.2 = (f32[2,448,128]{2,1,0:T(8,128)S(1)}, f32[2,448,128]{2,1,0:T(8,128)S(1)}, u32[]{:S(2)}, u32[]{:S(2)}) collective-permute-start(f32[2,448,128]{2,1,0:T(8,128)S(1)} %slice.113), channel_id=1, source_target_pairs={{0,2},{1,5},{2,0},{3,7},{4,6},{5,1},{6,4},{7,3},{8,10},{9,13},{10,... | collective-permute-start | bytes 1376264 | tf_op jit(solution)/shard_map/ppermute | solution.py:502
  10.0 6.5 %collective-permute-done.2 = f32[2,448,128]{2,1,0:T(8,128)S(1)} collective-permute-done((f32[2,448,128]{2,1,0:T(8,128)S(1)}, f32[2,448,128]{2,1,0:T(8,128)S(1)}, u32[]{:S(2)}, u32[]{:S(2)}) %collective-permute-start.2) | collective-permute-done | bytes 458784 | tf_op jit(solution)/shard_map/ppermute | solution.py:502
  18.7 4.0 %collective-permute-done.3 = f32[1,448,128]{2,1,0:T(8,128)S(1)} collective-permute-done((f32[1,448,128]{2,1,0:T(8,128)S(1)}, f32[1,448,128]{2,1,0:T(8,128)S(1)}, u32[]{:S(2)}, u32[]{:S(2)}) %collective-permute-start.3) | collective-permute-done | bytes 229408 | tf_op jit(solution)/shard_map/ppermute | solution.py:502
  24.9 4.2 %collective-permute-done.4 = f32[1,448,128]{2,1,0:T(8,128)S(1)} collective-permute-done((f32[1,448,128]{2,1,0:T(8,128)S(1)}, f32[1,448,128]{2,1,0:T(8,128)S(1)}, u32[]{:S(2)}, u32[]{:S(2)}) %collective-permute-start.4) | collective-permute-done | bytes 229408 | tf_op jit(solution)/shard_map/ppermute | solution.py:502
  29.1 3.1 %collective-permute-start.5 = (f32[1,448,128]{2,1,0:T(8,128)S(1)}, f32[1,448,128]{2,1,0:T(8,128)S(1)}, u32[]{:S(2)}, u32[]{:S(2)}) collective-permute-start(f32[1,448,128]{2,1,0:T(8,128)S(1)} %add.109), channel_id=1, source_target_pairs={{0,16},{1,17},{2,18},{3,19},{4,20},{5,21},{6,22},{7,23},{8,24},{9,... | collective-permute-start | bytes 688136 | tf_op jit(solution)/shard_map/ppermute | solution.py:502
  32.1 8.2 %collective-permute-done.5 = f32[1,448,128]{2,1,0:T(8,128)S(1)} collective-permute-done((f32[1,448,128]{2,1,0:T(8,128)S(1)}, f32[1,448,128]{2,1,0:T(8,128)S(1)}, u32[]{:S(2)}, u32[]{:S(2)}) %collective-permute-start.5) | collective-permute-done | bytes 229408 | tf_op jit(solution)/shard_map/ppermute | solution.py:502
  41.6 4.8 %collective-permute-done.6 = f32[1,448,128]{2,1,0:T(8,128)S(1)} collective-permute-done((f32[1,448,128]{2,1,0:T(8,128)S(1)}, f32[1,448,128]{2,1,0:T(8,128)S(1)}, u32[]{:S(2)}, u32[]{:S(2)}) %collective-permute-start.6) | collective-permute-done | bytes 229408 | tf_op jit(solution)/shard_map/ppermute | solution.py:502
  47.7 7.3 %collective-permute-done.7.p_ref = f32[2,448,128]{2,1,0:T(8,128)S(1)} collective-permute-done((f32[2,448,128]{2,1,0:T(8,128)S(1)}, f32[2,448,128]{2,1,0:T(8,128)S(1)}, u32[]{:S(2)}, u32[]{:S(2)}) %collective-permute-start.7) | collective-permute-done | bytes 458784 | tf_op jit(solution)/shard_map/ppermute | solution.py:502
  55.0 4.5 %features.4 = (bf16[1024,512]{1,0:T(8,128)(2,1)S(1)}, bf16[1024,512]{1,0:T(8,128)(2,1)S(1)}, bf16[1024,1024]{1,0:T(8,128)(2,1)S(1)}, bf16[1024,1024]{1,0:T(8,128)(2,1)S(1)}) custom-call(s32[9]{0:T(128)S(1)} %stack.39.s_ref, f32[440,1024]{1,0:T(8,128)S(1)} %bitcast.14, f32[2,448,128]{2,1,0:T(8,128)S(1)} %pad_maximum_fusion.5.p_ref), custom_call_target="tpu_custom_call" | custom-call | flops 1384120320 | bytes 3899392 | tf_op jit(solution)/shard_map/features/pallas_call | solution.py:128
  59.6 4.5 %features.5 = (bf16[1024,512]{1,0:T(8,128)(2,1)S(1)}, bf16[1024,512]{1,0:T(8,128)(2,1)S(1)}, bf16[1024,1024]{1,0:T(8,128)(2,1)S(1)}, bf16[1024,1024]{1,0:T(8,128)(2,1)S(1)}) custom-call(s32[9]{0:T(128)S(1)} %stack.39.s_ref, f32[440,1024]{1,0:T(8,128)S(1)} %bitcast.15, ...), custom_call_target="tpu_custom_call", output_to_operand_aliasing={{2}: (3, {}), {3}: (4, {})} | custom-call | flops 1384120320 | bytes 3899392 | tf_op jit(solution)/shard_map/features/pallas_call | solution.py:128
  64.1 4.5 %features.6 = (bf16[1024,512]{1,0:T(8,128)(2,1)S(1)}, bf16[1024,512]{1,0:T(8,128)(2,1)S(1)}, bf16[1024,1024]{1,0:T(8,128)(2,1)S(1)}, bf16[1024,1024]{1,0:T(8,128)(2,1)S(1)}) custom-call(s32[9]{0:T(128)S(1)} %stack.39.s_ref, f32[440,1024]{1,0:T(8,128)S(1)} %bitcast.16, ...), custom_call_target="tpu_custom_call", output_to_operand_aliasing={{0}: (3, {}), {1}: (4, {}), {2}: (5, {}), {3}: (6, {})} | custom-call | flops 1384120320 | bytes 3899392 | tf_op jit(solution)/shard_map/features/pallas_call | solution.py:128
  68.7 4.5 %features.7 = (bf16[1024,512]{1,0:T(8,128)(2,1)S(1)}, bf16[1024,512]{1,0:T(8,128)(2,1)S(1)}, bf16[1024,1024]{1,0:T(8,128)(2,1)S(1)}, bf16[1024,1024]{1,0:T(8,128)(2,1)S(1)}) custom-call(s32[9]{0:T(128)S(1)} %stack.39.s_ref, f32[440,1024]{1,0:T(8,128)S(1)} %bitcast.17, ...), custom_call_target="tpu_custom_call", output_to_operand_aliasing={{0}: (3, {}), {1}: (4, {}), {2}: (5, {}), {3}: (6, {})} | custom-call | flops 1384120320 | bytes 3899392 | tf_op jit(solution)/shard_map/features/pallas_call | solution.py:128
  73.3 3.0 %gram.2 = f32[16,5,16,256]{3,2,1,0:T(8,128)S(1)} custom-call(s32[9]{0:T(128)S(1)} %stack.39.s_ref, bf16[1024,512]{1,0:T(8,128)(2,1)S(1)} %get-tuple-element.46.ah, bf16[1024,512]{1,0:T(8,128)(2,1)S(1)} %get-tuple-element.47.al, bf16[1024,512]{1,0:T(8,128)(2,1)S(1)} %get-tuple-element.52.bh, bf16[1024,512]{1,0:T(8,128)(2,1)S(1)} %get-tuple-element.53.bl, ...), custom_call_target="tpu_custom_call" | custom-call | flops 2013265920 | bytes 8388608 | tf_op jit(solution)/shard_map/gram/pallas_call | solution.py:180
  76.3 5.1 %cross.4 = f32[4,1024,128]{2,1,0:T(8,128)S(1)} custom-call(s32[9]{0:T(128)S(1)} %stack.39.s_ref, f32[1024,2048]{1,0:T(8,128)S(1)} %bitcast.13, bf16[1024,1024]{1,0:T(8,128)(2,1)S(1)} %get-tuple-element.64.th, bf16[1024,1024]{1,0:T(8,128)(2,1)S(1)} %get-tuple-element.65.tl), custom_call_target="tpu_custom_call" | custom-call | flops 3221225472 | bytes 4194304 | tf_op jit(solution)/shard_map/cross/pallas_call | solution.py:220
  82.0 3.1 %gram.3 = f32[16,5,16,256]{3,2,1,0:T(8,128)S(1)} custom-call(s32[9]{0:T(128)S(1)} %stack.39.s_ref, bf16[1024,512]{1,0:T(8,128)(2,1)S(1)} %get-tuple-element.46.ah, bf16[1024,512]{1,0:T(8,128)(2,1)S(1)} %get-tuple-element.47.al, bf16[1024,512]{1,0:T(8,128)(2,1)S(1)} %get-tuple-element.52.bh, bf16[1024,512]{1,0:T(8,128)(2,1)S(1)} %get-tuple-element.53.bl, ...), custom_call_target="tpu_custom_call" | custom-call | flops 2013265920 | bytes 8388608 | tf_op jit(solution)/shard_map/gram/pallas_call | solution.py:180
  85.2 2.5 collective-permute-done.10
  87.9 5.1 %cross.5 = f32[4,1024,128]{2,1,0:T(8,128)S(1)} custom-call(s32[9]{0:T(128)S(1)} %stack.39.s_ref, f32[1024,2048]{1,0:T(8,128)S(1)} %bitcast.13, bf16[1024,1024]{1,0:T(8,128)(2,1)S(1)} %get-tuple-element.64.th, bf16[1024,1024]{1,0:T(8,128)(2,1)S(1)} %get-tuple-element.65.tl, f32[4,1024,128]{2,1,0:T(8,128)S(1)} %collective-permute-done.13.rest_0_), custom_call_target="tpu_custom_call" | custom-call | flops 3221225472 | bytes 4194304 | tf_op jit(solution)/shard_map/cross/pallas_call | solution.py:220
  93.0 5.1 %cross.6 = f32[4,1024,128]{2,1,0:T(8,128)S(1)} custom-call(s32[9]{0:T(128)S(1)} %stack.39.s_ref, f32[1024,2048]{1,0:T(8,128)S(1)} %bitcast.13, bf16[1024,1024]{1,0:T(8,128)(2,1)S(1)} %get-tuple-element.64.th, bf16[1024,1024]{1,0:T(8,128)(2,1)S(1)} %get-tuple-element.65.tl), custom_call_target="tpu_custom_call" | custom-call | flops 3221225472 | bytes 4194304 | tf_op jit(solution)/shard_map/cross/pallas_call | solution.py:220
  100.9 8.4 %collective-permute-done.11 = f32[8,5,16,256]{3,2,1,0:T(8,128)S(1)} collective-permute-done((f32[8,5,16,256]{3,2,1,0:T(8,128)S(1)}, f32[8,5,16,256]{3,2,1,0:T(8,128)S(1)}, u32[]{:S(2)}, u32[]{:S(2)}) %collective-permute-start.11) | collective-permute-done | bytes 655392 | tf_op jit(solution)/shard_map/ppermute | solution.py:502
  110.7 9.4 %collective-permute-done.12 = f32[4,5,16,256]{3,2,1,0:T(8,128)S(1)} collective-permute-done((f32[4,5,16,256]{3,2,1,0:T(8,128)S(1)}, f32[4,5,16,256]{3,2,1,0:T(8,128)S(1)}, u32[]{:S(2)}, u32[]{:S(2)}) %collective-permute-start.12) | collective-permute-done | bytes 327712 | tf_op jit(solution)/shard_map/ppermute | solution.py:502
  120.1 3.9 %collective-permute-done.32 = f32[2,1024,128]{2,1,0:T(8,128)S(1)} collective-permute-done((f32[2,1024,128]{2,1,0:T(8,128)S(1)}, f32[2,1024,128]{2,1,0:T(8,128)S(1)}, u32[]{:S(2)}, u32[]{:S(2)}) %collective-permute-start.32) | collective-permute-done | bytes 1048608 | tf_op jit(solution)/shard_map/ppermute | solution.py:502
  125.5 5.1 %cross.7 = f32[4,1024,128]{2,1,0:T(8,128)S(1)} custom-call(s32[9]{0:T(128)S(1)} %stack.39.s_ref, f32[1024,2048]{1,0:T(8,128)S(1)} %bitcast.13, bf16[1024,1024]{1,0:T(8,128)(2,1)S(1)} %get-tuple-element.64.th, bf16[1024,1024]{1,0:T(8,128)(2,1)S(1)} %get-tuple-element.65.tl, f32[4,1024,128]{2,1,0:T(8,128)S(1)} %collective-permute-done.14.rest_0_), custom_call_target="tpu_custom_call" | custom-call | flops 3221225472 | bytes 4194304 | tf_op jit(solution)/shard_map/cross/pallas_call | solution.py:220
  131.4 4.6 %collective-permute-done.15 = f32[2,5,16,256]{3,2,1,0:T(8,128)S(1)} collective-permute-done((f32[2,5,16,256]{3,2,1,0:T(8,128)S(1)}, f32[2,5,16,256]{3,2,1,0:T(8,128)S(1)}, u32[]{:S(2)}, u32[]{:S(2)}) %collective-permute-start.15) | collective-permute-done | bytes 163872 | tf_op jit(solution)/shard_map/ppermute | solution.py:502
  141.8 2.7 collective-permute-start.17
  149.3 3.2 %collective-permute-start.35 = (f32[1,256,128]{2,1,0:T(8,128)S(1)}, f32[1,256,128]{2,1,0:T(8,128)S(1)}, u32[]{:S(2)}, u32[]{:S(2)}) collective-permute-start(f32[1,256,128]{2,1,0:T(8,128)S(1)} %slice.135), channel_id=1, source_target_pairs={{0,16},{1,17},{2,18},{3,19},{4,20},{5,21},{6,22},{7,23},{8,24},{9,... | collective-permute-start | bytes 393224 | tf_op jit(solution)/shard_map/ppermute | solution.py:502
  152.7 2.8 collective-permute-start.19
  155.5 3.1 %collective-permute-done.35 = f32[1,256,128]{2,1,0:T(8,128)S(1)} collective-permute-done((f32[1,256,128]{2,1,0:T(8,128)S(1)}, f32[1,256,128]{2,1,0:T(8,128)S(1)}, u32[]{:S(2)}, u32[]{:S(2)}) %collective-permute-start.35) | collective-permute-done | bytes 131104 | tf_op jit(solution)/shard_map/ppermute | solution.py:502
  160.6 5.9 %collective-permute-start.20 = (f32[8,5,16,256]{3,2,1,0:T(8,128)S(1)}, f32[8,5,16,256]{3,2,1,0:T(8,128)S(1)}, u32[]{:S(2)}, u32[]{:S(2)}) collective-permute-start(f32[8,5,16,256]{3,2,1,0:T(8,128)S(1)} %pad_maximum_fusion.2), channel_id=1, source_target_pairs={{0,2},{1,5},{2,0},{3,7},{4,6},{5,1},{6,4},{7,3},{8,10},{9,13},{10,... | collective-permute-start | bytes 1966088 | tf_op jit(solution)/shard_map/ppermute | solution.py:502
  166.5 3.1 %collective-permute-start.37 = (f32[1,512,128]{2,1,0:T(8,128)S(1)}, f32[1,512,128]{2,1,0:T(8,128)S(1)}, u32[]{:S(2)}, u32[]{:S(2)}) collective-permute-start(f32[1,512,128]{2,1,0:T(8,128)S(1)} %pad_maximum_fusion.8), channel_id=1, source_target_pairs={{0,8},{1,9},{2,10},{3,11},{4,12},{5,13},{6,14},{7,15},{8,0},{9,1},... | collective-permute-start | bytes 786440 | tf_op jit(solution)/shard_map/ppermute | solution.py:502
  170.0 8.4 %collective-permute-done.20 = f32[8,5,16,256]{3,2,1,0:T(8,128)S(1)} collective-permute-done((f32[8,5,16,256]{3,2,1,0:T(8,128)S(1)}, f32[8,5,16,256]{3,2,1,0:T(8,128)S(1)}, u32[]{:S(2)}, u32[]{:S(2)}) %collective-permute-start.20) | collective-permute-done | bytes 655392 | tf_op jit(solution)/shard_map/ppermute | solution.py:502
  178.4 7.5 %assemble.1 = (f32[512,512]{1,0:T(8,128)S(1)}, f32[256,512]{1,0:T(8,128)S(1)}) custom-call(s32[9]{0:T(128)S(1)} %stack.39.s_ref, f32[16,5,16,256]{3,2,1,0:T(8,128)S(1)} %constant_dynamic-update-slice_fusion.g_ref), custom_call_target="tpu_custom_call" | custom-call | flops 10000000000 | bytes 4000000 | tf_op jit(solution)/shard_map/assemble/pallas_call | solution.py:337
  185.9 6.5 %factor.3.m_ref = f32[512,512]{1,0:T(8,128)S(1)} custom-call(f32[512,512]{1,0:T(8,128)S(1)} %get-tuple-element.67.m_ref), custom_call_target="tpu_custom_call" | custom-call | flops 10000000000 | bytes 4000000 | tf_op jit(solution)/shard_map/factor/pallas_call | solution.py:359
  193.5 6.3 %factor.4.m_ref = f32[512,512]{1,0:T(8,128)S(1)} custom-call(f32[512,512]{1,0:T(8,128)S(1)} %factor.3.m_ref), custom_call_target="tpu_custom_call" | custom-call | flops 10000000000 | bytes 4000000 | tf_op jit(solution)/shard_map/factor/pallas_call | solution.py:359
  200.0 4.1 %collective-permute-start.26 = (f32[1,256,128]{2,1,0:T(8,128)S(1)}, f32[1,256,128]{2,1,0:T(8,128)S(1)}, u32[]{:S(2)}, u32[]{:S(2)}) collective-permute-start(f32[1,256,128]{2,1,0:T(8,128)S(1)} %slice.127), channel_id=1, source_target_pairs={{0,16},{1,17},{2,18},{3,19},{4,20},{5,21},{6,22},{7,23},{8,24},{9,... | collective-permute-start | bytes 393224 | tf_op jit(solution)/shard_map/ppermute | solution.py:502
  204.1 7.8 %factor.5.own_ref = f32[512,512]{1,0:T(8,128)S(1)} custom-call(f32[512,512]{1,0:T(8,128)S(1)} %factor.4.m_ref), custom_call_target="tpu_custom_call" | custom-call | flops 10000000000 | bytes 4000000 | tf_op jit(solution)/shard_map/factor/pallas_call | solution.py:359
  212.2 8.9 %collective-permute-done.27 = f32[1,256,128]{2,1,0:T(8,128)S(1)} collective-permute-done((f32[1,256,128]{2,1,0:T(8,128)S(1)}, f32[1,256,128]{2,1,0:T(8,128)S(1)}, u32[]{:S(2)}, u32[]{:S(2)}) %collective-permute-start.27) | collective-permute-done | bytes 131104 | tf_op jit(solution)/shard_map/ppermute | solution.py:502
  221.3 8.1 %collective-permute-done.28 = f32[1,512,128]{2,1,0:T(8,128)S(1)} collective-permute-done((f32[1,512,128]{2,1,0:T(8,128)S(1)}, f32[1,512,128]{2,1,0:T(8,128)S(1)}, u32[]{:S(2)}, u32[]{:S(2)}) %collective-permute-start.28) | collective-permute-done | bytes 262176 | tf_op jit(solution)/shard_map/ppermute | solution.py:502
  229.7 4.7 %solve.3.wa_ref = f32[2,1024,128]{2,1,0:T(8,128)S(1)} custom-call(s32[9]{0:T(128)S(1)} %stack.39.s_ref, f32[512,512]{1,0:T(8,128)S(1)} %factor.5.own_ref, f32[512,512]{1,0:T(8,128)S(1)} %collective-permute-done.21.oth_ref, f32[256,512]{1,0:T(8,128)S(1)} %get-tuple-element.68.gown_ref, f32[256,512]{1,0:T(8,128)S(1)} %collective-permute-done.22.goth_ref, ...), custom_call_target="tpu_custom_call" | custom-call | flops 2415919104 | bytes 2097152 | tf_op jit(solution)/shard_map/solve/pallas_call | solution.py:419
  234.5 2.2 collective-permute-start.39
  236.7 2.6 collective-permute-done.29
  239.4 4.7 %solve.2.wa_ref = f32[2,1024,128]{2,1,0:T(8,128)S(1)} custom-call(s32[9]{0:T(128)S(1)} %stack.39.s_ref, f32[512,512]{1,0:T(8,128)S(1)} %factor.5.own_ref, f32[512,512]{1,0:T(8,128)S(1)} %collective-permute-done.21.oth_ref, f32[256,512]{1,0:T(8,128)S(1)} %get-tuple-element.68.gown_ref, f32[256,512]{1,0:T(8,128)S(1)} %collective-permute-done.22.goth_ref, ...), custom_call_target="tpu_custom_call" | custom-call | flops 2415919104 | bytes 2097152 | tf_op jit(solution)/shard_map/solve/pallas_call | solution.py:419
  244.1 4.1 %collective-permute-start.30 = (f32[2,1024,128]{2,1,0:T(8,128)S(1)}, f32[2,1024,128]{2,1,0:T(8,128)S(1)}, u32[]{:S(2)}, u32[]{:S(2)}) collective-permute-start(f32[2,1024,128]{2,1,0:T(8,128)S(1)} %solve.2.wa_ref), channel_id=1, source_target_pairs={{0,2},{1,5},{2,0},{3,7},{4,6},{5,1},{6,4},{7,3},{8,10},{9,13},{10,... | collective-permute-start | bytes 3145736 | tf_op jit(solution)/shard_map/ppermute | solution.py:502
  250.1 10.9 %collective-permute-done.30.wa_ref.wb_ref = f32[2,1024,128]{2,1,0:T(8,128)S(1)} collective-permute-done((f32[2,1024,128]{2,1,0:T(8,128)S(1)}, f32[2,1024,128]{2,1,0:T(8,128)S(1)}, u32[]{:S(2)}, u32[]{:S(2)}) %collective-permute-start.30) | collective-permute-done | bytes 1048608 | tf_op jit(solution)/shard_map/ppermute | solution.py:502
  261.1 6.1 %residual.5 = (f32[1024,2048]{1,0:T(8,128)}, f32[2,512,2048]{2,1,0:T(8,128)}) custom-call(s32[9]{0:T(128)S(1)} %stack.39.s_ref, f32[1024,2048]{1,0:T(8,128)S(1)} %bitcast.13, bf16[1024,512]{1,0:T(8,128)(2,1)S(1)} %get-tuple-element.46.ah, bf16[1024,512]{1,0:T(8,128)(2,1)S(1)} %get-tuple-element.47.al, bf16[1024,512]{1,0:T(8,128)(2,1)S(1)} %get-tuple-element.52.bh, ...), custom_call_target="tpu_custom_call" | custom-call | flops 3221225472 | bytes 6291456 | tf_op jit(solution)/shard_map/residual/pallas_call | solution.py:466
  267.2 6.1 %residual.6 = (f32[1024,2048]{1,0:T(8,128)}, f32[2,512,2048]{2,1,0:T(8,128)}) custom-call(s32[9]{0:T(128)S(1)} %stack.39.s_ref, f32[1024,2048]{1,0:T(8,128)S(1)} %bitcast.13, bf16[1024,512]{1,0:T(8,128)(2,1)S(1)} %get-tuple-element.46.ah, bf16[1024,512]{1,0:T(8,128)(2,1)S(1)} %get-tuple-element.47.al, ...), custom_call_target="tpu_custom_call", output_to_operand_aliasing={{0}: (8, {}), {1}: (9, {})} | custom-call | flops 3221225472 | bytes 6291456 | tf_op jit(solution)/shard_map/residual/pallas_call | solution.py:466
  273.4 6.1 %residual.7 = (f32[1024,2048]{1,0:T(8,128)}, f32[2,512,2048]{2,1,0:T(8,128)}) custom-call(s32[9]{0:T(128)S(1)} %stack.39.s_ref, f32[1024,2048]{1,0:T(8,128)S(1)} %bitcast.13, bf16[1024,512]{1,0:T(8,128)(2,1)S(1)} %get-tuple-element.46.ah, bf16[1024,512]{1,0:T(8,128)(2,1)S(1)} %get-tuple-element.47.al, ...), custom_call_target="tpu_custom_call", output_to_operand_aliasing={{0}: (8, {}), {1}: (9, {})} | custom-call | flops 3221225472 | bytes 6291456 | tf_op jit(solution)/shard_map/residual/pallas_call | solution.py:466
  279.5 3.7 %residual.8 = (f32[1024,2048]{1,0:T(8,128)}, f32[2,512,2048]{2,1,0:T(8,128)}) custom-call(s32[9]{0:T(128)S(1)} %stack.39.s_ref, f32[1024,2048]{1,0:T(8,128)S(1)} %bitcast.13, bf16[1024,512]{1,0:T(8,128)(2,1)S(1)} %get-tuple-element.46.ah, bf16[1024,512]{1,0:T(8,128)(2,1)S(1)} %get-tuple-element.47.al, ...), custom_call_target="tpu_custom_call", output_to_operand_aliasing={{0}: (8, {}), {1}: (9, {})} | custom-call | flops 3221225472 | bytes 6291456 | tf_op jit(solution)/shard_map/residual/pallas_call | solution.py:466
  283.2 3.7 %residual.9 = (f32[1024,2048]{1,0:T(8,128)}, f32[2,512,2048]{2,1,0:T(8,128)}) custom-call(s32[9]{0:T(128)S(1)} %stack.39.s_ref, f32[1024,2048]{1,0:T(8,128)S(1)} %bitcast.13, bf16[1024,512]{1,0:T(8,128)(2,1)S(1)} %get-tuple-element.46.ah, bf16[1024,512]{1,0:T(8,128)(2,1)S(1)} %get-tuple-element.47.al, ...), custom_call_target="tpu_custom_call", output_to_operand_aliasing={{0}: (8, {}), {1}: (9, {})} | custom-call | flops 3221225472 | bytes 6291456 | tf_op jit(solution)/shard_map/residual/pallas_call | solution.py:466
  (119 shorter events, 37.8 us)
Async XLA Ops:
  0.6 2.9 collective-permute-start
  1.2 2.3 collective-permute-start.1
  3.5 1.2 copy-start.1
  4.7 0.7 copy-start.2
  7.1 47.9 %copy-start = (f32[1024,440]{0,1:T(8,128)S(1)}, f32[1024,440]{0,1:T(8,128)}, u32[]{:S(2)}) copy-start(f32[1024,440]{0,1:T(8,128)} %param.5) | copy-start | bytes 5406724
  7.1 9.4 %collective-permute-start.2 = (f32[2,448,128]{2,1,0:T(8,128)S(1)}, f32[2,448,128]{2,1,0:T(8,128)S(1)}, u32[]{:S(2)}, u32[]{:S(2)}) collective-permute-start(f32[2,448,128]{2,1,0:T(8,128)S(1)} %slice.113), channel_id=1, source_target_pairs={{0,2},{1,5},{2,0},{3,7},{4,6},{5,1},{6,4},{7,3},{8,10},{9,13},{10,... | collective-permute-start | bytes 1376264 | tf_op jit(solution)/shard_map/ppermute | solution.py:502
  16.6 6.1 %collective-permute-start.3 = (f32[1,448,128]{2,1,0:T(8,128)S(1)}, f32[1,448,128]{2,1,0:T(8,128)S(1)}, u32[]{:S(2)}, u32[]{:S(2)}) collective-permute-start(f32[1,448,128]{2,1,0:T(8,128)S(1)} %slice.115), channel_id=1, source_target_pairs={{0,4},{1,3},{2,6},{3,1},{4,0},{5,7},{6,2},{7,5},{8,12},{9,11},{10,... | collective-permute-start | bytes 688136 | tf_op jit(solution)/shard_map/ppermute | solution.py:502
  22.7 6.3 %collective-permute-start.4 = (f32[1,448,128]{2,1,0:T(8,128)S(1)}, f32[1,448,128]{2,1,0:T(8,128)S(1)}, u32[]{:S(2)}, u32[]{:S(2)}) collective-permute-start(f32[1,448,128]{2,1,0:T(8,128)S(1)} %slice_add_fusion.9), channel_id=1, source_target_pairs={{0,8},{1,9},{2,10},{3,11},{4,12},{5,13},{6,14},{7,15},{8,0},{9,1},... | collective-permute-start | bytes 688136 | tf_op jit(solution)/shard_map/ppermute | solution.py:502
  29.1 11.2 %collective-permute-start.5 = (f32[1,448,128]{2,1,0:T(8,128)S(1)}, f32[1,448,128]{2,1,0:T(8,128)S(1)}, u32[]{:S(2)}, u32[]{:S(2)}) collective-permute-start(f32[1,448,128]{2,1,0:T(8,128)S(1)} %add.109), channel_id=1, source_target_pairs={{0,16},{1,17},{2,18},{3,19},{4,20},{5,21},{6,22},{7,23},{8,24},{9,... | collective-permute-start | bytes 688136 | tf_op jit(solution)/shard_map/ppermute | solution.py:502
  40.3 6.1 %collective-permute-start.6 = (f32[1,448,128]{2,1,0:T(8,128)S(1)}, f32[1,448,128]{2,1,0:T(8,128)S(1)}, u32[]{:S(2)}, u32[]{:S(2)}) collective-permute-start(f32[1,448,128]{2,1,0:T(8,128)S(1)} %add.110), channel_id=1, source_target_pairs={{0,4},{1,3},{2,6},{3,1},{4,0},{5,7},{6,2},{7,5},{8,12},{9,11},{10,... | collective-permute-start | bytes 688136 | tf_op jit(solution)/shard_map/ppermute | solution.py:502
  46.5 8.5 %collective-permute-start.7 = (f32[2,448,128]{2,1,0:T(8,128)S(1)}, f32[2,448,128]{2,1,0:T(8,128)S(1)}, u32[]{:S(2)}, u32[]{:S(2)}) collective-permute-start(f32[2,448,128]{2,1,0:T(8,128)S(1)} %pad_maximum_fusion.5.p_ref), channel_id=1, source_target_pairs={{0,2},{1,5},{2,0},{3,7},{4,6},{5,1},{6,4},{7,3},{8,10},{9,13},{10,... | collective-permute-start | bytes 1376264 | tf_op jit(solution)/shard_map/ppermute | solution.py:502
  47.7 11.9 %collective-permute-start.8 = (f32[2,448,128]{2,1,0:T(8,128)S(1)}, f32[2,448,128]{2,1,0:T(8,128)S(1)}, u32[]{:S(2)}, u32[]{:S(2)}) collective-permute-start(f32[2,448,128]{2,1,0:T(8,128)S(1)} %pad_maximum_fusion.5.p_ref), channel_id=1, source_target_pairs={{0,1},{1,0},{2,3},{3,2},{4,5},{5,4},{6,7},{7,6},{8,9},{9,8},{10,11... | collective-permute-start | bytes 1376264 | tf_op jit(solution)/shard_map/ppermute | solution.py:502
  55.0 13.7 %collective-permute-start.9 = (f32[2,448,128]{2,1,0:T(8,128)S(1)}, f32[2,448,128]{2,1,0:T(8,128)S(1)}, u32[]{:S(2)}, u32[]{:S(2)}) collective-permute-start(f32[2,448,128]{2,1,0:T(8,128)S(1)} %collective-permute-done.7.p_ref), channel_id=1, source_target_pairs={{0,1},{1,0},{2,3},{3,2},{4,5},{5,4},{6,7},{7,6},{8,9},{9,8},{10,11... | collective-permute-start | bytes 1376264 | tf_op jit(solution)/shard_map/ppermute | solution.py:502
  68.7 7.5 %slice-start = ((s8[8388608]{0:T(1024)(128)(4,1)}), s8[4194304]{0:T(1024)(128)(4,1)S(1)}, s32[]{:S(2)}) async-start(s8[8388608]{0:T(1024)(128)(4,1)} %bitcast.12), calls=%async_computation | async-start | bytes 8388608
  73.3 3.0 %slice-start.1 = ((s8[8388608]{0:T(1024)(128)(4,1)}), s8[4194304]{0:T(1024)(128)(4,1)S(1)}, s32[]{:S(2)}) async-start(s8[8388608]{0:T(1024)(128)(4,1)} %bitcast.12), calls=%async_computation.1 | async-start | bytes 8388608
  81.4 6.5 %collective-permute-start.13 = (f32[4,1024,128]{2,1,0:T(8,128)S(1)}, f32[4,1024,128]{2,1,0:T(8,128)S(1)}, u32[]{:S(2)}, u32[]{:S(2)}) collective-permute-start(f32[4,1024,128]{2,1,0:T(8,128)S(1)} %cross.4), channel_id=1, source_target_pairs={{0,1},{1,0},{2,3},{3,2},{4,5},{5,4},{6,7},{7,6},{8,9},{9,8},{10,11... | collective-permute-start | bytes 6291464 | tf_op jit(solution)/shard_map/ppermute | solution.py:502
  82.0 5.7 %collective-permute-start.10 = (f32[16,5,16,256]{3,2,1,0:T(8,128)S(1)}, f32[16,5,16,256]{3,2,1,0:T(8,128)S(1)}, u32[]{:S(2)}, u32[]{:S(2)}) collective-permute-start(f32[16,5,16,256]{3,2,1,0:T(8,128)S(1)} %gram.2), channel_id=1, source_target_pairs={{0,1},{1,0},{2,3},{3,2},{4,5},{5,4},{6,7},{7,6},{8,9},{9,8},{10,11... | collective-permute-start | bytes 3932168 | tf_op jit(solution)/shard_map/ppermute | solution.py:502
  98.2 27.3 %collective-permute-start.14 = (f32[4,1024,128]{2,1,0:T(8,128)S(1)}, f32[4,1024,128]{2,1,0:T(8,128)S(1)}, u32[]{:S(2)}, u32[]{:S(2)}) collective-permute-start(f32[4,1024,128]{2,1,0:T(8,128)S(1)} %cross.6), channel_id=1, source_target_pairs={{0,1},{1,0},{2,3},{3,2},{4,5},{5,4},{6,7},{7,6},{8,9},{9,8},{10,11... | collective-permute-start | bytes 6291464 | tf_op jit(solution)/shard_map/ppermute | solution.py:502
  98.6 10.7 %collective-permute-start.11 = (f32[8,5,16,256]{3,2,1,0:T(8,128)S(1)}, f32[8,5,16,256]{3,2,1,0:T(8,128)S(1)}, u32[]{:S(2)}, u32[]{:S(2)}) collective-permute-start(f32[8,5,16,256]{3,2,1,0:T(8,128)S(1)} %slice.117), channel_id=1, source_target_pairs={{0,2},{1,5},{2,0},{3,7},{4,6},{5,1},{6,4},{7,3},{8,10},{9,13},{10,... | collective-permute-start | bytes 1966088 | tf_op jit(solution)/shard_map/ppermute | solution.py:502
  100.0 24.1 %collective-permute-start.32 = (f32[2,1024,128]{2,1,0:T(8,128)S(1)}, f32[2,1024,128]{2,1,0:T(8,128)S(1)}, u32[]{:S(2)}, u32[]{:S(2)}) collective-permute-start(f32[2,1024,128]{2,1,0:T(8,128)S(1)} %slice.129), channel_id=1, source_target_pairs={{0,2},{1,5},{2,0},{3,7},{4,6},{5,1},{6,4},{7,3},{8,10},{9,13},{10,... | collective-permute-start | bytes 3145736 | tf_op jit(solution)/shard_map/ppermute | solution.py:502
  109.4 10.6 %collective-permute-start.12 = (f32[4,5,16,256]{3,2,1,0:T(8,128)S(1)}, f32[4,5,16,256]{3,2,1,0:T(8,128)S(1)}, u32[]{:S(2)}, u32[]{:S(2)}) collective-permute-start(f32[4,5,16,256]{3,2,1,0:T(8,128)S(1)} %slice.119), channel_id=1, source_target_pairs={{0,4},{1,3},{2,6},{3,1},{4,0},{5,7},{6,2},{7,5},{8,12},{9,11},{10,... | collective-permute-start | bytes 983048 | tf_op jit(solution)/shard_map/ppermute | solution.py:502
  124.2 14.0 %collective-permute-start.33 = (f32[1,1024,128]{2,1,0:T(8,128)S(1)}, f32[1,1024,128]{2,1,0:T(8,128)S(1)}, u32[]{:S(2)}, u32[]{:S(2)}) collective-permute-start(f32[1,1024,128]{2,1,0:T(8,128)S(1)} %slice.131), channel_id=1, source_target_pairs={{0,4},{1,3},{2,6},{3,1},{4,0},{5,7},{6,2},{7,5},{8,12},{9,11},{10,... | collective-permute-start | bytes 1572872 | tf_op jit(solution)/shard_map/ppermute | solution.py:502
  130.6 5.4 %collective-permute-start.15 = (f32[2,5,16,256]{3,2,1,0:T(8,128)S(1)}, f32[2,5,16,256]{3,2,1,0:T(8,128)S(1)}, u32[]{:S(2)}, u32[]{:S(2)}) collective-permute-start(f32[2,5,16,256]{3,2,1,0:T(8,128)S(1)} %slice.93), channel_id=1, source_target_pairs={{0,8},{1,9},{2,10},{3,11},{4,12},{5,13},{6,14},{7,15},{8,0},{9,1},... | collective-permute-start | bytes 491528 | tf_op jit(solution)/shard_map/ppermute | solution.py:502
  136.1 5.7 %collective-permute-start.16 = (f32[1,5,16,256]{3,2,1,0:T(8,128)S(1)}, f32[1,5,16,256]{3,2,1,0:T(8,128)S(1)}, u32[]{:S(2)}, u32[]{:S(2)}) collective-permute-start(f32[1,5,16,256]{3,2,1,0:T(8,128)S(1)} %slice.121), channel_id=1, source_target_pairs={{0,16},{1,17},{2,18},{3,19},{4,20},{5,21},{6,22},{7,23},{8,24},{9,... | collective-permute-start | bytes 245768 | tf_op jit(solution)/shard_map/ppermute | solution.py:502
  138.3 10.9 %collective-permute-start.34 = (f32[1,512,128]{2,1,0:T(8,128)S(1)}, f32[1,512,128]{2,1,0:T(8,128)S(1)}, u32[]{:S(2)}, u32[]{:S(2)}) collective-permute-start(f32[1,512,128]{2,1,0:T(8,128)S(1)} %slice.133), channel_id=1, source_target_pairs={{0,8},{1,9},{2,10},{3,11},{4,12},{5,13},{6,14},{7,15},{8,0},{9,1},... | collective-permute-start | bytes 786440 | tf_op jit(solution)/shard_map/ppermute | solution.py:502
  141.8 5.5 %collective-permute-start.17 = (f32[1,5,16,256]{3,2,1,0:T(8,128)S(1)}, f32[1,5,16,256]{3,2,1,0:T(8,128)S(1)}, u32[]{:S(2)}, u32[]{:S(2)}) collective-permute-start(f32[1,5,16,256]{3,2,1,0:T(8,128)S(1)} %get-tuple-element.79), channel_id=1, source_target_pairs={{0,16},{1,17},{2,18},{3,19},{4,20},{5,21},{6,22},{7,23},{8,24},{9,... | collective-permute-start | bytes 245768 | tf_op jit(solution)/shard_map/ppermute | solution.py:502
  144.6 25.2 %collective-permute-start.23 = (f32[2,1024,128]{2,1,0:T(8,128)S(1)}, f32[2,1024,128]{2,1,0:T(8,128)S(1)}, u32[]{:S(2)}, u32[]{:S(2)}) collective-permute-start(f32[2,1024,128]{2,1,0:T(8,128)S(1)} %slice.97), channel_id=1, source_target_pairs={{0,2},{1,5},{2,0},{3,7},{4,6},{5,1},{6,4},{7,3},{8,10},{9,13},{10,... | collective-permute-start | bytes 3145736 | tf_op jit(solution)/shard_map/ppermute | solution.py:502
  147.3 5.4 %collective-permute-start.18 = (f32[2,5,16,256]{3,2,1,0:T(8,128)S(1)}, f32[2,5,16,256]{3,2,1,0:T(8,128)S(1)}, u32[]{:S(2)}, u32[]{:S(2)}) collective-permute-start(f32[2,5,16,256]{3,2,1,0:T(8,128)S(1)} %pad_maximum_fusion.9), channel_id=1, source_target_pairs={{0,8},{1,9},{2,10},{3,11},{4,12},{5,13},{6,14},{7,15},{8,0},{9,1},... | collective-permute-start | bytes 491528 | tf_op jit(solution)/shard_map/ppermute | solution.py:502
  149.3 9.3 %collective-permute-start.35 = (f32[1,256,128]{2,1,0:T(8,128)S(1)}, f32[1,256,128]{2,1,0:T(8,128)S(1)}, u32[]{:S(2)}, u32[]{:S(2)}) collective-permute-start(f32[1,256,128]{2,1,0:T(8,128)S(1)} %slice.135), channel_id=1, source_target_pairs={{0,16},{1,17},{2,18},{3,19},{4,20},{5,21},{6,22},{7,23},{8,24},{9,... | collective-permute-start | bytes 393224 | tf_op jit(solution)/shard_map/ppermute | solution.py:502
  152.7 7.8 %collective-permute-start.19 = (f32[4,5,16,256]{3,2,1,0:T(8,128)S(1)}, f32[4,5,16,256]{3,2,1,0:T(8,128)S(1)}, u32[]{:S(2)}, u32[]{:S(2)}) collective-permute-start(f32[4,5,16,256]{3,2,1,0:T(8,128)S(1)} %pad_maximum_fusion.6), channel_id=1, source_target_pairs={{0,4},{1,3},{2,6},{3,1},{4,0},{5,7},{6,2},{7,5},{8,12},{9,11},{10,... | collective-permute-start | bytes 983048 | tf_op jit(solution)/shard_map/ppermute | solution.py:502
  158.6 7.9 %collective-permute-start.36 = (f32[1,256,128]{2,1,0:T(8,128)S(1)}, f32[1,256,128]{2,1,0:T(8,128)S(1)}, u32[]{:S(2)}, u32[]{:S(2)}) collective-permute-start(f32[1,256,128]{2,1,0:T(8,128)S(1)} %slice_add_fusion.11), channel_id=1, source_target_pairs={{0,16},{1,17},{2,18},{3,19},{4,20},{5,21},{6,22},{7,23},{8,24},{9,... | collective-permute-start | bytes 393224 | tf_op jit(solution)/shard_map/ppermute | solution.py:502
  160.6 17.8 %collective-permute-start.20 = (f32[8,5,16,256]{3,2,1,0:T(8,128)S(1)}, f32[8,5,16,256]{3,2,1,0:T(8,128)S(1)}, u32[]{:S(2)}, u32[]{:S(2)}) collective-permute-start(f32[8,5,16,256]{3,2,1,0:T(8,128)S(1)} %pad_maximum_fusion.2), channel_id=1, source_target_pairs={{0,2},{1,5},{2,0},{3,7},{4,6},{5,1},{6,4},{7,3},{8,10},{9,13},{10,... | collective-permute-start | bytes 1966088 | tf_op jit(solution)/shard_map/ppermute | solution.py:502
  166.5 45.5 %collective-permute-start.37 = (f32[1,512,128]{2,1,0:T(8,128)S(1)}, f32[1,512,128]{2,1,0:T(8,128)S(1)}, u32[]{:S(2)}, u32[]{:S(2)}) collective-permute-start(f32[1,512,128]{2,1,0:T(8,128)S(1)} %pad_maximum_fusion.8), channel_id=1, source_target_pairs={{0,8},{1,9},{2,10},{3,11},{4,12},{5,13},{6,14},{7,15},{8,0},{9,1},... | collective-permute-start | bytes 786440 | tf_op jit(solution)/shard_map/ppermute | solution.py:502
  169.9 22.5 %collective-permute-start.24 = (f32[1,1024,128]{2,1,0:T(8,128)S(1)}, f32[1,1024,128]{2,1,0:T(8,128)S(1)}, u32[]{:S(2)}, u32[]{:S(2)}) collective-permute-start(f32[1,1024,128]{2,1,0:T(8,128)S(1)} %slice.123), channel_id=1, source_target_pairs={{0,4},{1,3},{2,6},{3,1},{4,0},{5,7},{6,2},{7,5},{8,12},{9,11},{10,... | collective-permute-start | bytes 1572872 | tf_op jit(solution)/shard_map/ppermute | solution.py:502
  192.5 7.4 %collective-permute-start.25 = (f32[1,512,128]{2,1,0:T(8,128)S(1)}, f32[1,512,128]{2,1,0:T(8,128)S(1)}, u32[]{:S(2)}, u32[]{:S(2)}) collective-permute-start(f32[1,512,128]{2,1,0:T(8,128)S(1)} %slice.125), channel_id=1, source_target_pairs={{0,8},{1,9},{2,10},{3,11},{4,12},{5,13},{6,14},{7,15},{8,0},{9,1},... | collective-permute-start | bytes 786440 | tf_op jit(solution)/shard_map/ppermute | solution.py:502
  200.0 12.0 %collective-permute-start.26 = (f32[1,256,128]{2,1,0:T(8,128)S(1)}, f32[1,256,128]{2,1,0:T(8,128)S(1)}, u32[]{:S(2)}, u32[]{:S(2)}) collective-permute-start(f32[1,256,128]{2,1,0:T(8,128)S(1)} %slice.127), channel_id=1, source_target_pairs={{0,16},{1,17},{2,18},{3,19},{4,20},{5,21},{6,22},{7,23},{8,24},{9,... | collective-permute-start | bytes 393224 | tf_op jit(solution)/shard_map/ppermute | solution.py:502
  211.9 17.9 %collective-permute-start.21 = (f32[512,512]{1,0:T(8,128)S(1)}, f32[512,512]{1,0:T(8,128)S(1)}, u32[]{:S(2)}, u32[]{:S(2)}) collective-permute-start(f32[512,512]{1,0:T(8,128)S(1)} %factor.5.own_ref), channel_id=1, source_target_pairs={{0,1},{1,0},{2,3},{3,2},{4,5},{5,4},{6,7},{7,6},{8,9},{9,8},{10,11... | collective-permute-start | bytes 3145736 | tf_op jit(solution)/shard_map/ppermute | solution.py:502
  212.0 9.1 %collective-permute-start.27 = (f32[1,256,128]{2,1,0:T(8,128)S(1)}, f32[1,256,128]{2,1,0:T(8,128)S(1)}, u32[]{:S(2)}, u32[]{:S(2)}) collective-permute-start(f32[1,256,128]{2,1,0:T(8,128)S(1)} %slice_add_fusion.12), channel_id=1, source_target_pairs={{0,16},{1,17},{2,18},{3,19},{4,20},{5,21},{6,22},{7,23},{8,24},{9,... | collective-permute-start | bytes 393224 | tf_op jit(solution)/shard_map/ppermute | solution.py:502
  212.1 17.5 %collective-permute-start.38 = (f32[1,1024,128]{2,1,0:T(8,128)S(1)}, f32[1,1024,128]{2,1,0:T(8,128)S(1)}, u32[]{:S(2)}, u32[]{:S(2)}) collective-permute-start(f32[1,1024,128]{2,1,0:T(8,128)S(1)} %pad_maximum_fusion.4), channel_id=1, source_target_pairs={{0,4},{1,3},{2,6},{3,1},{4,0},{5,7},{6,2},{7,5},{8,12},{9,11},{10,... | collective-permute-start | bytes 1572872 | tf_op jit(solution)/shard_map/ppermute | solution.py:502
  221.1 8.3 %collective-permute-start.28 = (f32[1,512,128]{2,1,0:T(8,128)S(1)}, f32[1,512,128]{2,1,0:T(8,128)S(1)}, u32[]{:S(2)}, u32[]{:S(2)}) collective-permute-start(f32[1,512,128]{2,1,0:T(8,128)S(1)} %pad_maximum_fusion.7), channel_id=1, source_target_pairs={{0,8},{1,9},{2,10},{3,11},{4,12},{5,13},{6,14},{7,15},{8,0},{9,1},... | collective-permute-start | bytes 786440 | tf_op jit(solution)/shard_map/ppermute | solution.py:502
  221.2 8.5 %collective-permute-start.22 = (f32[256,512]{1,0:T(8,128)S(1)}, f32[256,512]{1,0:T(8,128)S(1)}, u32[]{:S(2)}, u32[]{:S(2)}) collective-permute-start(f32[256,512]{1,0:T(8,128)S(1)} %get-tuple-element.68.gown_ref), channel_id=1, source_target_pairs={{0,1},{1,0},{2,3},{3,2},{4,5},{5,4},{6,7},{7,6},{8,9},{9,8},{10,11... | collective-permute-start | bytes 1572872 | tf_op jit(solution)/shard_map/ppermute | solution.py:502
  229.5 9.8 %collective-permute-start.29 = (f32[1,1024,128]{2,1,0:T(8,128)S(1)}, f32[1,1024,128]{2,1,0:T(8,128)S(1)}, u32[]{:S(2)}, u32[]{:S(2)}) collective-permute-start(f32[1,1024,128]{2,1,0:T(8,128)S(1)} %pad_maximum_fusion.3), channel_id=1, source_target_pairs={{0,4},{1,3},{2,6},{3,1},{4,0},{5,7},{6,2},{7,5},{8,12},{9,11},{10,... | collective-permute-start | bytes 1572872 | tf_op jit(solution)/shard_map/ppermute | solution.py:502
  234.5 15.0 %collective-permute-start.39 = (f32[2,1024,128]{2,1,0:T(8,128)S(1)}, f32[2,1024,128]{2,1,0:T(8,128)S(1)}, u32[]{:S(2)}, u32[]{:S(2)}) collective-permute-start(f32[2,1024,128]{2,1,0:T(8,128)S(1)} %solve.3.wa_ref), channel_id=1, source_target_pairs={{0,2},{1,5},{2,0},{3,7},{4,6},{5,1},{6,4},{7,3},{8,10},{9,13},{10,... | collective-permute-start | bytes 3145736 | tf_op jit(solution)/shard_map/ppermute | solution.py:502
  244.1 16.9 %collective-permute-start.30 = (f32[2,1024,128]{2,1,0:T(8,128)S(1)}, f32[2,1024,128]{2,1,0:T(8,128)S(1)}, u32[]{:S(2)}, u32[]{:S(2)}) collective-permute-start(f32[2,1024,128]{2,1,0:T(8,128)S(1)} %solve.2.wa_ref), channel_id=1, source_target_pairs={{0,2},{1,5},{2,0},{3,7},{4,6},{5,1},{6,4},{7,3},{8,10},{9,13},{10,... | collective-permute-start | bytes 3145736 | tf_op jit(solution)/shard_map/ppermute | solution.py:502
  248.2 12.9 %collective-permute-start.42 = (f32[2,1024,128]{2,1,0:T(8,128)S(1)}, f32[2,1024,128]{2,1,0:T(8,128)S(1)}, u32[]{:S(2)}, u32[]{:S(2)}) collective-permute-start(f32[2,1024,128]{2,1,0:T(8,128)S(1)} %solve.3.wa_ref), channel_id=1, source_target_pairs={{0,1},{1,0},{2,3},{3,2},{4,5},{5,4},{6,7},{7,6},{8,9},{9,8},{10,11... | collective-permute-start | bytes 3145736 | tf_op jit(solution)/shard_map/ppermute | solution.py:502
  248.2 19.0 %collective-permute-start.41 = (f32[2,1024,128]{2,1,0:T(8,128)S(1)}, f32[2,1024,128]{2,1,0:T(8,128)S(1)}, u32[]{:S(2)}, u32[]{:S(2)}) collective-permute-start(f32[2,1024,128]{2,1,0:T(8,128)S(1)} %solve.2.wa_ref), channel_id=1, source_target_pairs={{0,1},{1,0},{2,3},{3,2},{4,5},{5,4},{6,7},{7,6},{8,9},{9,8},{10,11... | collective-permute-start | bytes 3145736 | tf_op jit(solution)/shard_map/ppermute | solution.py:502
  249.5 23.9 %collective-permute-start.40 = (f32[2,1024,128]{2,1,0:T(8,128)S(1)}, f32[2,1024,128]{2,1,0:T(8,128)S(1)}, u32[]{:S(2)}, u32[]{:S(2)}) collective-permute-start(f32[2,1024,128]{2,1,0:T(8,128)S(1)} %collective-permute-done.39.wa_ref), channel_id=1, source_target_pairs={{0,1},{1,0},{2,3},{3,2},{4,5},{5,4},{6,7},{7,6},{8,9},{9,8},{10,11... | collective-permute-start | bytes 3145736 | tf_op jit(solution)/shard_map/ppermute | solution.py:502
  261.0 22.2 %collective-permute-start.31 = (f32[2,1024,128]{2,1,0:T(8,128)S(1)}, f32[2,1024,128]{2,1,0:T(8,128)S(1)}, u32[]{:S(2)}, u32[]{:S(2)}) collective-permute-start(f32[2,1024,128]{2,1,0:T(8,128)S(1)} %collective-permute-done.30.wa_ref.wb_ref), channel_id=1, source_target_pairs={{0,1},{1,0},{2,3},{3,2},{4,5},{5,4},{6,7},{7,6},{8,9},{9,8},{10,11... | collective-permute-start | bytes 3145736 | tf_op jit(solution)/shard_map/ppermute | solution.py:502
  (1 other events, 0.7 us)
